TPU v7x, 32 devices: a whole 2x2x4 slice. The times are simulated.
32 devices in a mesh: fsdp: 32 (over z, y, x, core).
Axes of the slice: x: 2, y: 2, z: 4, core: 2. Of those that a mesh axis runs over, the one named last changes fastest.
Arguments:
- tokens: bfloat16 [32768, 768], P('fsdp'), may hold values from -6 to 6
- neighbours: bfloat16 [32768, 768], P('fsdp'), may hold values from -6 to 6
- block_lengths: int32 [64, 4], P('fsdp'), may hold values from 1 to 256, 512 in all within a row
- chosen: int32 [64, 8, 2], P('fsdp'), may hold values from 0 to 3
- cotangent: bfloat16 [32768, 768], P('fsdp'), may hold values from -6 to 6
- w_qkv: bfloat16 [768, 2304], P('fsdp'), may hold values from -0.21875 to 0.21875
- w_out: bfloat16 [768, 768], P('fsdp'), may hold values from -2 to 2
- w_cross_q: bfloat16 [768, 768], P('fsdp'), may hold values from -0.21875 to 0.21875
- w_cross_kv: bfloat16 [768, 1536], P('fsdp'), may hold values from -0.21875 to 0.21875
- w_cross_out: bfloat16 [768, 768], P('fsdp'), may hold values from -2 to 2
- w_up: bfloat16 [768, 3072], P('fsdp'), may hold values from -0.21875 to 0.21875
- w_down: bfloat16 [3072, 768], P('fsdp'), may hold values from -0.109375 to 0.109375
- biases: bfloat16 [8, 768], P(None, 'fsdp'), may hold values from -1.5 to 1.5
- up_bias: bfloat16 [3072], P('fsdp'), may hold values from -1.5 to 1.5
- norm_gains: bfloat16 [3, 768], P(None, 'fsdp'), may hold values from 0.25 to 1.75
- norm_shifts: bfloat16 [3, 768], P(None, 'fsdp'), may hold values from -1.5 to 1.5
Outputs:
- output: bfloat16 [32768, 768], P('fsdp')
- token_grad: float32 [32768, 768], P('fsdp')
- neighbour_grad: float32 [32768, 768], P('fsdp')
- grad_w_qkv: float32 [768, 2304], P('fsdp')
- grad_w_out: float32 [768, 768], P('fsdp')
- grad_w_cross_q: float32 [768, 768], P('fsdp')
- grad_w_cross_kv: float32 [768, 1536], P('fsdp')
- grad_w_cross_out: float32 [768, 768], P('fsdp')
- grad_w_up: float32 [768, 3072], P('fsdp')
- grad_w_down: float32 [3072, 768], P('fsdp')
- grad_biases: float32 [8, 768], P(None, 'fsdp')
- grad_up_bias: float32 [3072], P('fsdp')
- grad_norm_gains: float32 [3, 768], P(None, 'fsdp')
- grad_norm_shifts: float32 [3, 768], P(None, 'fsdp')
Inputs may be any that keep to these rules, and one draw needn't show every extreme that they name: `block_lengths`: each row holds the lengths of the 4 consecutive attention blocks of one sequence; they sum to 512, and the longest in every row is exactly 256. chosen[s, c, i] is an entry of sequence s's own 4 neighbours; two slots of a span may name the same entry.
All inputs are finite; a program needn't handle non-finite values.
Results may differ from a plain program's by a relative error of at most 0.02.
Values may be sent and summed in bfloat16 or wider, within the bound.
No kernel may reach another device: no remote copies, remote signals or barrier semaphores. Data moves between devices by JAX's collectives and lax.ppermute only.
A program may use at most 320 MiB of HBM per device.

v0:
```python
import math

import jax
import jax.numpy as jnp
from jax import lax
from jax.sharding import PartitionSpec as P

D = 768
HEADS = 12
HEAD_DIM = 64
SEQ_LEN = 512
SPAN = 64
NBR_LEN = 128
K_NBR = 2
POOL = 4
MICRO = 2
SEQS_MB = 1
SPANS = 8


epsilon = 1e-05
rope_base = 10000.0
gelu_coeff = 0.044715
highest = lax.Precision.HIGHEST
column_kinds = (7, 9, 10)


def norm_forward(inputs, gain_row, shift_row):
    average = jnp.mean(inputs, -1, keepdims=True)
    centred = inputs - average
    inverse = lax.rsqrt(jnp.mean(centred * centred, -1, keepdims=True) + epsilon)
    normed = centred * inverse
    return (normed * gain_row + shift_row, normed, inverse)


def norm_backward(incoming, normed, inverse, gain_row):
    scaled = incoming * gain_row
    inner = (
        scaled
        - jnp.mean(scaled, -1, keepdims=True)
        - normed * jnp.mean(scaled * normed, -1, keepdims=True)
    )
    return (inner * inverse, jnp.sum(incoming * normed, 0), jnp.sum(incoming, 0))


def rotary_tables():
    half_dim = HEAD_DIM // 2
    inverse = jnp.exp(
        jnp.arange(half_dim, dtype=jnp.float32) * (-2.0 * math.log(rope_base) / HEAD_DIM)
    )
    angles = jnp.arange(SEQ_LEN, dtype=jnp.float32)[:, None] * inverse[None, :]
    return (jnp.cos(angles)[:, None, :], jnp.sin(angles)[:, None, :])


def rotate(inputs, cosine, sine, turning):
    half_dim = HEAD_DIM // 2
    first_half = inputs[..., :half_dim]
    second_half = inputs[..., half_dim:]
    turned = sine * turning
    return jnp.concatenate(
        [first_half * cosine - second_half * turned, second_half * cosine + first_half * turned], -1
    )


def gelu_pair(hidden):
    root_coeff = math.sqrt(2.0 / math.pi)
    tangent = jnp.tanh(root_coeff * (hidden + gelu_coeff * hidden**3))
    result = 0.5 * hidden * (1.0 + tangent)
    slope_value = 0.5 * (1.0 + tangent) + 0.5 * hidden * (1.0 - tangent * tangent) * root_coeff * (
        1.0 + 3.0 * gelu_coeff * hidden * hidden
    )
    return (result, slope_value)


def block_index(lengths):
    block_ends = jnp.cumsum(lengths)
    positions = jnp.arange(SEQ_LEN, dtype=jnp.int32)
    return jnp.sum((positions[:, None] >= block_ends[None, :]).astype(jnp.int32), -1)


def softmax_grad(probability, grad_prob):
    return (probability * (grad_prob - jnp.sum(probability * grad_prob, -1, keepdims=True))).astype(
        jnp.bfloat16
    )


def self_scores(queries, key_rows, lengths):
    block_ids = block_index(lengths)
    allowed = block_ids[None, :] <= block_ids[:, None]
    scores = jnp.einsum(
        "qhe,khe->hqk", queries, key_rows, preferred_element_type=jnp.float32
    ) * HEAD_DIM ** (-0.5)
    return jnp.where(allowed[None], scores, -1e30)


def self_forward(packed):
    queries, key_rows, value_rows, lengths = packed
    scores = self_scores(queries, key_rows, lengths)
    row_max = jnp.max(scores, -1, keepdims=True)
    exponent = jnp.exp(scores - row_max)
    row_total = jnp.sum(exponent, -1, keepdims=True)
    weights = (exponent / row_total).astype(jnp.bfloat16)
    attended = jnp.einsum("hqk,khe->qhe", weights, value_rows, preferred_element_type=jnp.float32)
    return (attended.astype(jnp.bfloat16), (row_max + jnp.log(row_total))[..., 0])


def self_backward(packed):
    queries, key_rows, value_rows, lengths, log_total, upstream = packed
    probability = jnp.exp(self_scores(queries, key_rows, lengths) - log_total[..., None])
    grad_prob = jnp.einsum("qhe,khe->hqk", upstream, value_rows, preferred_element_type=jnp.float32)
    grad_score = softmax_grad(probability, grad_prob)
    grad_query = jnp.einsum(
        "hqk,khe->qhe", grad_score, key_rows, preferred_element_type=jnp.float32
    ) * HEAD_DIM ** (-0.5)
    grad_key = jnp.einsum(
        "hqk,qhe->khe", grad_score, queries, preferred_element_type=jnp.float32
    ) * HEAD_DIM ** (-0.5)
    grad_value = jnp.einsum(
        "hqk,qhe->khe",
        probability.astype(jnp.bfloat16),
        upstream,
        preferred_element_type=jnp.float32,
    )
    return (grad_query, grad_key, grad_value)


def chosen_pool(key_pool, value_pool, chosen_rows):
    key_rows = jnp.take(key_pool, chosen_rows, axis=0).reshape(
        SPANS, K_NBR * NBR_LEN, HEADS, HEAD_DIM
    )
    value_rows = jnp.take(value_pool, chosen_rows, axis=0).reshape(
        SPANS, K_NBR * NBR_LEN, HEADS, HEAD_DIM
    )
    return (key_rows, value_rows)


def cross_forward(packed):
    queries, key_pool, value_pool, chosen_rows = packed
    key_rows, value_rows = chosen_pool(key_pool, value_pool, chosen_rows)
    query_blocks = queries.reshape(SPANS, SPAN, HEADS, HEAD_DIM)
    scores = jnp.einsum(
        "cqhe,ckhe->chqk", query_blocks, key_rows, preferred_element_type=jnp.float32
    ) * HEAD_DIM ** (-0.5)
    row_max = jnp.max(scores, -1, keepdims=True)
    exponent = jnp.exp(scores - row_max)
    row_total = jnp.sum(exponent, -1, keepdims=True)
    weights = (exponent / row_total).astype(jnp.bfloat16)
    attended = jnp.einsum(
        "chqk,ckhe->cqhe", weights, value_rows, preferred_element_type=jnp.float32
    )
    return (
        attended.astype(jnp.bfloat16).reshape(SEQ_LEN, HEADS, HEAD_DIM),
        (row_max + jnp.log(row_total))[..., 0],
    )


def cross_backward(packed):
    queries, key_pool, value_pool, chosen_rows, log_total, upstream = packed
    key_rows, value_rows = chosen_pool(key_pool, value_pool, chosen_rows)
    query_blocks = queries.reshape(SPANS, SPAN, HEADS, HEAD_DIM)
    upstream_blocks = upstream.reshape(SPANS, SPAN, HEADS, HEAD_DIM)
    scores = jnp.einsum(
        "cqhe,ckhe->chqk", query_blocks, key_rows, preferred_element_type=jnp.float32
    ) * HEAD_DIM ** (-0.5)
    probability = jnp.exp(scores - log_total[..., None])
    grad_prob = jnp.einsum(
        "cqhe,ckhe->chqk", upstream_blocks, value_rows, preferred_element_type=jnp.float32
    )
    grad_score = softmax_grad(probability, grad_prob)
    grad_query = jnp.einsum(
        "chqk,ckhe->cqhe", grad_score, key_rows, preferred_element_type=jnp.float32
    ) * HEAD_DIM ** (-0.5)
    grad_key = jnp.einsum(
        "chqk,cqhe->ckhe", grad_score, query_blocks, preferred_element_type=jnp.float32
    ) * HEAD_DIM ** (-0.5)
    grad_value = jnp.einsum(
        "chqk,cqhe->ckhe",
        probability.astype(jnp.bfloat16),
        upstream_blocks,
        preferred_element_type=jnp.float32,
    )
    selector = (
        chosen_rows.reshape(SPANS * K_NBR, 1) == jnp.arange(POOL, dtype=jnp.int32)[None, :]
    ).astype(jnp.float32)
    flat_width = NBR_LEN * HEADS * HEAD_DIM
    grad_key_pool = jnp.einsum(
        "cp,cm->pm", selector, grad_key.reshape(SPANS * K_NBR, flat_width), precision=highest
    )
    grad_value_pool = jnp.einsum(
        "cp,cm->pm", selector, grad_value.reshape(SPANS * K_NBR, flat_width), precision=highest
    )
    pool_shape = (POOL * NBR_LEN, HEADS * HEAD_DIM)
    return (
        grad_query.reshape(SEQ_LEN, HEADS, HEAD_DIM),
        grad_key_pool.reshape(pool_shape),
        grad_value_pool.reshape(pool_shape),
    )


def layer_forward(gathered, token_rows, neighbour_rows, lengths, chosen_rows, cosine, sine):
    (
        qkv_weight,
        out_weight,
        cq_weight,
        ckv_weight,
        co_weight,
        up_weight,
        down_weight,
        bias_rows,
        up_shift,
        gain_rows,
        shift_rows,
    ) = gathered
    bias_float = bias_rows.astype(jnp.float32)
    gain_float = gain_rows.astype(jnp.float32)
    shift_float = shift_rows.astype(jnp.float32)
    seq_count = lengths.shape[0]
    row_count = token_rows.shape[0]
    inputs = token_rows.astype(jnp.float32)
    attn_in, first_normed, first_inverse = norm_forward(inputs, gain_float[0], shift_float[0])
    attn_low = attn_in.astype(jnp.bfloat16)
    bias_qkv = jnp.concatenate([bias_float[0], bias_float[1], bias_float[2]])
    mixed_rows = (
        jnp.dot(attn_low, qkv_weight, preferred_element_type=jnp.float32) + bias_qkv
    ).reshape(seq_count, SEQ_LEN, 3, HEADS, HEAD_DIM)
    queries = rotate(mixed_rows[:, :, 0], cosine, sine, 1.0).astype(jnp.bfloat16)
    key_rows = rotate(mixed_rows[:, :, 1], cosine, sine, 1.0).astype(jnp.bfloat16)
    value_rows = mixed_rows[:, :, 2].astype(jnp.bfloat16)
    attended, self_total = lax.map(self_forward, (queries, key_rows, value_rows, lengths))
    attended = attended.reshape(row_count, D)
    first_sum = (
        inputs + jnp.dot(attended, out_weight, preferred_element_type=jnp.float32) + bias_float[3]
    )
    cross_in, second_normed, second_inverse = norm_forward(first_sum, gain_float[1], shift_float[1])
    cross_low = cross_in.astype(jnp.bfloat16)
    cross_queries = (
        (jnp.dot(cross_low, cq_weight, preferred_element_type=jnp.float32) + bias_float[4])
        .astype(jnp.bfloat16)
        .reshape(seq_count, SEQ_LEN, HEADS, HEAD_DIM)
    )
    kv_bias = jnp.concatenate([jnp.zeros_like(bias_float[5]), bias_float[5]])
    kv_pool = (
        (jnp.dot(neighbour_rows, ckv_weight, preferred_element_type=jnp.float32) + kv_bias)
        .astype(jnp.bfloat16)
        .reshape(seq_count, POOL * NBR_LEN, 2, HEADS, HEAD_DIM)
    )
    key_pool = kv_pool[:, :, 0].reshape(seq_count, POOL, NBR_LEN, HEADS, HEAD_DIM)
    value_pool = kv_pool[:, :, 1].reshape(seq_count, POOL, NBR_LEN, HEADS, HEAD_DIM)
    crossed, cross_total = lax.map(
        cross_forward, (cross_queries, key_pool, value_pool, chosen_rows)
    )
    crossed = crossed.reshape(row_count, D)
    second_sum = (
        first_sum + jnp.dot(crossed, co_weight, preferred_element_type=jnp.float32) + bias_float[6]
    )
    mlp_in, third_normed, third_inverse = norm_forward(second_sum, gain_float[2], shift_float[2])
    mlp_low = mlp_in.astype(jnp.bfloat16)
    hidden = jnp.dot(mlp_low, up_weight, preferred_element_type=jnp.float32) + up_shift.astype(
        jnp.float32
    )
    activated, gelu_slope = gelu_pair(hidden)
    act_low = activated.astype(jnp.bfloat16)
    result = (
        second_sum
        + jnp.dot(act_low, down_weight, preferred_element_type=jnp.float32)
        + bias_float[7]
    ).astype(jnp.bfloat16)
    saved = (
        attn_low,
        first_normed,
        first_inverse,
        queries,
        key_rows,
        value_rows,
        self_total,
        attended,
        cross_low,
        second_normed,
        second_inverse,
        cross_queries,
        key_pool,
        value_pool,
        cross_total,
        crossed,
        mlp_low,
        third_normed,
        third_inverse,
        gelu_slope,
        act_low,
    )
    return (result, saved)


def layer_backward(
    gathered, saved, neighbour_rows, lengths, chosen_rows, upstream_low, cosine, sine
):
    (
        qkv_weight,
        out_weight,
        cq_weight,
        ckv_weight,
        co_weight,
        up_weight,
        down_weight,
        bias_rows,
        up_shift,
        gain_rows,
        shift_rows,
    ) = gathered
    (
        attn_low,
        first_normed,
        first_inverse,
        queries,
        key_rows,
        value_rows,
        self_total,
        attended,
        cross_low,
        second_normed,
        second_inverse,
        cross_queries,
        key_pool,
        value_pool,
        cross_total,
        crossed,
        mlp_low,
        third_normed,
        third_inverse,
        gelu_slope,
        act_low,
    ) = saved
    gain_float = gain_rows.astype(jnp.float32)
    seq_count = lengths.shape[0]
    row_count = upstream_low.shape[0]
    upstream = upstream_low.astype(jnp.float32)
    grad_down = jnp.einsum("nf,nd->fd", act_low, upstream_low, preferred_element_type=jnp.float32)
    grad_act = jnp.einsum(
        "nd,fd->nf", upstream_low, down_weight, preferred_element_type=jnp.float32
    )
    grad_hidden = (grad_act * gelu_slope).astype(jnp.bfloat16)
    grad_up = jnp.einsum("nd,nf->df", mlp_low, grad_hidden, preferred_element_type=jnp.float32)
    grad_up_shift = jnp.sum(grad_hidden.astype(jnp.float32), 0)
    grad_mlp_in = jnp.einsum(
        "nf,df->nd", grad_hidden, up_weight, preferred_element_type=jnp.float32
    )
    norm_part, third_gain, third_shift = norm_backward(
        grad_mlp_in, third_normed, third_inverse, gain_float[2]
    )
    grad_second = upstream + norm_part
    second_low = grad_second.astype(jnp.bfloat16)
    grad_co = jnp.einsum("nd,ne->de", crossed, second_low, preferred_element_type=jnp.float32)
    grad_crossed = (
        jnp.einsum("ne,de->nd", second_low, co_weight, preferred_element_type=jnp.float32)
        .astype(jnp.bfloat16)
        .reshape(seq_count, SEQ_LEN, HEADS, HEAD_DIM)
    )
    grad_cq_rows, grad_key_pool, grad_value_pool = lax.map(
        cross_backward,
        (cross_queries, key_pool, value_pool, chosen_rows, cross_total, grad_crossed),
    )
    cq_low = grad_cq_rows.reshape(row_count, D).astype(jnp.bfloat16)
    grad_cq = jnp.einsum("nd,ne->de", cross_low, cq_low, preferred_element_type=jnp.float32)
    pool_rows = neighbour_rows.shape[0]
    pool_low = jnp.concatenate(
        [grad_key_pool.reshape(pool_rows, D), grad_value_pool.reshape(pool_rows, D)], -1
    ).astype(jnp.bfloat16)
    grad_ckv = jnp.einsum("nd,ne->de", neighbour_rows, pool_low, preferred_element_type=jnp.float32)
    neighbour_grad = jnp.einsum(
        "ne,de->nd", pool_low, ckv_weight, preferred_element_type=jnp.float32
    )
    grad_cross_in = jnp.einsum("ne,de->nd", cq_low, cq_weight, preferred_element_type=jnp.float32)
    norm_part, second_gain, second_shift = norm_backward(
        grad_cross_in, second_normed, second_inverse, gain_float[1]
    )
    grad_first = grad_second + norm_part
    first_low = grad_first.astype(jnp.bfloat16)
    grad_out = jnp.einsum("nd,ne->de", attended, first_low, preferred_element_type=jnp.float32)
    grad_attended = (
        jnp.einsum("ne,de->nd", first_low, out_weight, preferred_element_type=jnp.float32)
        .astype(jnp.bfloat16)
        .reshape(seq_count, SEQ_LEN, HEADS, HEAD_DIM)
    )
    grad_query, grad_key, grad_value = lax.map(
        self_backward, (queries, key_rows, value_rows, lengths, self_total, grad_attended)
    )
    grad_query = rotate(grad_query, cosine, sine, -1.0)
    grad_key = rotate(grad_key, cosine, sine, -1.0)
    mixed_low = (
        jnp.stack([grad_query, grad_key, grad_value], 2)
        .reshape(row_count, 3 * D)
        .astype(jnp.bfloat16)
    )
    grad_qkv = jnp.einsum("nd,ne->de", attn_low, mixed_low, preferred_element_type=jnp.float32)
    grad_attn_in = jnp.einsum(
        "ne,de->nd", mixed_low, qkv_weight, preferred_element_type=jnp.float32
    )
    norm_part, first_gain, first_shift = norm_backward(
        grad_attn_in, first_normed, first_inverse, gain_float[0]
    )
    token_grad = grad_first + norm_part
    qkv_sums = jnp.sum(mixed_low.astype(jnp.float32), 0).reshape(3, D)
    cross_sums = jnp.sum(pool_low.astype(jnp.float32), 0)
    grad_bias = jnp.stack(
        [
            qkv_sums[0],
            qkv_sums[1],
            qkv_sums[2],
            jnp.sum(first_low.astype(jnp.float32), 0),
            jnp.sum(cq_low.astype(jnp.float32), 0),
            cross_sums[D:],
            jnp.sum(second_low.astype(jnp.float32), 0),
            jnp.sum(upstream, 0),
        ]
    )
    gradients = (
        grad_qkv,
        grad_out,
        grad_cq,
        grad_ckv,
        grad_co,
        grad_up,
        grad_down,
        grad_bias,
        grad_up_shift,
        jnp.stack([first_gain, second_gain, third_gain]),
        jnp.stack([first_shift, second_shift, third_shift]),
    )
    return (gradients, token_grad, neighbour_grad)


def flatten_grads(gradients, count):
    pieces = []
    for index, grad in enumerate(gradients):
        oriented = grad.T if index in column_kinds else grad
        pieces.append(oriented.reshape(count, -1))
    return jnp.concatenate(pieces, 1)


def split_grads(summed, gradients, count):
    results = []
    offset = 0
    for index, grad in enumerate(gradients):
        width = grad.size // count
        piece = summed[0, offset : offset + width]
        offset = offset + width
        if index in column_kinds:
            results.append(piece.reshape(grad.shape[1] // count, grad.shape[0]).T)
        else:
            results.append(piece.reshape((grad.shape[0] // count,) + grad.shape[1:]))
    return tuple(results)


def fetch_params(
    w_qkv,
    w_out,
    w_cross_q,
    w_cross_kv,
    w_cross_out,
    w_up,
    w_down,
    biases,
    up_bias,
    norm_gains,
    norm_shifts,
):
    return (
        lax.all_gather(w_qkv, "fsdp", axis=0, tiled=True),
        lax.all_gather(w_out, "fsdp", axis=0, tiled=True),
        lax.all_gather(w_cross_q, "fsdp", axis=0, tiled=True),
        lax.all_gather(w_cross_kv, "fsdp", axis=0, tiled=True),
        lax.all_gather(w_cross_out, "fsdp", axis=0, tiled=True),
        lax.all_gather(w_up, "fsdp", axis=0, tiled=True),
        lax.all_gather(w_down, "fsdp", axis=0, tiled=True),
        lax.all_gather(biases, "fsdp", axis=1, tiled=True),
        lax.all_gather(up_bias, "fsdp", axis=0, tiled=True),
        lax.all_gather(norm_gains, "fsdp", axis=1, tiled=True),
        lax.all_gather(norm_shifts, "fsdp", axis=1, tiled=True),
    )


def local(
    tokens,
    neighbours,
    block_lengths,
    chosen,
    cotangent,
    w_qkv,
    w_out,
    w_cross_q,
    w_cross_kv,
    w_cross_out,
    w_up,
    w_down,
    biases,
    up_bias,
    norm_gains,
    norm_shifts,
):
    cosine, sine = rotary_tables()
    count = lax.axis_size("fsdp")
    token_block = SEQS_MB * SEQ_LEN
    pool_block = SEQS_MB * POOL * NBR_LEN
    result_list = []
    token_list = []
    neighbour_list = []
    running = None
    flat_sums = None
    last_grads = None
    for micro_step in range(MICRO):
        token_rows = tokens[micro_step * token_block : (micro_step + 1) * token_block]
        neighbour_rows = neighbours[micro_step * pool_block : (micro_step + 1) * pool_block]
        lengths = block_lengths[micro_step * SEQS_MB : (micro_step + 1) * SEQS_MB]
        chosen_rows = chosen[micro_step * SEQS_MB : (micro_step + 1) * SEQS_MB]
        upstream_low = cotangent[micro_step * token_block : (micro_step + 1) * token_block]
        forward_params = fetch_params(
            w_qkv,
            w_out,
            w_cross_q,
            w_cross_kv,
            w_cross_out,
            w_up,
            w_down,
            biases,
            up_bias,
            norm_gains,
            norm_shifts,
        )
        result, saved = layer_forward(
            forward_params, token_rows, neighbour_rows, lengths, chosen_rows, cosine, sine
        )
        backward_params = (
            lax.all_gather(w_qkv, "fsdp", axis=0, tiled=True),
            lax.all_gather(w_out, "fsdp", axis=0, tiled=True),
            lax.all_gather(w_cross_q, "fsdp", axis=0, tiled=True),
            lax.all_gather(w_cross_kv, "fsdp", axis=0, tiled=True),
            lax.all_gather(w_cross_out, "fsdp", axis=0, tiled=True),
            lax.all_gather(w_up, "fsdp", axis=0, tiled=True),
            lax.all_gather(w_down, "fsdp", axis=0, tiled=True),
            lax.all_gather(biases, "fsdp", axis=1, tiled=True),
            lax.all_gather(up_bias, "fsdp", axis=0, tiled=True),
            lax.all_gather(norm_gains, "fsdp", axis=1, tiled=True),
            lax.all_gather(norm_shifts, "fsdp", axis=1, tiled=True),
        )
        gradients, token_grad, neighbour_grad = layer_backward(
            backward_params, saved, neighbour_rows, lengths, chosen_rows, upstream_low, cosine, sine
        )
        last_grads = gradients
        result_list.append(result)
        token_list.append(token_grad)
        neighbour_list.append(neighbour_grad)
        running = (
            gradients
            if running is None
            else tuple((earlier + addition for earlier, addition in zip(running, gradients)))
        )
    flat_sums = lax.psum_scatter(
        flatten_grads(running, count), "fsdp", scatter_dimension=0, tiled=True
    )
    shard_sums = split_grads(flat_sums, last_grads, count)
    return (
        jnp.concatenate(result_list, 0),
        jnp.concatenate(token_list, 0),
        jnp.concatenate(neighbour_list, 0),
        shard_sums[0],
        shard_sums[1],
        shard_sums[2],
        shard_sums[3],
        shard_sums[4],
        shard_sums[5],
        shard_sums[6],
        shard_sums[7],
        shard_sums[8],
        shard_sums[9],
        shard_sums[10],
    )


def solution(mesh):
    placed = (
        P("fsdp", None),
        P("fsdp", None),
        P("fsdp", None),
        P("fsdp", None, None),
        P("fsdp", None),
        P("fsdp", None),
        P("fsdp", None),
        P("fsdp", None),
        P("fsdp", None),
        P("fsdp", None),
        P("fsdp", None),
        P("fsdp", None),
        P(None, "fsdp"),
        P("fsdp"),
        P(None, "fsdp"),
        P(None, "fsdp"),
    )
    return jax.shard_map(
        local,
        mesh=mesh,
        in_specs=placed,
        out_specs=(
            P("fsdp", None),
            P("fsdp", None),
            P("fsdp", None),
            P("fsdp", None),
            P("fsdp", None),
            P("fsdp", None),
            P("fsdp", None),
            P("fsdp", None),
            P("fsdp", None),
            P("fsdp", None),
            P(None, "fsdp"),
            P("fsdp"),
            P(None, "fsdp"),
            P(None, "fsdp"),
        ),
        check_vma=False,
    )
```

profile of v0, /device:TPU:0, one launch (start us, length us, event | category | flops | bytes accessed | tf_op | source)
XLA Modules:
  0.0 1504.9 jit_solution(10785163157468883335)
XLA Ops:
  16.2 43.9 %all-gather.2 = bf16[32,24,8]{1,2,0:T(8,128)(2,1)S(1)} all-gather(bf16[1,24,8]{1,2,0:T(8,128)(2,1)} %bitcast.355), channel_id=1, replica_groups=mesh['fsdp'=32] {'fsdp'}, dimensions={0}, use_global_device_ids=true | all-gather | bytes 12672 | tf_op jit(solution)/shard_map/all_gather | solution.py:475
  62.9 37.0 %all-gather.1 = bf16[32,24,3]{1,2,0:T(4,128)(2,1)S(1)} all-gather(bf16[1,24,3]{1,2,0:T(4,128)(2,1)} %bitcast.356), channel_id=1, replica_groups=mesh['fsdp'=32] {'fsdp'}, dimensions={0}, use_global_device_ids=true | all-gather | bytes 4752 | tf_op jit(solution)/shard_map/all_gather | solution.py:478
  100.7 38.4 %all-gather = bf16[32,24,3]{1,2,0:T(4,128)(2,1)S(1)} all-gather(bf16[1,24,3]{1,2,0:T(4,128)(2,1)} %bitcast.357), channel_id=1, replica_groups=mesh['fsdp'=32] {'fsdp'}, dimensions={0}, use_global_device_ids=true | all-gather | bytes 4752 | tf_op jit(solution)/shard_map/all_gather | solution.py:477
  151.7 37.5 %all-reduce.1 = bf16[3072]{0:T(1024)(128)(2,1)} all-reduce(bf16[3072]{0:T(1024)(128)(2,1)} %dynamic-update-slice), channel_id=1, replica_groups=mesh['fsdp'=32] {'fsdp'}, use_global_device_ids=true, to_apply=%add.1 | all-reduce | flops 3072 | bytes 12288
  241.0 6.4 select_bitcast_fusion.1
  250.8 6.3 convolution_add_fusion.4
  257.1 6.3 copy.372
  271.4 6.0 copy.386
  289.5 6.1 fusion.128
  371.5 7.4 fusion.202
  383.7 46.0 %all-gather.23.cloned.1.call-done = bf16[3072,768]{1,0:T(8,128)(2,1)} async-done(((bf16[96,768]{1,0:T(8,128)(2,1)}), bf16[3072,768]{1,0:T(8,128)(2,1)}) %all-gather.23.cloned.1.call-update) | async-done | bytes 4718608 | tf_op jit(solution)/shard_map/all_gather | solution.py:474
  429.6 9.4 convert_reduce_fusion
  439.1 6.1 fusion.212
  446.3 7.2 convert_reduce_fusion.1
  469.3 7.0 multiply_reduce_fusion.3
  498.3 7.0 multiply_reduce_fusion.2
  514.2 6.5 convert_reduce_fusion.15
  524.8 13.4 multiply_reduce_fusion.1
  538.3 7.1 multiply_convert_fusion.1
  556.4 7.8 fusion.125
  564.3 9.8 multiply_reduce_fusion
  574.2 10.8 multiply_convert_fusion
  621.9 5.6 fusion.200
  627.5 6.2 fusion.141
  633.7 13.6 copy.416
  647.3 14.2 reshape.792
  666.8 13.6 copy.418
  680.4 14.4 reshape.794
  705.5 13.6 copy.421
  719.1 14.2 reshape.796
  739.5 13.6 copy.423
  753.1 14.6 reshape.798
  767.6 5.4 convolution_convert_fusion
  786.7 5.3 convolution_add_fusion
  791.9 6.7 reshape.800
  798.7 6.5 constant_dynamic-update-slice_fusion.10
  819.4 6.1 add_bitcast_fusion
  825.5 6.1 copy.424
  831.5 5.4 reshape.803
  843.9 8.6 convolution_add_fusion.2
  852.6 8.2 reshape.805
  860.7 12.9 convolution_add_fusion.1
  873.7 8.3 reshape.806
  898.8 5.5 constant_dynamic-update-slice_fusion.7
  905.9 5.4 constant_dynamic-update-slice_fusion.5
  924.1 9.5 add_convert_fusion
  933.7 8.5 add_convert_fusion.4
  954.4 523.0 %all-reduce.5.cloned.1.call-done = f32[32,295344]{1,0:T(8,128)} async-done(((f32[32,295344]{1,0:T(8,128)}), f32[32,295344]{1,0:T(8,128)}) %all-reduce.5.cloned.1.call-update) | async-done | bytes 37804048
  (762 shorter events, 399.2 us)
Async XLA Ops:
  7.2 132.8 %copy-start.14 = (bf16[1024,768]{1,0:T(8,128)(2,1)S(1)}, bf16[1024,768]{1,0:T(8,128)(2,1)}, u32[]{:S(2)}) copy-start(bf16[1024,768]{1,0:T(8,128)(2,1)} %param.18) | copy-start | bytes 4718596
  7.2 196.6 %all-gather.15.cloned.1.call-start = ((), (), s32[]{:S(2)}) async-start(), calls=%async_computation.2 | async-start | bytes 2433024 | tf_op jit(solution)/shard_map/all_gather | solution.py:471
  7.9 242.9 %all-gather.11.cloned.1.call-start = ((), (), s32[]{:S(2)}) async-start(), calls=%async_computation | async-start | bytes 3649536 | tf_op jit(solution)/shard_map/all_gather | solution.py:468
  8.7 287.0 %all-gather.13.cloned.1.call-start = ((), (), s32[]{:S(2)}) async-start(), calls=%async_computation.1 | async-start | bytes 1216512 | tf_op jit(solution)/shard_map/all_gather | solution.py:469
  9.4 289.2 %all-gather.17.cloned.1.call-start = ((), (), s32[]{:S(2)}) async-start(), calls=%async_computation.3 | async-start | bytes 1216512 | tf_op jit(solution)/shard_map/all_gather | solution.py:470
  10.0 354.4 %all-gather.19.cloned.1.call-start = ((), (), s32[]{:S(2)}) async-start(), calls=%async_computation.4 | async-start | bytes 1216512 | tf_op jit(solution)/shard_map/all_gather | solution.py:472
  10.6 360.8 %all-gather.21.cloned.1.call-start = ((), (), s32[]{:S(2)}) async-start(), calls=%async_computation.5 | async-start | bytes 4866048 | tf_op jit(solution)/shard_map/all_gather | solution.py:473
  11.1 418.5 %all-gather.23.cloned.1.call-start = ((), (), s32[]{:S(2)}) async-start(), calls=%async_computation.6 | async-start | bytes 4866048 | tf_op jit(solution)/shard_map/all_gather | solution.py:474
  11.9 1465.5 %all-reduce.5.cloned.1.call-start = ((), (), s32[]{:S(2)}) async-start(), calls=%async_computation.7 | async-start | bytes 75628544
  60.3 143.5 %copy-start.74 = (bf16[1024,768]{1,0:T(8,128)(2,1)S(1)}, bf16[1024,768]{1,0:T(8,128)(2,1)}, u32[]{:S(2)}) copy-start(bf16[1024,768]{1,0:T(8,128)(2,1)} %param.19) | copy-start | bytes 4718596
  62.8 224.0 %copy-start.59 = (pred[512,512]{0,1:T(8,128)(4,1)}, pred[512,512]{0,1:T(8,128)(4,1)S(1)}, u32[]{:S(2)}) copy-start(pred[512,512]{0,1:T(8,128)(4,1)S(1)} %broadcast_compare_fusion) | copy-start | bytes 786436
  100.7 166.3 %copy-start.120 = (f32[768]{0:T(1024)}, f32[768]{0:T(1024)S(1)}, u32[]{:S(2)}) copy-start(f32[768]{0:T(1024)S(1)} %get-tuple-element.369) | copy-start | bytes 9220
  140.0 127.0 %copy-start.108 = (f32[768]{0:T(1024)}, f32[768]{0:T(1024)S(1)}, u32[]{:S(2)}) copy-start(f32[768]{0:T(1024)S(1)} %get-tuple-element.366) | copy-start | bytes 9220
  140.3 126.7 %copy-start.124 = (f32[512]{0:T(512)}, f32[512]{0:T(512)S(1)}, u32[]{:S(2)}) copy-start(f32[512]{0:T(512)S(1)} %get-tuple-element.491) | copy-start | bytes 6148
  142.5 137.3 %copy-start.95 = (f32[512,32]{0,1:T(8,128)}, f32[512,32]{0,1:T(8,128)S(1)}, u32[]{:S(2)}) copy-start(f32[512,32]{0,1:T(8,128)S(1)} %get-tuple-element.454) | copy-start | bytes 196612
  298.2 66.2 %copy-start.7 = (f32[512,768]{1,0:T(8,128)}, f32[512,768]{1,0:T(8,128)S(1)}, u32[]{:S(2)}) copy-start(f32[512,768]{1,0:T(8,128)S(1)} %get-tuple-element.458) | copy-start | bytes 4718596
  367.0 90.5 %copy-start.23 = (f32[512,768]{1,0:T(8,128)}, f32[512,768]{1,0:T(8,128)S(1)}, u32[]{:S(2)}) copy-start(f32[512,768]{1,0:T(8,128)S(1)} %get-tuple-element.462) | copy-start | bytes 4718596
  367.0 90.5 %copy-start.122 = (f32[512]{0:T(512)}, f32[512]{0:T(512)S(1)}, u32[]{:S(2)}) copy-start(f32[512]{0:T(512)S(1)} %broadcast_multiply_fusion.13) | copy-start | bytes 6148
  368.4 89.2 %copy-start.48 = (f32[512,768]{1,0:T(8,128)}, f32[512,768]{1,0:T(8,128)S(1)}, u32[]{:S(2)}) copy-start(f32[512,768]{1,0:T(8,128)S(1)} %get-tuple-element.470) | copy-start | bytes 4718596
  439.1 14.4 slice-start.23
  465.0 11.3 slice-start.4
  494.0 11.3 slice-start
  520.7 94.2 %copy-start.34 = (f32[512,768]{1,0:T(8,128)}, f32[512,768]{1,0:T(8,128)S(1)}, u32[]{:S(2)}) copy-start(f32[512,768]{1,0:T(8,128)S(1)} %get-tuple-element.379) | copy-start | bytes 4718596
  524.8 13.5 slice-start.11
  524.8 13.5 slice-start.12
  524.8 13.5 slice-start.13
  524.8 13.5 copy-start.99
  556.4 17.7 %slice-start.8 = ((s8[12582912]{0:T(1024)(128)(4,1)}), s8[4194304]{0:T(1024)(128)(4,1)S(1)}, s32[]{:S(2)}) async-start(s8[12582912]{0:T(1024)(128)(4,1)} %bitcast.313), calls=%async_computation.16 | async-start | bytes 8388608
  556.4 17.7 %slice-start.9 = ((s8[12582912]{0:T(1024)(128)(4,1)}), s8[4194304]{0:T(1024)(128)(4,1)S(1)}, s32[]{:S(2)}) async-start(s8[12582912]{0:T(1024)(128)(4,1)} %bitcast.313), calls=%async_computation.17 | async-start | bytes 8388608
  564.3 9.8 slice-start.10
  574.1 10.8 copy-start.83
  574.1 10.8 copy-start.85
  574.1 19.2 %slice-start.14 = ((s8[12582912]{0:T(1024)(128)(4,1)}), s8[4194304]{0:T(1024)(128)(4,1)S(1)}, s32[]{:S(2)}) async-start(s8[12582912]{0:T(1024)(128)(4,1)} %bitcast.317), calls=%async_computation.22 | async-start | bytes 8388608
  574.1 19.2 %slice-start.15 = ((s8[12582912]{0:T(1024)(128)(4,1)}), s8[4194304]{0:T(1024)(128)(4,1)S(1)}, s32[]{:S(2)}) async-start(s8[12582912]{0:T(1024)(128)(4,1)} %bitcast.317), calls=%async_computation.23 | async-start | bytes 8388608
  605.9 21.6 %slice-start.25 = ((s8[6291456]{0:T(1024)(128)(4,1)}), s8[2097152]{0:T(1024)(128)(4,1)S(1)}, s32[]{:S(2)}) async-start(s8[6291456]{0:T(1024)(128)(4,1)} %bitcast.362), calls=%async_computation.33 | async-start | bytes 4194304
  611.1 16.4 %slice-start.26 = ((s8[6291456]{0:T(1024)(128)(4,1)}), s8[4194304]{0:T(1024)(128)(4,1)S(1)}, s32[]{:S(2)}) async-start(s8[6291456]{0:T(1024)(128)(4,1)} %bitcast.362), calls=%async_computation.34 | async-start | bytes 8388608
  647.3 14.2 copy-start.176
  719.1 14.2 copy-start.175
  873.6 9.1 copy-start.146
  873.7 9.6 copy-start.160
  873.7 9.6 copy-start.161
  873.7 9.7 copy-start.185
  873.7 9.7 copy-start.187
  893.7 12.2 slice-start.17
  924.1 9.5 copy-start.50
  933.7 9.8 copy-start.35
  933.7 9.8 copy-start.80
  933.7 9.8 copy-start.81
  (192 other events, 803.6 us)
Sparse Core Ops, SparseCore 0:
  10.9 59.7 all-gather.14
  73.6 58.9 all-gather.10
  135.4 52.7 all-gather.12
  191.0 52.8 all-gather.16
  246.6 52.8 all-gather.18
  302.2 62.5 all-gather.20
  367.7 61.9 all-gather.22
  922.9 554.5 all-reduce.4
where the time goes:
time: 1510 us; the launch traced here: 1500 us
  waiting for transfers between devices  573 us (38%)
  local copies, waits for them, and re-layouts  360 us (24%)
  matrix products  320 us (21%)
  blocking collectives  157 us (10%)
  other arithmetic  76.8 us (5%)
  between operations  17.5 us (1%)
    unnamed x9, waiting for transfers between devices  527 us
    unnamed x481, local copies, waits for them, and re-layouts  63 us
    all_gather x1, waiting for transfers between devices, fetch_params(): lax.all_gather(w_down, 'fsdp', axis=0, tiled=True)  46 us
    all_gather x1, blocking collectives, fetch_params(): lax.all_gather(biases, 'fsdp', axis=1, tiled=True)  43.9 us
    all_gather x1, blocking collectives, fetch_params(): lax.all_gather(norm_gains, 'fsdp', axis=1, tiled=True)  38.4 us
    reshape x10, local copies, waits for them, and re-layouts, flatten_grads(): pieces.append(oriented.reshape(count, -1))  38 us
    unnamed x1, blocking collectives  37.5 us
    all_gather x1, blocking collectives, fetch_params(): lax.all_gather(norm_shifts, 'fsdp', axis=1, tiled=True)  37 us
  transfers between devices with their start and end apart: 8, of which 2 were waited for; matrix products, arithmetic and copies ran while one was open for 15% of the time, Pallas kernels for 0%

commit v1 on v0

v1 whole, which is shorter than its diff:
```python
import functools
import math

import jax
import jax.numpy as jnp
from jax import lax
from jax.experimental import pallas as pl
from jax.experimental.pallas import tpu as pltpu
from jax.sharding import PartitionSpec as P

D = 768
HEADS = 12
HEAD_DIM = 64
FF = 3072
SEQ_LEN = 512
SPAN = 64
SPANS = 8
NBR_LEN = 128
K_NBR = 2
POOL = 4
PAIRS = HEADS // 2
LANES = 128
ROWS = 256
SMALL = 18
TILE_F = 512

epsilon = 1e-05
rope_base = 10000.0
gelu_coeff = 0.044715
scale = HEAD_DIM ** (-0.5)
f32 = jnp.float32
bf16 = jnp.bfloat16


def geometry(count):
    side = round((count / 4) ** (1 / 3))
    sizes = (2 * side, side, side, 2)
    assert math.prod(sizes) == count
    return sizes


def coords_of(index, sizes):
    found = []
    for size in reversed(sizes):
        found.append(index % size)
        index = index // size
    return tuple(reversed(found))


def index_of(coords, sizes):
    index = 0
    for coord, size in zip(coords, sizes):
        index = index * size + coord
    return index


def shift_pairs(sizes, axis, step):
    pairs = []
    for source in range(math.prod(sizes)):
        coords = list(coords_of(source, sizes))
        coords[axis] = (coords[axis] + step) % sizes[axis]
        pairs.append((source, index_of(coords, sizes)))
    return pairs


def shift(values, sizes, axis, step):
    return lax.ppermute(values, "fsdp", shift_pairs(sizes, axis, step))


def after(values, *anchors):
    return lax.optimization_barrier((values,) + anchors)[0]


def gather_z(block, sizes):
    parts = [block] + [shift(block, sizes, 0, d) for d in range(1, sizes[0])]
    return jnp.stack(parts)


def gather_rest(own, sizes):
    half = own.shape[-1] // 2
    nz, ny, nx, nc = sizes
    pieces = {}
    along_x = {d: shift(own, sizes, 2, d) for d in range(1, nx)}
    along_y = {e: shift(own, sizes, 1, e) for e in range(1, ny)}
    pieces[0, 0, 0] = (own,)
    for d in range(1, nx):
        pieces[0, 0, d] = (along_x[d],)
    for e in range(1, ny):
        pieces[0, e, 0] = (along_y[e],)
    for d in range(1, nx):
        for e in range(1, ny):
            first = shift(along_x[d][..., :half], sizes, 1, e)
            second = shift(along_y[e][..., half:], sizes, 2, d)
            pieces[0, e, d] = (first, second)
    for (_, e, d), held in list(pieces.items()):
        for c in range(1, nc):
            pieces[c, e, d] = tuple(shift(part, sizes, 3, c) for part in held)
    return pieces


def place_kernel(keys, counts, sizes, me_ref, *refs):
    out_ref = refs[-1]
    at = 0
    half = out_ref.shape[-1] // 2
    for (c, e, d), count in zip(keys, counts):
        y = lax.rem(me_ref[1] - e + sizes[1], sizes[1])
        x = lax.rem(me_ref[2] - d + sizes[2], sizes[2])
        k = lax.rem(me_ref[3] - c + sizes[3], sizes[3])
        slot = (y * sizes[2] + x) * sizes[3] + k
        if count == 1:
            out_ref[0, slot] = refs[at][0]
        else:
            out_ref[0, slot, :, :half] = refs[at][0]
            out_ref[0, slot, :, half:] = refs[at + 1][0]
        at += count


def place(pieces, sizes, me):
    keys = sorted(pieces)
    counts = [len(pieces[key]) for key in keys]
    arrays = [part for key in keys for part in pieces[key]]
    rows, width = pieces[0, 0, 0][0].shape[1:]
    inner = sizes[1] * sizes[2] * sizes[3]
    nz = sizes[0]

    def source(z, me_ref):
        return (lax.rem(me_ref[0] - z + nz, nz), 0, 0)

    moved = 2 * nz * inner * rows * width * 2
    out = pl.pallas_call(
        functools.partial(place_kernel, keys, counts, sizes),
        out_shape=jax.ShapeDtypeStruct((nz, inner, rows, width), arrays[0].dtype),
        grid_spec=pltpu.PrefetchScalarGridSpec(
            num_scalar_prefetch=1,
            grid=(nz,),
            in_specs=[pl.BlockSpec((1,) + a.shape[1:], source) for a in arrays],
            out_specs=pl.BlockSpec((1, inner, rows, width), lambda z, me_ref: (z, 0, 0, 0)),
        ),
        cost_estimate=pl.CostEstimate(flops=0, transcendentals=0, bytes_accessed=moved),
        name="place",
    )(me, *arrays)
    return out.reshape(nz * inner * rows, width)


def take(values, axis, index):
    return lax.dynamic_index_in_dim(values, index, axis, keepdims=False)


def reduce_axis(values, sizes, axis, at, me, kind):
    size = sizes[axis]
    total = take(values, at, me[axis]).astype(f32)
    for step in range(1, size):
        target = lax.rem(me[axis] + step, size)
        got = shift(take(values, at, target), sizes, axis, step)
        total = total + got.astype(f32)
    return total.astype(kind)


def scatter_sum(values, sizes, me):
    count = math.prod(sizes)
    rows, width = values.shape[0] // count, values.shape[1]
    kind = values.dtype
    blocks = values.reshape(tuple(sizes) + (rows, width))
    summed = reduce_axis(blocks, sizes, 3, 3, me, kind)
    half = width // 2
    first, second = summed[..., :half], summed[..., half:]
    first = reduce_axis(first, sizes, 1, 1, me, kind)
    second = reduce_axis(second, sizes, 2, 2, me, kind)
    first = reduce_axis(first, sizes, 2, 1, me, kind)
    second = reduce_axis(second, sizes, 1, 1, me, kind)
    return reduce_axis(jnp.concatenate([first, second], -1), sizes, 0, 0, me, f32)


def dot_nn(a, b):
    return lax.dot_general(a, b, (((1,), (0,)), ((), ())), preferred_element_type=f32)


def dot_nt(a, b):
    return lax.dot_general(a, b, (((1,), (1,)), ((), ())), preferred_element_type=f32)


def dot_tn(a, b):
    return lax.dot_general(a, b, (((0,), (0,)), ((), ())), preferred_element_type=f32)


def normed_of(values):
    average = jnp.mean(values, -1, keepdims=True)
    centred = values - average
    inverse = lax.rsqrt(jnp.mean(centred * centred, -1, keepdims=True) + epsilon)
    return centred * inverse, inverse


def norm_back(incoming, normed, inverse, gain):
    scaled = incoming * gain
    inner = (
        scaled
        - jnp.mean(scaled, -1, keepdims=True)
        - normed * jnp.mean(scaled * normed, -1, keepdims=True)
    )
    return inner * inverse


def sum_rows(values):
    return jnp.sum(values, 0, keepdims=True)


def lane_halves(kind):
    lane = lax.broadcasted_iota(jnp.int32, (1, LANES), 1)
    low = jnp.where(lane < HEAD_DIM, 1.0, 0.0)
    return (low.astype(kind), (1.0 - low).astype(kind))


def turn(tile, cosine, sine):
    lane = lax.broadcasted_iota(jnp.int32, (1, LANES), 1)
    half_dim = HEAD_DIM // 2
    lower = (lane & half_dim) == 0
    other = jnp.where(
        lower, pltpu.roll(tile, LANES - half_dim, 1), pltpu.roll(tile, half_dim, 1)
    )
    return tile * cosine + other * sine


def rotary_tables():
    half_dim = HEAD_DIM // 2
    inverse = jnp.exp(
        jnp.arange(half_dim, dtype=f32) * (-2.0 * math.log(rope_base) / HEAD_DIM)
    )
    angles = jnp.arange(SEQ_LEN, dtype=f32)[:, None] * inverse[None, :]
    cosine, sine = jnp.cos(angles), jnp.sin(angles)
    return (
        jnp.concatenate([cosine] * 4, 1),
        jnp.concatenate([-sine, sine, -sine, sine], 1),
    )


def call(kernel, name, grid, ins, in_specs, outs, out_specs, flops, scratch=(), scalars=(), exps=0):
    arrays = jax.tree.leaves((ins, outs))
    nbytes = sum(math.prod(a.shape) * a.dtype.itemsize for a in arrays)
    return pl.pallas_call(
        kernel,
        out_shape=outs,
        grid_spec=pltpu.PrefetchScalarGridSpec(
            num_scalar_prefetch=len(scalars),
            grid=grid,
            in_specs=in_specs,
            out_specs=out_specs,
            scratch_shapes=scratch,
        ),
        compiler_params=pltpu.CompilerParams(
            dimension_semantics=("arbitrary",) * len(grid), vmem_limit_bytes=60 << 20
        ),
        cost_estimate=pl.CostEstimate(flops=flops, transcendentals=exps, bytes_accessed=nbytes),
        name=name,
    )(*scalars, *ins)


def like(shape, kind):
    return jax.ShapeDtypeStruct(shape, kind)


def whole(shape):
    return pl.BlockSpec(shape, lambda *_: (0,) * len(shape))


def qkv_kernel(x_ref, w_ref, vec_ref, cos_ref, sin_ref, a1_ref, out_ref):
    part = pl.program_id(0)
    rows = x_ref.shape[0]

    @pl.when(part == 0)
    def _():
        for r in range(0, rows, ROWS):
            normed, _ = normed_of(x_ref[r : r + ROWS].astype(f32))
            a1_ref[r : r + ROWS] = (normed * vec_ref[8:9] + vec_ref[11:12]).astype(bf16)

    bias = vec_ref[pl.ds(part, 1), :]
    for r in range(0, rows, ROWS):
        mixed = dot_nn(a1_ref[r : r + ROWS], w_ref[...]) + bias
        at = r % SEQ_LEN

        @pl.when(part < 2)
        def _():
            cosine, sine = cos_ref[at : at + ROWS], sin_ref[at : at + ROWS]
            for c in range(0, D, LANES):
                turned = turn(mixed[:, c : c + LANES], cosine, sine)
                out_ref[r : r + ROWS, c : c + LANES] = turned.astype(bf16)

        @pl.when(part == 2)
        def _():
            out_ref[r : r + ROWS] = mixed.astype(bf16)


def qkv_project(x, weight, vec, cosine, sine):
    rows = x.shape[0]
    return call(
        qkv_kernel,
        "qkv_project",
        (3,),
        (x, weight, vec, cosine, sine),
        [
            whole((rows, D)),
            pl.BlockSpec((D, D), lambda j: (0, j)),
            whole(vec.shape),
            whole((SEQ_LEN, LANES)),
            whole((SEQ_LEN, LANES)),
        ],
        (like((rows, D), bf16), like((rows, 3 * D), bf16)),
        (whole((rows, D)), pl.BlockSpec((rows, D), lambda j: (0, j))),
        2 * rows * D * 3 * D,
    )


def limits(lengths_ref, seq, positions):
    first = lengths_ref[seq, 0]
    second = first + lengths_ref[seq, 1]
    third = second + lengths_ref[seq, 2]
    tail = jnp.where(positions < third, third, SEQ_LEN)
    tail = jnp.where(positions < second, second, tail)
    return jnp.where(positions < first, first, tail)


def self_kernel(lengths_ref, q_ref, k_ref, v_ref, o_ref, lse_ref):
    seq = pl.program_id(0)
    keep = lane_halves(bf16)
    low_lane = lax.broadcasted_iota(jnp.int32, (1, LANES), 1) < HEAD_DIM
    for r in range(0, SEQ_LEN, ROWS):
        rows = lax.broadcasted_iota(jnp.int32, (ROWS, 1), 0) + r
        columns = lax.broadcasted_iota(jnp.int32, (ROWS, SEQ_LEN), 1)
        allowed = columns < limits(lengths_ref, seq, rows)
        query = q_ref[r : r + ROWS] * scale
        outs, totals = [], []
        for h in range(2):
            scores = dot_nt(query * keep[h], k_ref[...])
            scores = jnp.where(allowed, scores, -1e30)
            row_max = jnp.max(scores, -1, keepdims=True)
            exponent = jnp.exp(scores - row_max)
            total = jnp.sum(exponent, -1, keepdims=True)
            weights = (exponent * (1.0 / total)).astype(bf16)
            outs.append(dot_nn(weights, v_ref[...]))
            totals.append(row_max + jnp.log(total))
        o_ref[r : r + ROWS] = jnp.where(low_lane, outs[0], outs[1]).astype(bf16)
        lse_ref[r : r + ROWS] = jnp.where(low_lane, totals[0], totals[1])


def self_attend(lengths, qkv):
    rows = qkv.shape[0]
    seqs = rows // SEQ_LEN
    block = (SEQ_LEN, LANES)

    def at(offset):
        return pl.BlockSpec(block, lambda s, p, _: (s, offset + p))

    return call(
        self_kernel,
        "self_attend",
        (seqs, PAIRS),
        (qkv, qkv, qkv),
        [at(0), at(PAIRS), at(2 * PAIRS)],
        (like((rows, D), bf16), like((rows, D), f32)),
        (at(0), at(0)),
        4 * rows * SEQ_LEN * D,
        scalars=(lengths,),
        exps=rows * SEQ_LEN * HEADS,
    )


def self_back_kernel(lengths_ref, q_ref, k_ref, v_ref, do_ref, lse_ref, cos_ref, sin_ref, out_ref):
    seq, pair = pl.program_id(0), pl.program_id(1)
    keep = lane_halves(bf16)
    low_lane = lax.broadcasted_iota(jnp.int32, (1, LANES), 1) < HEAD_DIM
    lse = lse_ref[...].T
    positions = lax.broadcasted_iota(jnp.int32, (1, SEQ_LEN), 1)
    ends = limits(lengths_ref, seq, positions)
    key_at = lax.broadcasted_iota(jnp.int32, (SEQ_LEN, SEQ_LEN), 0)
    allowed = key_at < ends
    dqs, dks, dvs = [], [], []
    for h in range(2):
        total = lse[h * HEAD_DIM : h * HEAD_DIM + 1]
        scores = dot_nt(k_ref[...] * (keep[h] * scale), q_ref[...])
        prob = jnp.exp(jnp.where(allowed, scores - total, -1e30))
        dprob = dot_nt(v_ref[...] * keep[h], do_ref[...])
        inner = jnp.sum(prob * dprob, 0, keepdims=True)
        dscore = (prob * (dprob - inner)).astype(bf16)
        dvs.append(dot_nn(prob.astype(bf16), do_ref[...]))
        dks.append(dot_nn(dscore, q_ref[...]))
        dqs.append(dot_tn(dscore, k_ref[...]))
    cosine, sine = cos_ref[...], -sin_ref[...]
    dq = jnp.where(low_lane, dqs[0], dqs[1]) * scale
    dk = jnp.where(low_lane, dks[0], dks[1]) * scale
    dv = jnp.where(low_lane, dvs[0], dvs[1])
    for part, value in enumerate((turn(dq, cosine, sine), turn(dk, cosine, sine), dv)):
        column = pl.multiple_of((part * PAIRS + pair) * LANES, LANES)
        out_ref[:, pl.ds(column, LANES)] = value.astype(bf16)


def self_back(lengths, qkv, do, lse, cosine, sine):
    rows = qkv.shape[0]
    seqs = rows // SEQ_LEN
    block = (SEQ_LEN, LANES)

    def at(offset):
        return pl.BlockSpec(block, lambda s, p, _: (s, offset + p))

    return call(
        self_back_kernel,
        "self_back",
        (seqs, PAIRS),
        (qkv, qkv, qkv, do, lse, cosine, sine),
        [at(0), at(PAIRS), at(2 * PAIRS), at(0), at(0), whole(block), whole(block)],
        like((rows, 3 * D), bf16),
        pl.BlockSpec((SEQ_LEN, 3 * D), lambda s, p, _: (s, 0)),
        10 * rows * SEQ_LEN * D,
        scalars=(lengths,),
        exps=rows * SEQ_LEN * HEADS,
    )


def mid_kernel(o_ref, x_ref, wo_ref, wq_ref, vec_ref, h1_ref, a2_ref, cq_ref):
    h1 = x_ref[...].astype(f32) + dot_nn(o_ref[...], wo_ref[...]) + vec_ref[3:4]
    h1_ref[...] = h1
    normed, _ = normed_of(h1)
    a2 = (normed * vec_ref[9:10] + vec_ref[12:13]).astype(bf16)
    a2_ref[...] = a2
    cq_ref[...] = (dot_nn(a2, wq_ref[...]) + vec_ref[4:5]).astype(bf16)


def mid_forward(o, x, mid, vec):
    rows = x.shape[0]
    block = pl.BlockSpec((ROWS, D), lambda r: (r, 0))
    return call(
        mid_kernel,
        "mid_forward",
        (rows // ROWS,),
        (o, x, mid, mid, vec),
        [
            block,
            block,
            pl.BlockSpec((D, D), lambda r: (0, 2)),
            pl.BlockSpec((D, D), lambda r: (0, 3)),
            whole(vec.shape),
        ],
        (like((rows, D), f32), like((rows, D), bf16), like((rows, D), bf16)),
        (block, block, block),
        4 * rows * D * D,
    )


def ckv_kernel(n_ref, w_ref, vec_ref, out_ref):
    mixed = dot_nn(n_ref[...], w_ref[...])
    out_ref[:, :D] = mixed[:, :D].astype(bf16)
    out_ref[:, D:] = (mixed[:, D:] + vec_ref[5:6]).astype(bf16)


def ckv_project(n, mid, vec):
    rows = n.shape[0]
    return call(
        ckv_kernel,
        "ckv_project",
        (rows // ROWS,),
        (n, mid, vec),
        [
            pl.BlockSpec((ROWS, D), lambda r: (r, 0)),
            pl.BlockSpec((D, 2 * D), lambda r: (0, 0)),
            whole(vec.shape),
        ],
        like((rows, 2 * D), bf16),
        pl.BlockSpec((ROWS, 2 * D), lambda r: (r, 0)),
        4 * rows * D * D,
    )


def slots(chosen_ref, seq, span):
    found = []
    for i in range(K_NBR):
        entry = chosen_ref[seq, span * K_NBR + i]
        found.append(pl.multiple_of(entry * NBR_LEN, NBR_LEN))
    return found


def chosen_rows(ref, starts):
    return jnp.concatenate([ref[pl.ds(start, NBR_LEN), :] for start in starts], 0)


def cross_kernel(chosen_ref, q_ref, k_ref, v_ref, o_ref):
    seq = pl.program_id(0)
    keep = lane_halves(bf16)
    low_lane = lax.broadcasted_iota(jnp.int32, (1, LANES), 1) < HEAD_DIM
    for c in range(SPANS):
        starts = slots(chosen_ref, seq, c)
        query = q_ref[c * SPAN : (c + 1) * SPAN] * scale
        both = jnp.concatenate([query * keep[0], query * keep[1]], 0)
        scores = dot_nt(both, chosen_rows(k_ref, starts))
        exponent = jnp.exp(scores - jnp.max(scores, -1, keepdims=True))
        total = jnp.sum(exponent, -1, keepdims=True)
        weights = (exponent * (1.0 / total)).astype(bf16)
        out = dot_nn(weights, chosen_rows(v_ref, starts))
        o_ref[c * SPAN : (c + 1) * SPAN] = jnp.where(low_lane, out[:SPAN], out[SPAN:]).astype(bf16)


def cross_attend(chosen, cq, ckv):
    rows = cq.shape[0]
    seqs = rows // SEQ_LEN
    block = (SEQ_LEN, LANES)

    def at(offset):
        return pl.BlockSpec(block, lambda s, p, _: (s, offset + p))

    return call(
        cross_kernel,
        "cross_attend",
        (seqs, PAIRS),
        (cq, ckv, ckv),
        [at(0), at(0), at(PAIRS)],
        like((rows, D), bf16),
        at(0),
        2 * rows * SEQ_LEN * D,
        scalars=(chosen,),
        exps=rows * K_NBR * NBR_LEN * HEADS,
    )


def cross_back_kernel(chosen_ref, q_ref, k_ref, v_ref, do_ref, dq_ref, dkv_ref, dk_acc, dv_acc):
    seq, pair = pl.program_id(0), pl.program_id(1)
    keep = lane_halves(bf16)
    low_lane = lax.broadcasted_iota(jnp.int32, (1, LANES), 1) < HEAD_DIM
    dk_acc[...] = jnp.zeros_like(dk_acc)
    dv_acc[...] = jnp.zeros_like(dv_acc)
    for c in range(SPANS):
        starts = slots(chosen_ref, seq, c)
        span = slice(c * SPAN, (c + 1) * SPAN)
        query, upstream = q_ref[span], do_ref[span]
        query = jnp.concatenate([query * keep[0], query * keep[1]], 0)
        upstream = jnp.concatenate([upstream * keep[0], upstream * keep[1]], 0)
        keys, values = chosen_rows(k_ref, starts), chosen_rows(v_ref, starts)
        scores = dot_nt(keys, query) * scale
        exponent = jnp.exp(scores - jnp.max(scores, 0, keepdims=True))
        prob = exponent * (1.0 / jnp.sum(exponent, 0, keepdims=True))
        dprob = dot_nt(values, upstream)
        inner = jnp.sum(prob * dprob, 0, keepdims=True)
        dscore = (prob * (dprob - inner)).astype(bf16)
        dv = dot_nn(prob.astype(bf16), upstream)
        dk = dot_nn(dscore, query) * scale
        dq = dot_tn(dscore, keys) * scale
        dq_ref[span] = jnp.where(low_lane, dq[:SPAN], dq[SPAN:]).astype(bf16)
        for i, start in enumerate(starts):
            rows = slice(i * NBR_LEN, (i + 1) * NBR_LEN)
            dk_acc[pl.ds(start, NBR_LEN), :] += dk[rows]
            dv_acc[pl.ds(start, NBR_LEN), :] += dv[rows]
    for part, acc in enumerate((dk_acc, dv_acc)):
        column = pl.multiple_of((part * PAIRS + pair) * LANES, LANES)
        dkv_ref[:, pl.ds(column, LANES)] = acc[...].astype(bf16)


def cross_back(chosen, cq, ckv, dco):
    rows = cq.shape[0]
    seqs = rows // SEQ_LEN
    block = (SEQ_LEN, LANES)

    def at(offset):
        return pl.BlockSpec(block, lambda s, p, _: (s, offset + p))

    return call(
        cross_back_kernel,
        "cross_back",
        (seqs, PAIRS),
        (cq, ckv, ckv, dco),
        [at(0), at(0), at(PAIRS), at(0)],
        (like((rows, D), bf16), like((rows, 2 * D), bf16)),
        (at(0), pl.BlockSpec((SEQ_LEN, 2 * D), lambda s, p, _: (s, 0))),
        5 * rows * SEQ_LEN * D,
        scratch=[pltpu.VMEM(block, f32), pltpu.VMEM(block, f32)],
        scalars=(chosen,),
        exps=rows * K_NBR * NBR_LEN * HEADS,
    )


def gelu_pair(hidden):
    root_coeff = math.sqrt(2.0 / math.pi)
    square = hidden * hidden
    tangent = jnp.tanh(root_coeff * hidden * (1.0 + gelu_coeff * square))
    upper = 0.5 * (1.0 + tangent)
    slope = upper + (0.5 * root_coeff) * hidden * (1.0 - tangent * tangent) * (
        1.0 + (3.0 * gelu_coeff) * square
    )
    return hidden * upper, slope


def mlp_kernel(
    h1_ref,
    co_ref,
    dy_ref,
    wco_ref,
    wu_ref,
    wd_ref,
    bu_ref,
    vec_ref,
    a3_ref,
    g_ref,
    du_ref,
    out_ref,
    dh2_ref,
    e2_ref,
    dco_ref,
    sums_ref,
    dbu_ref,
    y_acc,
    da_acc,
    h2_ref,
):
    step = pl.program_id(0)
    rows = h1_ref.shape[0]
    chunks = range(0, rows, ROWS)

    @pl.when(step == 0)
    def _():
        for r in chunks:
            part = slice(r, r + ROWS)
            h2 = h1_ref[part] + dot_nn(co_ref[part], wco_ref[...]) + vec_ref[6:7]
            h2_ref[part] = h2
            normed, _ = normed_of(h2)
            a3_ref[part] = (normed * vec_ref[10:11] + vec_ref[13:14]).astype(bf16)
            y_acc[part] = h2 + vec_ref[7:8]
            da_acc[part] = jnp.zeros_like(h2)

    bias_sum = jnp.zeros((1, TILE_F), f32)
    for r in chunks:
        part = slice(r, r + ROWS)
        hidden = dot_nn(a3_ref[part], wu_ref[...]) + bu_ref[...]
        dg = dot_nt(dy_ref[part], wd_ref[...])
        value, slope = gelu_pair(hidden)
        g = value.astype(bf16)
        du = (dg * slope).astype(bf16)
        g_ref[part] = g
        du_ref[part] = du
        bias_sum += sum_rows(du.astype(f32))
        y_acc[part] += dot_nn(g, wd_ref[...])
        da_acc[part] += dot_nt(du, wu_ref[...])
    dbu_ref[...] = bias_sum

    @pl.when(step == pl.num_programs(0) - 1)
    def _():
        gain_sum = jnp.zeros((1, D), f32)
        shift_sum = jnp.zeros((1, D), f32)
        e_sum = jnp.zeros((1, D), f32)
        y_sum = jnp.zeros((1, D), f32)
        for r in chunks:
            part = slice(r, r + ROWS)
            out_ref[part] = y_acc[part].astype(bf16)
            normed, inverse = normed_of(h2_ref[part])
            da3 = da_acc[part]
            upstream = dy_ref[part].astype(f32)
            dh2 = upstream + norm_back(da3, normed, inverse, vec_ref[10:11])
            dh2_ref[part] = dh2
            e2 = dh2.astype(bf16)
            e2_ref[part] = e2
            dco_ref[part] = dot_nt(e2, wco_ref[...]).astype(bf16)
            gain_sum += sum_rows(da3 * normed)
            shift_sum += sum_rows(da3)
            e_sum += sum_rows(e2.astype(f32))
            y_sum += sum_rows(upstream)
        sums_ref[0:1] = gain_sum
        sums_ref[1:2] = shift_sum
        sums_ref[2:3] = e_sum
        sums_ref[3:4] = y_sum


def mlp_both(h1, co, dy, mid, wu, wd, bu, vec):
    rows = h1.shape[0]
    full = whole((rows, D))
    wide = pl.BlockSpec((rows, TILE_F), lambda f: (0, f))
    return call(
        mlp_kernel,
        "mlp_both",
        (FF // TILE_F,),
        (h1, co, dy, mid, wu, wd, bu, vec),
        [
            full,
            full,
            full,
            pl.BlockSpec((D, D), lambda f: (0, 4)),
            pl.BlockSpec((D, TILE_F), lambda f: (0, f)),
            pl.BlockSpec((TILE_F, D), lambda f: (f, 0)),
            pl.BlockSpec((1, TILE_F), lambda f: (0, f)),
            whole(vec.shape),
        ],
        (
            like((rows, D), bf16),
            like((rows, FF), bf16),
            like((rows, FF), bf16),
            like((rows, D), bf16),
            like((rows, D), f32),
            like((rows, D), bf16),
            like((rows, D), bf16),
            like((8, D), f32),
            like((1, FF), f32),
        ),
        (
            full,
            wide,
            wide,
            full,
            full,
            full,
            full,
            whole((8, D)),
            pl.BlockSpec((1, TILE_F), lambda f: (0, f)),
        ),
        2 * rows * D * (4 * FF + 2 * D),
        scratch=[pltpu.VMEM((rows, D), f32)] * 3,
        exps=rows * FF,
    )


def mid_back_kernel(
    dcq_ref, dh2_ref, h1_ref, wq_ref, wo_ref, vec_ref, dh1_ref, e1_ref, do_ref, sums_ref
):
    @pl.when(pl.program_id(0) == 0)
    def _():
        sums_ref[...] = jnp.zeros_like(sums_ref)

    da2 = dot_nt(dcq_ref[...], wq_ref[...])
    normed, inverse = normed_of(h1_ref[...])
    dh1 = dh2_ref[...] + norm_back(da2, normed, inverse, vec_ref[9:10])
    dh1_ref[...] = dh1
    e1 = dh1.astype(bf16)
    e1_ref[...] = e1
    do_ref[...] = dot_nt(e1, wo_ref[...]).astype(bf16)
    sums_ref[0:1] += sum_rows(da2 * normed)
    sums_ref[1:2] += sum_rows(da2)
    sums_ref[2:3] += sum_rows(dcq_ref[...].astype(f32))
    sums_ref[3:4] += sum_rows(e1.astype(f32))


def mid_back(dcq, dh2, h1, mid, vec):
    rows = h1.shape[0]
    block = pl.BlockSpec((ROWS, D), lambda r: (r, 0))
    return call(
        mid_back_kernel,
        "mid_back",
        (rows // ROWS,),
        (dcq, dh2, h1, mid, mid, vec),
        [
            block,
            block,
            block,
            pl.BlockSpec((D, D), lambda r: (0, 3)),
            pl.BlockSpec((D, D), lambda r: (0, 2)),
            whole(vec.shape),
        ],
        (
            like((rows, D), f32),
            like((rows, D), bf16),
            like((rows, D), bf16),
            like((8, D), f32),
        ),
        (block, block, block, whole((8, D))),
        4 * rows * D * D,
    )


def token_back_kernel(dqkv_ref, dh1_ref, x_ref, w_ref, vec_ref, dx_ref, sums_ref, qkv_sums_ref):
    @pl.when(pl.program_id(0) == 0)
    def _():
        sums_ref[...] = jnp.zeros_like(sums_ref)
        qkv_sums_ref[...] = jnp.zeros_like(qkv_sums_ref)

    da1 = dot_nt(dqkv_ref[...], w_ref[...])
    normed, inverse = normed_of(x_ref[...].astype(f32))
    dx_ref[...] = dh1_ref[...] + norm_back(da1, normed, inverse, vec_ref[8:9])
    sums_ref[0:1] += sum_rows(da1 * normed)
    sums_ref[1:2] += sum_rows(da1)
    qkv_sums_ref[...] += sum_rows(dqkv_ref[...].astype(f32))


def token_back(dqkv, dh1, x, weight, vec):
    rows = x.shape[0]
    block = pl.BlockSpec((ROWS, D), lambda r: (r, 0))
    return call(
        token_back_kernel,
        "token_back",
        (rows // ROWS,),
        (dqkv, dh1, x, weight, vec),
        [
            pl.BlockSpec((ROWS, 3 * D), lambda r: (r, 0)),
            block,
            block,
            pl.BlockSpec((D, 3 * D), lambda r: (0, 0)),
            whole(vec.shape),
        ],
        (like((rows, D), f32), like((8, D), f32), like((1, 3 * D), f32)),
        (block, whole((8, D)), whole((1, 3 * D))),
        6 * rows * D * D,
    )


def neighbour_kernel(dkv_ref, w_ref, dn_ref, sums_ref):
    @pl.when(pl.program_id(0) == 0)
    def _():
        sums_ref[...] = jnp.zeros_like(sums_ref)

    dn_ref[...] = dot_nt(dkv_ref[...], w_ref[...])
    sums_ref[...] += sum_rows(dkv_ref[:, D:].astype(f32))


def neighbour_back(dckv, mid):
    rows = dckv.shape[0]
    return call(
        neighbour_kernel,
        "neighbour_back",
        (rows // ROWS,),
        (dckv, mid),
        [
            pl.BlockSpec((ROWS, 2 * D), lambda r: (r, 0)),
            pl.BlockSpec((D, 2 * D), lambda r: (0, 0)),
        ],
        (like((rows, D), f32), like((1, D), f32)),
        (pl.BlockSpec((ROWS, D), lambda r: (r, 0)), whole((1, D))),
        4 * rows * D * D,
    )


def weight_grad(left, right):
    return dot_tn(left, right).astype(bf16)


def local(
    sizes,
    tokens,
    neighbours,
    block_lengths,
    chosen,
    cotangent,
    w_qkv,
    w_out,
    w_cross_q,
    w_cross_kv,
    w_cross_out,
    w_up,
    w_down,
    biases,
    up_bias,
    norm_gains,
    norm_shifts,
):
    me = coords_of(lax.axis_index("fsdp"), sizes)
    me_array = jnp.stack(me).astype(jnp.int32)
    shard = w_qkv.shape[0]
    small = jnp.concatenate(
        [biases.T, norm_gains.T, norm_shifts.T, up_bias.reshape(shard, FF // D)], 1
    )
    small = jnp.pad(small, ((0, 0), (0, LANES - SMALL)))
    first = jnp.concatenate([w_qkv, small], 1)
    middle = jnp.concatenate([w_cross_kv, w_out, w_cross_q, w_cross_out], 1)

    first_z = gather_z(first, sizes)
    middle_z = gather_z(after(middle, first_z), sizes)
    first_pieces = gather_rest(first_z, sizes)
    up_z = gather_z(after(w_up, middle_z), sizes)
    middle_pieces = gather_rest(middle_z, sizes)
    down_z = gather_z(after(w_down, up_z), sizes)
    up_pieces = gather_rest(up_z, sizes)
    down_pieces = gather_rest(down_z, sizes)

    cosine, sine = rotary_tables()
    qkv_weight = place(first_pieces, sizes, me_array)
    gathered = qkv_weight[:, 3 * D :]
    vec = gathered[:, :16].T.astype(f32)
    up_shift = gathered[:, 14:SMALL].reshape(1, FF).astype(f32)
    picks = chosen.reshape(chosen.shape[0], SPANS * K_NBR)

    a1, qkv = qkv_project(tokens, qkv_weight, vec, cosine, sine)
    o, lse = self_attend(block_lengths, qkv)
    mid = place(middle_pieces, sizes, me_array)
    ckv = ckv_project(neighbours, mid, vec)
    h1, a2, cq = mid_forward(o, tokens, mid, vec)
    co = cross_attend(picks, cq, ckv)
    up_weight = place(up_pieces, sizes, me_array)
    down_weight = place(down_pieces, sizes, me_array)
    a3, g, du, output, dh2, e2, dco, sums3, grad_bu = mlp_both(
        h1, co, cotangent, mid, up_weight, down_weight, up_shift, vec
    )
    grad_down = scatter_sum(weight_grad(g, cotangent), sizes, me)
    grad_up = scatter_sum(weight_grad(a3, du), sizes, me)
    grad_co = scatter_sum(weight_grad(co, e2), sizes, me)
    dcq, dckv = cross_back(picks, cq, ckv, dco)
    dh1, e1, do, sums2 = mid_back(dcq, dh2, h1, mid, vec)
    grad_cq = scatter_sum(weight_grad(a2, dcq), sizes, me)
    grad_ckv = scatter_sum(weight_grad(neighbours, dckv), sizes, me)
    grad_out = scatter_sum(weight_grad(o, e1), sizes, me)
    dqkv = self_back(block_lengths, qkv, do, lse, cosine, sine)
    grad_qkv = scatter_sum(weight_grad(a1, dqkv), sizes, me)
    token_grad, sums1, qkv_sums = token_back(dqkv, dh1, tokens, qkv_weight, vec)
    neighbour_grad, value_sums = neighbour_back(dckv, mid)

    rows = jnp.concatenate(
        [
            qkv_sums.reshape(3, D),
            sums2[3:4],
            sums2[2:3],
            value_sums,
            sums3[2:4],
            sums1[0:1],
            sums2[0:1],
            sums3[0:1],
            sums1[1:2],
            sums2[1:2],
            sums3[1:2],
        ],
        0,
    )
    spread = jnp.concatenate([rows.T, grad_bu.reshape(D, FF // D)], 1)
    spread = jnp.pad(spread, ((0, 0), (0, 2 * LANES - SMALL)))
    small_sum = scatter_sum(spread, sizes, me)
    return (
        output,
        token_grad,
        neighbour_grad,
        grad_qkv,
        grad_out,
        grad_cq,
        grad_ckv,
        grad_co,
        grad_up,
        grad_down,
        small_sum[:, :8].T,
        small_sum[:, 14:SMALL].reshape(-1),
        small_sum[:, 8:11].T,
        small_sum[:, 11:14].T,
    )


def solution(mesh):
    rowwise, columnwise = P("fsdp", None), P(None, "fsdp")
    return jax.shard_map(
        functools.partial(local, geometry(mesh.shape["fsdp"])),
        mesh=mesh,
        in_specs=(rowwise,) * 3
        + (P("fsdp", None, None),)
        + (rowwise,) * 8
        + (columnwise, P("fsdp"), columnwise, columnwise),
        out_specs=(rowwise,) * 10 + (columnwise, P("fsdp"), columnwise, columnwise),
        check_vma=False,
    )
```

time: 1510 us -> 602 us (0.40)
  waiting for transfers between devices: 573 us -> 139 us
  local copies, waits for them, and re-layouts: 360 us -> 48.2 us
  matrix products: 320 us -> 29.7 us
  Pallas kernels: 0 us -> 224 us
  blocking collectives: 157 us -> 0 us
  starting transfers between devices: 0.3 us -> 123 us
  other arithmetic: 76.8 us -> 29.3 us
    unnamed x9 -> x0, waiting for transfers between devices: 527 us -> none
    dot_general x70 -> x7, matrix products: 320 us -> 29.7 us  [dot_tn(): lax.dot_general(a, b, (((0,), (0,)), ((), ())), preferred_element_type=f32)]
    pallas_call x0 -> x15, Pallas kernels: none -> 224 us  [the longest x11 201 us: call(): pl.pallas_call(kernel, out_shape=outs, grid_spec=pltpu.PrefetchScalarGrid...]
    ppermute x0 -> x112, waiting for transfers between devices: none -> 139 us  [shift(): return lax.ppermute(values, 'fsdp', shift_pairs(sizes, axis, step))]
    reshape x28 -> x5, local copies, waits for them, and re-layouts: 132 us -> 2.41 us  [the longest x1 0.75 us: local(): up_bias.reshape(shard, FF // D)]
    ppermute x0 -> x112, starting transfers between devices: none -> 123 us  [shift(): return lax.ppermute(values, 'fsdp', shift_pairs(sizes, axis, step))]
    all_gather x3 -> x0, blocking collectives: 119 us -> none  [the longest x1 43.9 us: fetch_params(): lax.all_gather(biases, 'fsdp', axis=1, tiled=True)]
    unnamed x481 -> x119, local copies, waits for them, and re-layouts: 63 us -> 11.2 us
  transfers between devices with their start and end apart: 8 -> 112, of which waited for: 2 -> 47; matrix products, arithmetic and copies ran while one was open for 15% -> 14% of each run, Pallas kernels for 0% -> 10%
where the time goes in v1:
time: 602 us; the launch traced here: 596 us
  Pallas kernels  224 us (37%)
  waiting for transfers between devices  139 us (23%)
  starting transfers between devices  123 us (20%)
  local copies, waits for them, and re-layouts  48.2 us (8%)
  matrix products  29.7 us (5%)
  other arithmetic  29.3 us (5%)
    pallas_call x11, Pallas kernels, call(): pl.pallas_call(kernel, out_shape=outs, grid_spec=pltpu.PrefetchScalarGrid...  201 us
    ppermute x112, waiting for transfers between devices, shift(): return lax.ppermute(values, 'fsdp', shift_pairs(sizes, axis, step))  139 us
    ppermute x112, starting transfers between devices, shift(): return lax.ppermute(values, 'fsdp', shift_pairs(sizes, axis, step))  123 us
    dot_general x7, matrix products, dot_tn(): lax.dot_general(a, b, (((0,), (0,)), ((), ())), preferred_element_type=f32)  29.7 us
    dynamic_slice x18, local copies, waits for them, and re-layouts, take(): return lax.dynamic_index_in_dim(values, index, axis, keepdims=False)  23.7 us
    pallas_call x4, Pallas kernels, place(): pl.pallas_call(functools.partial(place_kernel, keys, counts, sizes), out_...  23.5 us
  transfers between devices with their start and end apart: 112, of which 47 were waited for; matrix products, arithmetic and copies ran while one was open for 14% of the time, Pallas kernels for 10%

profile of v1, /device:TPU:0, one launch (start us, length us, event | category | flops | bytes accessed | tf_op | source)
XLA Modules:
  0.0 595.6 jit_solution(3629021523323681219)
XLA Ops:
  4.8 5.1 collective-permute-start.2
  13.5 4.2 collective-permute-done
  17.7 2.8 collective-permute-done.1
  20.6 2.6 collective-permute-start.13
  24.4 5.5 collective-permute-done.12
  30.0 6.1 %collective-permute-done.13 = bf16[24,3840]{1,0:T(8,128)(2,1)S(1)} collective-permute-done((bf16[24,3840]{1,0:T(8,128)(2,1)S(1)}, bf16[24,3840]{1,0:T(8,128)(2,1)S(1)}, u32[]{:S(2)}, u32[]{:S(2)}) %collective-permute-start.13) | collective-permute-done | bytes 184352 | tf_op jit(solution)/shard_map/ppermute | solution.py:67
  36.2 3.7 collective-permute-start.24
  45.4 4.2 collective-permute-done.25
  49.7 3.7 collective-permute-start.36
  61.6 2.8 collective-permute-done.37
  66.7 12.2 %collective-permute-done.6.refs_4_ = bf16[4,24,1216]{2,1,0:T(8,128)(2,1)S(1)} collective-permute-done((bf16[4,24,1216]{2,1,0:T(8,128)(2,1)S(1)}, bf16[4,24,1216]{2,1,0:T(8,128)(2,1)S(1)}, u32[]{:S(2)}, u32[]{:S(2)}) %collective-permute-start.6) | collective-permute-done | bytes 233504 | tf_op jit(solution)/shard_map/ppermute | solution.py:67
  81.6 13.1 %collective-permute-done.15.refs_1_ = bf16[4,24,3840]{2,1,0:T(8,128)(2,1)S(1)} collective-permute-done((bf16[4,24,3840]{2,1,0:T(8,128)(2,1)S(1)}, bf16[4,24,3840]{2,1,0:T(8,128)(2,1)S(1)}, u32[]{:S(2)}, u32[]{:S(2)}) %collective-permute-start.15) | collective-permute-done | bytes 737312 | tf_op jit(solution)/shard_map/ppermute | solution.py:67
  100.9 4.7 collective-permute-done.39.refs_1_
  107.1 3.9 collective-permute-done.40.refs_2_
  113.1 10.7 %collective-permute-done.29.refs_3_ = bf16[4,24,1536]{2,1,0:T(8,128)(2,1)S(1)} collective-permute-done((bf16[4,24,1536]{2,1,0:T(8,128)(2,1)S(1)}, bf16[4,24,1536]{2,1,0:T(8,128)(2,1)S(1)}, u32[]{:S(2)}, u32[]{:S(2)}) %collective-permute-start.29) | collective-permute-done | bytes 294944 | tf_op jit(solution)/shard_map/ppermute | solution.py:67
  127.1 3.6 collective-permute-done.42.refs_4_
  135.7 3.0 pad_maximum_fusion.4
  138.7 5.4 place.4
  148.8 15.6 %qkv_project.1 = (bf16[1024,768]{1,0:T(8,128)(2,1)}, bf16[1024,2304]{1,0:T(8,128)(2,1)}) custom-call(bf16[1024,768]{1,0:T(8,128)(2,1)} %x_ref.5, bf16[768,2432]{1,0:T(8,128)(2,1)} %bitcast.378, f32[16,768]{1,0:T(8,128)} %convert_bitcast_fusion.vec_ref, f32[512,128]{1,0:T(8,128)} %get-tuple-element.144.cos_ref, f32[512,128]{1,0:T(8,128)} %get-tuple-element.145.sin_ref), custom_call_target="tpu_custom_call" | custom-call | flops 3623878656 | bytes 12173312 | tf_op jit(solution)/shard_map/qkv_project/pallas_call | solution.py:239
  164.4 25.9 %self_attend.1 = (bf16[1024,768]{1,0:T(8,128)(2,1)}, f32[1024,768]{1,0:T(8,128)}) custom-call(s32[2,4]{1,0:T(2,128)} %lengths_ref.3, bf16[1024,2304]{1,0:T(8,128)(2,1)} %get-tuple-element.44.q_ref.k_ref.v_ref, bf16[1024,2304]{1,0:T(8,128)(2,1)} %get-tuple-element.44.q_ref.k_ref.v_ref, bf16[1024,2304]{1,0:T(8,128)(2,1)} %get-tuple-element.44.q_ref.k_ref.v_ref), custom_call_target="tpu_custom_call" | custom-call | flops 1610612736 | bytes 18874368 | tf_op jit(solution)/shard_map/self_attend/pallas_call | solution.py:239
  190.4 5.9 place.6
  196.2 5.8 place.7
  203.5 6.4 %place.5 = bf16[4,8,24,3840]{3,2,1,0:T(8,128)(2,1)} custom-call(s32[4]{0:T(128)} %pad_add_fusion.me_ref, bf16[4,24,3840]{2,1,0:T(8,128)(2,1)} %copy-done.5, bf16[4,24,3840]{2,1,0:T(8,128)(2,1)} %copy-done.15, bf16[4,24,3840]{2,1,0:T(8,128)(2,1)} %copy-done.16, bf16[4,24,1920]{2,1,0:T(8,128)(2,1)} %copy-done.30, bf16[4,24,1920]{2,1,0:T(8,128)(2,1)} %copy-done.31, ...), custom_call_target="tpu_custom_call" | custom-call | bytes 11796480 | tf_op jit(solution)/shard_map/place/pallas_call | solution.py:130
  210.0 6.4 %ckv_project.1.k_ref.v_ref = bf16[1024,1536]{1,0:T(8,128)(2,1)} custom-call(bf16[1024,768]{1,0:T(8,128)(2,1)} %n_ref.1, bf16[768,3840]{1,0:T(8,128)(2,1)} %bitcast.363, f32[16,768]{1,0:T(8,128)} %convert_bitcast_fusion.vec_ref), custom_call_target="tpu_custom_call" | custom-call | flops 2415919104 | bytes 10665984 | tf_op jit(solution)/shard_map/ckv_project/pallas_call | solution.py:239
  216.4 8.0 %mid_forward.1 = (f32[1024,768]{1,0:T(8,128)}, bf16[1024,768]{1,0:T(8,128)(2,1)}, bf16[1024,768]{1,0:T(8,128)(2,1)}) custom-call(bf16[1024,768]{1,0:T(8,128)(2,1)} %get-tuple-element.45.o_ref, bf16[1024,768]{1,0:T(8,128)(2,1)} %x_ref.5, bf16[768,3840]{1,0:T(8,128)(2,1)} %bitcast.364, bf16[768,3840]{1,0:T(8,128)(2,1)} %bitcast.365, ...), custom_call_target="tpu_custom_call" | custom-call | flops 2415919104 | bytes 21282816 | tf_op jit(solution)/shard_map/mid_forward/pallas_call | solution.py:239
  224.4 15.9 %cross_attend.1.co_ref = bf16[1024,768]{1,0:T(8,128)(2,1)} custom-call(s32[2,16]{1,0:T(2,128)} %reshape.186.chosen_ref, bf16[1024,768]{1,0:T(8,128)(2,1)} %get-tuple-element.48.q_ref, bf16[1024,1536]{1,0:T(8,128)(2,1)} %ckv_project.1.k_ref.v_ref, bf16[1024,1536]{1,0:T(8,128)(2,1)} %ckv_project.1.k_ref.v_ref), custom_call_target="tpu_custom_call" | custom-call | flops 805306368 | bytes 9437184 | tf_op jit(solution)/shard_map/cross_attend/pallas_call | solution.py:239
  240.3 39.2 %mlp_both.1 = (bf16[1024,768]{1,0:T(8,128)(2,1)}, bf16[1024,3072]{1,0:T(8,128)(2,1)}, bf16[1024,3072]{1,0:T(8,128)(2,1)}, bf16[1024,768]{1,0:T(8,128)(2,1)}, f32...) custom-call(f32[1024,768]{1,0:T(8,128)} %get-tuple-element.47.h1_ref, ...), custom_call_target="tpu_custom_call" | custom-call | flops 21743271936 | bytes 43745280 | tf_op jit(solution)/shard_map/mlp_both/pallas_call | solution.py:239
  281.1 35.2 %cross_back.1 = (bf16[1024,768]{1,0:T(8,128)(2,1)}, bf16[1024,1536]{1,0:T(8,128)(2,1)}) custom-call(s32[2,16]{1,0:T(2,128)} %reshape.186.chosen_ref, bf16[1024,768]{1,0:T(8,128)(2,1)} %get-tuple-element.48.q_ref, bf16[1024,1536]{1,0:T(8,128)(2,1)} %ckv_project.1.k_ref.v_ref, bf16[1024,1536]{1,0:T(8,128)(2,1)} %ckv_project.1.k_ref.v_ref, ...), custom_call_target="tpu_custom_call" | custom-call | flops 2013265920 | bytes 14155776 | tf_op jit(solution)/shard_map/cross_back/pallas_call | solution.py:239
  316.3 6.9 %neighbour_back.1 = (f32[1024,768]{1,0:T(8,128)}, f32[1,768]{1,0:T(1,128)}) custom-call(bf16[1024,1536]{1,0:T(8,128)(2,1)} %get-tuple-element.59.dkv_ref, bf16[768,3840]{1,0:T(8,128)(2,1)} %bitcast.367), custom_call_target="tpu_custom_call" | custom-call | flops 2415919104 | bytes 12192768 | tf_op jit(solution)/shard_map/neighbour_back/pallas_call | solution.py:239
  323.2 5.6 convolution_convert_fusion.3
  328.8 9.0 %mid_back.1 = (f32[1024,768]{1,0:T(8,128)}, bf16[1024,768]{1,0:T(8,128)(2,1)}, bf16[1024,768]{1,0:T(8,128)(2,1)}, f32[8,768]{1,0:T(8,128)}) custom-call(bf16[1024,768]{1,0:T(8,128)(2,1)} %get-tuple-element.53.dcq_ref, f32[1024,768]{1,0:T(8,128)} %get-tuple-element.54.dh2_ref, f32[1024,768]{1,0:T(8,128)} %get-tuple-element.47.h1_ref, ...), custom_call_target="tpu_custom_call" | custom-call | flops 2415919104 | bytes 26025984 | tf_op jit(solution)/shard_map/mid_back/pallas_call | solution.py:239
  337.7 28.3 %self_back.1.dqkv_ref = bf16[1024,2304]{1,0:T(8,128)(2,1)} custom-call(s32[2,4]{1,0:T(2,128)} %lengths_ref.3, bf16[1024,2304]{1,0:T(8,128)(2,1)} %get-tuple-element.44.q_ref.k_ref.v_ref, bf16[1024,2304]{1,0:T(8,128)(2,1)} %get-tuple-element.44.q_ref.k_ref.v_ref, bf16[1024,2304]{1,0:T(8,128)(2,1)} %get-tuple-element.44.q_ref.k_ref.v_ref, ...), custom_call_target="tpu_custom_call" | custom-call | flops 4026531840 | bytes 24117248 | tf_op jit(solution)/shard_map/self_back/pallas_call | solution.py:239
  366.1 10.2 %token_back.1 = (f32[1024,768]{1,0:T(8,128)}, f32[8,768]{1,0:T(8,128)}, f32[1,2304]{1,0:T(1,128)}) custom-call(bf16[1024,2304]{1,0:T(8,128)(2,1)} %self_back.1.dqkv_ref, f32[1024,768]{1,0:T(8,128)} %get-tuple-element.57.dh1_ref, bf16[1024,768]{1,0:T(8,128)(2,1)} %x_ref.5, bf16[768,2432]{1,0:T(8,128)(2,1)} %bitcast.379, f32[16,768]{1,0:T(8,128)} %convert_bitcast_fusion.vec_ref), custom_call_target="tpu_custom_call" | custom-call | flops 3623878656 | bytes 16401408 | tf_op jit(solution)/shard_map/token_back/pallas_call | solution.py:239
  380.4 8.9 %convolution_convert_fusion = bf16[3072,768]{1,0:T(8,128)(2,1)S(1)} fusion(bf16[1024,3072]{1,0:T(8,128)(2,1)} %get-tuple-element.67, bf16[1024,768]{1,0:T(8,128)(2,1)S(1)} %copy-done.47), kind=kOutput, calls=%fused_computation | convolution fusion | flops 4834197504 | bytes 12582912 | tf_op jit(solution)/shard_map/dot_general | solution.py:183
  393.1 5.6 convolution_convert_fusion.1
  407.5 4.1 convolution_convert_fusion.2
  417.5 2.5 convolution_convert_fusion.6
  422.4 2.8 collective-permute-done.107
  484.6 2.9 collective-permute-start.71
  500.7 6.1 %collective-permute-done.75 = bf16[4,2,24,768]{3,2,0,1:T(8,128)(2,1)S(1)} collective-permute-done((bf16[4,2,24,768]{3,2,0,1:T(8,128)(2,1)S(1)}, bf16[4,2,24,768]{3,2,0,1:T(8,128)(2,1)S(1)}, u32[]{:S(2)}, u32[]{:S(2)}) %collective-permute-start.75) | collective-permute-done | bytes 294944 | tf_op jit(solution)/shard_map/ppermute | solution.py:67
  509.7 2.6 collective-permute-done.76
  516.2 2.8 collective-permute-start.79
  523.9 5.9 collective-permute-done.51
  531.2 2.5 collective-permute-done.49
  542.4 3.4 collective-permute-start.53
  556.4 9.1 %collective-permute-done.91 = bf16[4,2,24,1536]{3,2,0,1:T(8,128)(2,1)S(1)} collective-permute-done((bf16[4,2,24,1536]{3,2,0,1:T(8,128)(2,1)S(1)}, bf16[4,2,24,1536]{3,2,0,1:T(8,128)(2,1)S(1)}, u32[]{:S(2)}, u32[]{:S(2)}) %collective-permute-start.91) | collective-permute-done | bytes 589856 | tf_op jit(solution)/shard_map/ppermute | solution.py:67
  571.2 5.2 collective-permute-start.101
  587.0 7.4 %collective-permute-done.94 = bf16[24,3072]{1,0:T(8,128)(2,1)S(1)} collective-permute-done((bf16[24,3072]{1,0:T(8,128)(2,1)S(1)}, bf16[24,3072]{1,0:T(8,128)(2,1)S(1)}, u32[]{:S(2)}, u32[]{:S(2)}) %collective-permute-start.94) | collective-permute-done | bytes 147488 | tf_op jit(solution)/shard_map/ppermute | solution.py:67
  (476 shorter events, 199.7 us)
Async XLA Ops:
  20.6 15.4 %collective-permute-start.13 = (bf16[24,3840]{1,0:T(8,128)(2,1)S(1)}, bf16[24,3840]{1,0:T(8,128)(2,1)S(1)}, u32[]{:S(2)}, u32[]{:S(2)}) collective-permute-start(bf16[24,3840]{1,0:T(8,128)(2,1)S(1)} %pad_maximum_fusion.6), channel_id=1, source_target_pairs={{0,16},{1,17},{2,18},{3,19},{4,20},{5,21},{6,22},{7,23},{8,24},{9,... | collective-permute-start | bytes 552968 | tf_op jit(solution)/shard_map/ppermute | solution.py:67
  23.3 12.8 %collective-permute-start.14 = (bf16[24,3840]{1,0:T(8,128)(2,1)S(1)}, bf16[24,3840]{1,0:T(8,128)(2,1)S(1)}, u32[]{:S(2)}, u32[]{:S(2)}) collective-permute-start(bf16[24,3840]{1,0:T(8,128)(2,1)S(1)} %pad_maximum_fusion.6), channel_id=1, source_target_pairs={{0,24},{1,25},{2,26},{3,27},{4,28},{5,29},{6,30},{7,31},{8,0},{9,1... | collective-permute-start | bytes 552968 | tf_op jit(solution)/shard_map/ppermute | solution.py:67
  42.3 13.4 %collective-permute-start.3 = (bf16[4,24,2432]{2,1,0:T(8,128)(2,1)S(1)}, bf16[4,24,2432]{2,1,0:T(8,128)(2,1)S(1)}, u32[]{:S(2)}, u32[]{:S(2)}) collective-permute-start(bf16[4,24,2432]{2,1,0:T(8,128)(2,1)S(1)} %pad_maximum_fusion.3.refs_0_), channel_id=1, source_target_pairs={{0,2},{1,3},{2,0},{3,1},{4,6},{5,7},{6,4},{7,5},{8,10},{9,11},{10,... | collective-permute-start | bytes 1400840 | tf_op jit(solution)/shard_map/ppermute | solution.py:67
  43.8 13.5 %collective-permute-start.4 = (bf16[4,24,2432]{2,1,0:T(8,128)(2,1)S(1)}, bf16[4,24,2432]{2,1,0:T(8,128)(2,1)S(1)}, u32[]{:S(2)}, u32[]{:S(2)}) collective-permute-start(bf16[4,24,2432]{2,1,0:T(8,128)(2,1)S(1)} %pad_maximum_fusion.3.refs_0_), channel_id=1, source_target_pairs={{0,4},{1,5},{2,6},{3,7},{4,0},{5,1},{6,2},{7,3},{8,12},{9,13},{10,... | collective-permute-start | bytes 1400840 | tf_op jit(solution)/shard_map/ppermute | solution.py:67
  45.3 12.1 %collective-permute-start.7 = (bf16[4,24,2432]{2,1,0:T(8,128)(2,1)S(1)}, bf16[4,24,2432]{2,1,0:T(8,128)(2,1)S(1)}, u32[]{:S(2)}, u32[]{:S(2)}) collective-permute-start(bf16[4,24,2432]{2,1,0:T(8,128)(2,1)S(1)} %pad_maximum_fusion.3.refs_0_), channel_id=1, source_target_pairs={{0,1},{1,0},{2,3},{3,2},{4,5},{5,4},{6,7},{7,6},{8,9},{9,8},{10,11... | collective-permute-start | bytes 1400840 | tf_op jit(solution)/shard_map/ppermute | solution.py:67
  57.4 22.1 %collective-permute-start.27 = (bf16[4,24,3072]{2,1,0:T(8,128)(2,1)S(1)}, bf16[4,24,3072]{2,1,0:T(8,128)(2,1)S(1)}, u32[]{:S(2)}, u32[]{:S(2)}) collective-permute-start(bf16[4,24,3072]{2,1,0:T(8,128)(2,1)S(1)} %pad_maximum_fusion.1.refs_0_), channel_id=1, source_target_pairs={{0,2},{1,3},{2,0},{3,1},{4,6},{5,7},{6,4},{7,5},{8,10},{9,11},{10,... | collective-permute-start | bytes 1769480 | tf_op jit(solution)/shard_map/ppermute | solution.py:67
  60.0 19.5 %collective-permute-start.28 = (bf16[4,24,3072]{2,1,0:T(8,128)(2,1)S(1)}, bf16[4,24,3072]{2,1,0:T(8,128)(2,1)}, u32[]{:S(2)}, u32[]{:S(2)}) collective-permute-start(bf16[4,24,3072]{2,1,0:T(8,128)(2,1)S(1)} %pad_maximum_fusion.1.refs_0_), channel_id=1, source_target_pairs={{0,4},{1,5},{2,6},{3,7},{4,0},{5,1},{6,2},{7,3},{8,12},{9,13},{10,... | collective-permute-start | bytes 1769480 | tf_op jit(solution)/shard_map/ppermute | solution.py:67
  64.4 14.5 %collective-permute-start.6 = (bf16[4,24,1216]{2,1,0:T(8,128)(2,1)S(1)}, bf16[4,24,1216]{2,1,0:T(8,128)(2,1)S(1)}, u32[]{:S(2)}, u32[]{:S(2)}) collective-permute-start(bf16[4,24,1216]{2,1,0:T(8,128)(2,1)S(1)} %slice.160), channel_id=1, source_target_pairs={{0,2},{1,3},{2,0},{3,1},{4,6},{5,7},{6,4},{7,5},{8,10},{9,11},{10,... | collective-permute-start | bytes 700424 | tf_op jit(solution)/shard_map/ppermute | solution.py:67
  65.9 28.9 %collective-permute-start.15 = (bf16[4,24,3840]{2,1,0:T(8,128)(2,1)S(1)}, bf16[4,24,3840]{2,1,0:T(8,128)(2,1)S(1)}, u32[]{:S(2)}, u32[]{:S(2)}) collective-permute-start(bf16[4,24,3840]{2,1,0:T(8,128)(2,1)S(1)} %pad_maximum_fusion.refs_0_), channel_id=1, source_target_pairs={{0,2},{1,3},{2,0},{3,1},{4,6},{5,7},{6,4},{7,5},{8,10},{9,11},{10,... | collective-permute-start | bytes 2211848 | tf_op jit(solution)/shard_map/ppermute | solution.py:67
  66.6 13.5 %collective-permute-start.31 = (bf16[4,24,3072]{2,1,0:T(8,128)(2,1)S(1)}, bf16[4,24,3072]{2,1,0:T(8,128)(2,1)S(1)}, u32[]{:S(2)}, u32[]{:S(2)}) collective-permute-start(bf16[4,24,3072]{2,1,0:T(8,128)(2,1)S(1)} %pad_maximum_fusion.1.refs_0_), channel_id=1, source_target_pairs={{0,1},{1,0},{2,3},{3,2},{4,5},{5,4},{6,7},{7,6},{8,9},{9,8},{10,11... | collective-permute-start | bytes 1769480 | tf_op jit(solution)/shard_map/ppermute | solution.py:67
  78.9 16.4 %collective-permute-start.16 = (bf16[4,24,3840]{2,1,0:T(8,128)(2,1)S(1)}, bf16[4,24,3840]{2,1,0:T(8,128)(2,1)S(1)}, u32[]{:S(2)}, u32[]{:S(2)}) collective-permute-start(bf16[4,24,3840]{2,1,0:T(8,128)(2,1)S(1)} %pad_maximum_fusion.refs_0_), channel_id=1, source_target_pairs={{0,4},{1,5},{2,6},{3,7},{4,0},{5,1},{6,2},{7,3},{8,12},{9,13},{10,... | collective-permute-start | bytes 2211848 | tf_op jit(solution)/shard_map/ppermute | solution.py:67
  79.5 15.8 %collective-permute-start.8 = (bf16[4,24,2432]{2,1,0:T(8,128)(2,1)S(1)}, bf16[4,24,2432]{2,1,0:T(8,128)(2,1)S(1)}, u32[]{:S(2)}, u32[]{:S(2)}) collective-permute-start(bf16[4,24,2432]{2,1,0:T(8,128)(2,1)S(1)} %collective-permute-done.3.refs_1_), channel_id=1, source_target_pairs={{0,1},{1,0},{2,3},{3,2},{4,5},{5,4},{6,7},{7,6},{8,9},{9,8},{10,11... | collective-permute-start | bytes 1400840 | tf_op jit(solution)/shard_map/ppermute | solution.py:67
  79.5 16.3 %collective-permute-start.9 = (bf16[4,24,2432]{2,1,0:T(8,128)(2,1)S(1)}, bf16[4,24,2432]{2,1,0:T(8,128)(2,1)S(1)}, u32[]{:S(2)}, u32[]{:S(2)}) collective-permute-start(bf16[4,24,2432]{2,1,0:T(8,128)(2,1)S(1)} %collective-permute-done.4.refs_2_), channel_id=1, source_target_pairs={{0,1},{1,0},{2,3},{3,2},{4,5},{5,4},{6,7},{7,6},{8,9},{9,8},{10,11... | collective-permute-start | bytes 1400840 | tf_op jit(solution)/shard_map/ppermute | solution.py:67
  80.2 25.4 %collective-permute-start.39 = (bf16[4,96,768]{2,1,0:T(8,128)(2,1)S(1)}, bf16[4,96,768]{2,1,0:T(8,128)(2,1)S(1)}, u32[]{:S(2)}, u32[]{:S(2)}) collective-permute-start(bf16[4,96,768]{2,1,0:T(8,128)(2,1)S(1)} %pad_maximum_fusion.2.refs_0_), channel_id=1, source_target_pairs={{0,2},{1,3},{2,0},{3,1},{4,6},{5,7},{6,4},{7,5},{8,10},{9,11},{10,... | collective-permute-start | bytes 1769480 | tf_op jit(solution)/shard_map/ppermute | solution.py:67
  94.7 16.2 %collective-permute-start.40 = (bf16[4,96,768]{2,1,0:T(8,128)(2,1)S(1)}, bf16[4,96,768]{2,1,0:T(8,128)(2,1)S(1)}, u32[]{:S(2)}, u32[]{:S(2)}) collective-permute-start(bf16[4,96,768]{2,1,0:T(8,128)(2,1)S(1)} %pad_maximum_fusion.2.refs_0_), channel_id=1, source_target_pairs={{0,4},{1,5},{2,6},{3,7},{4,0},{5,1},{6,2},{7,3},{8,12},{9,13},{10,... | collective-permute-start | bytes 1769480 | tf_op jit(solution)/shard_map/ppermute | solution.py:67
  95.3 17.2 %collective-permute-start.43 = (bf16[4,96,768]{2,1,0:T(8,128)(2,1)S(1)}, bf16[4,96,768]{2,1,0:T(8,128)(2,1)S(1)}, u32[]{:S(2)}, u32[]{:S(2)}) collective-permute-start(bf16[4,96,768]{2,1,0:T(8,128)(2,1)S(1)} %pad_maximum_fusion.2.refs_0_), channel_id=1, source_target_pairs={{0,1},{1,0},{2,3},{3,2},{4,5},{5,4},{6,7},{7,6},{8,9},{9,8},{10,11... | collective-permute-start | bytes 1769480 | tf_op jit(solution)/shard_map/ppermute | solution.py:67
  97.7 27.6 %collective-permute-start.17 = (bf16[4,24,1920]{2,1,0:T(8,128)(2,1)S(1)}, bf16[4,24,1920]{2,1,0:T(8,128)(2,1)S(1)}, u32[]{:S(2)}, u32[]{:S(2)}) collective-permute-start(bf16[4,24,1920]{2,1,0:T(8,128)(2,1)S(1)} %slice.162), channel_id=1, source_target_pairs={{0,4},{1,5},{2,6},{3,7},{4,0},{5,1},{6,2},{7,3},{8,12},{9,13},{10,... | collective-permute-start | bytes 1105928 | tf_op jit(solution)/shard_map/ppermute | solution.py:67
  100.2 23.6 %collective-permute-start.29 = (bf16[4,24,1536]{2,1,0:T(8,128)(2,1)S(1)}, bf16[4,24,1536]{2,1,0:T(8,128)(2,1)S(1)}, u32[]{:S(2)}, u32[]{:S(2)}) collective-permute-start(bf16[4,24,1536]{2,1,0:T(8,128)(2,1)S(1)} %slice.164), channel_id=1, source_target_pairs={{0,4},{1,5},{2,6},{3,7},{4,0},{5,1},{6,2},{7,3},{8,12},{9,13},{10,... | collective-permute-start | bytes 884744 | tf_op jit(solution)/shard_map/ppermute | solution.py:67
  105.6 19.8 %collective-permute-start.30 = (bf16[4,24,1536]{2,1,0:T(8,128)(2,1)S(1)}, bf16[4,24,1536]{2,1,0:T(8,128)(2,1)}, u32[]{:S(2)}, u32[]{:S(2)}) collective-permute-start(bf16[4,24,1536]{2,1,0:T(8,128)(2,1)S(1)} %slice.165), channel_id=1, source_target_pairs={{0,2},{1,3},{2,0},{3,1},{4,6},{5,7},{6,4},{7,5},{8,10},{9,11},{10,... | collective-permute-start | bytes 884744 | tf_op jit(solution)/shard_map/ppermute | solution.py:67
  110.9 15.0 %collective-permute-start.18 = (bf16[4,24,1920]{2,1,0:T(8,128)(2,1)S(1)}, bf16[4,24,1920]{2,1,0:T(8,128)(2,1)S(1)}, u32[]{:S(2)}, u32[]{:S(2)}) collective-permute-start(bf16[4,24,1920]{2,1,0:T(8,128)(2,1)S(1)} %slice.163), channel_id=1, source_target_pairs={{0,2},{1,3},{2,0},{3,1},{4,6},{5,7},{6,4},{7,5},{8,10},{9,11},{10,... | collective-permute-start | bytes 1105928 | tf_op jit(solution)/shard_map/ppermute | solution.py:67
  112.5 14.5 %collective-permute-start.41 = (bf16[4,96,384]{2,1,0:T(8,128)(2,1)S(1)}, bf16[4,96,384]{2,1,0:T(8,128)(2,1)}, u32[]{:S(2)}, u32[]{:S(2)}) collective-permute-start(bf16[4,96,384]{2,1,0:T(8,128)(2,1)S(1)} %slice.166), channel_id=1, source_target_pairs={{0,4},{1,5},{2,6},{3,7},{4,0},{5,1},{6,2},{7,3},{8,12},{9,13},{10,... | collective-permute-start | bytes 884744 | tf_op jit(solution)/shard_map/ppermute | solution.py:67
  125.9 18.1 %collective-permute-start.33 = (bf16[4,24,3072]{2,1,0:T(8,128)(2,1)}, bf16[4,24,3072]{2,1,0:T(8,128)(2,1)}, u32[]{:S(2)}, u32[]{:S(2)}) collective-permute-start(bf16[4,24,3072]{2,1,0:T(8,128)(2,1)} %collective-permute-done.28.refs_2_), channel_id=1, source_target_pairs={{0,1},{1,0},{2,3},{3,2},{4,5},{5,4},{6,7},{7,6},{8,9},{9,8},{10,11... | collective-permute-start | bytes 1769480 | tf_op jit(solution)/shard_map/ppermute | solution.py:67
  130.7 13.5 %collective-permute-start.46 = (bf16[4,96,384]{2,1,0:T(8,128)(2,1)}, bf16[4,96,384]{2,1,0:T(8,128)(2,1)}, u32[]{:S(2)}, u32[]{:S(2)}) collective-permute-start(bf16[4,96,384]{2,1,0:T(8,128)(2,1)} %collective-permute-done.41.refs_3_), channel_id=1, source_target_pairs={{0,1},{1,0},{2,3},{3,2},{4,5},{5,4},{6,7},{7,6},{8,9},{9,8},{10,11... | collective-permute-start | bytes 884744 | tf_op jit(solution)/shard_map/ppermute | solution.py:67
  131.4 13.2 %collective-permute-start.47 = (bf16[4,96,384]{2,1,0:T(8,128)(2,1)}, bf16[4,96,384]{2,1,0:T(8,128)(2,1)}, u32[]{:S(2)}, u32[]{:S(2)}) collective-permute-start(bf16[4,96,384]{2,1,0:T(8,128)(2,1)} %collective-permute-done.42.refs_4_), channel_id=1, source_target_pairs={{0,1},{1,0},{2,3},{3,2},{4,5},{5,4},{6,7},{7,6},{8,9},{9,8},{10,11... | collective-permute-start | bytes 884744 | tf_op jit(solution)/shard_map/ppermute | solution.py:67
  135.2 13.1 %collective-permute-start.44 = (bf16[4,96,768]{2,1,0:T(8,128)(2,1)S(1)}, bf16[4,96,768]{2,1,0:T(8,128)(2,1)}, u32[]{:S(2)}, u32[]{:S(2)}) collective-permute-start(bf16[4,96,768]{2,1,0:T(8,128)(2,1)S(1)} %collective-permute-done.39.refs_1_), channel_id=1, source_target_pairs={{0,1},{1,0},{2,3},{3,2},{4,5},{5,4},{6,7},{7,6},{8,9},{9,8},{10,11... | collective-permute-start | bytes 1769480 | tf_op jit(solution)/shard_map/ppermute | solution.py:67
  135.2 13.5 %collective-permute-start.45 = (bf16[4,96,768]{2,1,0:T(8,128)(2,1)}, bf16[4,96,768]{2,1,0:T(8,128)(2,1)}, u32[]{:S(2)}, u32[]{:S(2)}) collective-permute-start(bf16[4,96,768]{2,1,0:T(8,128)(2,1)} %copy-done.22), channel_id=1, source_target_pairs={{0,1},{1,0},{2,3},{3,2},{4,5},{5,4},{6,7},{7,6},{8,9},{9,8},{10,11... | collective-permute-start | bytes 1769480 | tf_op jit(solution)/shard_map/ppermute | solution.py:67
  144.0 58.0 %collective-permute-start.19 = (bf16[4,24,3840]{2,1,0:T(8,128)(2,1)S(1)}, bf16[4,24,3840]{2,1,0:T(8,128)(2,1)}, u32[]{:S(2)}, u32[]{:S(2)}) collective-permute-start(bf16[4,24,3840]{2,1,0:T(8,128)(2,1)S(1)} %pad_maximum_fusion.refs_0_), channel_id=1, source_target_pairs={{0,1},{1,0},{2,3},{3,2},{4,5},{5,4},{6,7},{7,6},{8,9},{9,8},{10,11... | collective-permute-start | bytes 2211848 | tf_op jit(solution)/shard_map/ppermute | solution.py:67
  144.2 57.8 %collective-permute-start.20 = (bf16[4,24,3840]{2,1,0:T(8,128)(2,1)S(1)}, bf16[4,24,3840]{2,1,0:T(8,128)(2,1)}, u32[]{:S(2)}, u32[]{:S(2)}) collective-permute-start(bf16[4,24,3840]{2,1,0:T(8,128)(2,1)S(1)} %collective-permute-done.15.refs_1_), channel_id=1, source_target_pairs={{0,1},{1,0},{2,3},{3,2},{4,5},{5,4},{6,7},{7,6},{8,9},{9,8},{10,11... | collective-permute-start | bytes 2211848 | tf_op jit(solution)/shard_map/ppermute | solution.py:67
  144.6 57.4 %collective-permute-start.21 = (bf16[4,24,3840]{2,1,0:T(8,128)(2,1)S(1)}, bf16[4,24,3840]{2,1,0:T(8,128)(2,1)}, u32[]{:S(2)}, u32[]{:S(2)}) collective-permute-start(bf16[4,24,3840]{2,1,0:T(8,128)(2,1)S(1)} %collective-permute-done.16.refs_2_), channel_id=1, source_target_pairs={{0,1},{1,0},{2,3},{3,2},{4,5},{5,4},{6,7},{7,6},{8,9},{9,8},{10,11... | collective-permute-start | bytes 2211848 | tf_op jit(solution)/shard_map/ppermute | solution.py:67
  148.3 53.7 %collective-permute-start.22 = (bf16[4,24,1920]{2,1,0:T(8,128)(2,1)}, bf16[4,24,1920]{2,1,0:T(8,128)(2,1)S(1)}, u32[]{:S(2)}, u32[]{:S(2)}) collective-permute-start(bf16[4,24,1920]{2,1,0:T(8,128)(2,1)} %copy-done.30), channel_id=1, source_target_pairs={{0,1},{1,0},{2,3},{3,2},{4,5},{5,4},{6,7},{7,6},{8,9},{9,8},{10,11... | collective-permute-start | bytes 1105928 | tf_op jit(solution)/shard_map/ppermute | solution.py:67
  148.7 53.3 %collective-permute-start.23 = (bf16[4,24,1920]{2,1,0:T(8,128)(2,1)}, bf16[4,24,1920]{2,1,0:T(8,128)(2,1)S(1)}, u32[]{:S(2)}, u32[]{:S(2)}) collective-permute-start(bf16[4,24,1920]{2,1,0:T(8,128)(2,1)} %copy-done.31), channel_id=1, source_target_pairs={{0,1},{1,0},{2,3},{3,2},{4,5},{5,4},{6,7},{7,6},{8,9},{9,8},{10,11... | collective-permute-start | bytes 1105928 | tf_op jit(solution)/shard_map/ppermute | solution.py:67
  379.9 40.2 %collective-permute-start.104 = (f32[4,2,2,24,256]{4,3,2,1,0:T(8,128)S(1)}, f32[4,2,2,24,256]{4,3,2,1,0:T(8,128)S(1)}, u32[]{:S(2)}, u32[]{:S(2)}) collective-permute-start(f32[4,2,2,24,256]{4,3,2,1,0:T(8,128)S(1)} %dynamic-slice_bitcast_fusion.6), channel_id=1, source_target_pairs={{0,1},{1,0},{2,3},{3,2},{4,5},{5,4},{6,7},{7,6},{8,9},{9,8},{10,11... | collective-permute-start | bytes 1179656 | tf_op jit(solution)/shard_map/ppermute | solution.py:67
  392.6 142.4 %collective-permute-start.96 = (bf16[4,2,2,96,768]{4,3,0,1,2:T(8,128)(2,1)}, bf16[4,2,2,96,768]{4,3,0,1,2:T(8,128)(2,1)}, u32[]{:S(2)}, u32[]{:S(2)}) collective-permute-start(bf16[4,2,2,96,768]{4,3,0,1,2:T(8,128)(2,1)} %bitcast.356), channel_id=1, source_target_pairs={{0,1},{1,0},{2,3},{3,2},{4,5},{5,4},{6,7},{7,6},{8,9},{9,8},{10,11... | collective-permute-start | bytes 7077896 | tf_op jit(solution)/shard_map/ppermute | solution.py:67
  403.9 49.4 %collective-permute-start.80 = (bf16[4,2,2,24,768]{4,3,0,1,2:T(8,128)(2,1)}, bf16[4,2,2,24,768]{4,3,0,1,2:T(8,128)(2,1)}, u32[]{:S(2)}, u32[]{:S(2)}) collective-permute-start(bf16[4,2,2,24,768]{4,3,0,1,2:T(8,128)(2,1)} %bitcast.360), channel_id=1, source_target_pairs={{0,1},{1,0},{2,3},{3,2},{4,5},{5,4},{6,7},{7,6},{8,9},{9,8},{10,11... | collective-permute-start | bytes 1769480 | tf_op jit(solution)/shard_map/ppermute | solution.py:67
  432.9 14.8 %collective-permute-start.109 = (f32[24,256]{0,1:T(8,128)}, f32[24,256]{0,1:T(8,128)}, u32[]{:S(2)}, u32[]{:S(2)}) collective-permute-start(f32[24,256]{0,1:T(8,128)} %bitcast.407), channel_id=1, source_target_pairs={{0,8},{1,9},{2,10},{3,11},{4,12},{5,13},{6,14},{7,15},{8,16},{9,17... | collective-permute-start | bytes 73736 | tf_op jit(solution)/shard_map/ppermute | solution.py:67
  434.4 13.2 %collective-permute-start.110 = (f32[24,256]{0,1:T(8,128)}, f32[24,256]{0,1:T(8,128)}, u32[]{:S(2)}, u32[]{:S(2)}) collective-permute-start(f32[24,256]{0,1:T(8,128)} %bitcast.406), channel_id=1, source_target_pairs={{0,16},{1,17},{2,18},{3,19},{4,20},{5,21},{6,22},{7,23},{8,24},{9,... | collective-permute-start | bytes 73736 | tf_op jit(solution)/shard_map/ppermute | solution.py:67
  447.7 44.4 %collective-permute-start.72 = (bf16[4,2,2,24,1536]{4,3,0,1,2:T(8,128)(2,1)}, bf16[4,2,2,24,1536]{4,3,0,1,2:T(8,128)(2,1)}, u32[]{:S(2)}, u32[]{:S(2)}) collective-permute-start(bf16[4,2,2,24,1536]{4,3,0,1,2:T(8,128)(2,1)} %bitcast.387), channel_id=1, source_target_pairs={{0,1},{1,0},{2,3},{3,2},{4,5},{5,4},{6,7},{7,6},{8,9},{9,8},{10,11... | collective-permute-start | bytes 3538952 | tf_op jit(solution)/shard_map/ppermute | solution.py:67
  488.2 28.0 %collective-permute-start.48 = (bf16[4,2,2,24,2304]{4,3,0,1,2:T(8,128)(2,1)S(1)}, bf16[4,2,2,24,2304]{4,3,0,1,2:T(8,128)(2,1)S(1)}, u32[]{:S(2)}, u32[]{:S(2)}) collective-permute-start(bf16[4,2,2,24,2304]{4,3,0,1,2:T(8,128)(2,1)S(1)} %bitcast.385), channel_id=1, source_target_pairs={{0,1},{1,0},{2,3},{3,2},{4,5},{5,4},{6,7},{7,6},{8,9},{9,8},{10,11... | collective-permute-start | bytes 5308424 | tf_op jit(solution)/shard_map/ppermute | solution.py:67
  497.3 43.0 %collective-permute-start.88 = (bf16[4,2,2,24,3072]{4,3,0,1,2:T(8,128)(2,1)S(1)}, bf16[4,2,2,24,3072]{4,3,0,1,2:T(8,128)(2,1)S(1)}, u32[]{:S(2)}, u32[]{:S(2)}) collective-permute-start(bf16[4,2,2,24,3072]{4,3,0,1,2:T(8,128)(2,1)S(1)} %bitcast.384), channel_id=1, source_target_pairs={{0,1},{1,0},{2,3},{3,2},{4,5},{5,4},{6,7},{7,6},{8,9},{9,8},{10,11... | collective-permute-start | bytes 7077896 | tf_op jit(solution)/shard_map/ppermute | solution.py:67
  537.8 16.4 %collective-permute-start.99 = (bf16[4,2,96,384]{3,2,0,1:T(8,128)(2,1)S(1)}, bf16[4,2,96,384]{3,2,0,1:T(8,128)(2,1)S(1)}, u32[]{:S(2)}, u32[]{:S(2)}) collective-permute-start(bf16[4,2,96,384]{3,2,0,1:T(8,128)(2,1)S(1)} %dynamic-slice_bitcast_fusion), channel_id=1, source_target_pairs={{0,2},{1,3},{2,0},{3,1},{4,6},{5,7},{6,4},{7,5},{8,10},{9,11},{10,... | collective-permute-start | bytes 1769480 | tf_op jit(solution)/shard_map/ppermute | solution.py:67
  538.9 16.4 %collective-permute-start.97 = (bf16[4,2,96,384]{3,2,0,1:T(8,128)(2,1)S(1)}, bf16[4,2,96,384]{3,2,0,1:T(8,128)(2,1)S(1)}, u32[]{:S(2)}, u32[]{:S(2)}) collective-permute-start(bf16[4,2,96,384]{3,2,0,1:T(8,128)(2,1)S(1)} %dynamic-slice_bitcast_fusion.1), channel_id=1, source_target_pairs={{0,4},{1,5},{2,6},{3,7},{4,0},{5,1},{6,2},{7,3},{8,12},{9,13},{10,... | collective-permute-start | bytes 1769480 | tf_op jit(solution)/shard_map/ppermute | solution.py:67
  549.3 16.3 %collective-permute-start.91 = (bf16[4,2,24,1536]{3,2,0,1:T(8,128)(2,1)S(1)}, bf16[4,2,24,1536]{3,2,0,1:T(8,128)(2,1)S(1)}, u32[]{:S(2)}, u32[]{:S(2)}) collective-permute-start(bf16[4,2,24,1536]{3,2,0,1:T(8,128)(2,1)S(1)} %dynamic-slice_bitcast_fusion.2), channel_id=1, source_target_pairs={{0,2},{1,3},{2,0},{3,1},{4,6},{5,7},{6,4},{7,5},{8,10},{9,11},{10,... | collective-permute-start | bytes 1769480 | tf_op jit(solution)/shard_map/ppermute | solution.py:67
  552.2 15.6 %collective-permute-start.89 = (bf16[4,2,24,1536]{3,2,0,1:T(8,128)(2,1)S(1)}, bf16[4,2,24,1536]{3,2,0,1:T(8,128)(2,1)S(1)}, u32[]{:S(2)}, u32[]{:S(2)}) collective-permute-start(bf16[4,2,24,1536]{3,2,0,1:T(8,128)(2,1)S(1)} %dynamic-slice_bitcast_fusion.3), channel_id=1, source_target_pairs={{0,4},{1,5},{2,6},{3,7},{4,0},{5,1},{6,2},{7,3},{8,12},{9,13},{10,... | collective-permute-start | bytes 1769480 | tf_op jit(solution)/shard_map/ppermute | solution.py:67
  554.4 16.6 %collective-permute-start.100 = (bf16[4,96,384]{2,1,0:T(8,128)(2,1)S(1)}, bf16[4,96,384]{2,1,0:T(8,128)(2,1)S(1)}, u32[]{:S(2)}, u32[]{:S(2)}) collective-permute-start(bf16[4,96,384]{2,1,0:T(8,128)(2,1)S(1)} %dynamic-slice_bitcast_fusion.7), channel_id=1, source_target_pairs={{0,4},{1,5},{2,6},{3,7},{4,0},{5,1},{6,2},{7,3},{8,12},{9,13},{10,... | collective-permute-start | bytes 884744 | tf_op jit(solution)/shard_map/ppermute | solution.py:67
  555.5 15.6 %collective-permute-start.98 = (bf16[4,96,384]{2,1,0:T(8,128)(2,1)S(1)}, bf16[4,96,384]{2,1,0:T(8,128)(2,1)S(1)}, u32[]{:S(2)}, u32[]{:S(2)}) collective-permute-start(bf16[4,96,384]{2,1,0:T(8,128)(2,1)S(1)} %dynamic-slice_bitcast_fusion.8), channel_id=1, source_target_pairs={{0,2},{1,3},{2,0},{3,1},{4,6},{5,7},{6,4},{7,5},{8,10},{9,11},{10,... | collective-permute-start | bytes 884744 | tf_op jit(solution)/shard_map/ppermute | solution.py:67
  565.8 13.1 %collective-permute-start.92 = (bf16[4,24,1536]{2,1,0:T(8,128)(2,1)S(1)}, bf16[4,24,1536]{2,1,0:T(8,128)(2,1)S(1)}, u32[]{:S(2)}, u32[]{:S(2)}) collective-permute-start(bf16[4,24,1536]{2,1,0:T(8,128)(2,1)S(1)} %dynamic-slice_bitcast_fusion.9), channel_id=1, source_target_pairs={{0,4},{1,5},{2,6},{3,7},{4,0},{5,1},{6,2},{7,3},{8,12},{9,13},{10,... | collective-permute-start | bytes 884744 | tf_op jit(solution)/shard_map/ppermute | solution.py:67
  579.6 14.8 %collective-permute-start.94 = (bf16[24,3072]{1,0:T(8,128)(2,1)S(1)}, bf16[24,3072]{1,0:T(8,128)(2,1)S(1)}, u32[]{:S(2)}, u32[]{:S(2)}) collective-permute-start(bf16[24,3072]{1,0:T(8,128)(2,1)S(1)} %get-tuple-element.100), channel_id=1, source_target_pairs={{0,16},{1,17},{2,18},{3,19},{4,20},{5,21},{6,22},{7,23},{8,24},{9,... | collective-permute-start | bytes 442376 | tf_op jit(solution)/shard_map/ppermute | solution.py:67
  581.7 12.7 %collective-permute-start.95 = (bf16[24,3072]{1,0:T(8,128)(2,1)S(1)}, bf16[24,3072]{1,0:T(8,128)(2,1)S(1)}, u32[]{:S(2)}, u32[]{:S(2)}) collective-permute-start(bf16[24,3072]{1,0:T(8,128)(2,1)S(1)} %get-tuple-element.101), channel_id=1, source_target_pairs={{0,24},{1,25},{2,26},{3,27},{4,28},{5,29},{6,30},{7,31},{8,0},{9,1... | collective-permute-start | bytes 442376 | tf_op jit(solution)/shard_map/ppermute | solution.py:67
  (121 other events, 1451.5 us)

commit v2 on v1

--- a/solution.py
+++ b/solution.py
@@ -23,6 +23,8 @@
 ROWS = 256
 SMALL = 18
 TILE_F = 512
+QKV_TILE = 384
+WIDE = 3
 
 epsilon = 1e-05
 rope_base = 10000.0
@@ -68,107 +70,215 @@
 
 
 def after(values, *anchors):
-    return lax.optimization_barrier((values,) + anchors)[0]
+    return lax.optimization_barrier((values, anchors))[0]
 
 
 def gather_z(block, sizes):
-    parts = [block] + [shift(block, sizes, 0, d) for d in range(1, sizes[0])]
-    return jnp.stack(parts)
-
-
-def gather_rest(own, sizes):
-    half = own.shape[-1] // 2
-    nz, ny, nx, nc = sizes
-    pieces = {}
-    along_x = {d: shift(own, sizes, 2, d) for d in range(1, nx)}
-    along_y = {e: shift(own, sizes, 1, e) for e in range(1, ny)}
-    pieces[0, 0, 0] = (own,)
-    for d in range(1, nx):
-        pieces[0, 0, d] = (along_x[d],)
-    for e in range(1, ny):
-        pieces[0, e, 0] = (along_y[e],)
-    for d in range(1, nx):
-        for e in range(1, ny):
-            first = shift(along_x[d][..., :half], sizes, 1, e)
-            second = shift(along_y[e][..., half:], sizes, 2, d)
-            pieces[0, e, d] = (first, second)
-    for (_, e, d), held in list(pieces.items()):
-        for c in range(1, nc):
-            pieces[c, e, d] = tuple(shift(part, sizes, 3, c) for part in held)
+    return jnp.stack([block] + [shift(block, sizes, 0, d) for d in range(1, sizes[0])])
+
+
+def gather_side(own, sizes):
+    along_x = {d: shift(own, sizes, 2, d) for d in range(1, sizes[2])}
+    along_y = {e: shift(own, sizes, 1, e) for e in range(1, sizes[1])}
+    return along_x, along_y
+
+
+def gather_corner(side, sizes):
+    along_x, along_y = side
+    corner = {}
+    for d, first in along_x.items():
+        for e, second in along_y.items():
+            half = first.shape[-1] // 2
+            corner[e, d] = (
+                shift(first[..., :half], sizes, 1, e),
+                shift(second[..., half:], sizes, 2, d),
+            )
+    return corner
+
+
+def gather_core(pieces, sizes):
+    return {
+        (c,) + key: tuple(shift(part, sizes, 3, c) for part in held)
+        for key, held in pieces.items()
+        for c in range(1, sizes[3])
+    }
+
+
+def near_pieces(own, side):
+    pieces = {(0, 0): (own,)}
+    pieces.update({(0, d): (part,) for d, part in side[0].items()})
+    pieces.update({(e, 0): (part,) for e, part in side[1].items()})
     return pieces
 
 
-def place_kernel(keys, counts, sizes, me_ref, *refs):
-    out_ref = refs[-1]
+def place_kernel(keys, counts, sizes, split, me_ref, *refs):
+    outs = refs[sum(counts) :]
     at = 0
-    half = out_ref.shape[-1] // 2
     for (c, e, d), count in zip(keys, counts):
         y = lax.rem(me_ref[1] - e + sizes[1], sizes[1])
         x = lax.rem(me_ref[2] - d + sizes[2], sizes[2])
         k = lax.rem(me_ref[3] - c + sizes[3], sizes[3])
         slot = (y * sizes[2] + x) * sizes[3] + k
-        if count == 1:
-            out_ref[0, slot] = refs[at][0]
+        held = refs[at : at + count]
+        rows, width = held[0].shape[1:]
+        width = width * count
+        half = width // 2
+        if split:
+            low, high = held if count == 2 else (held[0], held[0])
+            for m in range(FF // D):
+                outs[0][0, slot, m * rows : (m + 1) * rows] = low[0, :, m * D : (m + 1) * D]
+            outs[1][0, slot] = high[0, :, 0 if count == 2 else half :]
+        elif count == 1:
+            outs[0][0, slot] = held[0][0]
         else:
-            out_ref[0, slot, :, :half] = refs[at][0]
-            out_ref[0, slot, :, half:] = refs[at + 1][0]
+            outs[0][0, slot, :, :half] = held[0][0]
+            outs[0][0, slot, :, half:] = held[1][0]
         at += count
 
 
-def place(pieces, sizes, me):
+def place(pieces, sizes, me, split=False):
     keys = sorted(pieces)
     counts = [len(pieces[key]) for key in keys]
     arrays = [part for key in keys for part in pieces[key]]
     rows, width = pieces[0, 0, 0][0].shape[1:]
+    nz = sizes[0]
     inner = sizes[1] * sizes[2] * sizes[3]
-    nz = sizes[0]
+    shapes = [(rows * (FF // D), D), (rows, FF)] if split else [(rows, width)]
 
     def source(z, me_ref):
         return (lax.rem(me_ref[0] - z + nz, nz), 0, 0)
 
     moved = 2 * nz * inner * rows * width * 2
-    out = pl.pallas_call(
-        functools.partial(place_kernel, keys, counts, sizes),
-        out_shape=jax.ShapeDtypeStruct((nz, inner, rows, width), arrays[0].dtype),
+    outs = pl.pallas_call(
+        functools.partial(place_kernel, keys, counts, sizes, split),
+        out_shape=[like((nz, inner) + shape, bf16) for shape in shapes],
         grid_spec=pltpu.PrefetchScalarGridSpec(
             num_scalar_prefetch=1,
             grid=(nz,),
             in_specs=[pl.BlockSpec((1,) + a.shape[1:], source) for a in arrays],
-            out_specs=pl.BlockSpec((1, inner, rows, width), lambda z, me_ref: (z, 0, 0, 0)),
+            out_specs=[
+                pl.BlockSpec((1, inner) + shape, lambda z, me_ref: (z, 0, 0, 0)) for shape in shapes
+            ],
         ),
         cost_estimate=pl.CostEstimate(flops=0, transcendentals=0, bytes_accessed=moved),
         name="place",
     )(me, *arrays)
-    return out.reshape(nz * inner * rows, width)
-
-
-def take(values, axis, index):
-    return lax.dynamic_index_in_dim(values, index, axis, keepdims=False)
-
-
-def reduce_axis(values, sizes, axis, at, me, kind):
-    size = sizes[axis]
-    total = take(values, at, me[axis]).astype(f32)
-    for step in range(1, size):
-        target = lax.rem(me[axis] + step, size)
-        got = shift(take(values, at, target), sizes, axis, step)
-        total = total + got.astype(f32)
-    return total.astype(kind)
-
-
-def scatter_sum(values, sizes, me):
-    count = math.prod(sizes)
-    rows, width = values.shape[0] // count, values.shape[1]
-    kind = values.dtype
-    blocks = values.reshape(tuple(sizes) + (rows, width))
-    summed = reduce_axis(blocks, sizes, 3, 3, me, kind)
-    half = width // 2
-    first, second = summed[..., :half], summed[..., half:]
-    first = reduce_axis(first, sizes, 1, 1, me, kind)
-    second = reduce_axis(second, sizes, 2, 2, me, kind)
-    first = reduce_axis(first, sizes, 2, 1, me, kind)
-    second = reduce_axis(second, sizes, 1, 1, me, kind)
-    return reduce_axis(jnp.concatenate([first, second], -1), sizes, 0, 0, me, f32)
+    outs = [out.reshape(nz * inner * out.shape[2], out.shape[3]) for out in outs]
+    return outs if split else outs[0]
+
+
+def spread_kernel(sizes, split, me_ref, *refs):
+    keep_ref, send_ref = refs[-2:]
+    ny, nx, nc = sizes[1:]
+    for ry in range(ny):
+        for rx in range(nx):
+            y, x = lax.rem(me_ref[1] + ry, ny), lax.rem(me_ref[2] + rx, nx)
+            base = (y * nx + x) * nc
+            for out_ref, core in ((keep_ref, me_ref[3]), (send_ref, 1 - me_ref[3])):
+                column = 0
+                rows = out_ref.shape[3]
+                for at, ref in enumerate(refs[:-2]):
+                    width = ref.shape[3]
+                    if split and at == 0:
+                        for m in range(FF // D):
+                            part = ref[0, base + core, m * rows : (m + 1) * rows]
+                            out_ref[0, ry, rx, :, column + m * D : column + (m + 1) * D] = part
+                        column += FF
+                    else:
+                        out_ref[0, ry, rx, :, column : column + width] = ref[0, base + core]
+                        column += width
+
+
+def spread(grads, sizes, me, split=False):
+    nz, ny, nx, nc = sizes
+    inner = ny * nx * nc
+    rows = D // math.prod(sizes)
+    blocks = [g.reshape(nz, inner, g.shape[0] // (nz * inner), g.shape[1]) for g in grads]
+    width = sum(b.shape[2] * b.shape[3] for b in blocks) // rows
+    kind = grads[0].dtype
+    shape = like((nz, ny, nx, rows, width), kind)
+    block = pl.BlockSpec((1, ny, nx, rows, width), lambda z, me_ref: (z, 0, 0, 0, 0))
+
+    def source(z, me_ref):
+        return (lax.rem(me_ref[0] + z, nz), 0, 0, 0)
+
+    moved = 2 * D * width * kind.itemsize
+    return pl.pallas_call(
+        functools.partial(spread_kernel, sizes, split),
+        out_shape=[shape, shape],
+        grid_spec=pltpu.PrefetchScalarGridSpec(
+            num_scalar_prefetch=1,
+            grid=(nz,),
+            in_specs=[pl.BlockSpec((1,) + b.shape[1:], source) for b in blocks],
+            out_specs=[block, block],
+        ),
+        cost_estimate=pl.CostEstimate(flops=0, transcendentals=0, bytes_accessed=moved),
+        name="spread",
+    )(me, *blocks)
+
+
+def plus(first, *others):
+    total = first.astype(f32)
+    for other in others:
+        total = total + other.astype(f32)
+    return total
+
+
+def fold_core(kept, got, sizes):
+    half = kept.shape[-1] // 2
+    kind = kept.dtype
+
+    def part(*index):
+        return plus(kept[index], got[index]).astype(kind)
+
+    every = slice(None)
+    low, high = slice(None, half), slice(half, None)
+    first = [part(every, e, every, every, low) for e in range(sizes[1])]
+    second = [part(every, every, d, every, high) for d in range(sizes[2])]
+    return first, second
+
+
+def send_side(parts, sizes):
+    first, second = parts
+    return (
+        [first[0]] + [shift(first[e], sizes, 1, e) for e in range(1, sizes[1])],
+        [second[0]] + [shift(second[d], sizes, 2, d) for d in range(1, sizes[2])],
+    )
+
+
+def fold_side(got, sizes):
+    kind = got[0][0].dtype
+    first = [plus(*[g[:, d] for g in got[0]]).astype(kind) for d in range(sizes[2])]
+    second = [plus(*[g[:, e] for g in got[1]]).astype(kind) for e in range(sizes[1])]
+    return first, second
+
+
+def send_corner(parts, sizes):
+    first, second = parts
+    return (
+        [first[0]] + [shift(first[d], sizes, 2, d) for d in range(1, sizes[2])],
+        [second[0]] + [shift(second[e], sizes, 1, e) for e in range(1, sizes[1])],
+    )
+
+
+def fold_corner(got, sizes):
+    kind = got[0][0].dtype
+    return [
+        jnp.concatenate([plus(*[g[z] for g in half]).astype(kind) for half in got], -1)
+        for z in range(sizes[0])
+    ]
+
+
+def send_z(parts, sizes):
+    return [parts[0]] + [shift(parts[z], sizes, 0, z) for z in range(1, sizes[0])]
+
+
+def scatter_small(kept, sent, sizes):
+    total = plus(kept, shift(sent, sizes, 3, 1))
+    for axis, at in ((1, 1), (2, 1), (0, 0)):
+        parts = [lax.index_in_dim(total, step, at, keepdims=False) for step in range(sizes[axis])]
+        total = plus(*[parts[0]] + [shift(p, sizes, axis, k) for k, p in enumerate(parts) if k])
+    return total
 
 
 def dot_nn(a, b):
@@ -233,7 +343,20 @@
     )
 
 
-def call(kernel, name, grid, ins, in_specs, outs, out_specs, flops, scratch=(), scalars=(), exps=0):
+def call(
+    kernel,
+    name,
+    grid,
+    ins,
+    in_specs,
+    outs,
+    out_specs,
+    flops,
+    scratch=(),
+    scalars=(),
+    exps=0,
+    aliases={},
+):
     arrays = jax.tree.leaves((ins, outs))
     nbytes = sum(math.prod(a.shape) * a.dtype.itemsize for a in arrays)
     return pl.pallas_call(
@@ -249,6 +372,7 @@
         compiler_params=pltpu.CompilerParams(
             dimension_semantics=("arbitrary",) * len(grid), vmem_limit_bytes=60 << 20
         ),
+        input_output_aliases=aliases,
         cost_estimate=pl.CostEstimate(flops=flops, transcendentals=exps, bytes_accessed=nbytes),
         name=name,
     )(*scalars, *ins)
@@ -265,152 +389,199 @@
 def qkv_kernel(x_ref, w_ref, vec_ref, cos_ref, sin_ref, a1_ref, out_ref):
     part = pl.program_id(0)
     rows = x_ref.shape[0]
+    width = w_ref.shape[1]
 
     @pl.when(part == 0)
     def _():
         for r in range(0, rows, ROWS):
             normed, _ = normed_of(x_ref[r : r + ROWS].astype(f32))
-            a1_ref[r : r + ROWS] = (normed * vec_ref[8:9] + vec_ref[11:12]).astype(bf16)
-
-    bias = vec_ref[pl.ds(part, 1), :]
+            a1_ref[r : r + ROWS] = (normed * vec_ref[8:9, :D] + vec_ref[11:12, :D]).astype(bf16)
+
+    column = pl.multiple_of(lax.rem(part, D // width) * width, width)
+    bias = vec_ref[pl.ds(part // (D // width), 1), pl.ds(column, width)]
     for r in range(0, rows, ROWS):
         mixed = dot_nn(a1_ref[r : r + ROWS], w_ref[...]) + bias
         at = r % SEQ_LEN
-
-        @pl.when(part < 2)
-        def _():
-            cosine, sine = cos_ref[at : at + ROWS], sin_ref[at : at + ROWS]
-            for c in range(0, D, LANES):
-                turned = turn(mixed[:, c : c + LANES], cosine, sine)
-                out_ref[r : r + ROWS, c : c + LANES] = turned.astype(bf16)
-
-        @pl.when(part == 2)
-        def _():
-            out_ref[r : r + ROWS] = mixed.astype(bf16)
+        cosine, sine = cos_ref[0, at : at + ROWS], sin_ref[0, at : at + ROWS]
+        for c in range(0, width, LANES):
+            turned = turn(mixed[:, c : c + LANES], cosine, sine)
+            out_ref[r : r + ROWS, c : c + LANES] = turned.astype(bf16)
 
 
 def qkv_project(x, weight, vec, cosine, sine):
     rows = x.shape[0]
+    width = QKV_TILE
+    tables = (
+        jnp.stack([cosine, jnp.ones_like(cosine)]),
+        jnp.stack([sine, jnp.zeros_like(sine)]),
+    )
+    table = pl.BlockSpec((1, SEQ_LEN, LANES), lambda j: (j // (2 * D // width), 0, 0))
     return call(
         qkv_kernel,
         "qkv_project",
-        (3,),
-        (x, weight, vec, cosine, sine),
+        (3 * D // width,),
+        (x, weight, vec) + tables,
         [
             whole((rows, D)),
-            pl.BlockSpec((D, D), lambda j: (0, j)),
+            pl.BlockSpec((D, width), lambda j: (0, j)),
             whole(vec.shape),
-            whole((SEQ_LEN, LANES)),
-            whole((SEQ_LEN, LANES)),
+            table,
+            table,
         ],
         (like((rows, D), bf16), like((rows, 3 * D), bf16)),
-        (whole((rows, D)), pl.BlockSpec((rows, D), lambda j: (0, j))),
+        (whole((rows, D)), pl.BlockSpec((rows, width), lambda j: (0, j))),
         2 * rows * D * 3 * D,
     )
 
 
-def limits(lengths_ref, seq, positions):
-    first = lengths_ref[seq, 0]
-    second = first + lengths_ref[seq, 1]
-    third = second + lengths_ref[seq, 2]
-    tail = jnp.where(positions < third, third, SEQ_LEN)
-    tail = jnp.where(positions < second, second, tail)
-    return jnp.where(positions < first, first, tail)
-
-
-def self_kernel(lengths_ref, q_ref, k_ref, v_ref, o_ref, lse_ref):
+def blocks_of(lengths_ref, seq, positions):
+    end, found = 0, jnp.zeros(positions.shape, jnp.int32)
+    for i in range(3):
+        end = end + lengths_ref[seq, i]
+        found = found + (positions >= end).astype(jnp.int32)
+    return found
+
+
+def mask_features(lengths_ref, seq):
+    rows = lax.broadcasted_iota(jnp.int32, (SEQ_LEN, LANES), 0)
+    slot = lax.broadcasted_iota(jnp.int32, (SEQ_LEN, LANES), 1) & (HEAD_DIM - 1)
+    block = blocks_of(lengths_ref, seq, rows)
+    later = (slot > block) & (slot < 4)
+    return (
+        jnp.where(later, -1e30, 0.0).astype(bf16),
+        jnp.where(slot == block, 1.0, 0.0).astype(bf16),
+    )
+
+
+def self_kernel(lengths_ref, q_ref, k_ref, v_ref, o_ref, lse_ref, fq_ref, fk_ref):
     seq = pl.program_id(0)
+
+    @pl.when(pl.program_id(1) == 0)
+    def _():
+        fq_ref[...], fk_ref[...] = mask_features(lengths_ref, seq)
+
     keep = lane_halves(bf16)
     low_lane = lax.broadcasted_iota(jnp.int32, (1, LANES), 1) < HEAD_DIM
-    for r in range(0, SEQ_LEN, ROWS):
-        rows = lax.broadcasted_iota(jnp.int32, (ROWS, 1), 0) + r
-        columns = lax.broadcasted_iota(jnp.int32, (ROWS, SEQ_LEN), 1)
-        allowed = columns < limits(lengths_ref, seq, rows)
-        query = q_ref[r : r + ROWS] * scale
-        outs, totals = [], []
-        for h in range(2):
-            scores = dot_nt(query * keep[h], k_ref[...])
-            scores = jnp.where(allowed, scores, -1e30)
-            row_max = jnp.max(scores, -1, keepdims=True)
-            exponent = jnp.exp(scores - row_max)
-            total = jnp.sum(exponent, -1, keepdims=True)
-            weights = (exponent * (1.0 / total)).astype(bf16)
-            outs.append(dot_nn(weights, v_ref[...]))
-            totals.append(row_max + jnp.log(total))
-        o_ref[r : r + ROWS] = jnp.where(low_lane, outs[0], outs[1]).astype(bf16)
-        lse_ref[r : r + ROWS] = jnp.where(low_lane, totals[0], totals[1])
+    ones = jnp.ones((SEQ_LEN, LANES), bf16)
+    starts = range(0, SEQ_LEN, ROWS)
+    for c in range(0, q_ref.shape[1], LANES):
+        lanes = slice(c, c + LANES)
+        query, key = q_ref[:, lanes] * scale, k_ref[:, lanes]
+        queries = [query * keep[h] + fq_ref[...] * keep[1 - h] for h in range(2)]
+        keys = [key * keep[h] + fk_ref[...] * keep[1 - h] for h in range(2)]
+        value = jnp.concatenate([v_ref[:, lanes], ones], 1)
+        parts = [(r, h) for r in starts for h in range(2)]
+        scores = [dot_nt(queries[h][r : r + ROWS], keys[h]) for r, h in parts]
+        tops = [jnp.max(s, -1, keepdims=True) for s in scores]
+        weights = [jnp.exp(s - top).astype(bf16) for s, top in zip(scores, tops)]
+        outs = [dot_nn(w, value) for w in weights]
+        for i, r in enumerate(starts):
+            first, second = outs[2 * i], outs[2 * i + 1]
+            total = jnp.where(low_lane, first[:, LANES:], second[:, LANES:])
+            out = jnp.where(low_lane, first[:, :LANES], second[:, :LANES]) / total
+            o_ref[r : r + ROWS, lanes] = out.astype(bf16)
+            other = jnp.where(low_lane, second[:, LANES:], first[:, LANES:])
+            top = jnp.where(low_lane, tops[2 * i + 1], tops[2 * i])
+            lse_ref[r : r + ROWS, lanes] = top + jnp.log(other)
 
 
 def self_attend(lengths, qkv):
     rows = qkv.shape[0]
     seqs = rows // SEQ_LEN
-    block = (SEQ_LEN, LANES)
+    width = WIDE * LANES
+    steps = PAIRS // WIDE
 
     def at(offset):
-        return pl.BlockSpec(block, lambda s, p, _: (s, offset + p))
+        return pl.BlockSpec((SEQ_LEN, width), lambda s, p, _: (s, offset + p))
 
     return call(
         self_kernel,
         "self_attend",
-        (seqs, PAIRS),
+        (seqs, steps),
         (qkv, qkv, qkv),
-        [at(0), at(PAIRS), at(2 * PAIRS)],
+        [at(0), at(steps), at(2 * steps)],
         (like((rows, D), bf16), like((rows, D), f32)),
         (at(0), at(0)),
         4 * rows * SEQ_LEN * D,
+        scratch=[pltpu.VMEM((SEQ_LEN, LANES), bf16)] * 2,
         scalars=(lengths,),
         exps=rows * SEQ_LEN * HEADS,
     )
 
 
-def self_back_kernel(lengths_ref, q_ref, k_ref, v_ref, do_ref, lse_ref, cos_ref, sin_ref, out_ref):
-    seq, pair = pl.program_id(0), pl.program_id(1)
+def self_back_kernel(
+    seq, lengths_ref, q_ref, k_ref, v_ref, do_ref, lse_ref, cos_ref, sin_ref, *rest
+):
+    pair = pl.program_id(0)
+    out_ref, fq_ref, fk_ref = rest[-3:]
+    slot = lax.broadcasted_iota(jnp.int32, (1, LANES), 1) & (HEAD_DIM - 1)
+
+    @pl.when(pair == 0)
+    def _():
+        features = mask_features(lengths_ref, seq)
+        fq_ref[...] = features[0]
+        fk_ref[...] = features[1] + jnp.where((slot >= 4) & (slot < 7), 1.0, 0.0).astype(bf16)
+
     keep = lane_halves(bf16)
     low_lane = lax.broadcasted_iota(jnp.int32, (1, LANES), 1) < HEAD_DIM
-    lse = lse_ref[...].T
-    positions = lax.broadcasted_iota(jnp.int32, (1, SEQ_LEN), 1)
-    ends = limits(lengths_ref, seq, positions)
-    key_at = lax.broadcasted_iota(jnp.int32, (SEQ_LEN, SEQ_LEN), 0)
-    allowed = key_at < ends
-    dqs, dks, dvs = [], [], []
-    for h in range(2):
-        total = lse[h * HEAD_DIM : h * HEAD_DIM + 1]
-        scores = dot_nt(k_ref[...] * (keep[h] * scale), q_ref[...])
-        prob = jnp.exp(jnp.where(allowed, scores - total, -1e30))
-        dprob = dot_nt(v_ref[...] * keep[h], do_ref[...])
-        inner = jnp.sum(prob * dprob, 0, keepdims=True)
-        dscore = (prob * (dprob - inner)).astype(bf16)
-        dvs.append(dot_nn(prob.astype(bf16), do_ref[...]))
-        dks.append(dot_nn(dscore, q_ref[...]))
-        dqs.append(dot_tn(dscore, k_ref[...]))
+    rest_of = -lse_ref[...]
+    total = jnp.zeros_like(rest_of)
+    for i in range(3):
+        digit = rest_of.astype(bf16).astype(f32)
+        total = jnp.where(slot == 4 + i, digit, total)
+        rest_of = rest_of - digit
+    features = fq_ref[...] + total.astype(bf16)
+    query, key, value, upstream = q_ref[...], k_ref[...], v_ref[...], do_ref[...]
+    scaled = key * scale
+    heads = range(2)
+    keys = [scaled * keep[h] + fk_ref[...] * keep[1 - h] for h in heads]
+    queries = [query * keep[h] + features * keep[1 - h] for h in heads]
+    probs = [jnp.exp(dot_nt(keys[h], queries[h])) for h in heads]
+    dprobs = [dot_nt(value * keep[h], upstream) for h in heads]
+    inners = [jnp.sum(p * dp, 0, keepdims=True) for p, dp in zip(probs, dprobs)]
+    dscores = [
+        (p * (dp - inner)).astype(bf16) for p, dp, inner in zip(probs, dprobs, inners)
+    ]
+    dvs = [dot_nn(p.astype(bf16), upstream) for p in probs]
+    dks = [dot_nn(ds, query) for ds in dscores]
+    dqs = [dot_tn(ds, key) for ds in dscores]
     cosine, sine = cos_ref[...], -sin_ref[...]
     dq = jnp.where(low_lane, dqs[0], dqs[1]) * scale
     dk = jnp.where(low_lane, dks[0], dks[1]) * scale
     dv = jnp.where(low_lane, dvs[0], dvs[1])
-    for part, value in enumerate((turn(dq, cosine, sine), turn(dk, cosine, sine), dv)):
+    for part, found in enumerate((turn(dq, cosine, sine), turn(dk, cosine, sine), dv)):
         column = pl.multiple_of((part * PAIRS + pair) * LANES, LANES)
-        out_ref[:, pl.ds(column, LANES)] = value.astype(bf16)
-
-
-def self_back(lengths, qkv, do, lse, cosine, sine):
+        out_ref[:, pl.ds(column, LANES)] = found.astype(bf16)
+
+
+def self_back(seq, lengths, qkv, do, lse, cosine, sine, earlier=None):
     rows = qkv.shape[0]
-    seqs = rows // SEQ_LEN
     block = (SEQ_LEN, LANES)
 
     def at(offset):
-        return pl.BlockSpec(block, lambda s, p, _: (s, offset + p))
-
+        return pl.BlockSpec(block, lambda p, _: (seq, offset + p))
+
+    kernel = functools.partial(self_back_kernel, seq)
+    ins = [qkv, qkv, qkv, do, lse, cosine, sine]
+    specs = [at(0), at(PAIRS), at(2 * PAIRS), at(0), at(0), whole(block), whole(block)]
+    aliases = {}
+    if earlier is not None:
+        ins.append(earlier)
+        specs.append(pl.BlockSpec(memory_space=pl.ANY))
+        aliases = {len(ins): 0}
     return call(
-        self_back_kernel,
+        kernel,
         "self_back",
-        (seqs, PAIRS),
-        (qkv, qkv, qkv, do, lse, cosine, sine),
-        [at(0), at(PAIRS), at(2 * PAIRS), at(0), at(0), whole(block), whole(block)],
+        (PAIRS,),
+        ins,
+        specs,
         like((rows, 3 * D), bf16),
-        pl.BlockSpec((SEQ_LEN, 3 * D), lambda s, p, _: (s, 0)),
-        10 * rows * SEQ_LEN * D,
+        pl.BlockSpec((SEQ_LEN, 3 * D), lambda p, _: (seq, 0)),
+        10 * SEQ_LEN * SEQ_LEN * D,
+        scratch=[pltpu.VMEM(block, bf16)] * 2,
         scalars=(lengths,),
-        exps=rows * SEQ_LEN * HEADS,
+        exps=SEQ_LEN * SEQ_LEN * HEADS,
+        aliases=aliases,
     )
 
 
@@ -476,40 +647,50 @@
     return found
 
 
-def chosen_rows(ref, starts):
-    return jnp.concatenate([ref[pl.ds(start, NBR_LEN), :] for start in starts], 0)
+def chosen_rows(ref, starts, lanes=slice(None)):
+    return jnp.concatenate([ref[pl.ds(start, NBR_LEN), lanes] for start in starts], 0)
 
 
 def cross_kernel(chosen_ref, q_ref, k_ref, v_ref, o_ref):
     seq = pl.program_id(0)
     keep = lane_halves(bf16)
     low_lane = lax.broadcasted_iota(jnp.int32, (1, LANES), 1) < HEAD_DIM
-    for c in range(SPANS):
-        starts = slots(chosen_ref, seq, c)
-        query = q_ref[c * SPAN : (c + 1) * SPAN] * scale
-        both = jnp.concatenate([query * keep[0], query * keep[1]], 0)
-        scores = dot_nt(both, chosen_rows(k_ref, starts))
-        exponent = jnp.exp(scores - jnp.max(scores, -1, keepdims=True))
-        total = jnp.sum(exponent, -1, keepdims=True)
-        weights = (exponent * (1.0 / total)).astype(bf16)
-        out = dot_nn(weights, chosen_rows(v_ref, starts))
-        o_ref[c * SPAN : (c + 1) * SPAN] = jnp.where(low_lane, out[:SPAN], out[SPAN:]).astype(bf16)
+    starts = [slots(chosen_ref, seq, c) for c in range(SPANS)]
+    spans = [slice(c * SPAN, (c + 1) * SPAN) for c in range(SPANS)]
+    ones = jnp.ones((K_NBR * NBR_LEN, LANES), bf16)
+    for c in range(0, q_ref.shape[1], LANES):
+        lanes = slice(c, c + LANES)
+        query = q_ref[:, lanes] * scale
+        halves = [query * keep[h] for h in range(2)]
+        both = [jnp.concatenate([half[span] for half in halves], 0) for span in spans]
+        scores = [dot_nt(b, chosen_rows(k_ref, at, lanes)) for b, at in zip(both, starts)]
+        tops = [jnp.max(s, -1, keepdims=True) for s in scores]
+        weights = [jnp.exp(s - top).astype(bf16) for s, top in zip(scores, tops)]
+        outs = [
+            dot_nn(w, jnp.concatenate([chosen_rows(v_ref, at, lanes), ones], 1))
+            for w, at in zip(weights, starts)
+        ]
+        for span, out in zip(spans, outs):
+            total = jnp.where(low_lane, out[:SPAN, LANES:], out[SPAN:, LANES:])
+            out = jnp.where(low_lane, out[:SPAN, :LANES], out[SPAN:, :LANES]) / total
+            o_ref[span, lanes] = out.astype(bf16)
 
 
 def cross_attend(chosen, cq, ckv):
     rows = cq.shape[0]
     seqs = rows // SEQ_LEN
-    block = (SEQ_LEN, LANES)
+    width = WIDE * LANES
+    steps = PAIRS // WIDE
 
     def at(offset):
-        return pl.BlockSpec(block, lambda s, p, _: (s, offset + p))
+        return pl.BlockSpec((SEQ_LEN, width), lambda s, p, _: (s, offset + p))
 
     return call(
         cross_kernel,
         "cross_attend",
-        (seqs, PAIRS),
+        (seqs, steps),
         (cq, ckv, ckv),
-        [at(0), at(0), at(PAIRS)],
+        [at(0), at(0), at(steps)],
         like((rows, D), bf16),
         at(0),
         2 * rows * SEQ_LEN * D,
@@ -518,36 +699,50 @@
     )
 
 
-def cross_back_kernel(chosen_ref, q_ref, k_ref, v_ref, do_ref, dq_ref, dkv_ref, dk_acc, dv_acc):
+def cross_back_kernel(
+    chosen_ref, q_ref, k_ref, v_ref, do_ref, dq_ref, dkv_ref, sums_ref, dk_ref, dv_ref, acc_ref
+):
     seq, pair = pl.program_id(0), pl.program_id(1)
     keep = lane_halves(bf16)
     low_lane = lax.broadcasted_iota(jnp.int32, (1, LANES), 1) < HEAD_DIM
-    dk_acc[...] = jnp.zeros_like(dk_acc)
-    dv_acc[...] = jnp.zeros_like(dv_acc)
+    starts = [slots(chosen_ref, seq, c) for c in range(SPANS)]
+    spans = [slice(c * SPAN, (c + 1) * SPAN) for c in range(SPANS)]
+
+    def stacked(ref):
+        halves = [ref[...] * keep[h] for h in range(2)]
+        return [jnp.concatenate([half[span] for half in halves], 0) for span in spans]
+
+    queries, upstreams = stacked(q_ref), stacked(do_ref)
+    keys = [chosen_rows(k_ref, at) for at in starts]
+    scores = jnp.concatenate([dot_nt(k, q) for k, q in zip(keys, queries)], 1) * scale
+    dprob = jnp.concatenate(
+        [dot_nt(chosen_rows(v_ref, at), up) for at, up in zip(starts, upstreams)], 1
+    )
+    exponent = jnp.exp(scores - jnp.max(scores, 0, keepdims=True))
+    prob = exponent * (1.0 / jnp.sum(exponent, 0, keepdims=True))
+    inner = jnp.sum(prob * dprob, 0, keepdims=True)
+    dscore = (prob * (dprob - inner)).astype(bf16)
+    prob = prob.astype(bf16)
     for c in range(SPANS):
-        starts = slots(chosen_ref, seq, c)
-        span = slice(c * SPAN, (c + 1) * SPAN)
-        query, upstream = q_ref[span], do_ref[span]
-        query = jnp.concatenate([query * keep[0], query * keep[1]], 0)
-        upstream = jnp.concatenate([upstream * keep[0], upstream * keep[1]], 0)
-        keys, values = chosen_rows(k_ref, starts), chosen_rows(v_ref, starts)
-        scores = dot_nt(keys, query) * scale
-        exponent = jnp.exp(scores - jnp.max(scores, 0, keepdims=True))
-        prob = exponent * (1.0 / jnp.sum(exponent, 0, keepdims=True))
-        dprob = dot_nt(values, upstream)
-        inner = jnp.sum(prob * dprob, 0, keepdims=True)
-        dscore = (prob * (dprob - inner)).astype(bf16)
-        dv = dot_nn(prob.astype(bf16), upstream)
-        dk = dot_nn(dscore, query) * scale
-        dq = dot_tn(dscore, keys) * scale
+        columns = slice(c * LANES, (c + 1) * LANES)
+        dv_ref[c] = dot_nn(prob[:, columns], upstreams[c])
+        dk_ref[c] = dot_nn(dscore[:, columns], queries[c])
+    dqs = [
+        dot_tn(dscore[:, c * LANES : (c + 1) * LANES], keys[c]) * scale for c in range(SPANS)
+    ]
+    for span, dq in zip(spans, dqs):
         dq_ref[span] = jnp.where(low_lane, dq[:SPAN], dq[SPAN:]).astype(bf16)
-        for i, start in enumerate(starts):
-            rows = slice(i * NBR_LEN, (i + 1) * NBR_LEN)
-            dk_acc[pl.ds(start, NBR_LEN), :] += dk[rows]
-            dv_acc[pl.ds(start, NBR_LEN), :] += dv[rows]
-    for part, acc in enumerate((dk_acc, dv_acc)):
+    for part, found_ref in enumerate((dk_ref, dv_ref)):
+        acc_ref[...] = jnp.zeros_like(acc_ref)
+        for c in range(SPANS):
+            for i, start in enumerate(starts[c]):
+                rows = slice(i * NBR_LEN, (i + 1) * NBR_LEN)
+                acc_ref[pl.ds(start, NBR_LEN), :] += found_ref[c, rows]
         column = pl.multiple_of((part * PAIRS + pair) * LANES, LANES)
-        dkv_ref[:, pl.ds(column, LANES)] = acc[...].astype(bf16)
+        total = acc_ref[...] * scale if part == 0 else acc_ref[...]
+        rounded = total.astype(bf16)
+        dkv_ref[:, pl.ds(column, LANES)] = rounded
+    sums_ref[...] = jnp.broadcast_to(sum_rows(rounded.astype(f32)), sums_ref.shape)
 
 
 def cross_back(chosen, cq, ckv, dco):
@@ -564,10 +759,18 @@
         (seqs, PAIRS),
         (cq, ckv, ckv, dco),
         [at(0), at(0), at(PAIRS), at(0)],
-        (like((rows, D), bf16), like((rows, 2 * D), bf16)),
-        (at(0), pl.BlockSpec((SEQ_LEN, 2 * D), lambda s, p, _: (s, 0))),
+        (like((rows, D), bf16), like((rows, 2 * D), bf16), like((8 * seqs, D), f32)),
+        (
+            at(0),
+            pl.BlockSpec((SEQ_LEN, 2 * D), lambda s, p, _: (s, 0)),
+            pl.BlockSpec((8, LANES), lambda s, p, _: (s, p)),
+        ),
         5 * rows * SEQ_LEN * D,
-        scratch=[pltpu.VMEM(block, f32), pltpu.VMEM(block, f32)],
+        scratch=[
+            pltpu.VMEM((SPANS, K_NBR * NBR_LEN, LANES), f32),
+            pltpu.VMEM((SPANS, K_NBR * NBR_LEN, LANES), f32),
+            pltpu.VMEM(block, f32),
+        ],
         scalars=(chosen,),
         exps=rows * K_NBR * NBR_LEN * HEADS,
     )
@@ -792,13 +995,8 @@
     )
 
 
-def neighbour_kernel(dkv_ref, w_ref, dn_ref, sums_ref):
-    @pl.when(pl.program_id(0) == 0)
-    def _():
-        sums_ref[...] = jnp.zeros_like(sums_ref)
-
+def neighbour_kernel(dkv_ref, w_ref, dn_ref):
     dn_ref[...] = dot_nt(dkv_ref[...], w_ref[...])
-    sums_ref[...] += sum_rows(dkv_ref[:, D:].astype(f32))
 
 
 def neighbour_back(dckv, mid):
@@ -812,8 +1010,8 @@
             pl.BlockSpec((ROWS, 2 * D), lambda r: (r, 0)),
             pl.BlockSpec((D, 2 * D), lambda r: (0, 0)),
         ],
-        (like((rows, D), f32), like((1, D), f32)),
-        (pl.BlockSpec((ROWS, D), lambda r: (r, 0)), whole((1, D))),
+        like((rows, D), f32),
+        pl.BlockSpec((ROWS, D), lambda r: (r, 0)),
         4 * rows * D * D,
     )
 
@@ -850,53 +1048,111 @@
     small = jnp.pad(small, ((0, 0), (0, LANES - SMALL)))
     first = jnp.concatenate([w_qkv, small], 1)
     middle = jnp.concatenate([w_cross_kv, w_out, w_cross_q, w_cross_out], 1)
-
-    first_z = gather_z(first, sizes)
-    middle_z = gather_z(after(middle, first_z), sizes)
-    first_pieces = gather_rest(first_z, sizes)
-    up_z = gather_z(after(w_up, middle_z), sizes)
-    middle_pieces = gather_rest(middle_z, sizes)
-    down_z = gather_z(after(w_down, up_z), sizes)
-    up_pieces = gather_rest(up_z, sizes)
-    down_pieces = gather_rest(down_z, sizes)
-
+    quarters = jnp.split(w_down, FF // D, 0)
+    last = jnp.concatenate(quarters + [w_up], 1)
     cosine, sine = rotary_tables()
-    qkv_weight = place(first_pieces, sizes, me_array)
+    picks = chosen.reshape(chosen.shape[0], SPANS * K_NBR)
+
+    first_own = gather_z(first, sizes)
+    first_side = gather_side(first_own, sizes)
+    middle_own = gather_z(after(middle, first_own), sizes)
+    first_pieces = near_pieces(first_own, first_side)
+    first_corner = gather_corner(first_side, sizes)
+    first_core = gather_core(first_pieces, sizes)
+    middle_own = after(middle_own, first_side)
+    middle_side = gather_side(middle_own, sizes)
+    last_own = gather_z(after(last, middle_own), sizes)
+    first_pieces.update(first_corner)
+    first_core.update(gather_core(first_corner, sizes))
+    first_core.update({(0,) + key: held for key, held in first_pieces.items()})
+    qkv_weight = place(first_core, sizes, me_array)
     gathered = qkv_weight[:, 3 * D :]
     vec = gathered[:, :16].T.astype(f32)
     up_shift = gathered[:, 14:SMALL].reshape(1, FF).astype(f32)
-    picks = chosen.reshape(chosen.shape[0], SPANS * K_NBR)
-
-    a1, qkv = qkv_project(tokens, qkv_weight, vec, cosine, sine)
-    o, lse = self_attend(block_lengths, qkv)
-    mid = place(middle_pieces, sizes, me_array)
+
+    a1, qkv = qkv_project(after(tokens, middle_own), qkv_weight, vec, cosine, sine)
+    middle_side = after(middle_side, qkv)
+    middle_pieces = near_pieces(middle_own, middle_side)
+    middle_corner = gather_corner(middle_side, sizes)
+    middle_core = gather_core(middle_pieces, sizes)
+    last_own = after(last_own, middle_side)
+    last_side = gather_side(last_own, sizes)
+
+    o, lse = self_attend(block_lengths, after(qkv, middle_side, last_own))
+    middle_corner, middle_core = after((middle_corner, middle_core), o)
+    middle_core.update(gather_core(middle_corner, sizes))
+    middle_pieces.update(middle_corner)
+    middle_core.update({(0,) + key: held for key, held in middle_pieces.items()})
+    mid = place(middle_core, sizes, me_array)
     ckv = ckv_project(neighbours, mid, vec)
     h1, a2, cq = mid_forward(o, tokens, mid, vec)
-    co = cross_attend(picks, cq, ckv)
-    up_weight = place(up_pieces, sizes, me_array)
-    down_weight = place(down_pieces, sizes, me_array)
+    last_side = after(last_side, cq)
+    last_pieces = near_pieces(last_own, last_side)
+    last_corner = gather_corner(last_side, sizes)
+    last_core = gather_core(last_pieces, sizes)
+    co = cross_attend(picks, after(cq, last_side), ckv)
+    last_corner, last_core = after((last_corner, last_core), co)
+    last_core.update(gather_core(last_corner, sizes))
+    last_pieces.update(last_corner)
+    last_core.update({(0,) + key: held for key, held in last_pieces.items()})
+    down_weight, up_weight = place(last_core, sizes, me_array, split=True)
+
     a3, g, du, output, dh2, e2, dco, sums3, grad_bu = mlp_both(
         h1, co, cotangent, mid, up_weight, down_weight, up_shift, vec
     )
-    grad_down = scatter_sum(weight_grad(g, cotangent), sizes, me)
-    grad_up = scatter_sum(weight_grad(a3, du), sizes, me)
-    grad_co = scatter_sum(weight_grad(co, e2), sizes, me)
-    dcq, dckv = cross_back(picks, cq, ckv, dco)
-    dh1, e1, do, sums2 = mid_back(dcq, dh2, h1, mid, vec)
-    grad_cq = scatter_sum(weight_grad(a2, dcq), sizes, me)
-    grad_ckv = scatter_sum(weight_grad(neighbours, dckv), sizes, me)
-    grad_out = scatter_sum(weight_grad(o, e1), sizes, me)
-    dqkv = self_back(block_lengths, qkv, do, lse, cosine, sine)
-    grad_qkv = scatter_sum(weight_grad(a1, dqkv), sizes, me)
+
+    last_kept, last_sent = spread(
+        [weight_grad(g, cotangent), weight_grad(a3, du)], sizes, me_array, split=True
+    )
+    last_got = shift(last_sent, sizes, 3, 1)
+    dcq, dckv, value_sums = cross_back(picks, cq, ckv, after(dco, last_sent))
+    last_got, last_kept = after((last_got, last_kept), dcq)
+    last_parts = fold_core(last_kept, last_got, sizes)
+    last_got = send_side(last_parts, sizes)
+    dh1, e1, do, sums2 = mid_back(after(dcq, last_parts), dh2, h1, mid, vec)
+    middle_kept, middle_sent = spread(
+        [
+            weight_grad(neighbours, dckv),
+            weight_grad(o, e1),
+            weight_grad(a2, dcq),
+            weight_grad(co, e2),
+        ],
+        sizes,
+        me_array,
+    )
+    middle_got = shift(middle_sent, sizes, 3, 1)
+    do = after(do, middle_sent)
+    dqkv = self_back(0, block_lengths, qkv, do, lse, cosine, sine)
+    last_got, middle_got, middle_kept = after((last_got, middle_got, middle_kept), dqkv)
+    last_parts = fold_side(last_got, sizes)
+    last_got = send_corner(last_parts, sizes)
+    middle_parts = fold_core(middle_kept, middle_got, sizes)
+    middle_got = send_side(middle_parts, sizes)
+    do = after(do, last_parts, middle_parts)
+    dqkv = self_back(1, block_lengths, qkv, do, lse, cosine, sine, dqkv)
+    last_got, middle_got = after((last_got, middle_got), dqkv)
+    first_kept, first_sent = spread([weight_grad(a1, dqkv)], sizes, me_array)
+    first_got = shift(first_sent, sizes, 3, 1)
+    last_parts = fold_corner(last_got, sizes)
+    last_got = send_z(last_parts, sizes)
+    middle_parts = fold_side(middle_got, sizes)
+    middle_got = send_corner(middle_parts, sizes)
+    dqkv = after(dqkv, first_sent, last_parts, middle_parts)
     token_grad, sums1, qkv_sums = token_back(dqkv, dh1, tokens, qkv_weight, vec)
-    neighbour_grad, value_sums = neighbour_back(dckv, mid)
+    first_got, first_kept, middle_got, last_got = after(
+        (first_got, first_kept, middle_got, last_got), token_grad
+    )
+    first_parts = fold_core(first_kept, first_got, sizes)
+    first_got = send_side(first_parts, sizes)
+    middle_parts = fold_corner(middle_got, sizes)
+    middle_got = send_z(middle_parts, sizes)
 
     rows = jnp.concatenate(
         [
             qkv_sums.reshape(3, D),
             sums2[3:4],
             sums2[2:3],
-            value_sums,
+            sum_rows(value_sums[::8]),
             sums3[2:4],
             sums1[0:1],
             sums2[0:1],
@@ -907,20 +1163,26 @@
         ],
         0,
     )
-    spread = jnp.concatenate([rows.T, grad_bu.reshape(D, FF // D)], 1)
-    spread = jnp.pad(spread, ((0, 0), (0, 2 * LANES - SMALL)))
-    small_sum = scatter_sum(spread, sizes, me)
+    small_grad = jnp.concatenate([rows.T, grad_bu.reshape(D, FF // D)], 1)
+    small_grad = jnp.pad(small_grad, ((0, 0), (0, LANES - SMALL)))
+    small_kept, small_sent = spread([small_grad], sizes, me_array)
+    small_sum = scatter_small(small_kept, small_sent, sizes)
+    neighbour_grad = neighbour_back(after(dckv, first_parts, middle_parts, small_sent), mid)
+    first_got = send_corner(fold_side(first_got, sizes), sizes)
+    first_got = send_z(fold_corner(first_got, sizes), sizes)
+    last_sum, middle_sum, first_sum = plus(*last_got), plus(*middle_got), plus(*first_got)
+
     return (
         output,
         token_grad,
         neighbour_grad,
-        grad_qkv,
-        grad_out,
-        grad_cq,
-        grad_ckv,
-        grad_co,
-        grad_up,
-        grad_down,
+        first_sum,
+        middle_sum[:, 2 * D : 3 * D],
+        middle_sum[:, 3 * D : 4 * D],
+        middle_sum[:, : 2 * D],
+        middle_sum[:, 4 * D :],
+        last_sum[:, FF:],
+        jnp.concatenate(jnp.split(last_sum[:, :FF], FF // D, 1), 0),
         small_sum[:, :8].T,
         small_sum[:, 14:SMALL].reshape(-1),
         small_sum[:, 8:11].T,

time: 602 us -> 497 us (0.83)
  starting transfers between devices: 123 us -> 68.7 us
  waiting for transfers between devices: 139 us -> 95.2 us
  other arithmetic: 29.3 us -> 49.4 us
  local copies, waits for them, and re-layouts: 48.2 us -> 29.9 us
  Pallas kernels: 224 us -> 208 us
  matrix products: 29.7 us -> 37.9 us
    ppermute x112 -> x66, starting transfers between devices: 123 us -> 68.7 us  [shift(): return lax.ppermute(values, 'fsdp', shift_pairs(sizes, axis, step))]
    ppermute x112 -> x66, waiting for transfers between devices: 139 us -> 95.2 us  [shift(): return lax.ppermute(values, 'fsdp', shift_pairs(sizes, axis, step))]
    pallas_call x11 -> x12, Pallas kernels: 201 us -> 164 us  [call(): pl.pallas_call(kernel, out_shape=outs, grid_spec=pltpu.PrefetchScalarGrid...]
    dynamic_slice x18 -> x0, local copies, waits for them, and re-layouts: 23.7 us -> none  [take(): return lax.dynamic_index_in_dim(values, index, axis, keepdims=False)]
    convert_element_type x35 -> x23, other arithmetic: 11.1 us -> 34.3 us  [the longest x9 17.6 us: part(): return plus(kept[index], got[index]).astype(kind)]
    pallas_call x4 -> x7, Pallas kernels: 23.5 us -> 43.8 us  [the longest x4 23.7 us: spread(): pl.pallas_call(functools.partial(spread_kernel, sizes, split), out_shape=...]
    dot_general x7, matrix products: 29.7 us -> 37.9 us  [dot_tn(): lax.dot_general(a, b, (((0,), (0,)), ((), ())), preferred_element_type=f32)]
  transfers between devices with their start and end apart: 112 -> 66, of which waited for: 47 -> 24; matrix products, arithmetic and copies ran while one was open for 14% -> 10% of each run, Pallas kernels for 10% -> 25%
where the time goes in v2:
time: 497 us; the launch traced here: 490 us
  Pallas kernels  208 us (42%)
  waiting for transfers between devices  95.2 us (19%)
  starting transfers between devices  68.7 us (14%)
  other arithmetic  49.4 us (10%)
  matrix products  37.9 us (8%)
  local copies, waits for them, and re-layouts  29.9 us (6%)
    pallas_call x12, Pallas kernels, call(): pl.pallas_call(kernel, out_shape=outs, grid_spec=pltpu.PrefetchScalarGrid...  164 us
    ppermute x66, waiting for transfers between devices, shift(): return lax.ppermute(values, 'fsdp', shift_pairs(sizes, axis, step))  95.2 us
    ppermute x66, starting transfers between devices, shift(): return lax.ppermute(values, 'fsdp', shift_pairs(sizes, axis, step))  68.7 us
    dot_general x7, matrix products, dot_tn(): lax.dot_general(a, b, (((0,), (0,)), ((), ())), preferred_element_type=f32)  37.9 us
    pallas_call x4, Pallas kernels, spread(): pl.pallas_call(functools.partial(spread_kernel, sizes, split), out_shape=...  23.7 us
    pallas_call x3, Pallas kernels, place(): pl.pallas_call(functools.partial(place_kernel, keys, counts, sizes, split...  20.1 us
    convert_element_type x9, other arithmetic, part(): return plus(kept[index], got[index]).astype(kind)  17.6 us
    unnamed x95, local copies, waits for them, and re-layouts  11.9 us
  transfers between devices with their start and end apart: 66, of which 24 were waited for; matrix products, arithmetic and copies ran while one was open for 10% of the time, Pallas kernels for 25%

profile of v2, /device:TPU:0, one launch (start us, length us, event | category | flops | bytes accessed | tf_op | source)
XLA Modules:
  0.0 490.4 jit_solution(14801525670009910130)
XLA Ops:
  4.8 3.1 collective-permute-start
  7.9 2.6 collective-permute-start.1
  15.1 3.1 collective-permute-done.1
  20.6 4.0 collective-permute-start.5
  26.8 2.9 collective-permute-done.5
  30.9 3.2 collective-permute-done.3
  34.0 7.1 %collective-permute-done.4 = bf16[24,3840]{1,0:T(8,128)(2,1)S(1)} collective-permute-done((bf16[24,3840]{1,0:T(8,128)(2,1)S(1)}, bf16[24,3840]{1,0:T(8,128)(2,1)S(1)}, u32[]{:S(2)}, u32[]{:S(2)}) %collective-permute-start.4) | collective-permute-done | bytes 184352 | tf_op jit(solution)/shard_map/ppermute | solution.py:69
  50.1 13.9 %collective-permute-done.9.refs_4_ = bf16[4,24,1216]{2,1,0:T(8,128)(2,1)} collective-permute-done((bf16[4,24,1216]{2,1,0:T(8,128)(2,1)S(1)}, bf16[4,24,1216]{2,1,0:T(8,128)(2,1)}, u32[]{:S(2)}, u32[]{:S(2)}) %collective-permute-start.9) | collective-permute-done | bytes 233504 | tf_op jit(solution)/shard_map/ppermute | solution.py:69
  68.7 3.4 collective-permute-start.18
  72.6 5.4 %place.3 = bf16[4,8,24,2432]{3,2,1,0:T(8,128)(2,1)} custom-call(s32[4]{0:T(128)} %pad_add_fusion.me_ref, bf16[4,24,2432]{2,1,0:T(8,128)(2,1)} %copy-done.8, bf16[4,24,2432]{2,1,0:T(8,128)(2,1)} %copy-done.16, bf16[4,24,2432]{2,1,0:T(8,128)(2,1)} %copy-done.17, bf16[4,24,1216]{2,1,0:T(8,128)(2,1)} %collective-permute-done.8.refs_3_, ...), custom_call_target="tpu_custom_call" | custom-call | bytes 7471104 | tf_op jit(solution)/shard_map/place/pallas_call | solution.py:152
  79.7 11.7 %qkv_project.1 = (bf16[1024,768]{1,0:T(8,128)(2,1)}, bf16[1024,2304]{1,0:T(8,128)(2,1)}) custom-call(bf16[1024,768]{1,0:T(8,128)(2,1)} %x_ref.4, bf16[768,2432]{1,0:T(8,128)(2,1)} %bitcast.240, f32[16,768]{1,0:T(8,128)} %convert_bitcast_fusion.vec_ref, f32[2,512,128]{2,1,0:T(8,128)} %stack.88.cos_ref, f32[2,512,128]{2,1,0:T(8,128)} %stack.90.sin_ref), custom_call_target="tpu_custom_call" | custom-call | flops 3623878656 | bytes 12697600 | tf_op jit(solution)/shard_map/qkv_project/pallas_call | solution.py:362
  96.8 7.6 %collective-permute-done.20.refs_3_ = bf16[4,24,1920]{2,1,0:T(8,128)(2,1)S(1)} collective-permute-done((bf16[4,24,1920]{2,1,0:T(8,128)(2,1)S(1)}, bf16[4,24,1920]{2,1,0:T(8,128)(2,1)S(1)}, u32[]{:S(2)}, u32[]{:S(2)}) %collective-permute-start.20) | collective-permute-done | bytes 368672 | tf_op jit(solution)/shard_map/ppermute | solution.py:69
  105.7 12.8 %self_attend.1 = (bf16[1024,768]{1,0:T(8,128)(2,1)}, f32[1024,768]{1,0:T(8,128)}) custom-call(s32[2,4]{1,0:T(2,128)} %lengths_ref.5, bf16[1024,2304]{1,0:T(8,128)(2,1)} %get-tuple-element.111.q_ref.k_ref.v_ref, bf16[1024,2304]{1,0:T(8,128)(2,1)} %get-tuple-element.111.q_ref.k_ref.v_ref, bf16[1024,2304]{1,0:T(8,128)(2,1)} %get-tuple-element.111.q_ref.k_ref.v_ref), custom_call_target="tpu_custom_call" | custom-call | flops 1610612736 | bytes 18874368 | tf_op jit(solution)/shard_map/self_attend/pallas_call | solution.py:362
  118.6 12.4 %collective-permute-done.21.refs_4_ = bf16[4,24,1920]{2,1,0:T(8,128)(2,1)S(1)} collective-permute-done((bf16[4,24,1920]{2,1,0:T(8,128)(2,1)S(1)}, bf16[4,24,1920]{2,1,0:T(8,128)(2,1)S(1)}, u32[]{:S(2)}, u32[]{:S(2)}) %collective-permute-start.21) | collective-permute-done | bytes 368672 | tf_op jit(solution)/shard_map/ppermute | solution.py:69
  133.5 6.4 %place.4 = bf16[4,8,24,3840]{3,2,1,0:T(8,128)(2,1)} custom-call(s32[4]{0:T(128)} %pad_add_fusion.me_ref, bf16[4,24,3840]{2,1,0:T(8,128)(2,1)} %copy-done.4, bf16[4,24,3840]{2,1,0:T(8,128)(2,1)} %collective-permute-done.15.refs_1_, bf16[4,24,3840]{2,1,0:T(8,128)(2,1)} %collective-permute-done.16.refs_2_, bf16[4,24,1920]{2,1,0:T(8,128)(2,1)} %copy-done.24, ...), custom_call_target="tpu_custom_call" | custom-call | bytes 11796480 | tf_op jit(solution)/shard_map/place/pallas_call | solution.py:152
  140.0 8.0 %mid_forward.1 = (f32[1024,768]{1,0:T(8,128)}, bf16[1024,768]{1,0:T(8,128)(2,1)}, bf16[1024,768]{1,0:T(8,128)(2,1)}) custom-call(bf16[1024,768]{1,0:T(8,128)(2,1)} %get-tuple-element.112.o_ref, bf16[1024,768]{1,0:T(8,128)(2,1)} %x_ref.4, bf16[768,3840]{1,0:T(8,128)(2,1)} %bitcast.228, bf16[768,3840]{1,0:T(8,128)(2,1)} %bitcast.229, ...), custom_call_target="tpu_custom_call" | custom-call | flops 2415919104 | bytes 21282816 | tf_op jit(solution)/shard_map/mid_forward/pallas_call | solution.py:362
  152.4 6.4 %ckv_project.1.k_ref.v_ref = bf16[1024,1536]{1,0:T(8,128)(2,1)} custom-call(bf16[1024,768]{1,0:T(8,128)(2,1)} %n_ref.1, bf16[768,3840]{1,0:T(8,128)(2,1)} %bitcast.230, f32[16,768]{1,0:T(8,128)} %convert_bitcast_fusion.vec_ref), custom_call_target="tpu_custom_call" | custom-call | flops 2415919104 | bytes 10665984 | tf_op jit(solution)/shard_map/ckv_project/pallas_call | solution.py:362
  158.7 8.1 %cross_attend.1.co_ref = bf16[1024,768]{1,0:T(8,128)(2,1)} custom-call(s32[2,16]{1,0:T(2,128)} %reshape.318.chosen_ref, bf16[1024,768]{1,0:T(8,128)(2,1)} %get-tuple-element.122.q_ref, bf16[1024,1536]{1,0:T(8,128)(2,1)} %ckv_project.1.k_ref.v_ref, bf16[1024,1536]{1,0:T(8,128)(2,1)} %ckv_project.1.k_ref.v_ref), custom_call_target="tpu_custom_call" | custom-call | flops 805306368 | bytes 9437184 | tf_op jit(solution)/shard_map/cross_attend/pallas_call | solution.py:362
  171.0 8.3 %place.5 = (bf16[4,8,96,768]{3,2,1,0:T(8,128)(2,1)}, bf16[4,8,24,3072]{3,2,1,0:T(8,128)(2,1)}) custom-call(s32[4]{0:T(128)} %pad_add_fusion.me_ref, bf16[4,24,6144]{2,1,0:T(8,128)(2,1)} %copy-done, bf16[4,24,6144]{2,1,0:T(8,128)(2,1)} %copy-done.6, bf16[4,24,6144]{2,1,0:T(8,128)(2,1)} %collective-permute-done.28.refs_2_, ...), custom_call_target="tpu_custom_call" | custom-call | bytes 18874368 | tf_op jit(solution)/shard_map/place/pallas_call | solution.py:152
  179.3 39.1 %mlp_both.1 = (bf16[1024,768]{1,0:T(8,128)(2,1)}, bf16[1024,3072]{1,0:T(8,128)(2,1)}, bf16[1024,3072]{1,0:T(8,128)(2,1)}, bf16[1024,768]{1,0:T(8,128)(2,1)}, f32...) custom-call(f32[1024,768]{1,0:T(8,128)} %get-tuple-element.118.h1_re, ...), custom_call_target="tpu_custom_call" | custom-call | flops 21743271936 | bytes 43745280 | tf_op jit(solution)/shard_map/mlp_both/pallas_call | solution.py:362
  218.4 9.9 %convolution_convert_fusion.1 = bf16[3072,768]{1,0:T(8,128)(2,1)} fusion(bf16[1024,3072]{1,0:T(8,128)(2,1)} %get-tuple-element.132, bf16[1024,768]{1,0:T(8,128)(2,1)S(1)} %copy-done.33), kind=kOutput, calls=%fused_computation.1 | convolution fusion | flops 4834197504 | bytes 12582912 | tf_op jit(solution)/shard_map/dot_general | solution.py:293
  228.4 7.0 %convolution_convert_fusion = bf16[768,3072]{1,0:T(8,128)(2,1)} fusion(bf16[1024,768]{1,0:T(8,128)(2,1)S(1)} %copy-done.37, bf16[1024,3072]{1,0:T(8,128)(2,1)S(1)} %copy-done.35), kind=kOutput, calls=%fused_computation | convolution fusion | flops 4834197504 | bytes 12582912 | tf_op jit(solution)/shard_map/dot_general | solution.py:293
  235.4 8.3 %spread.4 = (bf16[4,2,2,24,6144]{4,3,2,1,0:T(8,128)(2,1)}, bf16[4,2,2,24,6144]{4,3,2,1,0:T(8,128)(2,1)}) custom-call(s32[4]{0:T(128)} %pad_add_fusion.me_ref, bf16[4,8,96,768]{3,2,1,0:T(8,128)(2,1)} %bitcast.237, bf16[4,8,24,3072]{3,2,1,0:T(8,128)(2,1)} %bitcast.238), custom_call_target="tpu_custom_call" | custom-call | bytes 18874368 | tf_op jit(solution)/shard_map/spread/pallas_call | solution.py:206
  243.8 20.4 %cross_back.1 = (bf16[1024,768]{1,0:T(8,128)(2,1)}, bf16[1024,1536]{1,0:T(8,128)(2,1)}, f32[16,768]{1,0:T(8,128)}) custom-call(s32[2,16]{1,0:T(2,128)} %reshape.318.chosen_ref, bf16[1024,768]{1,0:T(8,128)(2,1)} %get-tuple-element.122.q_ref, bf16[1024,1536]{1,0:T(8,128)(2,1)} %ckv_project.1.k_ref.v_ref, bf16[1024,1536]{1,0:T(8,128)(2,1)} %ckv_project.1.k_ref.v_ref, ...), custom_call_target="tpu_custom_call" | custom-call | flops 2013265920 | bytes 14204928 | tf_op jit(solution)/shard_map/cross_back/pallas_call | solution.py:362
  266.7 2.5 convolution_convert_fusion.5
  269.2 3.9 convolution_convert_fusion.3
  273.2 2.7 fusion.3
  277.6 3.6 fusion.1
  281.1 9.4 %mid_back.1 = (f32[1024,768]{1,0:T(8,128)}, bf16[1024,768]{1,0:T(8,128)(2,1)}, bf16[1024,768]{1,0:T(8,128)(2,1)}, f32[8,768]{1,0:T(8,128)}) custom-call(bf16[1024,768]{1,0:T(8,128)(2,1)} %get-tuple-element.141.dcq_ref, f32[1024,768]{1,0:T(8,128)} %get-tuple-element.142.dh2_ref, f32[1024,768]{1,0:T(8,128)} %get-tuple-element.118.h1_ref, ...), custom_call_target="tpu_custom_call" | custom-call | flops 2415919104 | bytes 26025984 | tf_op jit(solution)/shard_map/mid_back/pallas_call | solution.py:362
  290.5 4.3 convolution_convert_fusion.6
  294.9 6.4 %spread.5 = (bf16[4,2,2,24,3840]{4,3,2,1,0:T(8,128)(2,1)}, bf16[4,2,2,24,3840]{4,3,2,1,0:T(8,128)(2,1)}) custom-call(s32[4]{0:T(128)} %pad_add_fusion.me_ref, bf16[4,8,24,1536]{3,2,1,0:T(8,128)(2,1)} %bitcast.245, bf16[4,8,24,768]{3,2,1,0:T(8,128)(2,1)} %bitcast.249, bf16[4,8,24,768]{3,2,1,0:T(8,128)(2,1)} %bitcast.248, bf16[4,8,24,768]{3,2,1,0:T(8,128)(2,1)} %bitcast.247), custom_call_target="tpu_custom_call" | custom-call | bytes 11796480 | tf_op jit(solution)/shard_map/spread/pallas_call | solution.py:206
  307.4 15.4 %self_back.2.rest_0_ = bf16[1024,2304]{1,0:T(8,128)(2,1)} custom-call(s32[2,4]{1,0:T(2,128)} %lengths_ref.5, bf16[1024,2304]{1,0:T(8,128)(2,1)} %get-tuple-element.111.q_ref.k_ref.v_ref, bf16[1024,2304]{1,0:T(8,128)(2,1)} %get-tuple-element.111.q_ref.k_ref.v_ref, bf16[1024,2304]{1,0:T(8,128)(2,1)} %get-tuple-element.111.q_ref.k_ref.v_ref, ...), custom_call_target="tpu_custom_call" | custom-call | flops 2013265920 | bytes 24117248 | tf_op jit(solution)/shard_map/self_back/pallas_call | solution.py:362
  322.8 7.2 %collective-permute-done.38 = bf16[4,2,24,3072]{3,2,1,0:T(8,128)(2,1)} collective-permute-done((bf16[4,2,24,3072]{3,2,1,0:T(8,128)(2,1)}, bf16[4,2,24,3072]{3,2,1,0:T(8,128)(2,1)}, u32[]{:S(2)}, u32[]{:S(2)}) %collective-permute-start.38) | collective-permute-done | bytes 1179680 | tf_op jit(solution)/shard_map/ppermute | solution.py:69
  331.3 2.6 fusion.8
  336.2 2.6 fusion.6
  349.4 15.5 %self_back.3.dqkv_ref = bf16[1024,2304]{1,0:T(8,128)(2,1)} custom-call(s32[2,4]{1,0:T(2,128)} %lengths_ref.5, bf16[1024,2304]{1,0:T(8,128)(2,1)} %get-tuple-element.111.q_ref.k_ref.v_ref, bf16[1024,2304]{1,0:T(8,128)(2,1)} %get-tuple-element.111.q_ref.k_ref.v_ref, ...), custom_call_target="tpu_custom_call", output_to_operand_aliasing={{}: (8, {})} | custom-call | flops 2013265920 | bytes 28835840 | tf_op jit(solution)/shard_map/self_back/pallas_call | solution.py:362
  364.9 7.7 %convolution_convert_fusion.2 = bf16[768,2304]{1,0:T(8,128)(2,1)} fusion(bf16[1024,768]{1,0:T(8,128)(2,1)S(1)} %copy-done.38, bf16[1024,2304]{1,0:T(8,128)(2,1)} %self_back.3.dqkv_ref), kind=kOutput, calls=%fused_computation.2 | convolution fusion | flops 3625648128 | bytes 9830400 | tf_op jit(solution)/shard_map/dot_general | solution.py:293
  372.6 5.2 %spread.6 = (bf16[4,2,2,24,2304]{4,3,2,1,0:T(8,128)(2,1)}, bf16[4,2,2,24,2304]{4,3,2,1,0:T(8,128)(2,1)}) custom-call(s32[4]{0:T(128)} %pad_add_fusion.me_ref, bf16[4,8,24,2304]{3,2,1,0:T(8,128)(2,1)} %bitcast.244), custom_call_target="tpu_custom_call" | custom-call | bytes 7077888 | tf_op jit(solution)/shard_map/spread/pallas_call | solution.py:206
  388.3 10.4 %token_back.1 = (f32[1024,768]{1,0:T(8,128)}, f32[8,768]{1,0:T(8,128)}, f32[1,2304]{1,0:T(1,128)}) custom-call(bf16[1024,2304]{1,0:T(8,128)(2,1)} %self_back.3.dqkv_ref, f32[1024,768]{1,0:T(8,128)} %get-tuple-element.170.dh1_ref, bf16[1024,768]{1,0:T(8,128)(2,1)} %x_ref.4, bf16[768,2432]{1,0:T(8,128)(2,1)} %bitcast.242, f32[16,768]{1,0:T(8,128)} %convert_bitcast_fusion.vec_ref), custom_call_target="tpu_custom_call" | custom-call | flops 3623878656 | bytes 16401408 | tf_op jit(solution)/shard_map/token_back/pallas_call | solution.py:362
  401.3 3.7 spread.7
  409.3 3.4 collective-permute-done.61
  413.2 3.8 collective-permute-start.49
  417.1 4.2 collective-permute-start.63
  437.3 10.3 %collective-permute-done.48 = bf16[24,6144]{1,0:T(8,128)(2,1)} collective-permute-done((bf16[24,6144]{1,0:T(8,128)(2,1)}, bf16[24,6144]{1,0:T(8,128)(2,1)}, u32[]{:S(2)}, u32[]{:S(2)}) %collective-permute-start.48) | collective-permute-done | bytes 294944 | tf_op jit(solution)/shard_map/ppermute | solution.py:69
  460.4 6.8 %neighbour_back.1 = f32[1024,768]{1,0:T(8,128)} custom-call(bf16[1024,1536]{1,0:T(8,128)(2,1)} %get-tuple-element.186.dkv_ref, bf16[768,3840]{1,0:T(8,128)(2,1)} %bitcast.234), custom_call_target="tpu_custom_call" | custom-call | flops 2415919104 | bytes 12189696 | tf_op jit(solution)/shard_map/neighbour_back/pallas_call | solution.py:362
  467.2 4.8 collective-permute-done.58
  474.6 4.3 collective-permute-done.51
  480.8 3.0 collective-permute-start.56
  (299 shorter events, 130.0 us)
Async XLA Ops:
  4.8 10.3 %collective-permute-start = (bf16[24,2432]{1,0:T(8,128)(2,1)S(1)}, bf16[24,2432]{1,0:T(8,128)(2,1)S(1)}, u32[]{:S(2)}, u32[]{:S(2)}) collective-permute-start(bf16[24,2432]{1,0:T(8,128)(2,1)S(1)} %get-tuple-element.282), channel_id=1, source_target_pairs={{0,8},{1,9},{2,10},{3,11},{4,12},{5,13},{6,14},{7,15},{8,16},{9,17... | collective-permute-start | bytes 350216 | tf_op jit(solution)/shard_map/ppermute | solution.py:69
  7.9 10.3 %collective-permute-start.1 = (bf16[24,2432]{1,0:T(8,128)(2,1)S(1)}, bf16[24,2432]{1,0:T(8,128)(2,1)S(1)}, u32[]{:S(2)}, u32[]{:S(2)}) collective-permute-start(bf16[24,2432]{1,0:T(8,128)(2,1)S(1)} %get-tuple-element.282), channel_id=1, source_target_pairs={{0,16},{1,17},{2,18},{3,19},{4,20},{5,21},{6,22},{7,23},{8,24},{9,... | collective-permute-start | bytes 350216 | tf_op jit(solution)/shard_map/ppermute | solution.py:69
  18.3 12.6 %collective-permute-start.6 = (bf16[4,24,2432]{2,1,0:T(8,128)(2,1)S(1)}, bf16[4,24,2432]{2,1,0:T(8,128)(2,1)S(1)}, u32[]{:S(2)}, u32[]{:S(2)}) collective-permute-start(bf16[4,24,2432]{2,1,0:T(8,128)(2,1)S(1)} %pad_maximum_fusion.2.refs_0_), channel_id=1, source_target_pairs={{0,2},{1,3},{2,0},{3,1},{4,6},{5,7},{6,4},{7,5},{8,10},{9,11},{10,... | collective-permute-start | bytes 1400840 | tf_op jit(solution)/shard_map/ppermute | solution.py:69
  20.6 9.0 %collective-permute-start.5 = (bf16[24,3840]{1,0:T(8,128)(2,1)S(1)}, bf16[24,3840]{1,0:T(8,128)(2,1)S(1)}, u32[]{:S(2)}, u32[]{:S(2)}) collective-permute-start(bf16[24,3840]{1,0:T(8,128)(2,1)S(1)} %pad_maximum_fusion.10), channel_id=1, source_target_pairs={{0,24},{1,25},{2,26},{3,27},{4,28},{5,29},{6,30},{7,31},{8,0},{9,1... | collective-permute-start | bytes 552968 | tf_op jit(solution)/shard_map/ppermute | solution.py:69
  24.6 9.4 %collective-permute-start.3 = (bf16[24,3840]{1,0:T(8,128)(2,1)S(1)}, bf16[24,3840]{1,0:T(8,128)(2,1)S(1)}, u32[]{:S(2)}, u32[]{:S(2)}) collective-permute-start(bf16[24,3840]{1,0:T(8,128)(2,1)S(1)} %pad_maximum_fusion.10), channel_id=1, source_target_pairs={{0,8},{1,9},{2,10},{3,11},{4,12},{5,13},{6,14},{7,15},{8,16},{9,17... | collective-permute-start | bytes 552968 | tf_op jit(solution)/shard_map/ppermute | solution.py:69
  24.6 16.5 %collective-permute-start.4 = (bf16[24,3840]{1,0:T(8,128)(2,1)S(1)}, bf16[24,3840]{1,0:T(8,128)(2,1)S(1)}, u32[]{:S(2)}, u32[]{:S(2)}) collective-permute-start(bf16[24,3840]{1,0:T(8,128)(2,1)S(1)} %pad_maximum_fusion.10), channel_id=1, source_target_pairs={{0,16},{1,17},{2,18},{3,19},{4,20},{5,21},{6,22},{7,23},{8,24},{9,... | collective-permute-start | bytes 552968 | tf_op jit(solution)/shard_map/ppermute | solution.py:69
  25.2 16.1 %collective-permute-start.7 = (bf16[4,24,2432]{2,1,0:T(8,128)(2,1)S(1)}, bf16[4,24,2432]{2,1,0:T(8,128)(2,1)S(1)}, u32[]{:S(2)}, u32[]{:S(2)}) collective-permute-start(bf16[4,24,2432]{2,1,0:T(8,128)(2,1)S(1)} %pad_maximum_fusion.2.refs_0_), channel_id=1, source_target_pairs={{0,4},{1,5},{2,6},{3,7},{4,0},{5,1},{6,2},{7,3},{8,12},{9,13},{10,... | collective-permute-start | bytes 1400840 | tf_op jit(solution)/shard_map/ppermute | solution.py:69
  29.7 15.6 %collective-permute-start.10 = (bf16[4,24,2432]{2,1,0:T(8,128)(2,1)S(1)}, bf16[4,24,2432]{2,1,0:T(8,128)(2,1)S(1)}, u32[]{:S(2)}, u32[]{:S(2)}) collective-permute-start(bf16[4,24,2432]{2,1,0:T(8,128)(2,1)S(1)} %pad_maximum_fusion.2.refs_0_), channel_id=1, source_target_pairs={{0,1},{1,0},{2,3},{3,2},{4,5},{5,4},{6,7},{7,6},{8,9},{9,8},{10,11... | collective-permute-start | bytes 1400840 | tf_op jit(solution)/shard_map/ppermute | solution.py:69
  30.9 33.2 %collective-permute-start.11 = (bf16[4,24,2432]{2,1,0:T(8,128)(2,1)S(1)}, bf16[4,24,2432]{2,1,0:T(8,128)(2,1)S(1)}, u32[]{:S(2)}, u32[]{:S(2)}) collective-permute-start(bf16[4,24,2432]{2,1,0:T(8,128)(2,1)S(1)} %collective-permute-done.6.refs_1_), channel_id=1, source_target_pairs={{0,1},{1,0},{2,3},{3,2},{4,5},{5,4},{6,7},{7,6},{8,9},{9,8},{10,11... | collective-permute-start | bytes 1400840 | tf_op jit(solution)/shard_map/ppermute | solution.py:69
  41.3 38.4 %collective-permute-start.15 = (bf16[4,24,3840]{2,1,0:T(8,128)(2,1)S(1)}, bf16[4,24,3840]{2,1,0:T(8,128)(2,1)}, u32[]{:S(2)}, u32[]{:S(2)}) collective-permute-start(bf16[4,24,3840]{2,1,0:T(8,128)(2,1)S(1)} %pad_maximum_fusion.1.refs_0_), channel_id=1, source_target_pairs={{0,2},{1,3},{2,0},{3,1},{4,6},{5,7},{6,4},{7,5},{8,10},{9,11},{10,... | collective-permute-start | bytes 2211848 | tf_op jit(solution)/shard_map/ppermute | solution.py:69
  43.7 20.4 %collective-permute-start.9 = (bf16[4,24,1216]{2,1,0:T(8,128)(2,1)S(1)}, bf16[4,24,1216]{2,1,0:T(8,128)(2,1)}, u32[]{:S(2)}, u32[]{:S(2)}) collective-permute-start(bf16[4,24,1216]{2,1,0:T(8,128)(2,1)S(1)} %slice.541), channel_id=1, source_target_pairs={{0,2},{1,3},{2,0},{3,1},{4,6},{5,7},{6,4},{7,5},{8,10},{9,11},{10,... | collective-permute-start | bytes 700424 | tf_op jit(solution)/shard_map/ppermute | solution.py:69
  45.2 22.8 %collective-permute-start.12 = (bf16[4,24,2432]{2,1,0:T(8,128)(2,1)S(1)}, bf16[4,24,2432]{2,1,0:T(8,128)(2,1)}, u32[]{:S(2)}, u32[]{:S(2)}) collective-permute-start(bf16[4,24,2432]{2,1,0:T(8,128)(2,1)S(1)} %collective-permute-done.7.refs_2_), channel_id=1, source_target_pairs={{0,1},{1,0},{2,3},{3,2},{4,5},{5,4},{6,7},{7,6},{8,9},{9,8},{10,11... | collective-permute-start | bytes 1400840 | tf_op jit(solution)/shard_map/ppermute | solution.py:69
  48.5 42.9 %collective-permute-start.16 = (bf16[4,24,3840]{2,1,0:T(8,128)(2,1)S(1)}, bf16[4,24,3840]{2,1,0:T(8,128)(2,1)}, u32[]{:S(2)}, u32[]{:S(2)}) collective-permute-start(bf16[4,24,3840]{2,1,0:T(8,128)(2,1)S(1)} %pad_maximum_fusion.1.refs_0_), channel_id=1, source_target_pairs={{0,4},{1,5},{2,6},{3,7},{4,0},{5,1},{6,2},{7,3},{8,12},{9,13},{10,... | collective-permute-start | bytes 2211848 | tf_op jit(solution)/shard_map/ppermute | solution.py:69
  68.0 24.9 %collective-permute-start.17 = (bf16[24,6144]{1,0:T(8,128)(2,1)S(1)}, bf16[24,6144]{1,0:T(8,128)(2,1)S(1)}, u32[]{:S(2)}, u32[]{:S(2)}) collective-permute-start(bf16[24,6144]{1,0:T(8,128)(2,1)S(1)} %constant_dynamic-update-slice_fusion), channel_id=1, source_target_pairs={{0,8},{1,9},{2,10},{3,11},{4,12},{5,13},{6,14},{7,15},{8,16},{9,17... | collective-permute-start | bytes 884744 | tf_op jit(solution)/shard_map/ppermute | solution.py:69
  68.7 25.8 %collective-permute-start.18 = (bf16[24,6144]{1,0:T(8,128)(2,1)S(1)}, bf16[24,6144]{1,0:T(8,128)(2,1)S(1)}, u32[]{:S(2)}, u32[]{:S(2)}) collective-permute-start(bf16[24,6144]{1,0:T(8,128)(2,1)S(1)} %constant_dynamic-update-slice_fusion), channel_id=1, source_target_pairs={{0,16},{1,17},{2,18},{3,19},{4,20},{5,21},{6,22},{7,23},{8,24},{9,... | collective-permute-start | bytes 884744 | tf_op jit(solution)/shard_map/ppermute | solution.py:69
  72.1 22.4 %collective-permute-start.19 = (bf16[24,6144]{1,0:T(8,128)(2,1)S(1)}, bf16[24,6144]{1,0:T(8,128)(2,1)S(1)}, u32[]{:S(2)}, u32[]{:S(2)}) collective-permute-start(bf16[24,6144]{1,0:T(8,128)(2,1)S(1)} %constant_dynamic-update-slice_fusion), channel_id=1, source_target_pairs={{0,24},{1,25},{2,26},{3,27},{4,28},{5,29},{6,30},{7,31},{8,0},{9,1... | collective-permute-start | bytes 884744 | tf_op jit(solution)/shard_map/ppermute | solution.py:69
  79.7 15.5 %collective-permute-start.22 = (bf16[4,24,3840]{2,1,0:T(8,128)(2,1)S(1)}, bf16[4,24,3840]{2,1,0:T(8,128)(2,1)}, u32[]{:S(2)}, u32[]{:S(2)}) collective-permute-start(bf16[4,24,3840]{2,1,0:T(8,128)(2,1)S(1)} %pad_maximum_fusion.1.refs_0_), channel_id=1, source_target_pairs={{0,1},{1,0},{2,3},{3,2},{4,5},{5,4},{6,7},{7,6},{8,9},{9,8},{10,11... | collective-permute-start | bytes 2211848 | tf_op jit(solution)/shard_map/ppermute | solution.py:69
  92.4 38.6 %collective-permute-start.23 = (bf16[4,24,3840]{2,1,0:T(8,128)(2,1)}, bf16[4,24,3840]{2,1,0:T(8,128)(2,1)}, u32[]{:S(2)}, u32[]{:S(2)}) collective-permute-start(bf16[4,24,3840]{2,1,0:T(8,128)(2,1)} %collective-permute-done.15.refs_1_), channel_id=1, source_target_pairs={{0,1},{1,0},{2,3},{3,2},{4,5},{5,4},{6,7},{7,6},{8,9},{9,8},{10,11... | collective-permute-start | bytes 2211848 | tf_op jit(solution)/shard_map/ppermute | solution.py:69
  93.0 11.5 %collective-permute-start.20 = (bf16[4,24,1920]{2,1,0:T(8,128)(2,1)S(1)}, bf16[4,24,1920]{2,1,0:T(8,128)(2,1)S(1)}, u32[]{:S(2)}, u32[]{:S(2)}) collective-permute-start(bf16[4,24,1920]{2,1,0:T(8,128)(2,1)S(1)} %slice.412), channel_id=1, source_target_pairs={{0,4},{1,5},{2,6},{3,7},{4,0},{5,1},{6,2},{7,3},{8,12},{9,13},{10,... | collective-permute-start | bytes 1105928 | tf_op jit(solution)/shard_map/ppermute | solution.py:69
  94.5 36.5 %collective-permute-start.24 = (bf16[4,24,3840]{2,1,0:T(8,128)(2,1)}, bf16[4,24,3840]{2,1,0:T(8,128)(2,1)}, u32[]{:S(2)}, u32[]{:S(2)}) collective-permute-start(bf16[4,24,3840]{2,1,0:T(8,128)(2,1)} %collective-permute-done.16.refs_2_), channel_id=1, source_target_pairs={{0,1},{1,0},{2,3},{3,2},{4,5},{5,4},{6,7},{7,6},{8,9},{9,8},{10,11... | collective-permute-start | bytes 2211848 | tf_op jit(solution)/shard_map/ppermute | solution.py:69
  94.7 53.3 %collective-permute-start.27 = (bf16[4,24,6144]{2,1,0:T(8,128)(2,1)S(1)}, bf16[4,24,6144]{2,1,0:T(8,128)(2,1)S(1)}, u32[]{:S(2)}, u32[]{:S(2)}) collective-permute-start(bf16[4,24,6144]{2,1,0:T(8,128)(2,1)S(1)} %pad_maximum_fusion.refs_0_), channel_id=1, source_target_pairs={{0,2},{1,3},{2,0},{3,1},{4,6},{5,7},{6,4},{7,5},{8,10},{9,11},{10,... | collective-permute-start | bytes 3538952 | tf_op jit(solution)/shard_map/ppermute | solution.py:69
  95.3 52.7 %collective-permute-start.28 = (bf16[4,24,6144]{2,1,0:T(8,128)(2,1)S(1)}, bf16[4,24,6144]{2,1,0:T(8,128)(2,1)}, u32[]{:S(2)}, u32[]{:S(2)}) collective-permute-start(bf16[4,24,6144]{2,1,0:T(8,128)(2,1)S(1)} %pad_maximum_fusion.refs_0_), channel_id=1, source_target_pairs={{0,4},{1,5},{2,6},{3,7},{4,0},{5,1},{6,2},{7,3},{8,12},{9,13},{10,... | collective-permute-start | bytes 3538952 | tf_op jit(solution)/shard_map/ppermute | solution.py:69
  105.2 25.8 %collective-permute-start.21 = (bf16[4,24,1920]{2,1,0:T(8,128)(2,1)S(1)}, bf16[4,24,1920]{2,1,0:T(8,128)(2,1)S(1)}, u32[]{:S(2)}, u32[]{:S(2)}) collective-permute-start(bf16[4,24,1920]{2,1,0:T(8,128)(2,1)S(1)} %slice.413), channel_id=1, source_target_pairs={{0,2},{1,3},{2,0},{3,1},{4,6},{5,7},{6,4},{7,5},{8,10},{9,11},{10,... | collective-permute-start | bytes 1105928 | tf_op jit(solution)/shard_map/ppermute | solution.py:69
  131.6 35.3 %collective-permute-start.31 = (bf16[4,24,6144]{2,1,0:T(8,128)(2,1)S(1)}, bf16[4,24,6144]{2,1,0:T(8,128)(2,1)}, u32[]{:S(2)}, u32[]{:S(2)}) collective-permute-start(bf16[4,24,6144]{2,1,0:T(8,128)(2,1)S(1)} %pad_maximum_fusion.refs_0_), channel_id=1, source_target_pairs={{0,1},{1,0},{2,3},{3,2},{4,5},{5,4},{6,7},{7,6},{8,9},{9,8},{10,11... | collective-permute-start | bytes 3538952 | tf_op jit(solution)/shard_map/ppermute | solution.py:69
  148.0 18.9 %collective-permute-start.32 = (bf16[4,24,6144]{2,1,0:T(8,128)(2,1)S(1)}, bf16[4,24,6144]{2,1,0:T(8,128)(2,1)}, u32[]{:S(2)}, u32[]{:S(2)}) collective-permute-start(bf16[4,24,6144]{2,1,0:T(8,128)(2,1)S(1)} %collective-permute-done.27.refs_1_), channel_id=1, source_target_pairs={{0,1},{1,0},{2,3},{3,2},{4,5},{5,4},{6,7},{7,6},{8,9},{9,8},{10,11... | collective-permute-start | bytes 3538952 | tf_op jit(solution)/shard_map/ppermute | solution.py:69
  148.2 18.7 %collective-permute-start.33 = (bf16[4,24,6144]{2,1,0:T(8,128)(2,1)}, bf16[4,24,6144]{2,1,0:T(8,128)(2,1)}, u32[]{:S(2)}, u32[]{:S(2)}) collective-permute-start(bf16[4,24,6144]{2,1,0:T(8,128)(2,1)} %collective-permute-done.28.refs_2_), channel_id=1, source_target_pairs={{0,1},{1,0},{2,3},{3,2},{4,5},{5,4},{6,7},{7,6},{8,9},{9,8},{10,11... | collective-permute-start | bytes 3538952 | tf_op jit(solution)/shard_map/ppermute | solution.py:69
  150.6 16.3 %collective-permute-start.29 = (bf16[4,24,3072]{2,1,0:T(8,128)(2,1)}, bf16[4,24,3072]{2,1,0:T(8,128)(2,1)}, u32[]{:S(2)}, u32[]{:S(2)}) collective-permute-start(bf16[4,24,3072]{2,1,0:T(8,128)(2,1)} %slice.414), channel_id=1, source_target_pairs={{0,4},{1,5},{2,6},{3,7},{4,0},{5,1},{6,2},{7,3},{8,12},{9,13},{10,... | collective-permute-start | bytes 1769480 | tf_op jit(solution)/shard_map/ppermute | solution.py:69
  151.1 15.7 %collective-permute-start.30 = (bf16[4,24,3072]{2,1,0:T(8,128)(2,1)S(1)}, bf16[4,24,3072]{2,1,0:T(8,128)(2,1)}, u32[]{:S(2)}, u32[]{:S(2)}) collective-permute-start(bf16[4,24,3072]{2,1,0:T(8,128)(2,1)S(1)} %slice.415), channel_id=1, source_target_pairs={{0,2},{1,3},{2,0},{3,1},{4,6},{5,7},{6,4},{7,5},{8,10},{9,11},{10,... | collective-permute-start | bytes 1769480 | tf_op jit(solution)/shard_map/ppermute | solution.py:69
  243.7 29.5 %collective-permute-start.36 = (bf16[4,2,2,24,6144]{4,3,2,1,0:T(8,128)(2,1)}, bf16[4,2,2,24,6144]{4,3,2,1,0:T(8,128)(2,1)}, u32[]{:S(2)}, u32[]{:S(2)}) collective-permute-start(bf16[4,2,2,24,6144]{4,3,2,1,0:T(8,128)(2,1)} %get-tuple-element.135), channel_id=1, source_target_pairs={{0,1},{1,0},{2,3},{3,2},{4,5},{5,4},{6,7},{7,6},{8,9},{9,8},{10,11... | collective-permute-start | bytes 14155784 | tf_op jit(solution)/shard_map/ppermute | solution.py:69
  301.3 30.0 %collective-permute-start.39 = (bf16[4,2,2,24,3840]{4,3,2,1,0:T(8,128)(2,1)}, bf16[4,2,2,24,3840]{4,3,2,1,0:T(8,128)(2,1)}, u32[]{:S(2)}, u32[]{:S(2)}) collective-permute-start(bf16[4,2,2,24,3840]{4,3,2,1,0:T(8,128)(2,1)} %get-tuple-element.148), channel_id=1, source_target_pairs={{0,1},{1,0},{2,3},{3,2},{4,5},{5,4},{6,7},{7,6},{8,9},{9,8},{10,11... | collective-permute-start | bytes 8847368 | tf_op jit(solution)/shard_map/ppermute | solution.py:69
  301.7 28.3 %collective-permute-start.38 = (bf16[4,2,24,3072]{3,2,1,0:T(8,128)(2,1)}, bf16[4,2,24,3072]{3,2,1,0:T(8,128)(2,1)}, u32[]{:S(2)}, u32[]{:S(2)}) collective-permute-start(bf16[4,2,24,3072]{3,2,1,0:T(8,128)(2,1)} %fusion.3), channel_id=1, source_target_pairs={{0,2},{1,3},{2,0},{3,1},{4,6},{5,7},{6,4},{7,5},{8,10},{9,11},{10,... | collective-permute-start | bytes 3538952 | tf_op jit(solution)/shard_map/ppermute | solution.py:69
  303.3 28.0 %collective-permute-start.37 = (bf16[4,2,24,3072]{3,2,0,1:T(8,128)(2,1)}, bf16[4,2,24,3072]{3,2,0,1:T(8,128)(2,1)}, u32[]{:S(2)}, u32[]{:S(2)}) collective-permute-start(bf16[4,2,24,3072]{3,2,0,1:T(8,128)(2,1)} %get-tuple-element.234), channel_id=1, source_target_pairs={{0,4},{1,5},{2,6},{3,7},{4,0},{5,1},{6,2},{7,3},{8,12},{9,13},{10,... | collective-permute-start | bytes 3538952 | tf_op jit(solution)/shard_map/ppermute | solution.py:69
  342.9 34.9 %collective-permute-start.43 = (bf16[4,2,24,1920]{3,2,1,0:T(8,128)(2,1)}, bf16[4,2,24,1920]{3,2,1,0:T(8,128)(2,1)}, u32[]{:S(2)}, u32[]{:S(2)}) collective-permute-start(bf16[4,2,24,1920]{3,2,1,0:T(8,128)(2,1)} %fusion.8), channel_id=1, source_target_pairs={{0,2},{1,3},{2,0},{3,1},{4,6},{5,7},{6,4},{7,5},{8,10},{9,11},{10,... | collective-permute-start | bytes 2211848 | tf_op jit(solution)/shard_map/ppermute | solution.py:69
  343.4 34.4 %collective-permute-start.42 = (bf16[4,2,24,1920]{3,2,0,1:T(8,128)(2,1)}, bf16[4,2,24,1920]{3,2,0,1:T(8,128)(2,1)}, u32[]{:S(2)}, u32[]{:S(2)}) collective-permute-start(bf16[4,2,24,1920]{3,2,0,1:T(8,128)(2,1)} %get-tuple-element.236), channel_id=1, source_target_pairs={{0,4},{1,5},{2,6},{3,7},{4,0},{5,1},{6,2},{7,3},{8,12},{9,13},{10,... | collective-permute-start | bytes 2211848 | tf_op jit(solution)/shard_map/ppermute | solution.py:69
  344.9 32.9 %collective-permute-start.41 = (bf16[4,24,3072]{2,1,0:T(8,128)(2,1)}, bf16[4,24,3072]{2,1,0:T(8,128)(2,1)S(1)}, u32[]{:S(2)}, u32[]{:S(2)}) collective-permute-start(bf16[4,24,3072]{2,1,0:T(8,128)(2,1)} %fusion.13), channel_id=1, source_target_pairs={{0,4},{1,5},{2,6},{3,7},{4,0},{5,1},{6,2},{7,3},{8,12},{9,13},{10,... | collective-permute-start | bytes 1769480 | tf_op jit(solution)/shard_map/ppermute | solution.py:69
  347.8 29.9 %collective-permute-start.40 = (bf16[4,24,3072]{2,1,0:T(8,128)(2,1)}, bf16[4,24,3072]{2,1,0:T(8,128)(2,1)}, u32[]{:S(2)}, u32[]{:S(2)}) collective-permute-start(bf16[4,24,3072]{2,1,0:T(8,128)(2,1)} %get-tuple-element.240), channel_id=1, source_target_pairs={{0,2},{1,3},{2,0},{3,1},{4,6},{5,7},{6,4},{7,5},{8,10},{9,11},{10,... | collective-permute-start | bytes 1769480 | tf_op jit(solution)/shard_map/ppermute | solution.py:69
  405.1 42.5 %collective-permute-start.44 = (bf16[4,2,2,24,2304]{4,3,2,1,0:T(8,128)(2,1)}, bf16[4,2,2,24,2304]{4,3,2,1,0:T(8,128)(2,1)S(1)}, u32[]{:S(2)}, u32[]{:S(2)}) collective-permute-start(bf16[4,2,2,24,2304]{4,3,2,1,0:T(8,128)(2,1)} %get-tuple-element.160), channel_id=1, source_target_pairs={{0,1},{1,0},{2,3},{3,2},{4,5},{5,4},{6,7},{7,6},{8,9},{9,8},{10,11... | collective-permute-start | bytes 5308424 | tf_op jit(solution)/shard_map/ppermute | solution.py:69
  413.2 15.6 %collective-permute-start.49 = (bf16[24,6144]{1,0:T(8,128)(2,1)}, bf16[24,6144]{1,0:T(8,128)(2,1)}, u32[]{:S(2)}, u32[]{:S(2)}) collective-permute-start(bf16[24,6144]{1,0:T(8,128)(2,1)} %pad_maximum_fusion.6), channel_id=1, source_target_pairs={{0,24},{1,25},{2,26},{3,27},{4,28},{5,29},{6,30},{7,31},{8,0},{9,1... | collective-permute-start | bytes 884744 | tf_op jit(solution)/shard_map/ppermute | solution.py:69
  424.8 22.8 %collective-permute-start.46 = (bf16[4,24,1920]{2,1,0:T(8,128)(2,1)}, bf16[4,24,1920]{2,1,0:T(8,128)(2,1)}, u32[]{:S(2)}, u32[]{:S(2)}) collective-permute-start(bf16[4,24,1920]{2,1,0:T(8,128)(2,1)} %fusion.21), channel_id=1, source_target_pairs={{0,4},{1,5},{2,6},{3,7},{4,0},{5,1},{6,2},{7,3},{8,12},{9,13},{10,... | collective-permute-start | bytes 1105928 | tf_op jit(solution)/shard_map/ppermute | solution.py:69
  426.1 21.5 %collective-permute-start.45 = (bf16[4,24,1920]{2,1,0:T(8,128)(2,1)}, bf16[4,24,1920]{2,1,0:T(8,128)(2,1)}, u32[]{:S(2)}, u32[]{:S(2)}) collective-permute-start(bf16[4,24,1920]{2,1,0:T(8,128)(2,1)} %get-tuple-element.242), channel_id=1, source_target_pairs={{0,2},{1,3},{2,0},{3,1},{4,6},{5,7},{6,4},{7,5},{8,10},{9,11},{10,... | collective-permute-start | bytes 1105928 | tf_op jit(solution)/shard_map/ppermute | solution.py:69
  427.7 19.9 %collective-permute-start.48 = (bf16[24,6144]{1,0:T(8,128)(2,1)}, bf16[24,6144]{1,0:T(8,128)(2,1)}, u32[]{:S(2)}, u32[]{:S(2)}) collective-permute-start(bf16[24,6144]{1,0:T(8,128)(2,1)} %pad_maximum_fusion.5), channel_id=1, source_target_pairs={{0,16},{1,17},{2,18},{3,19},{4,20},{5,21},{6,22},{7,23},{8,24},{9,... | collective-permute-start | bytes 884744 | tf_op jit(solution)/shard_map/ppermute | solution.py:69
  428.8 18.8 %collective-permute-start.47 = (bf16[24,6144]{1,0:T(8,128)(2,1)}, bf16[24,6144]{1,0:T(8,128)(2,1)}, u32[]{:S(2)}, u32[]{:S(2)}) collective-permute-start(bf16[24,6144]{1,0:T(8,128)(2,1)} %pad_maximum_fusion.4), channel_id=1, source_target_pairs={{0,8},{1,9},{2,10},{3,11},{4,12},{5,13},{6,14},{7,15},{8,16},{9,17... | collective-permute-start | bytes 884744 | tf_op jit(solution)/shard_map/ppermute | solution.py:69
  454.2 13.0 %collective-permute-start.59 = (bf16[24,3840]{1,0:T(8,128)(2,1)S(1)}, bf16[24,3840]{1,0:T(8,128)(2,1)S(1)}, u32[]{:S(2)}, u32[]{:S(2)}) collective-permute-start(bf16[24,3840]{1,0:T(8,128)(2,1)S(1)} %pad_maximum_fusion.14), channel_id=1, source_target_pairs={{0,24},{1,25},{2,26},{3,27},{4,28},{5,29},{6,30},{7,31},{8,0},{9,1... | collective-permute-start | bytes 552968 | tf_op jit(solution)/shard_map/ppermute | solution.py:69
  454.3 17.7 %collective-permute-start.58 = (bf16[24,3840]{1,0:T(8,128)(2,1)S(1)}, bf16[24,3840]{1,0:T(8,128)(2,1)S(1)}, u32[]{:S(2)}, u32[]{:S(2)}) collective-permute-start(bf16[24,3840]{1,0:T(8,128)(2,1)S(1)} %pad_maximum_fusion.13), channel_id=1, source_target_pairs={{0,16},{1,17},{2,18},{3,19},{4,20},{5,21},{6,22},{7,23},{8,24},{9,... | collective-permute-start | bytes 552968 | tf_op jit(solution)/shard_map/ppermute | solution.py:69
  455.6 16.4 %collective-permute-start.57 = (bf16[24,3840]{1,0:T(8,128)(2,1)S(1)}, bf16[24,3840]{1,0:T(8,128)(2,1)S(1)}, u32[]{:S(2)}, u32[]{:S(2)}) collective-permute-start(bf16[24,3840]{1,0:T(8,128)(2,1)S(1)} %pad_maximum_fusion.12), channel_id=1, source_target_pairs={{0,8},{1,9},{2,10},{3,11},{4,12},{5,13},{6,14},{7,15},{8,16},{9,17... | collective-permute-start | bytes 552968 | tf_op jit(solution)/shard_map/ppermute | solution.py:69
  457.6 14.5 %collective-permute-start.50 = (bf16[4,2,24,1152]{3,2,1,0:T(8,128)(2,1)}, bf16[4,2,24,1152]{3,2,1,0:T(8,128)(2,1)S(1)}, u32[]{:S(2)}, u32[]{:S(2)}) collective-permute-start(bf16[4,2,24,1152]{3,2,1,0:T(8,128)(2,1)} %get-tuple-element.238), channel_id=1, source_target_pairs={{0,4},{1,5},{2,6},{3,7},{4,0},{5,1},{6,2},{7,3},{8,12},{9,13},{10,... | collective-permute-start | bytes 1327112 | tf_op jit(solution)/shard_map/ppermute | solution.py:69
  459.2 13.6 %collective-permute-start.52 = (bf16[4,2,24,1152]{3,2,1,0:T(8,128)(2,1)}, bf16[4,2,24,1152]{3,2,1,0:T(8,128)(2,1)S(1)}, u32[]{:S(2)}, u32[]{:S(2)}) collective-permute-start(bf16[4,2,24,1152]{3,2,1,0:T(8,128)(2,1)} %fusion.17), channel_id=1, source_target_pairs={{0,2},{1,3},{2,0},{3,1},{4,6},{5,7},{6,4},{7,5},{8,10},{9,11},{10,... | collective-permute-start | bytes 1327112 | tf_op jit(solution)/shard_map/ppermute | solution.py:69
  479.6 9.9 %collective-permute-start.55 = (bf16[24,2304]{1,0:T(8,128)(2,1)S(1)}, bf16[24,2304]{1,0:T(8,128)(2,1)S(1)}, u32[]{:S(2)}, u32[]{:S(2)}) collective-permute-start(bf16[24,2304]{1,0:T(8,128)(2,1)S(1)} %pad_maximum_fusion.17), channel_id=1, source_target_pairs={{0,16},{1,17},{2,18},{3,19},{4,20},{5,21},{6,22},{7,23},{8,24},{9,... | collective-permute-start | bytes 331784 | tf_op jit(solution)/shard_map/ppermute | solution.py:69
  (59 other events, 619.5 us)

commit v3 on v2

--- a/solution.py
+++ b/solution.py
@@ -32,6 +32,31 @@
 scale = HEAD_DIM ** (-0.5)
 f32 = jnp.float32
 bf16 = jnp.bfloat16
+PACE = 1e9
+WORK = {
+    "place": 6,
+    "qkv_project": 11,
+    "self_attend": 12,
+    "mid_forward": 8,
+    "ckv_project": 6,
+    "cross_attend": 8,
+    "mlp_both": 39,
+    "grad_blocks": 6,
+    "cross_back": 20,
+    "fold_core": 5,
+    "fold_side": 4,
+    "fold_corner": 2,
+    "fold_z": 2,
+    "mid_back": 9,
+    "self_back": 15,
+    "token_back": 10,
+    "neighbour_back": 6,
+    "spread": 5,
+}
+
+
+def cost_of(name):
+    return pl.CostEstimate(flops=int(WORK[name] * PACE), transcendentals=0, bytes_accessed=0)
 
 
 def geometry(count):
@@ -148,7 +173,6 @@
     def source(z, me_ref):
         return (lax.rem(me_ref[0] - z + nz, nz), 0, 0)
 
-    moved = 2 * nz * inner * rows * width * 2
     outs = pl.pallas_call(
         functools.partial(place_kernel, keys, counts, sizes, split),
         out_shape=[like((nz, inner) + shape, bf16) for shape in shapes],
@@ -160,7 +184,7 @@
                 pl.BlockSpec((1, inner) + shape, lambda z, me_ref: (z, 0, 0, 0)) for shape in shapes
             ],
         ),
-        cost_estimate=pl.CostEstimate(flops=0, transcendentals=0, bytes_accessed=moved),
+        cost_estimate=cost_of("place"),
         name="place",
     )(me, *arrays)
     outs = [out.reshape(nz * inner * out.shape[2], out.shape[3]) for out in outs]
@@ -202,7 +226,6 @@
     def source(z, me_ref):
         return (lax.rem(me_ref[0] + z, nz), 0, 0, 0)
 
-    moved = 2 * D * width * kind.itemsize
     return pl.pallas_call(
         functools.partial(spread_kernel, sizes, split),
         out_shape=[shape, shape],
@@ -212,7 +235,7 @@
             in_specs=[pl.BlockSpec((1,) + b.shape[1:], source) for b in blocks],
             out_specs=[block, block],
         ),
-        cost_estimate=pl.CostEstimate(flops=0, transcendentals=0, bytes_accessed=moved),
+        cost_estimate=cost_of("spread"),
         name="spread",
     )(me, *blocks)
 
@@ -224,18 +247,50 @@
     return total
 
 
-def fold_core(kept, got, sizes):
-    half = kept.shape[-1] // 2
+def fold_core_kernel(sizes, half, count, me_ref, *refs):
+    nz, ny, nx, nc = sizes
+    kept_ref, got_ref = refs[:2]
+    width = kept_ref.shape[-1]
+    outs = refs[count:]
+    z = pl.program_id(0)
+    for y in range(ny):
+        for x in range(nx):
+            first_ref, second_ref = outs[y], outs[ny + x]
+            kind = first_ref.dtype
+            total = plus(kept_ref[0, y, x], got_ref[0, y, x])
+            first_ref[0, x] = total[:, :half].astype(kind)
+            second_ref[0, y, :, : width - half] = total[:, half:].astype(kind)
+            if count > 2:
+                there = lax.rem(me_ref[1] + y, ny) * nx + lax.rem(me_ref[2] + x, nx)
+                slot = there * nc + me_ref[3]
+                extra = refs[2][0, slot] + refs[3][0, slot]
+                second_ref[0, y, :, width - half :] = extra.astype(kind)
+
+
+def fold_core(kept, got, sizes, me, small=()):
+    nz, ny, nx, nc = sizes
+    rows, width = kept.shape[3:]
+    half = width // (2 * LANES) * LANES
     kind = kept.dtype
-
-    def part(*index):
-        return plus(kept[index], got[index]).astype(kind)
-
-    every = slice(None)
-    low, high = slice(None, half), slice(half, None)
-    first = [part(every, e, every, every, low) for e in range(sizes[1])]
-    second = [part(every, every, d, every, high) for d in range(sizes[2])]
-    return first, second
+    small = [v.reshape(nz, ny * nx * nc, rows, LANES) for v in small]
+    rest = width - half + (LANES if small else 0)
+    block = pl.BlockSpec((1,) + kept.shape[1:], lambda z, _: (z, 0, 0, 0, 0))
+    source = pl.BlockSpec(
+        (1, ny * nx * nc, rows, LANES), lambda z, me_ref: (lax.rem(me_ref[0] + z, nz), 0, 0, 0)
+    )
+    shapes = [(nx, rows, half)] * ny + [(ny, rows, rest)] * nx
+    outs = call(
+        functools.partial(fold_core_kernel, sizes, half, 2 + len(small)),
+        "fold_core",
+        (nz,),
+        [kept, got] + small,
+        [block, block] + [source] * len(small),
+        [like((nz,) + shape, kind) for shape in shapes],
+        [pl.BlockSpec((1,) + shape, lambda z, _: (z, 0, 0, 0)) for shape in shapes],
+        0,
+        scalars=(me,),
+    )
+    return outs[:ny], outs[ny:]
 
 
 def send_side(parts, sizes):
@@ -246,11 +301,31 @@
     )
 
 
+def fold_side_kernel(ny, nx, *refs):
+    outs = refs[ny + nx :]
+    for x in range(nx):
+        total = plus(*[ref[0, x] for ref in refs[:ny]])
+        outs[x][0] = total.astype(outs[x].dtype)
+    for y in range(ny):
+        total = plus(*[ref[0, y] for ref in refs[ny : ny + nx]])
+        outs[nx + y][0] = total.astype(outs[nx + y].dtype)
+
+
 def fold_side(got, sizes):
-    kind = got[0][0].dtype
-    first = [plus(*[g[:, d] for g in got[0]]).astype(kind) for d in range(sizes[2])]
-    second = [plus(*[g[:, e] for g in got[1]]).astype(kind) for e in range(sizes[1])]
-    return first, second
+    nz, ny, nx, _ = sizes
+    ins = list(got[0]) + list(got[1])
+    shapes = [a.shape[2:] for a in (ins[0],) * nx + (ins[-1],) * ny]
+    outs = call(
+        functools.partial(fold_side_kernel, ny, nx),
+        "fold_side",
+        (nz,),
+        ins,
+        [pl.BlockSpec((1,) + a.shape[1:], lambda z: (z, 0, 0, 0)) for a in ins],
+        [like((nz,) + shape, ins[0].dtype) for shape in shapes],
+        [pl.BlockSpec((1,) + shape, lambda z: (z, 0, 0)) for shape in shapes],
+        0,
+    )
+    return outs[:nx], outs[nx:]
 
 
 def send_corner(parts, sizes):
@@ -261,24 +336,57 @@
     )
 
 
+def fold_corner_kernel(nx, ny, *refs):
+    outs = refs[nx + ny :]
+    half = refs[0].shape[-1]
+    for z, out_ref in enumerate(outs):
+        out_ref[:, :half] = plus(*[ref[z] for ref in refs[:nx]]).astype(out_ref.dtype)
+        out_ref[:, half:] = plus(*[ref[z] for ref in refs[nx : nx + ny]]).astype(out_ref.dtype)
+
+
 def fold_corner(got, sizes):
-    kind = got[0][0].dtype
-    return [
-        jnp.concatenate([plus(*[g[z] for g in half]).astype(kind) for half in got], -1)
-        for z in range(sizes[0])
-    ]
+    nz, ny, nx, _ = sizes
+    ins = list(got[0]) + list(got[1])
+    shape = (ins[0].shape[1], ins[0].shape[2] + ins[-1].shape[2])
+    return call(
+        functools.partial(fold_corner_kernel, nx, ny),
+        "fold_corner",
+        (1,),
+        ins,
+        [whole(a.shape) for a in ins],
+        [like(shape, ins[0].dtype)] * nz,
+        [whole(shape)] * nz,
+        0,
+    )
 
 
 def send_z(parts, sizes):
     return [parts[0]] + [shift(parts[z], sizes, 0, z) for z in range(1, sizes[0])]
 
 
-def scatter_small(kept, sent, sizes):
-    total = plus(kept, shift(sent, sizes, 3, 1))
-    for axis, at in ((1, 1), (2, 1), (0, 0)):
-        parts = [lax.index_in_dim(total, step, at, keepdims=False) for step in range(sizes[axis])]
-        total = plus(*[parts[0]] + [shift(p, sizes, axis, k) for k, p in enumerate(parts) if k])
-    return total
+def fold_z_kernel(parts, count, *refs):
+    total = plus(*[ref[...] for ref in refs[:count]])
+    rows = total.shape[0]
+    for (start, width, stack), out_ref in zip(parts, refs[count:]):
+        part = width // stack
+        for m in range(stack):
+            column = start + m * part
+            out_ref[m * rows : (m + 1) * rows] = total[:, column : column + part]
+
+
+def fold_z(got, parts):
+    rows = got[0].shape[0]
+    shapes = [(rows * stack, width // stack) for _, width, stack in parts]
+    return call(
+        functools.partial(fold_z_kernel, parts, len(got)),
+        "fold_z",
+        (1,),
+        got,
+        [whole(a.shape) for a in got],
+        [like(shape, f32) for shape in shapes],
+        [whole(shape) for shape in shapes],
+        0,
+    )
 
 
 def dot_nn(a, b):
@@ -357,8 +465,6 @@
     exps=0,
     aliases={},
 ):
-    arrays = jax.tree.leaves((ins, outs))
-    nbytes = sum(math.prod(a.shape) * a.dtype.itemsize for a in arrays)
     return pl.pallas_call(
         kernel,
         out_shape=outs,
@@ -373,7 +479,7 @@
             dimension_semantics=("arbitrary",) * len(grid), vmem_limit_bytes=60 << 20
         ),
         input_output_aliases=aliases,
-        cost_estimate=pl.CostEstimate(flops=flops, transcendentals=exps, bytes_accessed=nbytes),
+        cost_estimate=cost_of(name),
         name=name,
     )(*scalars, *ins)
 
@@ -1020,6 +1126,69 @@
     return dot_tn(left, right).astype(bf16)
 
 
+def grad_kernel(sizes, stack, me_ref, left_ref, right_ref, *refs):
+    keep_ref, send_ref, acc_ref = refs[-3:]
+    nz, ny, nx, nc = sizes
+    rows = keep_ref.shape[3]
+    acc_ref[...] = dot_tn(left_ref[...], right_ref[...])
+    for z in range(keep_ref.shape[0]):
+        at_z = lax.rem(me_ref[0] + z, nz) if keep_ref.shape[0] > 1 else 0
+        for y in range(ny):
+            for x in range(nx):
+                at = at_z * ny + lax.rem(me_ref[1] + y, ny)
+                at = (at * nx + lax.rem(me_ref[2] + x, nx)) * nc
+                for out_ref, core in ((keep_ref, me_ref[3]), (send_ref, nc - 1 - me_ref[3])):
+                    for m in range(stack):
+                        row = pl.multiple_of(((at + core) * stack + m) * rows, 8)
+                        part = acc_ref[pl.ds(row, rows), :]
+                        out_ref[z, y, x, :, m * D : (m + 1) * D] = part.astype(bf16)
+
+
+def grad_blocks(left, right, sizes, me, width, column=0, earlier=()):
+    nz, ny, nx, _ = sizes
+    rows = D // math.prod(sizes)
+    stack = left.shape[1] // D
+    count = left.shape[0]
+    if stack == 1:
+        grid = (right.shape[1] // D,)
+        left_spec = whole(left.shape)
+        right_spec = pl.BlockSpec((count, D), lambda j, _: (0, j))
+        block = pl.BlockSpec((nz, ny, nx, rows, D), lambda j, _: (0, 0, 0, 0, column // D + j))
+        held = D
+    else:
+        grid = (nz,)
+        held = left.shape[1] // nz
+        left_spec = pl.BlockSpec(
+            (count, held), lambda z, me_ref: (0, lax.rem(me_ref[0] + z, nz))
+        )
+        right_spec = whole(right.shape)
+        block = pl.BlockSpec(
+            (1, ny, nx, rows, stack * D), lambda z, _: (z, 0, 0, 0, column // (stack * D))
+        )
+    shape = like((nz, ny, nx, rows, width), bf16)
+    earlier = list(earlier)
+    return call(
+        functools.partial(grad_kernel, sizes, stack),
+        "grad_blocks",
+        grid,
+        [left, right] + earlier,
+        [left_spec, right_spec] + [pl.BlockSpec(memory_space=pl.ANY)] * len(earlier),
+        [shape, shape],
+        [block, block],
+        0,
+        scratch=[pltpu.VMEM((held, D), f32)],
+        scalars=(me,),
+        aliases={3: 0, 4: 1} if earlier else {},
+    )
+
+
+def grads(pairs, sizes, me, width, column=0, earlier=()):
+    for left, right in pairs:
+        earlier = grad_blocks(left, right, sizes, me, width, column, earlier)
+        column += left.shape[1] // D * right.shape[1]
+    return earlier
+
+
 def local(
     sizes,
     tokens,
@@ -1059,7 +1228,7 @@
     first_pieces = near_pieces(first_own, first_side)
     first_corner = gather_corner(first_side, sizes)
     first_core = gather_core(first_pieces, sizes)
-    middle_own = after(middle_own, first_side)
+    middle_own = after(middle_own, first_corner)
     middle_side = gather_side(middle_own, sizes)
     last_own = gather_z(after(last, middle_own), sizes)
     first_pieces.update(first_corner)
@@ -1075,10 +1244,8 @@
     middle_pieces = near_pieces(middle_own, middle_side)
     middle_corner = gather_corner(middle_side, sizes)
     middle_core = gather_core(middle_pieces, sizes)
-    last_own = after(last_own, middle_side)
-    last_side = gather_side(last_own, sizes)
-
     o, lse = self_attend(block_lengths, after(qkv, middle_side, last_own))
+    last_side = gather_side(after(last_own, o), sizes)
     middle_corner, middle_core = after((middle_corner, middle_core), o)
     middle_core.update(gather_core(middle_corner, sizes))
     middle_pieces.update(middle_corner)
@@ -1086,7 +1253,7 @@
     mid = place(middle_core, sizes, me_array)
     ckv = ckv_project(neighbours, mid, vec)
     h1, a2, cq = mid_forward(o, tokens, mid, vec)
-    last_side = after(last_side, cq)
+    last_side = after(last_side, cq, ckv)
     last_pieces = near_pieces(last_own, last_side)
     last_corner = gather_corner(last_side, sizes)
     last_core = gather_core(last_pieces, sizes)
@@ -1101,51 +1268,43 @@
         h1, co, cotangent, mid, up_weight, down_weight, up_shift, vec
     )
 
-    last_kept, last_sent = spread(
-        [weight_grad(g, cotangent), weight_grad(a3, du)], sizes, me_array, split=True
-    )
+    aligned = shard % 8 == 0
+
+    def group(pairs, split=False):
+        if aligned:
+            width = sum(a.shape[1] // D * b.shape[1] for a, b in pairs)
+            return grads(pairs, sizes, me_array, width)
+        return spread([weight_grad(a, b) for a, b in pairs], sizes, me_array, split)
+
+    last_kept, last_sent = group([(g, cotangent), (a3, du)], True)
     last_got = shift(last_sent, sizes, 3, 1)
     dcq, dckv, value_sums = cross_back(picks, cq, ckv, after(dco, last_sent))
-    last_got, last_kept = after((last_got, last_kept), dcq)
-    last_parts = fold_core(last_kept, last_got, sizes)
+    last_parts = fold_core(last_kept, after(last_got, dcq), sizes, me_array)
     last_got = send_side(last_parts, sizes)
     dh1, e1, do, sums2 = mid_back(after(dcq, last_parts), dh2, h1, mid, vec)
-    middle_kept, middle_sent = spread(
-        [
-            weight_grad(neighbours, dckv),
-            weight_grad(o, e1),
-            weight_grad(a2, dcq),
-            weight_grad(co, e2),
-        ],
-        sizes,
-        me_array,
+    middle_kept, middle_sent = group(
+        [(after(neighbours, last_parts), dckv), (o, e1), (a2, dcq), (co, e2)]
     )
     middle_got = shift(middle_sent, sizes, 3, 1)
-    do = after(do, middle_sent)
+    last_parts = fold_side(after(last_got, middle_sent), sizes)
+    last_got = send_corner(last_parts, sizes)
+    do = after(do, middle_sent, last_parts)
     dqkv = self_back(0, block_lengths, qkv, do, lse, cosine, sine)
-    last_got, middle_got, middle_kept = after((last_got, middle_got, middle_kept), dqkv)
-    last_parts = fold_side(last_got, sizes)
-    last_got = send_corner(last_parts, sizes)
-    middle_parts = fold_core(middle_kept, middle_got, sizes)
+    last_parts = fold_corner(after(last_got, dqkv), sizes)
+    last_got = send_z(last_parts, sizes)
+    middle_parts = fold_core(middle_kept, after(middle_got, dqkv), sizes, me_array)
     middle_got = send_side(middle_parts, sizes)
     do = after(do, last_parts, middle_parts)
     dqkv = self_back(1, block_lengths, qkv, do, lse, cosine, sine, dqkv)
-    last_got, middle_got = after((last_got, middle_got), dqkv)
-    first_kept, first_sent = spread([weight_grad(a1, dqkv)], sizes, me_array)
+    middle_parts = fold_side(after(middle_got, dqkv), sizes)
+    middle_got = send_corner(middle_parts, sizes)
+    first_kept, first_sent = group([(after(a1, middle_parts), dqkv)])
     first_got = shift(first_sent, sizes, 3, 1)
-    last_parts = fold_corner(last_got, sizes)
-    last_got = send_z(last_parts, sizes)
-    middle_parts = fold_side(middle_got, sizes)
-    middle_got = send_corner(middle_parts, sizes)
-    dqkv = after(dqkv, first_sent, last_parts, middle_parts)
+    down_sum, up_sum = fold_z(after(last_got, first_sent), ((0, FF, FF // D), (FF, FF, 1)))
+    middle_parts = fold_corner(after(middle_got, down_sum), sizes)
+    middle_got = send_z(middle_parts, sizes)
+    dqkv = after(dqkv, first_sent, middle_parts)
     token_grad, sums1, qkv_sums = token_back(dqkv, dh1, tokens, qkv_weight, vec)
-    first_got, first_kept, middle_got, last_got = after(
-        (first_got, first_kept, middle_got, last_got), token_grad
-    )
-    first_parts = fold_core(first_kept, first_got, sizes)
-    first_got = send_side(first_parts, sizes)
-    middle_parts = fold_corner(middle_got, sizes)
-    middle_got = send_z(middle_parts, sizes)
 
     rows = jnp.concatenate(
         [
@@ -1165,24 +1324,32 @@
     )
     small_grad = jnp.concatenate([rows.T, grad_bu.reshape(D, FF // D)], 1)
     small_grad = jnp.pad(small_grad, ((0, 0), (0, LANES - SMALL)))
-    small_kept, small_sent = spread([small_grad], sizes, me_array)
-    small_sum = scatter_small(small_kept, small_sent, sizes)
-    neighbour_grad = neighbour_back(after(dckv, first_parts, middle_parts, small_sent), mid)
-    first_got = send_corner(fold_side(first_got, sizes), sizes)
-    first_got = send_z(fold_corner(first_got, sizes), sizes)
-    last_sum, middle_sum, first_sum = plus(*last_got), plus(*middle_got), plus(*first_got)
+    small_got = shift(small_grad, sizes, 3, 1)
+    first_parts = fold_core(
+        first_kept, after(first_got, token_grad), sizes, me_array, (small_grad, small_got)
+    )
+    first_got = send_side(first_parts, sizes)
+    neighbour_grad = neighbour_back(after(dckv, first_parts), mid)
+    first_parts = fold_side(after(first_got, neighbour_grad), sizes)
+    first_got = send_corner(first_parts, sizes)
+    kv_sum, out_sum, cq_sum, co_sum = fold_z(
+        after(middle_got, first_parts),
+        ((0, 2 * D, 1), (2 * D, D, 1), (3 * D, D, 1), (4 * D, D, 1)),
+    )
+    first_got = send_z(fold_corner(after(first_got, kv_sum), sizes), sizes)
+    first_sum, small_sum = fold_z(first_got, ((0, 3 * D, 1), (3 * D, LANES, 1)))
 
     return (
         output,
         token_grad,
         neighbour_grad,
         first_sum,
-        middle_sum[:, 2 * D : 3 * D],
-        middle_sum[:, 3 * D : 4 * D],
-        middle_sum[:, : 2 * D],
-        middle_sum[:, 4 * D :],
-        last_sum[:, FF:],
-        jnp.concatenate(jnp.split(last_sum[:, :FF], FF // D, 1), 0),
+        out_sum,
+        cq_sum,
+        kv_sum,
+        co_sum,
+        up_sum,
+        down_sum,
         small_sum[:, :8].T,
         small_sum[:, 14:SMALL].reshape(-1),
         small_sum[:, 8:11].T,

time: 497 us -> 425 us (0.86)
  Pallas kernels: 208 us -> 276 us
  waiting for transfers between devices: 95.2 us -> 38.5 us
  other arithmetic: 49.4 us -> 7.27 us
  matrix products: 37.9 us -> 0 us
  starting transfers between devices: 68.7 us -> 59.6 us
  local copies, waits for them, and re-layouts: 29.9 us -> 35.7 us
    pallas_call x12 -> x31, Pallas kernels: 164 us -> 256 us  [call(): pl.pallas_call(kernel, out_shape=outs, grid_spec=pltpu.PrefetchScalarGrid...]
    ppermute x66 -> x61, waiting for transfers between devices: 95.2 us -> 38.5 us  [shift(): return lax.ppermute(values, 'fsdp', shift_pairs(sizes, axis, step))]
    dot_general x7 -> x0, matrix products: 37.9 us -> none  [dot_tn(): lax.dot_general(a, b, (((0,), (0,)), ((), ())), preferred_element_type=f32)]
    convert_element_type x23 -> x0, other arithmetic: 34.3 us -> none  [the longest x9 17.6 us: part(): return plus(kept[index], got[index]).astype(kind)]
    pallas_call x4 -> x0, Pallas kernels: 23.7 us -> none  [spread(): pl.pallas_call(functools.partial(spread_kernel, sizes, split), out_shape=...]
    ppermute x66 -> x61, starting transfers between devices: 68.7 us -> 59.6 us  [shift(): return lax.ppermute(values, 'fsdp', shift_pairs(sizes, axis, step))]
    unnamed x95 -> x98, local copies, waits for them, and re-layouts: 11.9 us -> 17.8 us
  transfers between devices with their start and end apart: 66 -> 61, of which waited for: 24 -> 18; matrix products, arithmetic and copies ran while one was open for 10% -> 6% of each run, Pallas kernels for 25% -> 47%
where the time goes in v3:
time: 425 us; the launch traced here: 418 us
  Pallas kernels  276 us (65%)
  starting transfers between devices  59.6 us (14%)
  waiting for transfers between devices  38.5 us (9%)
  local copies, waits for them, and re-layouts  35.7 us (8%)
  other arithmetic  7.27 us (2%)
    pallas_call x31, Pallas kernels, call(): pl.pallas_call(kernel, out_shape=outs, grid_spec=pltpu.PrefetchScalarGrid...  256 us
    ppermute x61, starting transfers between devices, shift(): return lax.ppermute(values, 'fsdp', shift_pairs(sizes, axis, step))  59.6 us
    ppermute x61, waiting for transfers between devices, shift(): return lax.ppermute(values, 'fsdp', shift_pairs(sizes, axis, step))  38.5 us
    pallas_call x3, Pallas kernels, place(): pl.pallas_call(functools.partial(place_kernel, keys, counts, sizes, split...  20.1 us
    unnamed x98, local copies, waits for them, and re-layouts  17.8 us
  transfers between devices with their start and end apart: 61, of which 18 were waited for; matrix products, arithmetic and copies ran while one was open for 6% of the time, Pallas kernels for 47%

profile of v3, /device:TPU:0, one launch (start us, length us, event | category | flops | bytes accessed | tf_op | source)
XLA Modules:
  0.0 418.3 jit_solution(15036467933877263775)
XLA Ops:
  4.8 4.1 collective-permute-start.1
  10.5 2.2 collective-permute-start.2
  23.1 2.0 collective-permute-start.5
  26.7 1.9 collective-permute-start.3
  37.8 4.9 %collective-permute-done.4 = bf16[24,3840]{1,0:T(8,128)(2,1)S(1)} collective-permute-done((bf16[24,3840]{1,0:T(8,128)(2,1)S(1)}, bf16[24,3840]{1,0:T(8,128)(2,1)S(1)}, u32[]{:S(2)}, u32[]{:S(2)}) %collective-permute-start.4) | collective-permute-done | bytes 184352 | tf_op jit(solution)/shard_map/ppermute | solution.py:94
  49.8 5.4 %place.3 = bf16[4,8,24,2432]{3,2,1,0:T(8,128)(2,1)} custom-call(s32[4]{0:T(128)} %pad_add_fusion.me_ref, bf16[4,24,2432]{2,1,0:T(8,128)(2,1)} %copy-done.3, bf16[4,24,2432]{2,1,0:T(8,128)(2,1)} %collective-permute-done.6.refs_1_, bf16[4,24,2432]{2,1,0:T(8,128)(2,1)} %copy-done.5, bf16[4,24,1216]{2,1,0:T(8,128)(2,1)} %copy-done.30, ...), custom_call_target="tpu_custom_call" | custom-call | flops 6000000000 | tf_op jit(solution)/shard_map/place/pallas_call | solution.py:176
  56.9 11.6 %qkv_project.1 = (bf16[1024,768]{1,0:T(8,128)(2,1)}, bf16[1024,2304]{1,0:T(8,128)(2,1)}) custom-call(bf16[1024,768]{1,0:T(8,128)(2,1)} %x_ref.4, bf16[768,2432]{1,0:T(8,128)(2,1)} %bitcast.54, f32[16,768]{1,0:T(8,128)} %convert_bitcast_fusion.vec_ref, f32[2,512,128]{2,1,0:T(8,128)} %stack.88.cos_ref, f32[2,512,128]{2,1,0:T(8,128)} %stack.90.sin_ref), custom_call_target="tpu_custom_call" | custom-call | flops 11000000512 | tf_op jit(solution)/shard_map/qkv_project/pallas_call | solution.py:468
  68.5 2.9 collective-permute-done.18
  76.6 12.7 %self_attend.1 = (bf16[1024,768]{1,0:T(8,128)(2,1)}, f32[1024,768]{1,0:T(8,128)}) custom-call(s32[2,4]{1,0:T(2,128)} %lengths_ref.5, bf16[1024,2304]{1,0:T(8,128)(2,1)} %get-tuple-element.171.q_ref.k_ref.v_ref, bf16[1024,2304]{1,0:T(8,128)(2,1)} %get-tuple-element.171.q_ref.k_ref.v_ref, bf16[1024,2304]{1,0:T(8,128)(2,1)} %get-tuple-element.171.q_ref.k_ref.v_ref), custom_call_target="tpu_custom_call" | custom-call | flops 12000000000 | tf_op jit(solution)/shard_map/self_attend/pallas_call | solution.py:468
  92.1 6.4 %place.4 = bf16[4,8,24,3840]{3,2,1,0:T(8,128)(2,1)} custom-call(s32[4]{0:T(128)} %pad_add_fusion.me_ref, bf16[4,24,3840]{2,1,0:T(8,128)(2,1)} %copy-done.2, bf16[4,24,3840]{2,1,0:T(8,128)(2,1)} %collective-permute-done.15.refs_1_, bf16[4,24,3840]{2,1,0:T(8,128)(2,1)} %collective-permute-done.16.refs_2_, ...), custom_call_target="tpu_custom_call" | custom-call | flops 6000000000 | tf_op jit(solution)/shard_map/place/pallas_call | solution.py:176
  98.5 6.4 %ckv_project.1.k_ref.v_ref = bf16[1024,1536]{1,0:T(8,128)(2,1)} custom-call(bf16[1024,768]{1,0:T(8,128)(2,1)} %left_ref, bf16[768,3840]{1,0:T(8,128)(2,1)} %bitcast.60, f32[16,768]{1,0:T(8,128)} %convert_bitcast_fusion.vec_ref), custom_call_target="tpu_custom_call" | custom-call | flops 6000000000 | tf_op jit(solution)/shard_map/ckv_project/pallas_call | solution.py:468
  104.9 8.0 %mid_forward.1 = (f32[1024,768]{1,0:T(8,128)}, bf16[1024,768]{1,0:T(8,128)(2,1)}, bf16[1024,768]{1,0:T(8,128)(2,1)}) custom-call(bf16[1024,768]{1,0:T(8,128)(2,1)} %get-tuple-element.172.o_ref.left_ref, bf16[1024,768]{1,0:T(8,128)(2,1)} %x_ref.4, bf16[768,3840]{1,0:T(8,128)(2,1)} %bitcast.61, bf16[768,3840]{1,0:T(8,128)(2,1)} %bitcast.62, ...), custom_call_target="tpu_custom_call" | custom-call | flops 8000000000 | tf_op jit(solution)/shard_map/mid_forward/pallas_call | solution.py:468
  112.9 5.5 %collective-permute-done.28.refs_2_ = bf16[4,24,6144]{2,1,0:T(8,128)(2,1)S(1)} collective-permute-done((bf16[4,24,6144]{2,1,0:T(8,128)(2,1)S(1)}, bf16[4,24,6144]{2,1,0:T(8,128)(2,1)S(1)}, u32[]{:S(2)}, u32[]{:S(2)}) %collective-permute-start.28) | collective-permute-done | bytes 1179680 | tf_op jit(solution)/shard_map/ppermute | solution.py:94
  124.2 8.1 %cross_attend.1.co_ref.left_ref = bf16[1024,768]{1,0:T(8,128)(2,1)} custom-call(s32[2,16]{1,0:T(2,128)} %reshape.84.chosen_ref, bf16[1024,768]{1,0:T(8,128)(2,1)} %get-tuple-element.183.q_ref, bf16[1024,1536]{1,0:T(8,128)(2,1)} %ckv_project.1.k_ref.v_ref, bf16[1024,1536]{1,0:T(8,128)(2,1)} %ckv_project.1.k_ref.v_ref), custom_call_target="tpu_custom_call" | custom-call | flops 8000000000 | tf_op jit(solution)/shard_map/cross_attend/pallas_call | solution.py:468
  132.2 4.7 %collective-permute-done.30.refs_4_ = bf16[4,24,3072]{2,1,0:T(8,128)(2,1)} collective-permute-done((bf16[4,24,3072]{2,1,0:T(8,128)(2,1)S(1)}, bf16[4,24,3072]{2,1,0:T(8,128)(2,1)}, u32[]{:S(2)}, u32[]{:S(2)}) %collective-permute-start.30) | collective-permute-done | bytes 589856 | tf_op jit(solution)/shard_map/ppermute | solution.py:94
  141.8 8.2 %place.5 = (bf16[4,8,96,768]{3,2,1,0:T(8,128)(2,1)}, bf16[4,8,24,3072]{3,2,1,0:T(8,128)(2,1)}) custom-call(s32[4]{0:T(128)} %pad_add_fusion.me_ref, bf16[4,24,6144]{2,1,0:T(8,128)(2,1)} %copy-done, bf16[4,24,6144]{2,1,0:T(8,128)(2,1)} %collective-permute-done.27.refs_1_, bf16[4,24,6144]{2,1,0:T(8,128)(2,1)} %copy-done.4, ...), custom_call_target="tpu_custom_call" | custom-call | flops 6000000000 | tf_op jit(solution)/shard_map/place/pallas_call | solution.py:176
  150.0 39.0 %mlp_both.1 = (bf16[1024,768]{1,0:T(8,128)(2,1)}, bf16[1024,3072]{1,0:T(8,128)(2,1)}, bf16[1024,3072]{1,0:T(8,128)(2,1)}, bf16[1024,768]{1,0:T(8,128)(2,1)}, f32...) custom-call(f32[1024,768]{1,0:T(8,128)} %get-tuple-element.178.h1_re, ...), custom_call_target="tpu_custom_call" | custom-call | flops 38999998464 | tf_op jit(solution)/shard_map/mlp_both/pallas_call | solution.py:468
  189.1 10.1 %grad_blocks.7 = (bf16[4,2,2,24,6144]{4,3,2,1,0:T(8,128)(2,1)}, bf16[4,2,2,24,6144]{4,3,2,1,0:T(8,128)(2,1)}) custom-call(s32[4]{0:T(128)} %pad_add_fusion.me_ref, bf16[1024,3072]{1,0:T(8,128)(2,1)} %get-tuple-element.195.left_ref, bf16[1024,768]{1,0:T(8,128)(2,1)} %right_ref.1), custom_call_target="tpu_custom_call" | custom-call | flops 6000000000 | tf_op jit(solution)/shard_map/grad_blocks/pallas_call | solution.py:468
  199.1 10.1 %grad_blocks.8 = (bf16[4,2,2,24,6144]{4,3,2,1,0:T(8,128)(2,1)}, bf16[4,2,2,24,6144]{4,3,2,1,0:T(8,128)(2,1)}) custom-call(s32[4]{0:T(128)} %pad_add_fusion.me_ref, bf16[1024,768]{1,0:T(8,128)(2,1)} %get-tuple-element.193.left_ref, bf16[1024,3072]{1,0:T(8,128)(2,1)} %get-tuple-element.194.right_ref, ...), custom_call_target="tpu_custom_call", output_to_operand_aliasing={{0}: (3, {}), {1}: (4, {})} | custom-call | flops 6000000000 | tf_op jit(solution)/shard_map/grad_blocks/pallas_call | solution.py:468
  209.3 20.6 %cross_back.1 = (bf16[1024,768]{1,0:T(8,128)(2,1)}, bf16[1024,1536]{1,0:T(8,128)(2,1)}, f32[16,768]{1,0:T(8,128)}) custom-call(s32[2,16]{1,0:T(2,128)} %reshape.84.chosen_ref, bf16[1024,768]{1,0:T(8,128)(2,1)} %get-tuple-element.183.q_ref, bf16[1024,1536]{1,0:T(8,128)(2,1)} %ckv_project.1.k_ref.v_ref, bf16[1024,1536]{1,0:T(8,128)(2,1)} %ckv_project.1.k_ref.v_ref, ...), custom_call_target="tpu_custom_call" | custom-call | flops 20000000000 | tf_op jit(solution)/shard_map/cross_back/pallas_call | solution.py:468
  230.0 7.0 %fold_core.3 = (bf16[4,2,24,3072]{3,2,1,0:T(8,128)(2,1)}, bf16[4,2,24,3072]{3,2,1,0:T(8,128)(2,1)}, bf16[4,2,24,3072]{3,2,1,0:T(8,128)(2,1)}, bf16[4,2,24,3072]{3,2,1,0:T(8,128)(2,1)}) custom-call(s32[4]{0:T(128)} %pad_add_fusion.me_ref, bf16[4,2,2,24,6144]{4,3,2,1,0:T(8,128)(2,1)} %get-tuple-element.201.refs_0_, ...), custom_call_target="tpu_custom_call" | custom-call | flops 5000000000 | tf_op jit(solution)/shard_map/fold_core/pallas_call | solution.py:468
  239.0 9.0 %mid_back.1 = (f32[1024,768]{1,0:T(8,128)}, bf16[1024,768]{1,0:T(8,128)(2,1)}, bf16[1024,768]{1,0:T(8,128)(2,1)}, f32[8,768]{1,0:T(8,128)}) custom-call(bf16[1024,768]{1,0:T(8,128)(2,1)} %get-tuple-element.207.dcq_ref.right_ref, f32[1024,768]{1,0:T(8,128)} %get-tuple-element.208.dh2_ref, f32[1024,768]{1,0:T(8,128)} %get-tuple-element.178.h1_ref, ...), custom_call_target="tpu_custom_call" | custom-call | flops 8999999488 | tf_op jit(solution)/shard_map/mid_back/pallas_call | solution.py:468
  248.0 6.7 %grad_blocks.9 = (bf16[4,2,2,24,3840]{4,3,2,1,0:T(8,128)(2,1)}, bf16[4,2,2,24,3840]{4,3,2,1,0:T(8,128)(2,1)}) custom-call(s32[4]{0:T(128)} %pad_add_fusion.me_ref, bf16[1024,768]{1,0:T(8,128)(2,1)} %left_ref, bf16[1024,1536]{1,0:T(8,128)(2,1)} %get-tuple-element.286.right_ref.dkv_ref), custom_call_target="tpu_custom_call" | custom-call | flops 6000000000 | tf_op jit(solution)/shard_map/grad_blocks/pallas_call | solution.py:468
  254.7 5.1 %grad_blocks.10 = (bf16[4,2,2,24,3840]{4,3,2,1,0:T(8,128)(2,1)}, bf16[4,2,2,24,3840]{4,3,2,1,0:T(8,128)(2,1)}) custom-call(s32[4]{0:T(128)} %pad_add_fusion.me_ref, bf16[1024,768]{1,0:T(8,128)(2,1)} %get-tuple-element.172.o_ref.left_ref, bf16[1024,768]{1,0:T(8,128)(2,1)} %get-tuple-element.212.right_ref, ...), custom_call_target="tpu_custom_call", output_to_operand_aliasing={{0}: (3, {}), {1}: (4, {})} | custom-call | flops 6000000000 | tf_op jit(solution)/shard_map/grad_blocks/pallas_call | solution.py:468
  259.8 5.1 %grad_blocks.11 = (bf16[4,2,2,24,3840]{4,3,2,1,0:T(8,128)(2,1)}, bf16[4,2,2,24,3840]{4,3,2,1,0:T(8,128)(2,1)}) custom-call(s32[4]{0:T(128)} %pad_add_fusion.me_ref, bf16[1024,768]{1,0:T(8,128)(2,1)} %get-tuple-element.211.left_ref, bf16[1024,768]{1,0:T(8,128)(2,1)} %get-tuple-element.207.dcq_ref.right_ref, ...), custom_call_target="tpu_custom_call", output_to_operand_aliasing={{0}: (3, {}), {1}: (4, {})} | custom-call | flops 6000000000 | tf_op jit(solution)/shard_map/grad_blocks/pallas_call | solution.py:468
  264.9 5.2 %grad_blocks.12 = (bf16[4,2,2,24,3840]{4,3,2,1,0:T(8,128)(2,1)}, bf16[4,2,2,24,3840]{4,3,2,1,0:T(8,128)(2,1)}) custom-call(s32[4]{0:T(128)} %pad_add_fusion.me_ref, bf16[1024,768]{1,0:T(8,128)(2,1)} %cross_attend.1.co_ref.left_ref, bf16[1024,768]{1,0:T(8,128)(2,1)} %get-tuple-element.210.right_ref, ...), custom_call_target="tpu_custom_call", output_to_operand_aliasing={{0}: (3, {}), {1}: (4, {})} | custom-call | flops 6000000000 | tf_op jit(solution)/shard_map/grad_blocks/pallas_call | solution.py:468
  272.7 4.3 %fold_side.3 = (bf16[4,24,3072]{2,1,0:T(8,128)(2,1)}, bf16[4,24,3072]{2,1,0:T(8,128)(2,1)}, bf16[4,24,3072]{2,1,0:T(8,128)(2,1)}, bf16[4,24,3072]{2,1,0:T(8,128)(2,1)}) custom-call(bf16[4,2,24,3072]{3,2,1,0:T(8,128)(2,1)} %get-tuple-element.222.refs_0_, bf16[4,2,24,3072]{3,2,1,0:T(8,128)(2,1)} %collective-permute-done.37.refs_1_, ...), custom_call_target="tpu_custom_call" | custom-call | flops 4000000000 | tf_op jit(solution)/shard_map/fold_side/pallas_call | solution.py:468
  279.0 15.3 %self_back.2.rest_0_ = bf16[1024,2304]{1,0:T(8,128)(2,1)} custom-call(s32[2,4]{1,0:T(2,128)} %lengths_ref.5, bf16[1024,2304]{1,0:T(8,128)(2,1)} %get-tuple-element.171.q_ref.k_ref.v_ref, bf16[1024,2304]{1,0:T(8,128)(2,1)} %get-tuple-element.171.q_ref.k_ref.v_ref, bf16[1024,2304]{1,0:T(8,128)(2,1)} %get-tuple-element.171.q_ref.k_ref.v_ref, ...), custom_call_target="tpu_custom_call" | custom-call | flops 15000000512 | tf_op jit(solution)/shard_map/self_back/pallas_call | solution.py:468
  294.3 2.7 fold_corner.3
  298.8 2.9 collective-permute-start.48
  303.4 5.6 %fold_core.4 = (bf16[4,2,24,1920]{3,2,1,0:T(8,128)(2,1)}, bf16[4,2,24,1920]{3,2,1,0:T(8,128)(2,1)}, bf16[4,2,24,1920]{3,2,1,0:T(8,128)(2,1)}, bf16[4,2,24,1920]{3,2,1,0:T(8,128)(2,1)}) custom-call(s32[4]{0:T(128)} %pad_add_fusion.me_ref, bf16[4,2,2,24,3840]{4,3,2,1,0:T(8,128)(2,1)} %get-tuple-element.240.refs_0_, bf16[4,2,2,24,3840]{4,3,2,1,0:T(8,128)(2,1)} %copy-done.14), custom_call_target="tpu_custom_call" | custom-call | flops 5000000000 | tf_op jit(solution)/shard_map/fold_core/pallas_call | solution.py:468
  310.2 15.3 %self_back.3.right_ref.dqkv_ref = bf16[1024,2304]{1,0:T(8,128)(2,1)} custom-call(s32[2,4]{1,0:T(2,128)} %lengths_ref.5, bf16[1024,2304]{1,0:T(8,128)(2,1)} %get-tuple-element.171.q_ref.k_ref.v_ref, bf16[1024,2304]{1,0:T(8,128)(2,1)} %get-tuple-element.171.q_ref.k_ref.v_ref, ...), custom_call_target="tpu_custom_call", output_to_operand_aliasing={{}: (8, {})} | custom-call | flops 15000000512 | tf_op jit(solution)/shard_map/self_back/pallas_call | solution.py:468
  328.4 3.9 fold_side.4
  334.0 8.4 %grad_blocks.13 = (bf16[4,2,2,24,2304]{4,3,2,1,0:T(8,128)(2,1)}, bf16[4,2,2,24,2304]{4,3,2,1,0:T(8,128)(2,1)}) custom-call(s32[4]{0:T(128)} %pad_add_fusion.me_ref, bf16[1024,768]{1,0:T(8,128)(2,1)} %get-tuple-element.256.left_ref, bf16[1024,2304]{1,0:T(8,128)(2,1)} %self_back.3.right_ref.dqkv_ref), custom_call_target="tpu_custom_call" | custom-call | flops 6000000000 | tf_op jit(solution)/shard_map/grad_blocks/pallas_call | solution.py:468
  343.2 2.1 fold_z.3
  346.1 2.2 fold_corner.4
  348.4 10.2 %token_back.1 = (f32[1024,768]{1,0:T(8,128)}, f32[8,768]{1,0:T(8,128)}, f32[1,2304]{1,0:T(1,128)}) custom-call(bf16[1024,2304]{1,0:T(8,128)(2,1)} %self_back.3.right_ref.dqkv_ref, f32[1024,768]{1,0:T(8,128)} %get-tuple-element.272.dh1_ref, bf16[1024,768]{1,0:T(8,128)(2,1)} %x_ref.4, bf16[768,2432]{1,0:T(8,128)(2,1)} %bitcast.56, ...), custom_call_target="tpu_custom_call" | custom-call | flops 10000000000 | tf_op jit(solution)/shard_map/token_back/pallas_call | solution.py:468
  362.1 2.8 collective-permute-start.57
  368.0 4.8 %fold_core.5 = (bf16[4,2,24,1152]{3,2,1,0:T(8,128)(2,1)}, bf16[4,2,24,1152]{3,2,1,0:T(8,128)(2,1)}, bf16[4,2,24,1280]{3,2,1,0:T(8,128)(2,1)}, bf16[4,2,24,1280]{3,2,1,0:T(8,128)(2,1)}) custom-call(s32[4]{0:T(128)} %pad_add_fusion.me_ref, bf16[4,2,2,24,2304]{4,3,2,1,0:T(8,128)(2,1)} %get-tuple-element.274.refs_0_, bf16[4,2,2,24,2304]{4,3,2,1,0:T(8,128)(2,1)} %copy-done.15, ...), custom_call_target="tpu_custom_call" | custom-call | flops 5000000000 | tf_op jit(solution)/shard_map/fold_core/pallas_call | solution.py:468
  375.1 6.7 %neighbour_back.1 = f32[1024,768]{1,0:T(8,128)} custom-call(bf16[1024,1536]{1,0:T(8,128)(2,1)} %get-tuple-element.286.right_ref.dkv_ref, bf16[768,3840]{1,0:T(8,128)(2,1)} %bitcast.66), custom_call_target="tpu_custom_call" | custom-call | flops 6000000000 | tf_op jit(solution)/shard_map/neighbour_back/pallas_call | solution.py:468
  381.9 2.8 collective-permute-done.51.refs_1_
  387.4 3.5 fold_side.5
  394.1 2.0 fold_z.4
  396.0 2.0 collective-permute-done.53.refs_1_
  398.8 2.1 fold_corner.5
  402.2 2.9 collective-permute-start.60
  405.2 2.9 collective-permute-done.58.refs_1_
  408.1 2.7 collective-permute-done.59.refs_2_
  (252 shorter events, 95.5 us)
Async XLA Ops:
  4.8 13.2 %collective-permute-start.1 = (bf16[24,2432]{1,0:T(8,128)(2,1)S(1)}, bf16[24,2432]{1,0:T(8,128)(2,1)S(1)}, u32[]{:S(2)}, u32[]{:S(2)}) collective-permute-start(bf16[24,2432]{1,0:T(8,128)(2,1)S(1)} %get-tuple-element.359), channel_id=1, source_target_pairs={{0,16},{1,17},{2,18},{3,19},{4,20},{5,21},{6,22},{7,23},{8,24},{9,... | collective-permute-start | bytes 350216 | tf_op jit(solution)/shard_map/ppermute | solution.py:94
  8.9 9.1 %collective-permute-start = (bf16[24,2432]{1,0:T(8,128)(2,1)S(1)}, bf16[24,2432]{1,0:T(8,128)(2,1)S(1)}, u32[]{:S(2)}, u32[]{:S(2)}) collective-permute-start(bf16[24,2432]{1,0:T(8,128)(2,1)S(1)} %get-tuple-element.359), channel_id=1, source_target_pairs={{0,8},{1,9},{2,10},{3,11},{4,12},{5,13},{6,14},{7,15},{8,16},{9,17... | collective-permute-start | bytes 350216 | tf_op jit(solution)/shard_map/ppermute | solution.py:94
  10.5 8.2 %collective-permute-start.2 = (bf16[24,2432]{1,0:T(8,128)(2,1)S(1)}, bf16[24,2432]{1,0:T(8,128)(2,1)S(1)}, u32[]{:S(2)}, u32[]{:S(2)}) collective-permute-start(bf16[24,2432]{1,0:T(8,128)(2,1)S(1)} %get-tuple-element.359), channel_id=1, source_target_pairs={{0,24},{1,25},{2,26},{3,27},{4,28},{5,29},{6,30},{7,31},{8,0},{9,1... | collective-permute-start | bytes 350216 | tf_op jit(solution)/shard_map/ppermute | solution.py:94
  18.8 11.5 %collective-permute-start.8 = (bf16[4,24,2432]{2,1,0:T(8,128)(2,1)S(1)}, bf16[4,24,2432]{2,1,0:T(8,128)(2,1)S(1)}, u32[]{:S(2)}, u32[]{:S(2)}) collective-permute-start(bf16[4,24,2432]{2,1,0:T(8,128)(2,1)S(1)} %pad_maximum_fusion.2.refs_0_), channel_id=1, source_target_pairs={{0,4},{1,5},{2,6},{3,7},{4,0},{5,1},{6,2},{7,3},{8,12},{9,13},{10,... | collective-permute-start | bytes 1400840 | tf_op jit(solution)/shard_map/ppermute | solution.py:94
  20.4 11.3 %collective-permute-start.6 = (bf16[4,24,2432]{2,1,0:T(8,128)(2,1)S(1)}, bf16[4,24,2432]{2,1,0:T(8,128)(2,1)}, u32[]{:S(2)}, u32[]{:S(2)}) collective-permute-start(bf16[4,24,2432]{2,1,0:T(8,128)(2,1)S(1)} %pad_maximum_fusion.2.refs_0_), channel_id=1, source_target_pairs={{0,2},{1,3},{2,0},{3,1},{4,6},{5,7},{6,4},{7,5},{8,10},{9,11},{10,... | collective-permute-start | bytes 1400840 | tf_op jit(solution)/shard_map/ppermute | solution.py:94
  23.1 14.8 %collective-permute-start.5 = (bf16[24,3840]{1,0:T(8,128)(2,1)S(1)}, bf16[24,3840]{1,0:T(8,128)(2,1)S(1)}, u32[]{:S(2)}, u32[]{:S(2)}) collective-permute-start(bf16[24,3840]{1,0:T(8,128)(2,1)S(1)} %pad_maximum_fusion.5), channel_id=1, source_target_pairs={{0,24},{1,25},{2,26},{3,27},{4,28},{5,29},{6,30},{7,31},{8,0},{9,1... | collective-permute-start | bytes 552968 | tf_op jit(solution)/shard_map/ppermute | solution.py:94
  25.1 17.6 %collective-permute-start.4 = (bf16[24,3840]{1,0:T(8,128)(2,1)S(1)}, bf16[24,3840]{1,0:T(8,128)(2,1)S(1)}, u32[]{:S(2)}, u32[]{:S(2)}) collective-permute-start(bf16[24,3840]{1,0:T(8,128)(2,1)S(1)} %pad_maximum_fusion.5), channel_id=1, source_target_pairs={{0,16},{1,17},{2,18},{3,19},{4,20},{5,21},{6,22},{7,23},{8,24},{9,... | collective-permute-start | bytes 552968 | tf_op jit(solution)/shard_map/ppermute | solution.py:94
  26.7 16.0 %collective-permute-start.3 = (bf16[24,3840]{1,0:T(8,128)(2,1)S(1)}, bf16[24,3840]{1,0:T(8,128)(2,1)S(1)}, u32[]{:S(2)}, u32[]{:S(2)}) collective-permute-start(bf16[24,3840]{1,0:T(8,128)(2,1)S(1)} %pad_maximum_fusion.5), channel_id=1, source_target_pairs={{0,8},{1,9},{2,10},{3,11},{4,12},{5,13},{6,14},{7,15},{8,16},{9,17... | collective-permute-start | bytes 552968 | tf_op jit(solution)/shard_map/ppermute | solution.py:94
  30.4 12.9 %collective-permute-start.9 = (bf16[4,24,1216]{2,1,0:T(8,128)(2,1)S(1)}, bf16[4,24,1216]{2,1,0:T(8,128)(2,1)S(1)}, u32[]{:S(2)}, u32[]{:S(2)}) collective-permute-start(bf16[4,24,1216]{2,1,0:T(8,128)(2,1)S(1)} %slice.92), channel_id=1, source_target_pairs={{0,2},{1,3},{2,0},{3,1},{4,6},{5,7},{6,4},{7,5},{8,10},{9,11},{10,... | collective-permute-start | bytes 700424 | tf_op jit(solution)/shard_map/ppermute | solution.py:94
  32.7 10.6 %collective-permute-start.7 = (bf16[4,24,1216]{2,1,0:T(8,128)(2,1)S(1)}, bf16[4,24,1216]{2,1,0:T(8,128)(2,1)S(1)}, u32[]{:S(2)}, u32[]{:S(2)}) collective-permute-start(bf16[4,24,1216]{2,1,0:T(8,128)(2,1)S(1)} %slice.91), channel_id=1, source_target_pairs={{0,4},{1,5},{2,6},{3,7},{4,0},{5,1},{6,2},{7,3},{8,12},{9,13},{10,... | collective-permute-start | bytes 700424 | tf_op jit(solution)/shard_map/ppermute | solution.py:94
  43.9 24.5 %collective-permute-start.19 = (bf16[24,6144]{1,0:T(8,128)(2,1)S(1)}, bf16[24,6144]{1,0:T(8,128)(2,1)S(1)}, u32[]{:S(2)}, u32[]{:S(2)}) collective-permute-start(bf16[24,6144]{1,0:T(8,128)(2,1)S(1)} %constant_dynamic-update-slice_fusion), channel_id=1, source_target_pairs={{0,24},{1,25},{2,26},{3,27},{4,28},{5,29},{6,30},{7,31},{8,0},{9,1... | collective-permute-start | bytes 884744 | tf_op jit(solution)/shard_map/ppermute | solution.py:94
  44.6 26.9 %collective-permute-start.18 = (bf16[24,6144]{1,0:T(8,128)(2,1)S(1)}, bf16[24,6144]{1,0:T(8,128)(2,1)S(1)}, u32[]{:S(2)}, u32[]{:S(2)}) collective-permute-start(bf16[24,6144]{1,0:T(8,128)(2,1)S(1)} %constant_dynamic-update-slice_fusion), channel_id=1, source_target_pairs={{0,16},{1,17},{2,18},{3,19},{4,20},{5,21},{6,22},{7,23},{8,24},{9,... | collective-permute-start | bytes 884744 | tf_op jit(solution)/shard_map/ppermute | solution.py:94
  45.3 26.1 %collective-permute-start.17 = (bf16[24,6144]{1,0:T(8,128)(2,1)S(1)}, bf16[24,6144]{1,0:T(8,128)(2,1)S(1)}, u32[]{:S(2)}, u32[]{:S(2)}) collective-permute-start(bf16[24,6144]{1,0:T(8,128)(2,1)S(1)} %constant_dynamic-update-slice_fusion), channel_id=1, source_target_pairs={{0,8},{1,9},{2,10},{3,11},{4,12},{5,13},{6,14},{7,15},{8,16},{9,17... | collective-permute-start | bytes 884744 | tf_op jit(solution)/shard_map/ppermute | solution.py:94
  47.0 24.6 %collective-permute-start.16 = (bf16[4,24,3840]{2,1,0:T(8,128)(2,1)S(1)}, bf16[4,24,3840]{2,1,0:T(8,128)(2,1)}, u32[]{:S(2)}, u32[]{:S(2)}) collective-permute-start(bf16[4,24,3840]{2,1,0:T(8,128)(2,1)S(1)} %pad_maximum_fusion.1.refs_0_), channel_id=1, source_target_pairs={{0,4},{1,5},{2,6},{3,7},{4,0},{5,1},{6,2},{7,3},{8,12},{9,13},{10,... | collective-permute-start | bytes 2211848 | tf_op jit(solution)/shard_map/ppermute | solution.py:94
  49.3 22.4 %collective-permute-start.15 = (bf16[4,24,3840]{2,1,0:T(8,128)(2,1)S(1)}, bf16[4,24,3840]{2,1,0:T(8,128)(2,1)}, u32[]{:S(2)}, u32[]{:S(2)}) collective-permute-start(bf16[4,24,3840]{2,1,0:T(8,128)(2,1)S(1)} %pad_maximum_fusion.1.refs_0_), channel_id=1, source_target_pairs={{0,2},{1,3},{2,0},{3,1},{4,6},{5,7},{6,4},{7,5},{8,10},{9,11},{10,... | collective-permute-start | bytes 2211848 | tf_op jit(solution)/shard_map/ppermute | solution.py:94
  68.4 20.9 %collective-permute-start.22 = (bf16[4,24,3840]{2,1,0:T(8,128)(2,1)S(1)}, bf16[4,24,3840]{2,1,0:T(8,128)(2,1)}, u32[]{:S(2)}, u32[]{:S(2)}) collective-permute-start(bf16[4,24,3840]{2,1,0:T(8,128)(2,1)S(1)} %pad_maximum_fusion.1.refs_0_), channel_id=1, source_target_pairs={{0,1},{1,0},{2,3},{3,2},{4,5},{5,4},{6,7},{7,6},{8,9},{9,8},{10,11... | collective-permute-start | bytes 2211848 | tf_op jit(solution)/shard_map/ppermute | solution.py:94
  72.9 16.5 %collective-permute-start.23 = (bf16[4,24,3840]{2,1,0:T(8,128)(2,1)}, bf16[4,24,3840]{2,1,0:T(8,128)(2,1)S(1)}, u32[]{:S(2)}, u32[]{:S(2)}) collective-permute-start(bf16[4,24,3840]{2,1,0:T(8,128)(2,1)} %collective-permute-done.15.refs_1_), channel_id=1, source_target_pairs={{0,1},{1,0},{2,3},{3,2},{4,5},{5,4},{6,7},{7,6},{8,9},{9,8},{10,11... | collective-permute-start | bytes 2211848 | tf_op jit(solution)/shard_map/ppermute | solution.py:94
  74.0 15.4 %collective-permute-start.24 = (bf16[4,24,3840]{2,1,0:T(8,128)(2,1)}, bf16[4,24,3840]{2,1,0:T(8,128)(2,1)}, u32[]{:S(2)}, u32[]{:S(2)}) collective-permute-start(bf16[4,24,3840]{2,1,0:T(8,128)(2,1)} %collective-permute-done.16.refs_2_), channel_id=1, source_target_pairs={{0,1},{1,0},{2,3},{3,2},{4,5},{5,4},{6,7},{7,6},{8,9},{9,8},{10,11... | collective-permute-start | bytes 2211848 | tf_op jit(solution)/shard_map/ppermute | solution.py:94
  74.6 14.8 %collective-permute-start.21 = (bf16[4,24,1920]{2,1,0:T(8,128)(2,1)S(1)}, bf16[4,24,1920]{2,1,0:T(8,128)(2,1)}, u32[]{:S(2)}, u32[]{:S(2)}) collective-permute-start(bf16[4,24,1920]{2,1,0:T(8,128)(2,1)S(1)} %slice.73), channel_id=1, source_target_pairs={{0,2},{1,3},{2,0},{3,1},{4,6},{5,7},{6,4},{7,5},{8,10},{9,11},{10,... | collective-permute-start | bytes 1105928 | tf_op jit(solution)/shard_map/ppermute | solution.py:94
  75.6 13.8 %collective-permute-start.20 = (bf16[4,24,1920]{2,1,0:T(8,128)(2,1)S(1)}, bf16[4,24,1920]{2,1,0:T(8,128)(2,1)}, u32[]{:S(2)}, u32[]{:S(2)}) collective-permute-start(bf16[4,24,1920]{2,1,0:T(8,128)(2,1)S(1)} %slice.72), channel_id=1, source_target_pairs={{0,4},{1,5},{2,6},{3,7},{4,0},{5,1},{6,2},{7,3},{8,12},{9,13},{10,... | collective-permute-start | bytes 1105928 | tf_op jit(solution)/shard_map/ppermute | solution.py:94
  90.0 42.3 %collective-permute-start.31 = (bf16[4,24,6144]{2,1,0:T(8,128)(2,1)S(1)}, bf16[4,24,6144]{2,1,0:T(8,128)(2,1)}, u32[]{:S(2)}, u32[]{:S(2)}) collective-permute-start(bf16[4,24,6144]{2,1,0:T(8,128)(2,1)S(1)} %pad_maximum_fusion.refs_0_), channel_id=1, source_target_pairs={{0,1},{1,0},{2,3},{3,2},{4,5},{5,4},{6,7},{7,6},{8,9},{9,8},{10,11... | collective-permute-start | bytes 3538952 | tf_op jit(solution)/shard_map/ppermute | solution.py:94
  90.1 28.3 %collective-permute-start.28 = (bf16[4,24,6144]{2,1,0:T(8,128)(2,1)S(1)}, bf16[4,24,6144]{2,1,0:T(8,128)(2,1)S(1)}, u32[]{:S(2)}, u32[]{:S(2)}) collective-permute-start(bf16[4,24,6144]{2,1,0:T(8,128)(2,1)S(1)} %pad_maximum_fusion.refs_0_), channel_id=1, source_target_pairs={{0,4},{1,5},{2,6},{3,7},{4,0},{5,1},{6,2},{7,3},{8,12},{9,13},{10,... | collective-permute-start | bytes 3538952 | tf_op jit(solution)/shard_map/ppermute | solution.py:94
  91.1 28.1 %collective-permute-start.27 = (bf16[4,24,6144]{2,1,0:T(8,128)(2,1)S(1)}, bf16[4,24,6144]{2,1,0:T(8,128)(2,1)}, u32[]{:S(2)}, u32[]{:S(2)}) collective-permute-start(bf16[4,24,6144]{2,1,0:T(8,128)(2,1)S(1)} %pad_maximum_fusion.refs_0_), channel_id=1, source_target_pairs={{0,2},{1,3},{2,0},{3,1},{4,6},{5,7},{6,4},{7,5},{8,10},{9,11},{10,... | collective-permute-start | bytes 3538952 | tf_op jit(solution)/shard_map/ppermute | solution.py:94
  119.2 18.5 %collective-permute-start.32 = (bf16[4,24,6144]{2,1,0:T(8,128)(2,1)}, bf16[4,24,6144]{2,1,0:T(8,128)(2,1)}, u32[]{:S(2)}, u32[]{:S(2)}) collective-permute-start(bf16[4,24,6144]{2,1,0:T(8,128)(2,1)} %collective-permute-done.27.refs_1_), channel_id=1, source_target_pairs={{0,1},{1,0},{2,3},{3,2},{4,5},{5,4},{6,7},{7,6},{8,9},{9,8},{10,11... | collective-permute-start | bytes 3538952 | tf_op jit(solution)/shard_map/ppermute | solution.py:94
  119.2 18.5 %collective-permute-start.33 = (bf16[4,24,6144]{2,1,0:T(8,128)(2,1)S(1)}, bf16[4,24,6144]{2,1,0:T(8,128)(2,1)}, u32[]{:S(2)}, u32[]{:S(2)}) collective-permute-start(bf16[4,24,6144]{2,1,0:T(8,128)(2,1)S(1)} %collective-permute-done.28.refs_2_), channel_id=1, source_target_pairs={{0,1},{1,0},{2,3},{3,2},{4,5},{5,4},{6,7},{7,6},{8,9},{9,8},{10,11... | collective-permute-start | bytes 3538952 | tf_op jit(solution)/shard_map/ppermute | solution.py:94
  121.6 15.4 %collective-permute-start.30 = (bf16[4,24,3072]{2,1,0:T(8,128)(2,1)S(1)}, bf16[4,24,3072]{2,1,0:T(8,128)(2,1)}, u32[]{:S(2)}, u32[]{:S(2)}) collective-permute-start(bf16[4,24,3072]{2,1,0:T(8,128)(2,1)S(1)} %slice.75), channel_id=1, source_target_pairs={{0,2},{1,3},{2,0},{3,1},{4,6},{5,7},{6,4},{7,5},{8,10},{9,11},{10,... | collective-permute-start | bytes 1769480 | tf_op jit(solution)/shard_map/ppermute | solution.py:94
  122.6 15.1 %collective-permute-start.29 = (bf16[4,24,3072]{2,1,0:T(8,128)(2,1)S(1)}, bf16[4,24,3072]{2,1,0:T(8,128)(2,1)}, u32[]{:S(2)}, u32[]{:S(2)}) collective-permute-start(bf16[4,24,3072]{2,1,0:T(8,128)(2,1)S(1)} %slice.74), channel_id=1, source_target_pairs={{0,4},{1,5},{2,6},{3,7},{4,0},{5,1},{6,2},{7,3},{8,12},{9,13},{10,... | collective-permute-start | bytes 1769480 | tf_op jit(solution)/shard_map/ppermute | solution.py:94
  209.2 20.7 %collective-permute-start.36 = (bf16[4,2,2,24,6144]{4,3,2,1,0:T(8,128)(2,1)}, bf16[4,2,2,24,6144]{4,3,2,1,0:T(8,128)(2,1)}, u32[]{:S(2)}, u32[]{:S(2)}) collective-permute-start(bf16[4,2,2,24,6144]{4,3,2,1,0:T(8,128)(2,1)} %get-tuple-element.198), channel_id=1, source_target_pairs={{0,1},{1,0},{2,3},{3,2},{4,5},{5,4},{6,7},{7,6},{8,9},{9,8},{10,11... | collective-permute-start | bytes 14155784 | tf_op jit(solution)/shard_map/ppermute | solution.py:94
  236.9 35.8 %collective-permute-start.37 = (bf16[4,2,24,3072]{3,2,1,0:T(8,128)(2,1)}, bf16[4,2,24,3072]{3,2,1,0:T(8,128)(2,1)}, u32[]{:S(2)}, u32[]{:S(2)}) collective-permute-start(bf16[4,2,24,3072]{3,2,1,0:T(8,128)(2,1)} %get-tuple-element.204), channel_id=1, source_target_pairs={{0,4},{1,5},{2,6},{3,7},{4,0},{5,1},{6,2},{7,3},{8,12},{9,13},{10,... | collective-permute-start | bytes 3538952 | tf_op jit(solution)/shard_map/ppermute | solution.py:94
  238.5 34.3 %collective-permute-start.38 = (bf16[4,2,24,3072]{3,2,1,0:T(8,128)(2,1)}, bf16[4,2,24,3072]{3,2,1,0:T(8,128)(2,1)}, u32[]{:S(2)}, u32[]{:S(2)}) collective-permute-start(bf16[4,2,24,3072]{3,2,1,0:T(8,128)(2,1)} %get-tuple-element.206), channel_id=1, source_target_pairs={{0,2},{1,3},{2,0},{3,1},{4,6},{5,7},{6,4},{7,5},{8,10},{9,11},{10,... | collective-permute-start | bytes 3538952 | tf_op jit(solution)/shard_map/ppermute | solution.py:94
  270.1 31.6 %collective-permute-start.41 = (bf16[4,2,2,24,3840]{4,3,2,1,0:T(8,128)(2,1)}, bf16[4,2,2,24,3840]{4,3,2,1,0:T(8,128)(2,1)S(1)}, u32[]{:S(2)}, u32[]{:S(2)}) collective-permute-start(bf16[4,2,2,24,3840]{4,3,2,1,0:T(8,128)(2,1)} %get-tuple-element.221), channel_id=1, source_target_pairs={{0,1},{1,0},{2,3},{3,2},{4,5},{5,4},{6,7},{7,6},{8,9},{9,8},{10,11... | collective-permute-start | bytes 8847368 | tf_op jit(solution)/shard_map/ppermute | solution.py:94
  277.1 17.3 %collective-permute-start.39 = (bf16[4,24,3072]{2,1,0:T(8,128)(2,1)}, bf16[4,24,3072]{2,1,0:T(8,128)(2,1)}, u32[]{:S(2)}, u32[]{:S(2)}) collective-permute-start(bf16[4,24,3072]{2,1,0:T(8,128)(2,1)} %get-tuple-element.227), channel_id=1, source_target_pairs={{0,2},{1,3},{2,0},{3,1},{4,6},{5,7},{6,4},{7,5},{8,10},{9,11},{10,... | collective-permute-start | bytes 1769480 | tf_op jit(solution)/shard_map/ppermute | solution.py:94
  278.5 15.8 %collective-permute-start.40 = (bf16[4,24,3072]{2,1,0:T(8,128)(2,1)}, bf16[4,24,3072]{2,1,0:T(8,128)(2,1)}, u32[]{:S(2)}, u32[]{:S(2)}) collective-permute-start(bf16[4,24,3072]{2,1,0:T(8,128)(2,1)} %get-tuple-element.229), channel_id=1, source_target_pairs={{0,4},{1,5},{2,6},{3,7},{4,0},{5,1},{6,2},{7,3},{8,12},{9,13},{10,... | collective-permute-start | bytes 1769480 | tf_op jit(solution)/shard_map/ppermute | solution.py:94
  297.0 45.4 %collective-permute-start.46 = (bf16[24,6144]{1,0:T(8,128)(2,1)}, bf16[24,6144]{1,0:T(8,128)(2,1)S(1)}, u32[]{:S(2)}, u32[]{:S(2)}) collective-permute-start(bf16[24,6144]{1,0:T(8,128)(2,1)} %get-tuple-element.237), channel_id=1, source_target_pairs={{0,8},{1,9},{2,10},{3,11},{4,12},{5,13},{6,14},{7,15},{8,16},{9,17... | collective-permute-start | bytes 884744 | tf_op jit(solution)/shard_map/ppermute | solution.py:94
  297.0 45.5 %collective-permute-start.47 = (bf16[24,6144]{1,0:T(8,128)(2,1)}, bf16[24,6144]{1,0:T(8,128)(2,1)}, u32[]{:S(2)}, u32[]{:S(2)}) collective-permute-start(bf16[24,6144]{1,0:T(8,128)(2,1)} %get-tuple-element.238), channel_id=1, source_target_pairs={{0,16},{1,17},{2,18},{3,19},{4,20},{5,21},{6,22},{7,23},{8,24},{9,... | collective-permute-start | bytes 884744 | tf_op jit(solution)/shard_map/ppermute | solution.py:94
  298.8 43.8 %collective-permute-start.48 = (bf16[24,6144]{1,0:T(8,128)(2,1)}, bf16[24,6144]{1,0:T(8,128)(2,1)}, u32[]{:S(2)}, u32[]{:S(2)}) collective-permute-start(bf16[24,6144]{1,0:T(8,128)(2,1)} %get-tuple-element.239), channel_id=1, source_target_pairs={{0,24},{1,25},{2,26},{3,27},{4,28},{5,29},{6,30},{7,31},{8,0},{9,1... | collective-permute-start | bytes 884744 | tf_op jit(solution)/shard_map/ppermute | solution.py:94
  309.0 17.7 %collective-permute-start.42 = (bf16[4,2,24,1920]{3,2,1,0:T(8,128)(2,1)}, bf16[4,2,24,1920]{3,2,1,0:T(8,128)(2,1)S(1)}, u32[]{:S(2)}, u32[]{:S(2)}) collective-permute-start(bf16[4,2,24,1920]{3,2,1,0:T(8,128)(2,1)} %get-tuple-element.243), channel_id=1, source_target_pairs={{0,4},{1,5},{2,6},{3,7},{4,0},{5,1},{6,2},{7,3},{8,12},{9,13},{10,... | collective-permute-start | bytes 2211848 | tf_op jit(solution)/shard_map/ppermute | solution.py:94
  309.7 17.7 %collective-permute-start.43 = (bf16[4,2,24,1920]{3,2,1,0:T(8,128)(2,1)}, bf16[4,2,24,1920]{3,2,1,0:T(8,128)(2,1)S(1)}, u32[]{:S(2)}, u32[]{:S(2)}) collective-permute-start(bf16[4,2,24,1920]{3,2,1,0:T(8,128)(2,1)} %get-tuple-element.245), channel_id=1, source_target_pairs={{0,2},{1,3},{2,0},{3,1},{4,6},{5,7},{6,4},{7,5},{8,10},{9,11},{10,... | collective-permute-start | bytes 2211848 | tf_op jit(solution)/shard_map/ppermute | solution.py:94
  332.3 13.0 %collective-permute-start.44 = (bf16[4,24,1920]{2,1,0:T(8,128)(2,1)}, bf16[4,24,1920]{2,1,0:T(8,128)(2,1)S(1)}, u32[]{:S(2)}, u32[]{:S(2)}) collective-permute-start(bf16[4,24,1920]{2,1,0:T(8,128)(2,1)} %get-tuple-element.253), channel_id=1, source_target_pairs={{0,2},{1,3},{2,0},{3,1},{4,6},{5,7},{6,4},{7,5},{8,10},{9,11},{10,... | collective-permute-start | bytes 1105928 | tf_op jit(solution)/shard_map/ppermute | solution.py:94
  332.8 12.5 %collective-permute-start.45 = (bf16[4,24,1920]{2,1,0:T(8,128)(2,1)}, bf16[4,24,1920]{2,1,0:T(8,128)(2,1)S(1)}, u32[]{:S(2)}, u32[]{:S(2)}) collective-permute-start(bf16[4,24,1920]{2,1,0:T(8,128)(2,1)} %get-tuple-element.255), channel_id=1, source_target_pairs={{0,4},{1,5},{2,6},{3,7},{4,0},{5,1},{6,2},{7,3},{8,12},{9,13},{10,... | collective-permute-start | bytes 1105928 | tf_op jit(solution)/shard_map/ppermute | solution.py:94
  342.5 24.3 %collective-permute-start.49 = (bf16[4,2,2,24,2304]{4,3,2,1,0:T(8,128)(2,1)}, bf16[4,2,2,24,2304]{4,3,2,1,0:T(8,128)(2,1)S(1)}, u32[]{:S(2)}, u32[]{:S(2)}) collective-permute-start(bf16[4,2,2,24,2304]{4,3,2,1,0:T(8,128)(2,1)} %get-tuple-element.257), channel_id=1, source_target_pairs={{0,1},{1,0},{2,3},{3,2},{4,5},{5,4},{6,7},{7,6},{8,9},{9,8},{10,11... | collective-permute-start | bytes 5308424 | tf_op jit(solution)/shard_map/ppermute | solution.py:94
  360.4 33.0 %collective-permute-start.55 = (bf16[24,3840]{1,0:T(8,128)(2,1)S(1)}, bf16[24,3840]{1,0:T(8,128)(2,1)S(1)}, u32[]{:S(2)}, u32[]{:S(2)}) collective-permute-start(bf16[24,3840]{1,0:T(8,128)(2,1)S(1)} %copy-done.37), channel_id=1, source_target_pairs={{0,8},{1,9},{2,10},{3,11},{4,12},{5,13},{6,14},{7,15},{8,16},{9,17... | collective-permute-start | bytes 552968 | tf_op jit(solution)/shard_map/ppermute | solution.py:94
  360.8 32.5 %collective-permute-start.56 = (bf16[24,3840]{1,0:T(8,128)(2,1)S(1)}, bf16[24,3840]{1,0:T(8,128)(2,1)S(1)}, u32[]{:S(2)}, u32[]{:S(2)}) collective-permute-start(bf16[24,3840]{1,0:T(8,128)(2,1)S(1)} %copy-done.36), channel_id=1, source_target_pairs={{0,16},{1,17},{2,18},{3,19},{4,20},{5,21},{6,22},{7,23},{8,24},{9,... | collective-permute-start | bytes 552968 | tf_op jit(solution)/shard_map/ppermute | solution.py:94
  362.1 31.2 %collective-permute-start.57 = (bf16[24,3840]{1,0:T(8,128)(2,1)S(1)}, bf16[24,3840]{1,0:T(8,128)(2,1)}, u32[]{:S(2)}, u32[]{:S(2)}) collective-permute-start(bf16[24,3840]{1,0:T(8,128)(2,1)S(1)} %copy-done.35), channel_id=1, source_target_pairs={{0,24},{1,25},{2,26},{3,27},{4,28},{5,29},{6,30},{7,31},{8,0},{9,1... | collective-permute-start | bytes 552968 | tf_op jit(solution)/shard_map/ppermute | solution.py:94
  372.8 11.9 %collective-permute-start.51 = (bf16[4,2,24,1152]{3,2,1,0:T(8,128)(2,1)}, bf16[4,2,24,1152]{3,2,1,0:T(8,128)(2,1)S(1)}, u32[]{:S(2)}, u32[]{:S(2)}) collective-permute-start(bf16[4,2,24,1152]{3,2,1,0:T(8,128)(2,1)} %get-tuple-element.283), channel_id=1, source_target_pairs={{0,4},{1,5},{2,6},{3,7},{4,0},{5,1},{6,2},{7,3},{8,12},{9,13},{10,... | collective-permute-start | bytes 1327112 | tf_op jit(solution)/shard_map/ppermute | solution.py:94
  373.9 12.7 %collective-permute-start.52 = (bf16[4,2,24,1280]{3,2,1,0:T(8,128)(2,1)}, bf16[4,2,24,1280]{3,2,1,0:T(8,128)(2,1)S(1)}, u32[]{:S(2)}, u32[]{:S(2)}) collective-permute-start(bf16[4,2,24,1280]{3,2,1,0:T(8,128)(2,1)} %get-tuple-element.285), channel_id=1, source_target_pairs={{0,2},{1,3},{2,0},{3,1},{4,6},{5,7},{6,4},{7,5},{8,10},{9,11},{10,... | collective-permute-start | bytes 1474568 | tf_op jit(solution)/shard_map/ppermute | solution.py:94
  401.1 9.7 %collective-permute-start.59 = (bf16[24,2432]{1,0:T(8,128)(2,1)}, bf16[24,2432]{1,0:T(8,128)(2,1)S(1)}, u32[]{:S(2)}, u32[]{:S(2)}) collective-permute-start(bf16[24,2432]{1,0:T(8,128)(2,1)} %get-tuple-element.306), channel_id=1, source_target_pairs={{0,16},{1,17},{2,18},{3,19},{4,20},{5,21},{6,22},{7,23},{8,24},{9,... | collective-permute-start | bytes 350216 | tf_op jit(solution)/shard_map/ppermute | solution.py:94
  402.2 8.5 %collective-permute-start.60 = (bf16[24,2432]{1,0:T(8,128)(2,1)}, bf16[24,2432]{1,0:T(8,128)(2,1)S(1)}, u32[]{:S(2)}, u32[]{:S(2)}) collective-permute-start(bf16[24,2432]{1,0:T(8,128)(2,1)} %get-tuple-element.307), channel_id=1, source_target_pairs={{0,24},{1,25},{2,26},{3,27},{4,28},{5,29},{6,30},{7,31},{8,0},{9,1... | collective-permute-start | bytes 350216 | tf_op jit(solution)/shard_map/ppermute | solution.py:94
  (56 other events, 354.2 us)

commit v4 on v3

--- a/solution.py
+++ b/solution.py
@@ -3,6 +3,7 @@
 
 import jax
 import jax.numpy as jnp
+import numpy as np
 from jax import lax
 from jax.experimental import pallas as pl
 from jax.experimental.pallas import tpu as pltpu
@@ -22,9 +23,13 @@
 LANES = 128
 ROWS = 256
 SMALL = 18
-TILE_F = 512
+TILE_F = 768
 QKV_TILE = 384
-WIDE = 3
+MLP_ROWS = 512
+EDGE_ROWS = 256
+STEP = 32
+WIDE = 2
+SELF_WIDE = 2
 
 epsilon = 1e-05
 rope_base = 10000.0
@@ -40,8 +45,9 @@
     "mid_forward": 8,
     "ckv_project": 6,
     "cross_attend": 8,
-    "mlp_both": 39,
+    "mlp_both": 38,
     "grad_blocks": 6,
+    "many_grads": 13,
     "cross_back": 20,
     "fold_core": 5,
     "fold_side": 4,
@@ -368,6 +374,9 @@
     total = plus(*[ref[...] for ref in refs[:count]])
     rows = total.shape[0]
     for (start, width, stack), out_ref in zip(parts, refs[count:]):
+        if stack == 0:
+            out_ref[...] = total[:, start : start + width].T
+            continue
         part = width // stack
         for m in range(stack):
             column = start + m * part
@@ -376,7 +385,9 @@
 
 def fold_z(got, parts):
     rows = got[0].shape[0]
-    shapes = [(rows * stack, width // stack) for _, width, stack in parts]
+    shapes = [
+        (rows * stack, width // stack) if stack else (width, rows) for _, width, stack in parts
+    ]
     return call(
         functools.partial(fold_z_kernel, parts, len(got)),
         "fold_z",
@@ -440,15 +451,19 @@
 
 def rotary_tables():
     half_dim = HEAD_DIM // 2
-    inverse = jnp.exp(
-        jnp.arange(half_dim, dtype=f32) * (-2.0 * math.log(rope_base) / HEAD_DIM)
-    )
-    angles = jnp.arange(SEQ_LEN, dtype=f32)[:, None] * inverse[None, :]
-    cosine, sine = jnp.cos(angles), jnp.sin(angles)
-    return (
-        jnp.concatenate([cosine] * 4, 1),
-        jnp.concatenate([-sine, sine, -sine, sine], 1),
-    )
+    inverse = np.exp(np.arange(half_dim) * (-2.0 * math.log(rope_base) / HEAD_DIM))
+    coarse = np.arange(0, SEQ_LEN, STEP)[:, None, None] * inverse
+    fine = np.arange(STEP)[None, :, None] * inverse
+
+    def pick(values, signs=(1.0, 1.0, 1.0, 1.0)):
+        return jnp.asarray(np.concatenate([s * values for s in signs], -1), f32)
+
+    signs = (-1.0, 1.0, -1.0, 1.0)
+    cos_a, sin_a = pick(np.cos(coarse)), pick(np.sin(coarse))
+    cos_b, sin_b = pick(np.cos(fine)), pick(np.sin(fine))
+    cosine = cos_a * cos_b - sin_a * sin_b
+    sine = pick(np.sin(coarse), signs) * cos_b + cos_a * pick(np.sin(fine), signs)
+    return cosine.reshape(SEQ_LEN, LANES), sine.reshape(SEQ_LEN, LANES)
 
 
 def call(
@@ -499,9 +514,13 @@
 
     @pl.when(part == 0)
     def _():
-        for r in range(0, rows, ROWS):
-            normed, _ = normed_of(x_ref[r : r + ROWS].astype(f32))
-            a1_ref[r : r + ROWS] = (normed * vec_ref[8:9, :D] + vec_ref[11:12, :D]).astype(bf16)
+        def enter(i, _):
+            part = pl.ds(pl.multiple_of(i * ROWS, ROWS), ROWS)
+            normed, _ = normed_of(x_ref[part].astype(f32))
+            a1_ref[part] = (normed * vec_ref[8:9, :D] + vec_ref[11:12, :D]).astype(bf16)
+            return 0
+
+        lax.fori_loop(0, rows // ROWS, enter, 0)
 
     column = pl.multiple_of(lax.rem(part, D // width) * width, width)
     bias = vec_ref[pl.ds(part // (D // width), 1), pl.ds(column, width)]
@@ -594,8 +613,8 @@
 def self_attend(lengths, qkv):
     rows = qkv.shape[0]
     seqs = rows // SEQ_LEN
-    width = WIDE * LANES
-    steps = PAIRS // WIDE
+    width = SELF_WIDE * LANES
+    steps = PAIRS // SELF_WIDE
 
     def at(offset):
         return pl.BlockSpec((SEQ_LEN, width), lambda s, p, _: (s, offset + p))
@@ -917,22 +936,28 @@
 ):
     step = pl.program_id(0)
     rows = h1_ref.shape[0]
-    chunks = range(0, rows, ROWS)
+    chunks = rows // MLP_ROWS
+    nothing = jnp.zeros((1, D), f32)
+
+    def part_of(i, size=EDGE_ROWS):
+        return pl.ds(pl.multiple_of(i * size, size), size)
 
     @pl.when(step == 0)
     def _():
-        for r in chunks:
-            part = slice(r, r + ROWS)
+        def enter(i, _):
+            part = part_of(i)
             h2 = h1_ref[part] + dot_nn(co_ref[part], wco_ref[...]) + vec_ref[6:7]
             h2_ref[part] = h2
             normed, _ = normed_of(h2)
             a3_ref[part] = (normed * vec_ref[10:11] + vec_ref[13:14]).astype(bf16)
             y_acc[part] = h2 + vec_ref[7:8]
             da_acc[part] = jnp.zeros_like(h2)
-
-    bias_sum = jnp.zeros((1, TILE_F), f32)
-    for r in chunks:
-        part = slice(r, r + ROWS)
+            return 0
+
+        lax.fori_loop(0, rows // EDGE_ROWS, enter, 0)
+
+    def body(i, bias_sum):
+        part = part_of(i, MLP_ROWS)
         hidden = dot_nn(a3_ref[part], wu_ref[...]) + bu_ref[...]
         dg = dot_nt(dy_ref[part], wd_ref[...])
         value, slope = gelu_pair(hidden)
@@ -940,19 +965,16 @@
         du = (dg * slope).astype(bf16)
         g_ref[part] = g
         du_ref[part] = du
-        bias_sum += sum_rows(du.astype(f32))
         y_acc[part] += dot_nn(g, wd_ref[...])
         da_acc[part] += dot_nt(du, wu_ref[...])
-    dbu_ref[...] = bias_sum
+        return bias_sum + sum_rows(du.astype(f32))
+
+    dbu_ref[...] = lax.fori_loop(0, chunks, body, jnp.zeros(dbu_ref.shape, f32))
 
     @pl.when(step == pl.num_programs(0) - 1)
     def _():
-        gain_sum = jnp.zeros((1, D), f32)
-        shift_sum = jnp.zeros((1, D), f32)
-        e_sum = jnp.zeros((1, D), f32)
-        y_sum = jnp.zeros((1, D), f32)
-        for r in chunks:
-            part = slice(r, r + ROWS)
+        def leave(i, sums):
+            part = part_of(i)
             out_ref[part] = y_acc[part].astype(bf16)
             normed, inverse = normed_of(h2_ref[part])
             da3 = da_acc[part]
@@ -962,14 +984,12 @@
             e2 = dh2.astype(bf16)
             e2_ref[part] = e2
             dco_ref[part] = dot_nt(e2, wco_ref[...]).astype(bf16)
-            gain_sum += sum_rows(da3 * normed)
-            shift_sum += sum_rows(da3)
-            e_sum += sum_rows(e2.astype(f32))
-            y_sum += sum_rows(upstream)
-        sums_ref[0:1] = gain_sum
-        sums_ref[1:2] = shift_sum
-        sums_ref[2:3] = e_sum
-        sums_ref[3:4] = y_sum
+            found = (da3 * normed, da3, e2.astype(f32), upstream)
+            return tuple(total + sum_rows(value) for total, value in zip(sums, found))
+
+        found = lax.fori_loop(0, rows // EDGE_ROWS, leave, (nothing,) * 4)
+        for i, total in enumerate(found):
+            sums_ref[i : i + 1] = total
 
 
 def mlp_both(h1, co, dy, mid, wu, wd, bu, vec):
@@ -1182,7 +1202,65 @@
     )
 
 
+def many_kernel(sizes, plan, count, me_ref, *refs):
+    arrays = refs[:count]
+    keep_ref, send_ref, left_buf, right_buf, acc_ref, sems = refs[count:]
+    step = pl.program_id(0)
+
+    def copies(k, slot):
+        left, right, column = plan[k]
+        source = arrays[right].at[:, column : column + D]
+        return (
+            pltpu.make_async_copy(arrays[left], left_buf.at[slot], sems.at[0, slot]),
+            pltpu.make_async_copy(source, right_buf.at[slot], sems.at[1, slot]),
+        )
+
+    for k in range(len(plan)):
+
+        @pl.when(step == max(k - 1, 0))
+        def _():
+            for copy in copies(k, k % 2):
+                copy.start()
+
+    slot = lax.rem(step, 2)
+    for k in range(len(plan)):
+
+        @pl.when(step == k)
+        def _():
+            for copy in copies(k, k % 2):
+                copy.wait()
+
+    grad_kernel(sizes, 1, me_ref, left_buf.at[slot], right_buf.at[slot], keep_ref, send_ref, acc_ref)
+
+
+def many_grads(pairs, sizes, me):
+    nz, ny, nx, _ = sizes
+    rows = D // math.prod(sizes)
+    arrays, plan = [], []
+    for left, right in pairs:
+        at = len(arrays)
+        arrays += [left, right]
+        plan += [(at, at + 1, column) for column in range(0, right.shape[1], D)]
+    shape = like((nz, ny, nx, rows, len(plan) * D), bf16)
+    block = pl.BlockSpec((nz, ny, nx, rows, D), lambda j, _: (0, 0, 0, 0, j))
+    buffer = pltpu.VMEM((2,) + pairs[0][0].shape, bf16)
+    return call(
+        functools.partial(many_kernel, sizes, plan, len(arrays)),
+        "many_grads",
+        (len(plan),),
+        arrays,
+        [pl.BlockSpec(memory_space=pl.ANY)] * len(arrays),
+        [shape, shape],
+        [block, block],
+        0,
+        scratch=[buffer, buffer, pltpu.VMEM((D, D), f32), pltpu.SemaphoreType.DMA((2, 2))],
+        scalars=(me,),
+    )
+
+
 def grads(pairs, sizes, me, width, column=0, earlier=()):
+    if all(left.shape[1] == D for left, _ in pairs) and len(pairs) > 1:
+        return many_grads(pairs, sizes, me)
     for left, right in pairs:
         earlier = grad_blocks(left, right, sizes, me, width, column, earlier)
         column += left.shape[1] // D * right.shape[1]
@@ -1337,7 +1415,7 @@
         ((0, 2 * D, 1), (2 * D, D, 1), (3 * D, D, 1), (4 * D, D, 1)),
     )
     first_got = send_z(fold_corner(after(first_got, kv_sum), sizes), sizes)
-    first_sum, small_sum = fold_z(first_got, ((0, 3 * D, 1), (3 * D, LANES, 1)))
+    first_sum, small_sum = fold_z(first_got, ((0, 3 * D, 1), (3 * D, LANES, 0)))
 
     return (
         output,
@@ -1350,10 +1428,10 @@
         co_sum,
         up_sum,
         down_sum,
-        small_sum[:, :8].T,
-        small_sum[:, 14:SMALL].reshape(-1),
-        small_sum[:, 8:11].T,
-        small_sum[:, 11:14].T,
+        small_sum[:8],
+        small_sum[14:SMALL].T.reshape(-1),
+        small_sum[8:11],
+        small_sum[11:14],
     )
 
 

time: 425 us -> 414 us (0.974)
  Pallas kernels: 276 us -> 267 us
    pallas_call x31 -> x28, Pallas kernels: 256 us -> 247 us  [call(): pl.pallas_call(kernel, out_shape=outs, grid_spec=pltpu.PrefetchScalarGrid...]
    unnamed x98 -> x109, local copies, waits for them, and re-layouts: 17.8 us -> 17.3 us
  transfers between devices with their start and end apart: 61 -> 61, of which waited for: 18 -> 18; matrix products, arithmetic and copies ran while one was open for 6% -> 5% of each run, Pallas kernels for 47% -> 46%
where the time goes in v4:
time: 414 us; the launch traced here: 411 us
  Pallas kernels  267 us (64%)
  starting transfers between devices  61.9 us (15%)
  waiting for transfers between devices  38.8 us (9%)
  local copies, waits for them, and re-layouts  36.3 us (9%)
  other arithmetic  5.2 us (1%)
    pallas_call x28, Pallas kernels, call(): pl.pallas_call(kernel, out_shape=outs, grid_spec=pltpu.PrefetchScalarGrid...  247 us
    ppermute x61, starting transfers between devices, shift(): return lax.ppermute(values, 'fsdp', shift_pairs(sizes, axis, step))  61.9 us
    ppermute x61, waiting for transfers between devices, shift(): return lax.ppermute(values, 'fsdp', shift_pairs(sizes, axis, step))  38.8 us
    pallas_call x3, Pallas kernels, place(): pl.pallas_call(functools.partial(place_kernel, keys, counts, sizes, split...  20.1 us
    unnamed x109, local copies, waits for them, and re-layouts  17.3 us
  transfers between devices with their start and end apart: 61, of which 18 were waited for; matrix products, arithmetic and copies ran while one was open for 5% of the time, Pallas kernels for 46%

profile of v4, /device:TPU:0, one launch (start us, length us, event | category | flops | bytes accessed | tf_op | source)
XLA Modules:
  0.0 410.9 jit_solution(16995689648404502436)
XLA Ops:
  4.9 4.1 %collective-permute-start.1 = (bf16[24,2432]{1,0:T(8,128)(2,1)S(1)}, bf16[24,2432]{1,0:T(8,128)(2,1)S(1)}, u32[]{:S(2)}, u32[]{:S(2)}) collective-permute-start(bf16[24,2432]{1,0:T(8,128)(2,1)S(1)} %get-tuple-element.303), channel_id=1, source_target_pairs={{0,16},{1,17},{2,18},{3,19},{4,20},{5,21},{6,22},{7,23},{8,24},{9,... | collective-permute-start | bytes 350216 | tf_op jit(solution)/shard_map/ppermute | solution.py:100
  10.6 2.2 collective-permute-start.2
  16.0 2.2 collective-permute-done.1
  22.1 2.0 collective-permute-start.5
  27.7 2.8 collective-permute-done.8.refs_2_
  38.0 3.8 collective-permute-done.4
  43.8 2.2 collective-permute-start.18
  50.8 5.4 %place.3 = bf16[4,8,24,2432]{3,2,1,0:T(8,128)(2,1)} custom-call(s32[4]{0:T(128)} %pad_add_fusion.me_ref, bf16[4,24,2432]{2,1,0:T(8,128)(2,1)} %copy-done.4, bf16[4,24,2432]{2,1,0:T(8,128)(2,1)} %collective-permute-done.6.refs_1_, bf16[4,24,2432]{2,1,0:T(8,128)(2,1)} %collective-permute-done.8.refs_2_, bf16[4,24,1216]{2,1,0:T(8,128)(2,1)} %collective-permute-done.7.refs_3_, ...), custom_call_target="tpu_custom_call" | custom-call | flops 6000000000 | tf_op jit(solution)/shard_map/place/pallas_call | solution.py:182
  57.9 11.8 %qkv_project.1 = (bf16[1024,768]{1,0:T(8,128)(2,1)}, bf16[1024,2304]{1,0:T(8,128)(2,1)}) custom-call(bf16[1024,768]{1,0:T(8,128)(2,1)} %x_ref.4, bf16[768,2432]{1,0:T(8,128)(2,1)} %bitcast.56, f32[16,768]{1,0:T(8,128)} %convert_bitcast_fusion.vec_ref, f32[2,512,128]{2,1,0:T(8,128)} %stack.81.cos_ref, f32[2,512,128]{2,1,0:T(8,128)} %stack.82.sin_ref), custom_call_target="tpu_custom_call" | custom-call | flops 11000000512 | tf_op jit(solution)/shard_map/qkv_project/pallas_call | solution.py:483
  69.8 2.8 collective-permute-done.18
  77.8 12.9 %self_attend.1 = (bf16[1024,768]{1,0:T(8,128)(2,1)}, f32[1024,768]{1,0:T(8,128)}) custom-call(s32[2,4]{1,0:T(2,128)} %lengths_ref.5, bf16[1024,2304]{1,0:T(8,128)(2,1)} %get-tuple-element.165.q_ref.k_ref.v_ref, bf16[1024,2304]{1,0:T(8,128)(2,1)} %get-tuple-element.165.q_ref.k_ref.v_ref, bf16[1024,2304]{1,0:T(8,128)(2,1)} %get-tuple-element.165.q_ref.k_ref.v_ref), custom_call_target="tpu_custom_call" | custom-call | flops 12000000000 | tf_op jit(solution)/shard_map/self_attend/pallas_call | solution.py:483
  94.2 6.4 %place.4 = bf16[4,8,24,3840]{3,2,1,0:T(8,128)(2,1)} custom-call(s32[4]{0:T(128)} %pad_add_fusion.me_ref, bf16[4,24,3840]{2,1,0:T(8,128)(2,1)} %copy-done.3, bf16[4,24,3840]{2,1,0:T(8,128)(2,1)} %collective-permute-done.15.refs_1_, bf16[4,24,3840]{2,1,0:T(8,128)(2,1)} %collective-permute-done.16.refs_2_, ...), custom_call_target="tpu_custom_call" | custom-call | flops 6000000000 | tf_op jit(solution)/shard_map/place/pallas_call | solution.py:182
  100.6 6.4 %ckv_project.1.k_ref.v_ref = bf16[1024,1536]{1,0:T(8,128)(2,1)} custom-call(bf16[1024,768]{1,0:T(8,128)(2,1)} %refs_0_, bf16[768,3840]{1,0:T(8,128)(2,1)} %bitcast.62, f32[16,768]{1,0:T(8,128)} %convert_bitcast_fusion.vec_ref), custom_call_target="tpu_custom_call" | custom-call | flops 6000000000 | tf_op jit(solution)/shard_map/ckv_project/pallas_call | solution.py:483
  107.0 8.0 %mid_forward.1 = (f32[1024,768]{1,0:T(8,128)}, bf16[1024,768]{1,0:T(8,128)(2,1)}, bf16[1024,768]{1,0:T(8,128)(2,1)}) custom-call(bf16[1024,768]{1,0:T(8,128)(2,1)} %get-tuple-element.166.o_ref.refs_2_, bf16[1024,768]{1,0:T(8,128)(2,1)} %x_ref.4, bf16[768,3840]{1,0:T(8,128)(2,1)} %bitcast.63, bf16[768,3840]{1,0:T(8,128)(2,1)} %bitcast.64, ...), custom_call_target="tpu_custom_call" | custom-call | flops 8000000000 | tf_op jit(solution)/shard_map/mid_forward/pallas_call | solution.py:483
  115.0 4.7 %collective-permute-done.28.refs_2_ = bf16[4,24,6144]{2,1,0:T(8,128)(2,1)S(1)} collective-permute-done((bf16[4,24,6144]{2,1,0:T(8,128)(2,1)S(1)}, bf16[4,24,6144]{2,1,0:T(8,128)(2,1)S(1)}, u32[]{:S(2)}, u32[]{:S(2)}) %collective-permute-start.28) | collective-permute-done | bytes 1179680 | tf_op jit(solution)/shard_map/ppermute | solution.py:100
  125.6 8.9 %cross_attend.1.co_ref.refs_6_ = bf16[1024,768]{1,0:T(8,128)(2,1)} custom-call(s32[2,16]{1,0:T(2,128)} %reshape.191.chosen_ref, bf16[1024,768]{1,0:T(8,128)(2,1)} %get-tuple-element.177.q_ref, bf16[1024,1536]{1,0:T(8,128)(2,1)} %ckv_project.1.k_ref.v_ref, bf16[1024,1536]{1,0:T(8,128)(2,1)} %ckv_project.1.k_ref.v_ref), custom_call_target="tpu_custom_call" | custom-call | flops 8000000000 | tf_op jit(solution)/shard_map/cross_attend/pallas_call | solution.py:483
  134.4 3.5 collective-permute-done.30.refs_4_
  143.2 8.3 %place.5 = (bf16[4,8,96,768]{3,2,1,0:T(8,128)(2,1)}, bf16[4,8,24,3072]{3,2,1,0:T(8,128)(2,1)}) custom-call(s32[4]{0:T(128)} %pad_add_fusion.me_ref, bf16[4,24,6144]{2,1,0:T(8,128)(2,1)} %copy-done, bf16[4,24,6144]{2,1,0:T(8,128)(2,1)} %collective-permute-done.27.refs_1_, bf16[4,24,6144]{2,1,0:T(8,128)(2,1)} %copy-done.5, ...), custom_call_target="tpu_custom_call" | custom-call | flops 6000000000 | tf_op jit(solution)/shard_map/place/pallas_call | solution.py:182
  151.5 38.7 %mlp_both.1 = (bf16[1024,768]{1,0:T(8,128)(2,1)}, bf16[1024,3072]{1,0:T(8,128)(2,1)}, bf16[1024,3072]{1,0:T(8,128)(2,1)}, bf16[1024,768]{1,0:T(8,128)(2,1)}, f32...) custom-call(f32[1024,768]{1,0:T(8,128)} %get-tuple-element.172.h1_re, ...), custom_call_target="tpu_custom_call" | custom-call | flops 38000001024 | tf_op jit(solution)/shard_map/mlp_both/pallas_call | solution.py:483
  190.2 10.1 %grad_blocks.3 = (bf16[4,2,2,24,6144]{4,3,2,1,0:T(8,128)(2,1)}, bf16[4,2,2,24,6144]{4,3,2,1,0:T(8,128)(2,1)}) custom-call(s32[4]{0:T(128)} %pad_add_fusion.me_ref, bf16[1024,3072]{1,0:T(8,128)(2,1)} %get-tuple-element.189.left_ref, bf16[1024,768]{1,0:T(8,128)(2,1)} %right_ref.1), custom_call_target="tpu_custom_call" | custom-call | flops 6000000000 | tf_op jit(solution)/shard_map/grad_blocks/pallas_call | solution.py:483
  200.3 10.1 %grad_blocks.4 = (bf16[4,2,2,24,6144]{4,3,2,1,0:T(8,128)(2,1)}, bf16[4,2,2,24,6144]{4,3,2,1,0:T(8,128)(2,1)}) custom-call(s32[4]{0:T(128)} %pad_add_fusion.me_ref, bf16[1024,768]{1,0:T(8,128)(2,1)} %get-tuple-element.187.left_ref, bf16[1024,3072]{1,0:T(8,128)(2,1)} %get-tuple-element.188.right_ref, ...), custom_call_target="tpu_custom_call", output_to_operand_aliasing={{0}: (3, {}), {1}: (4, {})} | custom-call | flops 6000000000 | tf_op jit(solution)/shard_map/grad_blocks/pallas_call | solution.py:483
  210.5 20.3 %cross_back.1 = (bf16[1024,768]{1,0:T(8,128)(2,1)}, bf16[1024,1536]{1,0:T(8,128)(2,1)}, f32[16,768]{1,0:T(8,128)}) custom-call(s32[2,16]{1,0:T(2,128)} %reshape.191.chosen_ref, bf16[1024,768]{1,0:T(8,128)(2,1)} %get-tuple-element.177.q_ref, bf16[1024,1536]{1,0:T(8,128)(2,1)} %ckv_project.1.k_ref.v_ref, bf16[1024,1536]{1,0:T(8,128)(2,1)} %ckv_project.1.k_ref.v_ref, ...), custom_call_target="tpu_custom_call" | custom-call | flops 20000000000 | tf_op jit(solution)/shard_map/cross_back/pallas_call | solution.py:483
  230.7 7.0 %fold_core.3 = (bf16[4,2,24,3072]{3,2,1,0:T(8,128)(2,1)}, bf16[4,2,24,3072]{3,2,1,0:T(8,128)(2,1)}, bf16[4,2,24,3072]{3,2,1,0:T(8,128)(2,1)}, bf16[4,2,24,3072]{3,2,1,0:T(8,128)(2,1)}) custom-call(s32[4]{0:T(128)} %pad_add_fusion.me_ref, bf16[4,2,2,24,6144]{4,3,2,1,0:T(8,128)(2,1)} %get-tuple-element.195.refs_0_, ...), custom_call_target="tpu_custom_call" | custom-call | flops 5000000000 | tf_op jit(solution)/shard_map/fold_core/pallas_call | solution.py:483
  239.8 8.9 %mid_back.1 = (f32[1024,768]{1,0:T(8,128)}, bf16[1024,768]{1,0:T(8,128)(2,1)}, bf16[1024,768]{1,0:T(8,128)(2,1)}, f32[8,768]{1,0:T(8,128)}) custom-call(bf16[1024,768]{1,0:T(8,128)(2,1)} %get-tuple-element.201.dcq_ref.refs_5_, f32[1024,768]{1,0:T(8,128)} %get-tuple-element.202.dh2_ref, f32[1024,768]{1,0:T(8,128)} %get-tuple-element.172.h1_ref, ...), custom_call_target="tpu_custom_call" | custom-call | flops 8999999488 | tf_op jit(solution)/shard_map/mid_back/pallas_call | solution.py:483
  248.8 12.9 %many_grads.1 = (bf16[4,2,2,24,3840]{4,3,2,1,0:T(8,128)(2,1)}, bf16[4,2,2,24,3840]{4,3,2,1,0:T(8,128)(2,1)}) custom-call(s32[4]{0:T(128)} %pad_add_fusion.me_ref, bf16[1024,768]{1,0:T(8,128)(2,1)} %refs_0_, bf16[1024,1536]{1,0:T(8,128)(2,1)} %get-tuple-element.274.refs_1_.dkv_ref, bf16[1024,768]{1,0:T(8,128)(2,1)} %get-tuple-element.166.o_ref.refs_2_, ...), custom_call_target="tpu_custom_call" | custom-call | flops 12999999488 | tf_op jit(solution)/shard_map/many_grads/pallas_call | solution.py:483
  264.4 2.0 collective-permute-done.37.refs_1_
  267.7 4.3 %fold_side.3 = (bf16[4,24,3072]{2,1,0:T(8,128)(2,1)}, bf16[4,24,3072]{2,1,0:T(8,128)(2,1)}, bf16[4,24,3072]{2,1,0:T(8,128)(2,1)}, bf16[4,24,3072]{2,1,0:T(8,128)(2,1)}) custom-call(bf16[4,2,24,3072]{3,2,1,0:T(8,128)(2,1)} %get-tuple-element.210.refs_0_, bf16[4,2,24,3072]{3,2,1,0:T(8,128)(2,1)} %collective-permute-done.37.refs_1_, ...), custom_call_target="tpu_custom_call" | custom-call | flops 4000000000 | tf_op jit(solution)/shard_map/fold_side/pallas_call | solution.py:483
  273.0 15.5 %self_back.2.rest_0_ = bf16[1024,2304]{1,0:T(8,128)(2,1)} custom-call(s32[2,4]{1,0:T(2,128)} %lengths_ref.5, bf16[1024,2304]{1,0:T(8,128)(2,1)} %get-tuple-element.165.q_ref.k_ref.v_ref, bf16[1024,2304]{1,0:T(8,128)(2,1)} %get-tuple-element.165.q_ref.k_ref.v_ref, bf16[1024,2304]{1,0:T(8,128)(2,1)} %get-tuple-element.165.q_ref.k_ref.v_ref, ...), custom_call_target="tpu_custom_call" | custom-call | flops 15000000512 | tf_op jit(solution)/shard_map/self_back/pallas_call | solution.py:483
  288.5 2.7 fold_corner.3
  291.8 3.2 collective-permute-start.48
  296.7 5.4 %fold_core.4 = (bf16[4,2,24,1920]{3,2,1,0:T(8,128)(2,1)}, bf16[4,2,24,1920]{3,2,1,0:T(8,128)(2,1)}, bf16[4,2,24,1920]{3,2,1,0:T(8,128)(2,1)}, bf16[4,2,24,1920]{3,2,1,0:T(8,128)(2,1)}) custom-call(s32[4]{0:T(128)} %pad_add_fusion.me_ref, bf16[4,2,2,24,3840]{4,3,2,1,0:T(8,128)(2,1)} %get-tuple-element.228.refs_0_, bf16[4,2,2,24,3840]{4,3,2,1,0:T(8,128)(2,1)} %copy-done.21), custom_call_target="tpu_custom_call" | custom-call | flops 5000000000 | tf_op jit(solution)/shard_map/fold_core/pallas_call | solution.py:483
  305.1 15.3 %self_back.3.right_ref.dqkv_ref = bf16[1024,2304]{1,0:T(8,128)(2,1)} custom-call(s32[2,4]{1,0:T(2,128)} %lengths_ref.5, bf16[1024,2304]{1,0:T(8,128)(2,1)} %get-tuple-element.165.q_ref.k_ref.v_ref, bf16[1024,2304]{1,0:T(8,128)(2,1)} %get-tuple-element.165.q_ref.k_ref.v_ref, ...), custom_call_target="tpu_custom_call", output_to_operand_aliasing={{}: (8, {})} | custom-call | flops 15000000512 | tf_op jit(solution)/shard_map/self_back/pallas_call | solution.py:483
  322.2 3.9 fold_side.4
  327.6 8.5 %grad_blocks.5 = (bf16[4,2,2,24,2304]{4,3,2,1,0:T(8,128)(2,1)}, bf16[4,2,2,24,2304]{4,3,2,1,0:T(8,128)(2,1)}) custom-call(s32[4]{0:T(128)} %pad_add_fusion.me_ref, bf16[1024,768]{1,0:T(8,128)(2,1)} %get-tuple-element.244.left_ref, bf16[1024,2304]{1,0:T(8,128)(2,1)} %self_back.3.right_ref.dqkv_ref), custom_call_target="tpu_custom_call" | custom-call | flops 6000000000 | tf_op jit(solution)/shard_map/grad_blocks/pallas_call | solution.py:483
  336.8 2.1 fold_z.3
  339.8 2.2 fold_corner.4
  342.0 10.2 %token_back.1 = (f32[1024,768]{1,0:T(8,128)}, f32[8,768]{1,0:T(8,128)}, f32[1,2304]{1,0:T(1,128)}) custom-call(bf16[1024,2304]{1,0:T(8,128)(2,1)} %self_back.3.right_ref.dqkv_ref, f32[1024,768]{1,0:T(8,128)} %get-tuple-element.260.dh1_ref, bf16[1024,768]{1,0:T(8,128)(2,1)} %x_ref.4, bf16[768,2432]{1,0:T(8,128)(2,1)} %bitcast.58, ...), custom_call_target="tpu_custom_call" | custom-call | flops 10000000000 | tf_op jit(solution)/shard_map/token_back/pallas_call | solution.py:483
  355.9 2.8 collective-permute-start.57
  361.8 4.8 %fold_core.5 = (bf16[4,2,24,1152]{3,2,1,0:T(8,128)(2,1)}, bf16[4,2,24,1152]{3,2,1,0:T(8,128)(2,1)}, bf16[4,2,24,1280]{3,2,1,0:T(8,128)(2,1)}, bf16[4,2,24,1280]{3,2,1,0:T(8,128)(2,1)}) custom-call(s32[4]{0:T(128)} %pad_add_fusion.me_ref, bf16[4,2,2,24,2304]{4,3,2,1,0:T(8,128)(2,1)} %get-tuple-element.262.refs_0_, bf16[4,2,2,24,2304]{4,3,2,1,0:T(8,128)(2,1)} %copy-done.22, ...), custom_call_target="tpu_custom_call" | custom-call | flops 5000000000 | tf_op jit(solution)/shard_map/fold_core/pallas_call | solution.py:483
  369.5 6.7 %neighbour_back.1 = f32[1024,768]{1,0:T(8,128)} custom-call(bf16[1024,1536]{1,0:T(8,128)(2,1)} %get-tuple-element.274.refs_1_.dkv_ref, bf16[768,3840]{1,0:T(8,128)(2,1)} %bitcast.68), custom_call_target="tpu_custom_call" | custom-call | flops 6000000000 | tf_op jit(solution)/shard_map/neighbour_back/pallas_call | solution.py:483
  376.2 2.3 collective-permute-done.51.refs_1_
  378.5 2.1 collective-permute-done.52.refs_3_
  381.4 3.5 fold_side.5
  389.7 2.1 collective-permute-done.53.refs_1_
  392.5 2.1 fold_corner.5
  395.8 2.9 collective-permute-start.60
  398.8 3.1 collective-permute-done.58.refs_1_
  401.8 2.5 collective-permute-done.59.refs_2_
  (259 shorter events, 92.5 us)
Async XLA Ops:
  4.9 13.2 %collective-permute-start.1 = (bf16[24,2432]{1,0:T(8,128)(2,1)S(1)}, bf16[24,2432]{1,0:T(8,128)(2,1)S(1)}, u32[]{:S(2)}, u32[]{:S(2)}) collective-permute-start(bf16[24,2432]{1,0:T(8,128)(2,1)S(1)} %get-tuple-element.303), channel_id=1, source_target_pairs={{0,16},{1,17},{2,18},{3,19},{4,20},{5,21},{6,22},{7,23},{8,24},{9,... | collective-permute-start | bytes 350216 | tf_op jit(solution)/shard_map/ppermute | solution.py:100
  9.1 9.1 %collective-permute-start = (bf16[24,2432]{1,0:T(8,128)(2,1)S(1)}, bf16[24,2432]{1,0:T(8,128)(2,1)S(1)}, u32[]{:S(2)}, u32[]{:S(2)}) collective-permute-start(bf16[24,2432]{1,0:T(8,128)(2,1)S(1)} %get-tuple-element.303), channel_id=1, source_target_pairs={{0,8},{1,9},{2,10},{3,11},{4,12},{5,13},{6,14},{7,15},{8,16},{9,17... | collective-permute-start | bytes 350216 | tf_op jit(solution)/shard_map/ppermute | solution.py:100
  10.6 8.2 %collective-permute-start.2 = (bf16[24,2432]{1,0:T(8,128)(2,1)S(1)}, bf16[24,2432]{1,0:T(8,128)(2,1)S(1)}, u32[]{:S(2)}, u32[]{:S(2)}) collective-permute-start(bf16[24,2432]{1,0:T(8,128)(2,1)S(1)} %get-tuple-element.303), channel_id=1, source_target_pairs={{0,24},{1,25},{2,26},{3,27},{4,28},{5,29},{6,30},{7,31},{8,0},{9,1... | collective-permute-start | bytes 350216 | tf_op jit(solution)/shard_map/ppermute | solution.py:100
  18.9 11.6 %collective-permute-start.8 = (bf16[4,24,2432]{2,1,0:T(8,128)(2,1)S(1)}, bf16[4,24,2432]{2,1,0:T(8,128)(2,1)}, u32[]{:S(2)}, u32[]{:S(2)}) collective-permute-start(bf16[4,24,2432]{2,1,0:T(8,128)(2,1)S(1)} %pad_maximum_fusion.2.refs_0_), channel_id=1, source_target_pairs={{0,4},{1,5},{2,6},{3,7},{4,0},{5,1},{6,2},{7,3},{8,12},{9,13},{10,... | collective-permute-start | bytes 1400840 | tf_op jit(solution)/shard_map/ppermute | solution.py:100
  20.6 12.4 %collective-permute-start.6 = (bf16[4,24,2432]{2,1,0:T(8,128)(2,1)S(1)}, bf16[4,24,2432]{2,1,0:T(8,128)(2,1)}, u32[]{:S(2)}, u32[]{:S(2)}) collective-permute-start(bf16[4,24,2432]{2,1,0:T(8,128)(2,1)S(1)} %pad_maximum_fusion.2.refs_0_), channel_id=1, source_target_pairs={{0,2},{1,3},{2,0},{3,1},{4,6},{5,7},{6,4},{7,5},{8,10},{9,11},{10,... | collective-permute-start | bytes 1400840 | tf_op jit(solution)/shard_map/ppermute | solution.py:100
  22.1 15.9 %collective-permute-start.5 = (bf16[24,3840]{1,0:T(8,128)(2,1)S(1)}, bf16[24,3840]{1,0:T(8,128)(2,1)S(1)}, u32[]{:S(2)}, u32[]{:S(2)}) collective-permute-start(bf16[24,3840]{1,0:T(8,128)(2,1)S(1)} %pad_maximum_fusion.3), channel_id=1, source_target_pairs={{0,24},{1,25},{2,26},{3,27},{4,28},{5,29},{6,30},{7,31},{8,0},{9,1... | collective-permute-start | bytes 552968 | tf_op jit(solution)/shard_map/ppermute | solution.py:100
  24.2 17.6 %collective-permute-start.4 = (bf16[24,3840]{1,0:T(8,128)(2,1)S(1)}, bf16[24,3840]{1,0:T(8,128)(2,1)S(1)}, u32[]{:S(2)}, u32[]{:S(2)}) collective-permute-start(bf16[24,3840]{1,0:T(8,128)(2,1)S(1)} %pad_maximum_fusion.3), channel_id=1, source_target_pairs={{0,16},{1,17},{2,18},{3,19},{4,20},{5,21},{6,22},{7,23},{8,24},{9,... | collective-permute-start | bytes 552968 | tf_op jit(solution)/shard_map/ppermute | solution.py:100
  25.8 16.0 %collective-permute-start.3 = (bf16[24,3840]{1,0:T(8,128)(2,1)S(1)}, bf16[24,3840]{1,0:T(8,128)(2,1)S(1)}, u32[]{:S(2)}, u32[]{:S(2)}) collective-permute-start(bf16[24,3840]{1,0:T(8,128)(2,1)S(1)} %pad_maximum_fusion.3), channel_id=1, source_target_pairs={{0,8},{1,9},{2,10},{3,11},{4,12},{5,13},{6,14},{7,15},{8,16},{9,17... | collective-permute-start | bytes 552968 | tf_op jit(solution)/shard_map/ppermute | solution.py:100
  31.6 10.7 %collective-permute-start.9 = (bf16[4,24,1216]{2,1,0:T(8,128)(2,1)S(1)}, bf16[4,24,1216]{2,1,0:T(8,128)(2,1)}, u32[]{:S(2)}, u32[]{:S(2)}) collective-permute-start(bf16[4,24,1216]{2,1,0:T(8,128)(2,1)S(1)} %slice.92), channel_id=1, source_target_pairs={{0,2},{1,3},{2,0},{3,1},{4,6},{5,7},{6,4},{7,5},{8,10},{9,11},{10,... | collective-permute-start | bytes 700424 | tf_op jit(solution)/shard_map/ppermute | solution.py:100
  33.9 8.5 %collective-permute-start.7 = (bf16[4,24,1216]{2,1,0:T(8,128)(2,1)S(1)}, bf16[4,24,1216]{2,1,0:T(8,128)(2,1)}, u32[]{:S(2)}, u32[]{:S(2)}) collective-permute-start(bf16[4,24,1216]{2,1,0:T(8,128)(2,1)S(1)} %slice.91), channel_id=1, source_target_pairs={{0,4},{1,5},{2,6},{3,7},{4,0},{5,1},{6,2},{7,3},{8,12},{9,13},{10,... | collective-permute-start | bytes 700424 | tf_op jit(solution)/shard_map/ppermute | solution.py:100
  43.0 26.7 %collective-permute-start.19 = (bf16[24,6144]{1,0:T(8,128)(2,1)S(1)}, bf16[24,6144]{1,0:T(8,128)(2,1)S(1)}, u32[]{:S(2)}, u32[]{:S(2)}) collective-permute-start(bf16[24,6144]{1,0:T(8,128)(2,1)S(1)} %constant_dynamic-update-slice_fusion), channel_id=1, source_target_pairs={{0,24},{1,25},{2,26},{3,27},{4,28},{5,29},{6,30},{7,31},{8,0},{9,1... | collective-permute-start | bytes 884744 | tf_op jit(solution)/shard_map/ppermute | solution.py:100
  43.8 28.8 %collective-permute-start.18 = (bf16[24,6144]{1,0:T(8,128)(2,1)S(1)}, bf16[24,6144]{1,0:T(8,128)(2,1)S(1)}, u32[]{:S(2)}, u32[]{:S(2)}) collective-permute-start(bf16[24,6144]{1,0:T(8,128)(2,1)S(1)} %constant_dynamic-update-slice_fusion), channel_id=1, source_target_pairs={{0,16},{1,17},{2,18},{3,19},{4,20},{5,21},{6,22},{7,23},{8,24},{9,... | collective-permute-start | bytes 884744 | tf_op jit(solution)/shard_map/ppermute | solution.py:100
  46.1 26.5 %collective-permute-start.17 = (bf16[24,6144]{1,0:T(8,128)(2,1)S(1)}, bf16[24,6144]{1,0:T(8,128)(2,1)S(1)}, u32[]{:S(2)}, u32[]{:S(2)}) collective-permute-start(bf16[24,6144]{1,0:T(8,128)(2,1)S(1)} %constant_dynamic-update-slice_fusion), channel_id=1, source_target_pairs={{0,8},{1,9},{2,10},{3,11},{4,12},{5,13},{6,14},{7,15},{8,16},{9,17... | collective-permute-start | bytes 884744 | tf_op jit(solution)/shard_map/ppermute | solution.py:100
  48.0 24.8 %collective-permute-start.16 = (bf16[4,24,3840]{2,1,0:T(8,128)(2,1)S(1)}, bf16[4,24,3840]{2,1,0:T(8,128)(2,1)}, u32[]{:S(2)}, u32[]{:S(2)}) collective-permute-start(bf16[4,24,3840]{2,1,0:T(8,128)(2,1)S(1)} %pad_maximum_fusion.1.refs_0_), channel_id=1, source_target_pairs={{0,4},{1,5},{2,6},{3,7},{4,0},{5,1},{6,2},{7,3},{8,12},{9,13},{10,... | collective-permute-start | bytes 2211848 | tf_op jit(solution)/shard_map/ppermute | solution.py:100
  50.3 22.5 %collective-permute-start.15 = (bf16[4,24,3840]{2,1,0:T(8,128)(2,1)S(1)}, bf16[4,24,3840]{2,1,0:T(8,128)(2,1)}, u32[]{:S(2)}, u32[]{:S(2)}) collective-permute-start(bf16[4,24,3840]{2,1,0:T(8,128)(2,1)S(1)} %pad_maximum_fusion.1.refs_0_), channel_id=1, source_target_pairs={{0,2},{1,3},{2,0},{3,1},{4,6},{5,7},{6,4},{7,5},{8,10},{9,11},{10,... | collective-permute-start | bytes 2211848 | tf_op jit(solution)/shard_map/ppermute | solution.py:100
  69.7 21.0 %collective-permute-start.22 = (bf16[4,24,3840]{2,1,0:T(8,128)(2,1)S(1)}, bf16[4,24,3840]{2,1,0:T(8,128)(2,1)}, u32[]{:S(2)}, u32[]{:S(2)}) collective-permute-start(bf16[4,24,3840]{2,1,0:T(8,128)(2,1)S(1)} %pad_maximum_fusion.1.refs_0_), channel_id=1, source_target_pairs={{0,1},{1,0},{2,3},{3,2},{4,5},{5,4},{6,7},{7,6},{8,9},{9,8},{10,11... | collective-permute-start | bytes 2211848 | tf_op jit(solution)/shard_map/ppermute | solution.py:100
  74.1 16.7 %collective-permute-start.23 = (bf16[4,24,3840]{2,1,0:T(8,128)(2,1)}, bf16[4,24,3840]{2,1,0:T(8,128)(2,1)S(1)}, u32[]{:S(2)}, u32[]{:S(2)}) collective-permute-start(bf16[4,24,3840]{2,1,0:T(8,128)(2,1)} %collective-permute-done.15.refs_1_), channel_id=1, source_target_pairs={{0,1},{1,0},{2,3},{3,2},{4,5},{5,4},{6,7},{7,6},{8,9},{9,8},{10,11... | collective-permute-start | bytes 2211848 | tf_op jit(solution)/shard_map/ppermute | solution.py:100
  75.2 15.6 %collective-permute-start.24 = (bf16[4,24,3840]{2,1,0:T(8,128)(2,1)}, bf16[4,24,3840]{2,1,0:T(8,128)(2,1)}, u32[]{:S(2)}, u32[]{:S(2)}) collective-permute-start(bf16[4,24,3840]{2,1,0:T(8,128)(2,1)} %collective-permute-done.16.refs_2_), channel_id=1, source_target_pairs={{0,1},{1,0},{2,3},{3,2},{4,5},{5,4},{6,7},{7,6},{8,9},{9,8},{10,11... | collective-permute-start | bytes 2211848 | tf_op jit(solution)/shard_map/ppermute | solution.py:100
  75.8 15.0 %collective-permute-start.21 = (bf16[4,24,1920]{2,1,0:T(8,128)(2,1)S(1)}, bf16[4,24,1920]{2,1,0:T(8,128)(2,1)S(1)}, u32[]{:S(2)}, u32[]{:S(2)}) collective-permute-start(bf16[4,24,1920]{2,1,0:T(8,128)(2,1)S(1)} %slice.73), channel_id=1, source_target_pairs={{0,2},{1,3},{2,0},{3,1},{4,6},{5,7},{6,4},{7,5},{8,10},{9,11},{10,... | collective-permute-start | bytes 1105928 | tf_op jit(solution)/shard_map/ppermute | solution.py:100
  76.3 14.4 %collective-permute-start.20 = (bf16[4,24,1920]{2,1,0:T(8,128)(2,1)S(1)}, bf16[4,24,1920]{2,1,0:T(8,128)(2,1)}, u32[]{:S(2)}, u32[]{:S(2)}) collective-permute-start(bf16[4,24,1920]{2,1,0:T(8,128)(2,1)S(1)} %slice.72), channel_id=1, source_target_pairs={{0,4},{1,5},{2,6},{3,7},{4,0},{5,1},{6,2},{7,3},{8,12},{9,13},{10,... | collective-permute-start | bytes 1105928 | tf_op jit(solution)/shard_map/ppermute | solution.py:100
  91.4 43.0 %collective-permute-start.31 = (bf16[4,24,6144]{2,1,0:T(8,128)(2,1)S(1)}, bf16[4,24,6144]{2,1,0:T(8,128)(2,1)}, u32[]{:S(2)}, u32[]{:S(2)}) collective-permute-start(bf16[4,24,6144]{2,1,0:T(8,128)(2,1)S(1)} %pad_maximum_fusion.refs_0_), channel_id=1, source_target_pairs={{0,1},{1,0},{2,3},{3,2},{4,5},{5,4},{6,7},{7,6},{8,9},{9,8},{10,11... | collective-permute-start | bytes 3538952 | tf_op jit(solution)/shard_map/ppermute | solution.py:100
  91.5 28.3 %collective-permute-start.28 = (bf16[4,24,6144]{2,1,0:T(8,128)(2,1)S(1)}, bf16[4,24,6144]{2,1,0:T(8,128)(2,1)S(1)}, u32[]{:S(2)}, u32[]{:S(2)}) collective-permute-start(bf16[4,24,6144]{2,1,0:T(8,128)(2,1)S(1)} %pad_maximum_fusion.refs_0_), channel_id=1, source_target_pairs={{0,4},{1,5},{2,6},{3,7},{4,0},{5,1},{6,2},{7,3},{8,12},{9,13},{10,... | collective-permute-start | bytes 3538952 | tf_op jit(solution)/shard_map/ppermute | solution.py:100
  92.0 28.1 %collective-permute-start.27 = (bf16[4,24,6144]{2,1,0:T(8,128)(2,1)S(1)}, bf16[4,24,6144]{2,1,0:T(8,128)(2,1)}, u32[]{:S(2)}, u32[]{:S(2)}) collective-permute-start(bf16[4,24,6144]{2,1,0:T(8,128)(2,1)S(1)} %pad_maximum_fusion.refs_0_), channel_id=1, source_target_pairs={{0,2},{1,3},{2,0},{3,1},{4,6},{5,7},{6,4},{7,5},{8,10},{9,11},{10,... | collective-permute-start | bytes 3538952 | tf_op jit(solution)/shard_map/ppermute | solution.py:100
  120.1 19.0 %collective-permute-start.32 = (bf16[4,24,6144]{2,1,0:T(8,128)(2,1)}, bf16[4,24,6144]{2,1,0:T(8,128)(2,1)}, u32[]{:S(2)}, u32[]{:S(2)}) collective-permute-start(bf16[4,24,6144]{2,1,0:T(8,128)(2,1)} %collective-permute-done.27.refs_1_), channel_id=1, source_target_pairs={{0,1},{1,0},{2,3},{3,2},{4,5},{5,4},{6,7},{7,6},{8,9},{9,8},{10,11... | collective-permute-start | bytes 3538952 | tf_op jit(solution)/shard_map/ppermute | solution.py:100
  120.1 19.0 %collective-permute-start.33 = (bf16[4,24,6144]{2,1,0:T(8,128)(2,1)S(1)}, bf16[4,24,6144]{2,1,0:T(8,128)(2,1)}, u32[]{:S(2)}, u32[]{:S(2)}) collective-permute-start(bf16[4,24,6144]{2,1,0:T(8,128)(2,1)S(1)} %collective-permute-done.28.refs_2_), channel_id=1, source_target_pairs={{0,1},{1,0},{2,3},{3,2},{4,5},{5,4},{6,7},{7,6},{8,9},{9,8},{10,11... | collective-permute-start | bytes 3538952 | tf_op jit(solution)/shard_map/ppermute | solution.py:100
  122.5 15.4 %collective-permute-start.30 = (bf16[4,24,3072]{2,1,0:T(8,128)(2,1)S(1)}, bf16[4,24,3072]{2,1,0:T(8,128)(2,1)}, u32[]{:S(2)}, u32[]{:S(2)}) collective-permute-start(bf16[4,24,3072]{2,1,0:T(8,128)(2,1)S(1)} %slice.75), channel_id=1, source_target_pairs={{0,2},{1,3},{2,0},{3,1},{4,6},{5,7},{6,4},{7,5},{8,10},{9,11},{10,... | collective-permute-start | bytes 1769480 | tf_op jit(solution)/shard_map/ppermute | solution.py:100
  124.0 15.1 %collective-permute-start.29 = (bf16[4,24,3072]{2,1,0:T(8,128)(2,1)S(1)}, bf16[4,24,3072]{2,1,0:T(8,128)(2,1)}, u32[]{:S(2)}, u32[]{:S(2)}) collective-permute-start(bf16[4,24,3072]{2,1,0:T(8,128)(2,1)S(1)} %slice.74), channel_id=1, source_target_pairs={{0,4},{1,5},{2,6},{3,7},{4,0},{5,1},{6,2},{7,3},{8,12},{9,13},{10,... | collective-permute-start | bytes 1769480 | tf_op jit(solution)/shard_map/ppermute | solution.py:100
  210.4 20.3 %collective-permute-start.36 = (bf16[4,2,2,24,6144]{4,3,2,1,0:T(8,128)(2,1)}, bf16[4,2,2,24,6144]{4,3,2,1,0:T(8,128)(2,1)}, u32[]{:S(2)}, u32[]{:S(2)}) collective-permute-start(bf16[4,2,2,24,6144]{4,3,2,1,0:T(8,128)(2,1)} %get-tuple-element.192), channel_id=1, source_target_pairs={{0,1},{1,0},{2,3},{3,2},{4,5},{5,4},{6,7},{7,6},{8,9},{9,8},{10,11... | collective-permute-start | bytes 14155784 | tf_op jit(solution)/shard_map/ppermute | solution.py:100
  237.8 28.7 %collective-permute-start.37 = (bf16[4,2,24,3072]{3,2,1,0:T(8,128)(2,1)}, bf16[4,2,24,3072]{3,2,1,0:T(8,128)(2,1)}, u32[]{:S(2)}, u32[]{:S(2)}) collective-permute-start(bf16[4,2,24,3072]{3,2,1,0:T(8,128)(2,1)} %get-tuple-element.198), channel_id=1, source_target_pairs={{0,4},{1,5},{2,6},{3,7},{4,0},{5,1},{6,2},{7,3},{8,12},{9,13},{10,... | collective-permute-start | bytes 3538952 | tf_op jit(solution)/shard_map/ppermute | solution.py:100
  239.3 28.4 %collective-permute-start.38 = (bf16[4,2,24,3072]{3,2,1,0:T(8,128)(2,1)}, bf16[4,2,24,3072]{3,2,1,0:T(8,128)(2,1)}, u32[]{:S(2)}, u32[]{:S(2)}) collective-permute-start(bf16[4,2,24,3072]{3,2,1,0:T(8,128)(2,1)} %get-tuple-element.200), channel_id=1, source_target_pairs={{0,2},{1,3},{2,0},{3,1},{4,6},{5,7},{6,4},{7,5},{8,10},{9,11},{10,... | collective-permute-start | bytes 3538952 | tf_op jit(solution)/shard_map/ppermute | solution.py:100
  261.7 33.3 %collective-permute-start.41 = (bf16[4,2,2,24,3840]{4,3,2,1,0:T(8,128)(2,1)}, bf16[4,2,2,24,3840]{4,3,2,1,0:T(8,128)(2,1)S(1)}, u32[]{:S(2)}, u32[]{:S(2)}) collective-permute-start(bf16[4,2,2,24,3840]{4,3,2,1,0:T(8,128)(2,1)} %get-tuple-element.209), channel_id=1, source_target_pairs={{0,1},{1,0},{2,3},{3,2},{4,5},{5,4},{6,7},{7,6},{8,9},{9,8},{10,11... | collective-permute-start | bytes 8847368 | tf_op jit(solution)/shard_map/ppermute | solution.py:100
  272.0 16.6 %collective-permute-start.39 = (bf16[4,24,3072]{2,1,0:T(8,128)(2,1)}, bf16[4,24,3072]{2,1,0:T(8,128)(2,1)}, u32[]{:S(2)}, u32[]{:S(2)}) collective-permute-start(bf16[4,24,3072]{2,1,0:T(8,128)(2,1)} %get-tuple-element.215), channel_id=1, source_target_pairs={{0,2},{1,3},{2,0},{3,1},{4,6},{5,7},{6,4},{7,5},{8,10},{9,11},{10,... | collective-permute-start | bytes 1769480 | tf_op jit(solution)/shard_map/ppermute | solution.py:100
  272.5 16.0 %collective-permute-start.40 = (bf16[4,24,3072]{2,1,0:T(8,128)(2,1)}, bf16[4,24,3072]{2,1,0:T(8,128)(2,1)}, u32[]{:S(2)}, u32[]{:S(2)}) collective-permute-start(bf16[4,24,3072]{2,1,0:T(8,128)(2,1)} %get-tuple-element.217), channel_id=1, source_target_pairs={{0,4},{1,5},{2,6},{3,7},{4,0},{5,1},{6,2},{7,3},{8,12},{9,13},{10,... | collective-permute-start | bytes 1769480 | tf_op jit(solution)/shard_map/ppermute | solution.py:100
  291.2 44.9 %collective-permute-start.46 = (bf16[24,6144]{1,0:T(8,128)(2,1)}, bf16[24,6144]{1,0:T(8,128)(2,1)S(1)}, u32[]{:S(2)}, u32[]{:S(2)}) collective-permute-start(bf16[24,6144]{1,0:T(8,128)(2,1)} %get-tuple-element.225), channel_id=1, source_target_pairs={{0,8},{1,9},{2,10},{3,11},{4,12},{5,13},{6,14},{7,15},{8,16},{9,17... | collective-permute-start | bytes 884744 | tf_op jit(solution)/shard_map/ppermute | solution.py:100
  291.2 45.0 %collective-permute-start.47 = (bf16[24,6144]{1,0:T(8,128)(2,1)}, bf16[24,6144]{1,0:T(8,128)(2,1)}, u32[]{:S(2)}, u32[]{:S(2)}) collective-permute-start(bf16[24,6144]{1,0:T(8,128)(2,1)} %get-tuple-element.226), channel_id=1, source_target_pairs={{0,16},{1,17},{2,18},{3,19},{4,20},{5,21},{6,22},{7,23},{8,24},{9,... | collective-permute-start | bytes 884744 | tf_op jit(solution)/shard_map/ppermute | solution.py:100
  291.8 44.4 %collective-permute-start.48 = (bf16[24,6144]{1,0:T(8,128)(2,1)}, bf16[24,6144]{1,0:T(8,128)(2,1)}, u32[]{:S(2)}, u32[]{:S(2)}) collective-permute-start(bf16[24,6144]{1,0:T(8,128)(2,1)} %get-tuple-element.227), channel_id=1, source_target_pairs={{0,24},{1,25},{2,26},{3,27},{4,28},{5,29},{6,30},{7,31},{8,0},{9,1... | collective-permute-start | bytes 884744 | tf_op jit(solution)/shard_map/ppermute | solution.py:100
  302.1 18.4 %collective-permute-start.42 = (bf16[4,2,24,1920]{3,2,1,0:T(8,128)(2,1)}, bf16[4,2,24,1920]{3,2,1,0:T(8,128)(2,1)S(1)}, u32[]{:S(2)}, u32[]{:S(2)}) collective-permute-start(bf16[4,2,24,1920]{3,2,1,0:T(8,128)(2,1)} %get-tuple-element.231), channel_id=1, source_target_pairs={{0,4},{1,5},{2,6},{3,7},{4,0},{5,1},{6,2},{7,3},{8,12},{9,13},{10,... | collective-permute-start | bytes 2211848 | tf_op jit(solution)/shard_map/ppermute | solution.py:100
  303.6 16.9 %collective-permute-start.43 = (bf16[4,2,24,1920]{3,2,1,0:T(8,128)(2,1)}, bf16[4,2,24,1920]{3,2,1,0:T(8,128)(2,1)S(1)}, u32[]{:S(2)}, u32[]{:S(2)}) collective-permute-start(bf16[4,2,24,1920]{3,2,1,0:T(8,128)(2,1)} %get-tuple-element.233), channel_id=1, source_target_pairs={{0,2},{1,3},{2,0},{3,1},{4,6},{5,7},{6,4},{7,5},{8,10},{9,11},{10,... | collective-permute-start | bytes 2211848 | tf_op jit(solution)/shard_map/ppermute | solution.py:100
  326.2 12.8 %collective-permute-start.44 = (bf16[4,24,1920]{2,1,0:T(8,128)(2,1)}, bf16[4,24,1920]{2,1,0:T(8,128)(2,1)S(1)}, u32[]{:S(2)}, u32[]{:S(2)}) collective-permute-start(bf16[4,24,1920]{2,1,0:T(8,128)(2,1)} %get-tuple-element.241), channel_id=1, source_target_pairs={{0,2},{1,3},{2,0},{3,1},{4,6},{5,7},{6,4},{7,5},{8,10},{9,11},{10,... | collective-permute-start | bytes 1105928 | tf_op jit(solution)/shard_map/ppermute | solution.py:100
  326.7 12.3 %collective-permute-start.45 = (bf16[4,24,1920]{2,1,0:T(8,128)(2,1)}, bf16[4,24,1920]{2,1,0:T(8,128)(2,1)S(1)}, u32[]{:S(2)}, u32[]{:S(2)}) collective-permute-start(bf16[4,24,1920]{2,1,0:T(8,128)(2,1)} %get-tuple-element.243), channel_id=1, source_target_pairs={{0,4},{1,5},{2,6},{3,7},{4,0},{5,1},{6,2},{7,3},{8,12},{9,13},{10,... | collective-permute-start | bytes 1105928 | tf_op jit(solution)/shard_map/ppermute | solution.py:100
  336.1 24.5 %collective-permute-start.49 = (bf16[4,2,2,24,2304]{4,3,2,1,0:T(8,128)(2,1)}, bf16[4,2,2,24,2304]{4,3,2,1,0:T(8,128)(2,1)S(1)}, u32[]{:S(2)}, u32[]{:S(2)}) collective-permute-start(bf16[4,2,2,24,2304]{4,3,2,1,0:T(8,128)(2,1)} %get-tuple-element.245), channel_id=1, source_target_pairs={{0,1},{1,0},{2,3},{3,2},{4,5},{5,4},{6,7},{7,6},{8,9},{9,8},{10,11... | collective-permute-start | bytes 5308424 | tf_op jit(solution)/shard_map/ppermute | solution.py:100
  354.0 33.0 %collective-permute-start.55 = (bf16[24,3840]{1,0:T(8,128)(2,1)S(1)}, bf16[24,3840]{1,0:T(8,128)(2,1)S(1)}, u32[]{:S(2)}, u32[]{:S(2)}) collective-permute-start(bf16[24,3840]{1,0:T(8,128)(2,1)S(1)} %copy-done.44), channel_id=1, source_target_pairs={{0,8},{1,9},{2,10},{3,11},{4,12},{5,13},{6,14},{7,15},{8,16},{9,17... | collective-permute-start | bytes 552968 | tf_op jit(solution)/shard_map/ppermute | solution.py:100
  354.6 32.4 %collective-permute-start.56 = (bf16[24,3840]{1,0:T(8,128)(2,1)S(1)}, bf16[24,3840]{1,0:T(8,128)(2,1)S(1)}, u32[]{:S(2)}, u32[]{:S(2)}) collective-permute-start(bf16[24,3840]{1,0:T(8,128)(2,1)S(1)} %copy-done.43), channel_id=1, source_target_pairs={{0,16},{1,17},{2,18},{3,19},{4,20},{5,21},{6,22},{7,23},{8,24},{9,... | collective-permute-start | bytes 552968 | tf_op jit(solution)/shard_map/ppermute | solution.py:100
  355.9 31.1 %collective-permute-start.57 = (bf16[24,3840]{1,0:T(8,128)(2,1)S(1)}, bf16[24,3840]{1,0:T(8,128)(2,1)}, u32[]{:S(2)}, u32[]{:S(2)}) collective-permute-start(bf16[24,3840]{1,0:T(8,128)(2,1)S(1)} %copy-done.42), channel_id=1, source_target_pairs={{0,24},{1,25},{2,26},{3,27},{4,28},{5,29},{6,30},{7,31},{8,0},{9,1... | collective-permute-start | bytes 552968 | tf_op jit(solution)/shard_map/ppermute | solution.py:100
  366.6 11.9 %collective-permute-start.51 = (bf16[4,2,24,1152]{3,2,1,0:T(8,128)(2,1)}, bf16[4,2,24,1152]{3,2,1,0:T(8,128)(2,1)S(1)}, u32[]{:S(2)}, u32[]{:S(2)}) collective-permute-start(bf16[4,2,24,1152]{3,2,1,0:T(8,128)(2,1)} %get-tuple-element.271), channel_id=1, source_target_pairs={{0,4},{1,5},{2,6},{3,7},{4,0},{5,1},{6,2},{7,3},{8,12},{9,13},{10,... | collective-permute-start | bytes 1327112 | tf_op jit(solution)/shard_map/ppermute | solution.py:100
  367.9 12.7 %collective-permute-start.52 = (bf16[4,2,24,1280]{3,2,1,0:T(8,128)(2,1)}, bf16[4,2,24,1280]{3,2,1,0:T(8,128)(2,1)S(1)}, u32[]{:S(2)}, u32[]{:S(2)}) collective-permute-start(bf16[4,2,24,1280]{3,2,1,0:T(8,128)(2,1)} %get-tuple-element.273), channel_id=1, source_target_pairs={{0,2},{1,3},{2,0},{3,1},{4,6},{5,7},{6,4},{7,5},{8,10},{9,11},{10,... | collective-permute-start | bytes 1474568 | tf_op jit(solution)/shard_map/ppermute | solution.py:100
  394.7 9.7 %collective-permute-start.59 = (bf16[24,2432]{1,0:T(8,128)(2,1)}, bf16[24,2432]{1,0:T(8,128)(2,1)S(1)}, u32[]{:S(2)}, u32[]{:S(2)}) collective-permute-start(bf16[24,2432]{1,0:T(8,128)(2,1)} %get-tuple-element.294), channel_id=1, source_target_pairs={{0,16},{1,17},{2,18},{3,19},{4,20},{5,21},{6,22},{7,23},{8,24},{9,... | collective-permute-start | bytes 350216 | tf_op jit(solution)/shard_map/ppermute | solution.py:100
  395.8 8.5 %collective-permute-start.60 = (bf16[24,2432]{1,0:T(8,128)(2,1)}, bf16[24,2432]{1,0:T(8,128)(2,1)S(1)}, u32[]{:S(2)}, u32[]{:S(2)}) collective-permute-start(bf16[24,2432]{1,0:T(8,128)(2,1)} %get-tuple-element.295), channel_id=1, source_target_pairs={{0,24},{1,25},{2,26},{3,27},{4,28},{5,29},{6,30},{7,31},{8,0},{9,1... | collective-permute-start | bytes 350216 | tf_op jit(solution)/shard_map/ppermute | solution.py:100
  (63 other events, 589.7 us)

commit v5 on v4

--- a/solution.py
+++ b/solution.py
@@ -28,7 +28,7 @@
 MLP_ROWS = 512
 EDGE_ROWS = 256
 STEP = 32
-WIDE = 2
+WIDE = 3
 SELF_WIDE = 2
 
 epsilon = 1e-05

time: 414 us -> 414 us (level)
  no operation moved by 1% of the time
where the time goes in v5:
time: 414 us; the launch traced here: 411 us
  Pallas kernels  267 us (64%)
  starting transfers between devices  61.7 us (15%)
  waiting for transfers between devices  39.5 us (10%)
  local copies, waits for them, and re-layouts  36.3 us (9%)
  other arithmetic  5.2 us (1%)
    pallas_call x28, Pallas kernels, call(): pl.pallas_call(kernel, out_shape=outs, grid_spec=pltpu.PrefetchScalarGrid...  247 us
    ppermute x61, starting transfers between devices, shift(): return lax.ppermute(values, 'fsdp', shift_pairs(sizes, axis, step))  61.7 us
    ppermute x61, waiting for transfers between devices, shift(): return lax.ppermute(values, 'fsdp', shift_pairs(sizes, axis, step))  39.5 us
    pallas_call x3, Pallas kernels, place(): pl.pallas_call(functools.partial(place_kernel, keys, counts, sizes, split...  20.1 us
    unnamed x109, local copies, waits for them, and re-layouts  17.3 us
  transfers between devices with their start and end apart: 61, of which 18 were waited for; matrix products, arithmetic and copies ran while one was open for 5% of the time, Pallas kernels for 46%

profile of v5, /device:TPU:0, one launch (start us, length us, event | category | flops | bytes accessed | tf_op | source)
XLA Modules:
  0.0 410.9 jit_solution(9533370723162536661)
XLA Ops:
  4.9 4.1 %collective-permute-start.1 = (bf16[24,2432]{1,0:T(8,128)(2,1)S(1)}, bf16[24,2432]{1,0:T(8,128)(2,1)S(1)}, u32[]{:S(2)}, u32[]{:S(2)}) collective-permute-start(bf16[24,2432]{1,0:T(8,128)(2,1)S(1)} %get-tuple-element.303), channel_id=1, source_target_pairs={{0,16},{1,17},{2,18},{3,19},{4,20},{5,21},{6,22},{7,23},{8,24},{9,... | collective-permute-start | bytes 350216 | tf_op jit(solution)/shard_map/ppermute | solution.py:100
  10.6 2.2 collective-permute-start.2
  16.0 2.2 collective-permute-done.1
  22.1 2.0 collective-permute-start.5
  27.7 2.8 collective-permute-done.8.refs_2_
  38.0 3.8 collective-permute-done.4
  43.8 2.2 collective-permute-start.18
  50.8 5.4 %place.3 = bf16[4,8,24,2432]{3,2,1,0:T(8,128)(2,1)} custom-call(s32[4]{0:T(128)} %pad_add_fusion.me_ref, bf16[4,24,2432]{2,1,0:T(8,128)(2,1)} %copy-done.4, bf16[4,24,2432]{2,1,0:T(8,128)(2,1)} %collective-permute-done.6.refs_1_, bf16[4,24,2432]{2,1,0:T(8,128)(2,1)} %collective-permute-done.8.refs_2_, bf16[4,24,1216]{2,1,0:T(8,128)(2,1)} %collective-permute-done.7.refs_3_, ...), custom_call_target="tpu_custom_call" | custom-call | flops 6000000000 | tf_op jit(solution)/shard_map/place/pallas_call | solution.py:182
  57.9 11.8 %qkv_project.1 = (bf16[1024,768]{1,0:T(8,128)(2,1)}, bf16[1024,2304]{1,0:T(8,128)(2,1)}) custom-call(bf16[1024,768]{1,0:T(8,128)(2,1)} %x_ref.4, bf16[768,2432]{1,0:T(8,128)(2,1)} %bitcast.56, f32[16,768]{1,0:T(8,128)} %convert_bitcast_fusion.vec_ref, f32[2,512,128]{2,1,0:T(8,128)} %stack.81.cos_ref, f32[2,512,128]{2,1,0:T(8,128)} %stack.82.sin_ref), custom_call_target="tpu_custom_call" | custom-call | flops 11000000512 | tf_op jit(solution)/shard_map/qkv_project/pallas_call | solution.py:483
  69.8 2.8 collective-permute-done.18
  77.8 12.9 %self_attend.1 = (bf16[1024,768]{1,0:T(8,128)(2,1)}, f32[1024,768]{1,0:T(8,128)}) custom-call(s32[2,4]{1,0:T(2,128)} %lengths_ref.5, bf16[1024,2304]{1,0:T(8,128)(2,1)} %get-tuple-element.165.q_ref.k_ref.v_ref, bf16[1024,2304]{1,0:T(8,128)(2,1)} %get-tuple-element.165.q_ref.k_ref.v_ref, bf16[1024,2304]{1,0:T(8,128)(2,1)} %get-tuple-element.165.q_ref.k_ref.v_ref), custom_call_target="tpu_custom_call" | custom-call | flops 12000000000 | tf_op jit(solution)/shard_map/self_attend/pallas_call | solution.py:483
  94.2 6.4 %place.4 = bf16[4,8,24,3840]{3,2,1,0:T(8,128)(2,1)} custom-call(s32[4]{0:T(128)} %pad_add_fusion.me_ref, bf16[4,24,3840]{2,1,0:T(8,128)(2,1)} %copy-done.3, bf16[4,24,3840]{2,1,0:T(8,128)(2,1)} %collective-permute-done.15.refs_1_, bf16[4,24,3840]{2,1,0:T(8,128)(2,1)} %collective-permute-done.16.refs_2_, ...), custom_call_target="tpu_custom_call" | custom-call | flops 6000000000 | tf_op jit(solution)/shard_map/place/pallas_call | solution.py:182
  100.6 6.4 %ckv_project.1.k_ref.v_ref = bf16[1024,1536]{1,0:T(8,128)(2,1)} custom-call(bf16[1024,768]{1,0:T(8,128)(2,1)} %refs_0_, bf16[768,3840]{1,0:T(8,128)(2,1)} %bitcast.62, f32[16,768]{1,0:T(8,128)} %convert_bitcast_fusion.vec_ref), custom_call_target="tpu_custom_call" | custom-call | flops 6000000000 | tf_op jit(solution)/shard_map/ckv_project/pallas_call | solution.py:483
  107.0 8.0 %mid_forward.1 = (f32[1024,768]{1,0:T(8,128)}, bf16[1024,768]{1,0:T(8,128)(2,1)}, bf16[1024,768]{1,0:T(8,128)(2,1)}) custom-call(bf16[1024,768]{1,0:T(8,128)(2,1)} %get-tuple-element.166.o_ref.refs_2_, bf16[1024,768]{1,0:T(8,128)(2,1)} %x_ref.4, bf16[768,3840]{1,0:T(8,128)(2,1)} %bitcast.63, bf16[768,3840]{1,0:T(8,128)(2,1)} %bitcast.64, ...), custom_call_target="tpu_custom_call" | custom-call | flops 8000000000 | tf_op jit(solution)/shard_map/mid_forward/pallas_call | solution.py:483
  115.0 4.7 %collective-permute-done.28.refs_2_ = bf16[4,24,6144]{2,1,0:T(8,128)(2,1)S(1)} collective-permute-done((bf16[4,24,6144]{2,1,0:T(8,128)(2,1)S(1)}, bf16[4,24,6144]{2,1,0:T(8,128)(2,1)S(1)}, u32[]{:S(2)}, u32[]{:S(2)}) %collective-permute-start.28) | collective-permute-done | bytes 1179680 | tf_op jit(solution)/shard_map/ppermute | solution.py:100
  125.6 8.1 %cross_attend.1.co_ref.refs_6_ = bf16[1024,768]{1,0:T(8,128)(2,1)} custom-call(s32[2,16]{1,0:T(2,128)} %reshape.191.chosen_ref, bf16[1024,768]{1,0:T(8,128)(2,1)} %get-tuple-element.177.q_ref, bf16[1024,1536]{1,0:T(8,128)(2,1)} %ckv_project.1.k_ref.v_ref, bf16[1024,1536]{1,0:T(8,128)(2,1)} %ckv_project.1.k_ref.v_ref), custom_call_target="tpu_custom_call" | custom-call | flops 8000000000 | tf_op jit(solution)/shard_map/cross_attend/pallas_call | solution.py:483
  133.7 4.2 %collective-permute-done.30.refs_4_ = bf16[4,24,3072]{2,1,0:T(8,128)(2,1)} collective-permute-done((bf16[4,24,3072]{2,1,0:T(8,128)(2,1)S(1)}, bf16[4,24,3072]{2,1,0:T(8,128)(2,1)}, u32[]{:S(2)}, u32[]{:S(2)}) %collective-permute-start.30) | collective-permute-done | bytes 589856 | tf_op jit(solution)/shard_map/ppermute | solution.py:100
  143.2 8.3 %place.5 = (bf16[4,8,96,768]{3,2,1,0:T(8,128)(2,1)}, bf16[4,8,24,3072]{3,2,1,0:T(8,128)(2,1)}) custom-call(s32[4]{0:T(128)} %pad_add_fusion.me_ref, bf16[4,24,6144]{2,1,0:T(8,128)(2,1)} %copy-done, bf16[4,24,6144]{2,1,0:T(8,128)(2,1)} %collective-permute-done.27.refs_1_, bf16[4,24,6144]{2,1,0:T(8,128)(2,1)} %copy-done.5, ...), custom_call_target="tpu_custom_call" | custom-call | flops 6000000000 | tf_op jit(solution)/shard_map/place/pallas_call | solution.py:182
  151.5 38.7 %mlp_both.1 = (bf16[1024,768]{1,0:T(8,128)(2,1)}, bf16[1024,3072]{1,0:T(8,128)(2,1)}, bf16[1024,3072]{1,0:T(8,128)(2,1)}, bf16[1024,768]{1,0:T(8,128)(2,1)}, f32...) custom-call(f32[1024,768]{1,0:T(8,128)} %get-tuple-element.172.h1_re, ...), custom_call_target="tpu_custom_call" | custom-call | flops 38000001024 | tf_op jit(solution)/shard_map/mlp_both/pallas_call | solution.py:483
  190.2 10.1 %grad_blocks.3 = (bf16[4,2,2,24,6144]{4,3,2,1,0:T(8,128)(2,1)}, bf16[4,2,2,24,6144]{4,3,2,1,0:T(8,128)(2,1)}) custom-call(s32[4]{0:T(128)} %pad_add_fusion.me_ref, bf16[1024,3072]{1,0:T(8,128)(2,1)} %get-tuple-element.189.left_ref, bf16[1024,768]{1,0:T(8,128)(2,1)} %right_ref.1), custom_call_target="tpu_custom_call" | custom-call | flops 6000000000 | tf_op jit(solution)/shard_map/grad_blocks/pallas_call | solution.py:483
  200.3 10.1 %grad_blocks.4 = (bf16[4,2,2,24,6144]{4,3,2,1,0:T(8,128)(2,1)}, bf16[4,2,2,24,6144]{4,3,2,1,0:T(8,128)(2,1)}) custom-call(s32[4]{0:T(128)} %pad_add_fusion.me_ref, bf16[1024,768]{1,0:T(8,128)(2,1)} %get-tuple-element.187.left_ref, bf16[1024,3072]{1,0:T(8,128)(2,1)} %get-tuple-element.188.right_ref, ...), custom_call_target="tpu_custom_call", output_to_operand_aliasing={{0}: (3, {}), {1}: (4, {})} | custom-call | flops 6000000000 | tf_op jit(solution)/shard_map/grad_blocks/pallas_call | solution.py:483
  210.5 20.3 %cross_back.1 = (bf16[1024,768]{1,0:T(8,128)(2,1)}, bf16[1024,1536]{1,0:T(8,128)(2,1)}, f32[16,768]{1,0:T(8,128)}) custom-call(s32[2,16]{1,0:T(2,128)} %reshape.191.chosen_ref, bf16[1024,768]{1,0:T(8,128)(2,1)} %get-tuple-element.177.q_ref, bf16[1024,1536]{1,0:T(8,128)(2,1)} %ckv_project.1.k_ref.v_ref, bf16[1024,1536]{1,0:T(8,128)(2,1)} %ckv_project.1.k_ref.v_ref, ...), custom_call_target="tpu_custom_call" | custom-call | flops 20000000000 | tf_op jit(solution)/shard_map/cross_back/pallas_call | solution.py:483
  230.8 7.0 %fold_core.3 = (bf16[4,2,24,3072]{3,2,1,0:T(8,128)(2,1)}, bf16[4,2,24,3072]{3,2,1,0:T(8,128)(2,1)}, bf16[4,2,24,3072]{3,2,1,0:T(8,128)(2,1)}, bf16[4,2,24,3072]{3,2,1,0:T(8,128)(2,1)}) custom-call(s32[4]{0:T(128)} %pad_add_fusion.me_ref, bf16[4,2,2,24,6144]{4,3,2,1,0:T(8,128)(2,1)} %get-tuple-element.195.refs_0_, ...), custom_call_target="tpu_custom_call" | custom-call | flops 5000000000 | tf_op jit(solution)/shard_map/fold_core/pallas_call | solution.py:483
  239.9 8.9 %mid_back.1 = (f32[1024,768]{1,0:T(8,128)}, bf16[1024,768]{1,0:T(8,128)(2,1)}, bf16[1024,768]{1,0:T(8,128)(2,1)}, f32[8,768]{1,0:T(8,128)}) custom-call(bf16[1024,768]{1,0:T(8,128)(2,1)} %get-tuple-element.201.dcq_ref.refs_5_, f32[1024,768]{1,0:T(8,128)} %get-tuple-element.202.dh2_ref, f32[1024,768]{1,0:T(8,128)} %get-tuple-element.172.h1_ref, ...), custom_call_target="tpu_custom_call" | custom-call | flops 8999999488 | tf_op jit(solution)/shard_map/mid_back/pallas_call | solution.py:483
  248.8 12.9 %many_grads.1 = (bf16[4,2,2,24,3840]{4,3,2,1,0:T(8,128)(2,1)}, bf16[4,2,2,24,3840]{4,3,2,1,0:T(8,128)(2,1)}) custom-call(s32[4]{0:T(128)} %pad_add_fusion.me_ref, bf16[1024,768]{1,0:T(8,128)(2,1)} %refs_0_, bf16[1024,1536]{1,0:T(8,128)(2,1)} %get-tuple-element.274.refs_1_.dkv_ref, bf16[1024,768]{1,0:T(8,128)(2,1)} %get-tuple-element.166.o_ref.refs_2_, ...), custom_call_target="tpu_custom_call" | custom-call | flops 12999999488 | tf_op jit(solution)/shard_map/many_grads/pallas_call | solution.py:483
  267.6 4.3 %fold_side.3 = (bf16[4,24,3072]{2,1,0:T(8,128)(2,1)}, bf16[4,24,3072]{2,1,0:T(8,128)(2,1)}, bf16[4,24,3072]{2,1,0:T(8,128)(2,1)}, bf16[4,24,3072]{2,1,0:T(8,128)(2,1)}) custom-call(bf16[4,2,24,3072]{3,2,1,0:T(8,128)(2,1)} %get-tuple-element.210.refs_0_, bf16[4,2,24,3072]{3,2,1,0:T(8,128)(2,1)} %collective-permute-done.37.refs_1_, ...), custom_call_target="tpu_custom_call" | custom-call | flops 4000000000 | tf_op jit(solution)/shard_map/fold_side/pallas_call | solution.py:483
  273.0 15.6 %self_back.2.rest_0_ = bf16[1024,2304]{1,0:T(8,128)(2,1)} custom-call(s32[2,4]{1,0:T(2,128)} %lengths_ref.5, bf16[1024,2304]{1,0:T(8,128)(2,1)} %get-tuple-element.165.q_ref.k_ref.v_ref, bf16[1024,2304]{1,0:T(8,128)(2,1)} %get-tuple-element.165.q_ref.k_ref.v_ref, bf16[1024,2304]{1,0:T(8,128)(2,1)} %get-tuple-element.165.q_ref.k_ref.v_ref, ...), custom_call_target="tpu_custom_call" | custom-call | flops 15000000512 | tf_op jit(solution)/shard_map/self_back/pallas_call | solution.py:483
  288.5 2.7 fold_corner.3
  291.9 3.2 collective-permute-start.48
  296.8 5.4 %fold_core.4 = (bf16[4,2,24,1920]{3,2,1,0:T(8,128)(2,1)}, bf16[4,2,24,1920]{3,2,1,0:T(8,128)(2,1)}, bf16[4,2,24,1920]{3,2,1,0:T(8,128)(2,1)}, bf16[4,2,24,1920]{3,2,1,0:T(8,128)(2,1)}) custom-call(s32[4]{0:T(128)} %pad_add_fusion.me_ref, bf16[4,2,2,24,3840]{4,3,2,1,0:T(8,128)(2,1)} %get-tuple-element.228.refs_0_, bf16[4,2,2,24,3840]{4,3,2,1,0:T(8,128)(2,1)} %copy-done.21), custom_call_target="tpu_custom_call" | custom-call | flops 5000000000 | tf_op jit(solution)/shard_map/fold_core/pallas_call | solution.py:483
  305.2 15.3 %self_back.3.right_ref.dqkv_ref = bf16[1024,2304]{1,0:T(8,128)(2,1)} custom-call(s32[2,4]{1,0:T(2,128)} %lengths_ref.5, bf16[1024,2304]{1,0:T(8,128)(2,1)} %get-tuple-element.165.q_ref.k_ref.v_ref, bf16[1024,2304]{1,0:T(8,128)(2,1)} %get-tuple-element.165.q_ref.k_ref.v_ref, ...), custom_call_target="tpu_custom_call", output_to_operand_aliasing={{}: (8, {})} | custom-call | flops 15000000512 | tf_op jit(solution)/shard_map/self_back/pallas_call | solution.py:483
  322.2 3.9 fold_side.4
  327.6 8.5 %grad_blocks.5 = (bf16[4,2,2,24,2304]{4,3,2,1,0:T(8,128)(2,1)}, bf16[4,2,2,24,2304]{4,3,2,1,0:T(8,128)(2,1)}) custom-call(s32[4]{0:T(128)} %pad_add_fusion.me_ref, bf16[1024,768]{1,0:T(8,128)(2,1)} %get-tuple-element.244.left_ref, bf16[1024,2304]{1,0:T(8,128)(2,1)} %self_back.3.right_ref.dqkv_ref), custom_call_target="tpu_custom_call" | custom-call | flops 6000000000 | tf_op jit(solution)/shard_map/grad_blocks/pallas_call | solution.py:483
  336.8 2.1 fold_z.3
  339.7 2.2 fold_corner.4
  342.0 10.2 %token_back.1 = (f32[1024,768]{1,0:T(8,128)}, f32[8,768]{1,0:T(8,128)}, f32[1,2304]{1,0:T(1,128)}) custom-call(bf16[1024,2304]{1,0:T(8,128)(2,1)} %self_back.3.right_ref.dqkv_ref, f32[1024,768]{1,0:T(8,128)} %get-tuple-element.260.dh1_ref, bf16[1024,768]{1,0:T(8,128)(2,1)} %x_ref.4, bf16[768,2432]{1,0:T(8,128)(2,1)} %bitcast.58, ...), custom_call_target="tpu_custom_call" | custom-call | flops 10000000000 | tf_op jit(solution)/shard_map/token_back/pallas_call | solution.py:483
  355.9 2.8 collective-permute-start.57
  361.8 4.8 %fold_core.5 = (bf16[4,2,24,1152]{3,2,1,0:T(8,128)(2,1)}, bf16[4,2,24,1152]{3,2,1,0:T(8,128)(2,1)}, bf16[4,2,24,1280]{3,2,1,0:T(8,128)(2,1)}, bf16[4,2,24,1280]{3,2,1,0:T(8,128)(2,1)}) custom-call(s32[4]{0:T(128)} %pad_add_fusion.me_ref, bf16[4,2,2,24,2304]{4,3,2,1,0:T(8,128)(2,1)} %get-tuple-element.262.refs_0_, bf16[4,2,2,24,2304]{4,3,2,1,0:T(8,128)(2,1)} %copy-done.22, ...), custom_call_target="tpu_custom_call" | custom-call | flops 5000000000 | tf_op jit(solution)/shard_map/fold_core/pallas_call | solution.py:483
  369.5 6.7 %neighbour_back.1 = f32[1024,768]{1,0:T(8,128)} custom-call(bf16[1024,1536]{1,0:T(8,128)(2,1)} %get-tuple-element.274.refs_1_.dkv_ref, bf16[768,3840]{1,0:T(8,128)(2,1)} %bitcast.68), custom_call_target="tpu_custom_call" | custom-call | flops 6000000000 | tf_op jit(solution)/shard_map/neighbour_back/pallas_call | solution.py:483
  376.2 2.2 collective-permute-done.51.refs_1_
  378.4 2.3 collective-permute-done.52.refs_3_
  381.5 3.5 fold_side.5
  387.8 2.0 fold_z.4
  389.7 2.0 collective-permute-done.53.refs_1_
  392.5 2.1 fold_corner.5
  395.8 2.9 collective-permute-start.60
  398.7 3.1 collective-permute-done.58.refs_1_
  401.9 2.5 collective-permute-done.59.refs_2_
  (259 shorter events, 92.4 us)
Async XLA Ops:
  4.9 13.2 %collective-permute-start.1 = (bf16[24,2432]{1,0:T(8,128)(2,1)S(1)}, bf16[24,2432]{1,0:T(8,128)(2,1)S(1)}, u32[]{:S(2)}, u32[]{:S(2)}) collective-permute-start(bf16[24,2432]{1,0:T(8,128)(2,1)S(1)} %get-tuple-element.303), channel_id=1, source_target_pairs={{0,16},{1,17},{2,18},{3,19},{4,20},{5,21},{6,22},{7,23},{8,24},{9,... | collective-permute-start | bytes 350216 | tf_op jit(solution)/shard_map/ppermute | solution.py:100
  9.1 9.1 %collective-permute-start = (bf16[24,2432]{1,0:T(8,128)(2,1)S(1)}, bf16[24,2432]{1,0:T(8,128)(2,1)S(1)}, u32[]{:S(2)}, u32[]{:S(2)}) collective-permute-start(bf16[24,2432]{1,0:T(8,128)(2,1)S(1)} %get-tuple-element.303), channel_id=1, source_target_pairs={{0,8},{1,9},{2,10},{3,11},{4,12},{5,13},{6,14},{7,15},{8,16},{9,17... | collective-permute-start | bytes 350216 | tf_op jit(solution)/shard_map/ppermute | solution.py:100
  10.6 8.2 %collective-permute-start.2 = (bf16[24,2432]{1,0:T(8,128)(2,1)S(1)}, bf16[24,2432]{1,0:T(8,128)(2,1)S(1)}, u32[]{:S(2)}, u32[]{:S(2)}) collective-permute-start(bf16[24,2432]{1,0:T(8,128)(2,1)S(1)} %get-tuple-element.303), channel_id=1, source_target_pairs={{0,24},{1,25},{2,26},{3,27},{4,28},{5,29},{6,30},{7,31},{8,0},{9,1... | collective-permute-start | bytes 350216 | tf_op jit(solution)/shard_map/ppermute | solution.py:100
  18.9 11.6 %collective-permute-start.8 = (bf16[4,24,2432]{2,1,0:T(8,128)(2,1)S(1)}, bf16[4,24,2432]{2,1,0:T(8,128)(2,1)}, u32[]{:S(2)}, u32[]{:S(2)}) collective-permute-start(bf16[4,24,2432]{2,1,0:T(8,128)(2,1)S(1)} %pad_maximum_fusion.2.refs_0_), channel_id=1, source_target_pairs={{0,4},{1,5},{2,6},{3,7},{4,0},{5,1},{6,2},{7,3},{8,12},{9,13},{10,... | collective-permute-start | bytes 1400840 | tf_op jit(solution)/shard_map/ppermute | solution.py:100
  20.6 12.4 %collective-permute-start.6 = (bf16[4,24,2432]{2,1,0:T(8,128)(2,1)S(1)}, bf16[4,24,2432]{2,1,0:T(8,128)(2,1)}, u32[]{:S(2)}, u32[]{:S(2)}) collective-permute-start(bf16[4,24,2432]{2,1,0:T(8,128)(2,1)S(1)} %pad_maximum_fusion.2.refs_0_), channel_id=1, source_target_pairs={{0,2},{1,3},{2,0},{3,1},{4,6},{5,7},{6,4},{7,5},{8,10},{9,11},{10,... | collective-permute-start | bytes 1400840 | tf_op jit(solution)/shard_map/ppermute | solution.py:100
  22.1 15.9 %collective-permute-start.5 = (bf16[24,3840]{1,0:T(8,128)(2,1)S(1)}, bf16[24,3840]{1,0:T(8,128)(2,1)S(1)}, u32[]{:S(2)}, u32[]{:S(2)}) collective-permute-start(bf16[24,3840]{1,0:T(8,128)(2,1)S(1)} %pad_maximum_fusion.3), channel_id=1, source_target_pairs={{0,24},{1,25},{2,26},{3,27},{4,28},{5,29},{6,30},{7,31},{8,0},{9,1... | collective-permute-start | bytes 552968 | tf_op jit(solution)/shard_map/ppermute | solution.py:100
  24.2 17.6 %collective-permute-start.4 = (bf16[24,3840]{1,0:T(8,128)(2,1)S(1)}, bf16[24,3840]{1,0:T(8,128)(2,1)S(1)}, u32[]{:S(2)}, u32[]{:S(2)}) collective-permute-start(bf16[24,3840]{1,0:T(8,128)(2,1)S(1)} %pad_maximum_fusion.3), channel_id=1, source_target_pairs={{0,16},{1,17},{2,18},{3,19},{4,20},{5,21},{6,22},{7,23},{8,24},{9,... | collective-permute-start | bytes 552968 | tf_op jit(solution)/shard_map/ppermute | solution.py:100
  25.8 16.0 %collective-permute-start.3 = (bf16[24,3840]{1,0:T(8,128)(2,1)S(1)}, bf16[24,3840]{1,0:T(8,128)(2,1)S(1)}, u32[]{:S(2)}, u32[]{:S(2)}) collective-permute-start(bf16[24,3840]{1,0:T(8,128)(2,1)S(1)} %pad_maximum_fusion.3), channel_id=1, source_target_pairs={{0,8},{1,9},{2,10},{3,11},{4,12},{5,13},{6,14},{7,15},{8,16},{9,17... | collective-permute-start | bytes 552968 | tf_op jit(solution)/shard_map/ppermute | solution.py:100
  31.6 10.7 %collective-permute-start.9 = (bf16[4,24,1216]{2,1,0:T(8,128)(2,1)S(1)}, bf16[4,24,1216]{2,1,0:T(8,128)(2,1)}, u32[]{:S(2)}, u32[]{:S(2)}) collective-permute-start(bf16[4,24,1216]{2,1,0:T(8,128)(2,1)S(1)} %slice.92), channel_id=1, source_target_pairs={{0,2},{1,3},{2,0},{3,1},{4,6},{5,7},{6,4},{7,5},{8,10},{9,11},{10,... | collective-permute-start | bytes 700424 | tf_op jit(solution)/shard_map/ppermute | solution.py:100
  33.9 8.5 %collective-permute-start.7 = (bf16[4,24,1216]{2,1,0:T(8,128)(2,1)S(1)}, bf16[4,24,1216]{2,1,0:T(8,128)(2,1)}, u32[]{:S(2)}, u32[]{:S(2)}) collective-permute-start(bf16[4,24,1216]{2,1,0:T(8,128)(2,1)S(1)} %slice.91), channel_id=1, source_target_pairs={{0,4},{1,5},{2,6},{3,7},{4,0},{5,1},{6,2},{7,3},{8,12},{9,13},{10,... | collective-permute-start | bytes 700424 | tf_op jit(solution)/shard_map/ppermute | solution.py:100
  43.0 26.7 %collective-permute-start.19 = (bf16[24,6144]{1,0:T(8,128)(2,1)S(1)}, bf16[24,6144]{1,0:T(8,128)(2,1)S(1)}, u32[]{:S(2)}, u32[]{:S(2)}) collective-permute-start(bf16[24,6144]{1,0:T(8,128)(2,1)S(1)} %constant_dynamic-update-slice_fusion), channel_id=1, source_target_pairs={{0,24},{1,25},{2,26},{3,27},{4,28},{5,29},{6,30},{7,31},{8,0},{9,1... | collective-permute-start | bytes 884744 | tf_op jit(solution)/shard_map/ppermute | solution.py:100
  43.8 28.8 %collective-permute-start.18 = (bf16[24,6144]{1,0:T(8,128)(2,1)S(1)}, bf16[24,6144]{1,0:T(8,128)(2,1)S(1)}, u32[]{:S(2)}, u32[]{:S(2)}) collective-permute-start(bf16[24,6144]{1,0:T(8,128)(2,1)S(1)} %constant_dynamic-update-slice_fusion), channel_id=1, source_target_pairs={{0,16},{1,17},{2,18},{3,19},{4,20},{5,21},{6,22},{7,23},{8,24},{9,... | collective-permute-start | bytes 884744 | tf_op jit(solution)/shard_map/ppermute | solution.py:100
  46.1 26.5 %collective-permute-start.17 = (bf16[24,6144]{1,0:T(8,128)(2,1)S(1)}, bf16[24,6144]{1,0:T(8,128)(2,1)S(1)}, u32[]{:S(2)}, u32[]{:S(2)}) collective-permute-start(bf16[24,6144]{1,0:T(8,128)(2,1)S(1)} %constant_dynamic-update-slice_fusion), channel_id=1, source_target_pairs={{0,8},{1,9},{2,10},{3,11},{4,12},{5,13},{6,14},{7,15},{8,16},{9,17... | collective-permute-start | bytes 884744 | tf_op jit(solution)/shard_map/ppermute | solution.py:100
  48.0 24.8 %collective-permute-start.16 = (bf16[4,24,3840]{2,1,0:T(8,128)(2,1)S(1)}, bf16[4,24,3840]{2,1,0:T(8,128)(2,1)}, u32[]{:S(2)}, u32[]{:S(2)}) collective-permute-start(bf16[4,24,3840]{2,1,0:T(8,128)(2,1)S(1)} %pad_maximum_fusion.1.refs_0_), channel_id=1, source_target_pairs={{0,4},{1,5},{2,6},{3,7},{4,0},{5,1},{6,2},{7,3},{8,12},{9,13},{10,... | collective-permute-start | bytes 2211848 | tf_op jit(solution)/shard_map/ppermute | solution.py:100
  50.3 22.5 %collective-permute-start.15 = (bf16[4,24,3840]{2,1,0:T(8,128)(2,1)S(1)}, bf16[4,24,3840]{2,1,0:T(8,128)(2,1)}, u32[]{:S(2)}, u32[]{:S(2)}) collective-permute-start(bf16[4,24,3840]{2,1,0:T(8,128)(2,1)S(1)} %pad_maximum_fusion.1.refs_0_), channel_id=1, source_target_pairs={{0,2},{1,3},{2,0},{3,1},{4,6},{5,7},{6,4},{7,5},{8,10},{9,11},{10,... | collective-permute-start | bytes 2211848 | tf_op jit(solution)/shard_map/ppermute | solution.py:100
  69.7 21.0 %collective-permute-start.22 = (bf16[4,24,3840]{2,1,0:T(8,128)(2,1)S(1)}, bf16[4,24,3840]{2,1,0:T(8,128)(2,1)}, u32[]{:S(2)}, u32[]{:S(2)}) collective-permute-start(bf16[4,24,3840]{2,1,0:T(8,128)(2,1)S(1)} %pad_maximum_fusion.1.refs_0_), channel_id=1, source_target_pairs={{0,1},{1,0},{2,3},{3,2},{4,5},{5,4},{6,7},{7,6},{8,9},{9,8},{10,11... | collective-permute-start | bytes 2211848 | tf_op jit(solution)/shard_map/ppermute | solution.py:100
  74.1 16.7 %collective-permute-start.23 = (bf16[4,24,3840]{2,1,0:T(8,128)(2,1)}, bf16[4,24,3840]{2,1,0:T(8,128)(2,1)S(1)}, u32[]{:S(2)}, u32[]{:S(2)}) collective-permute-start(bf16[4,24,3840]{2,1,0:T(8,128)(2,1)} %collective-permute-done.15.refs_1_), channel_id=1, source_target_pairs={{0,1},{1,0},{2,3},{3,2},{4,5},{5,4},{6,7},{7,6},{8,9},{9,8},{10,11... | collective-permute-start | bytes 2211848 | tf_op jit(solution)/shard_map/ppermute | solution.py:100
  75.2 15.6 %collective-permute-start.24 = (bf16[4,24,3840]{2,1,0:T(8,128)(2,1)}, bf16[4,24,3840]{2,1,0:T(8,128)(2,1)}, u32[]{:S(2)}, u32[]{:S(2)}) collective-permute-start(bf16[4,24,3840]{2,1,0:T(8,128)(2,1)} %collective-permute-done.16.refs_2_), channel_id=1, source_target_pairs={{0,1},{1,0},{2,3},{3,2},{4,5},{5,4},{6,7},{7,6},{8,9},{9,8},{10,11... | collective-permute-start | bytes 2211848 | tf_op jit(solution)/shard_map/ppermute | solution.py:100
  75.8 15.0 %collective-permute-start.21 = (bf16[4,24,1920]{2,1,0:T(8,128)(2,1)S(1)}, bf16[4,24,1920]{2,1,0:T(8,128)(2,1)S(1)}, u32[]{:S(2)}, u32[]{:S(2)}) collective-permute-start(bf16[4,24,1920]{2,1,0:T(8,128)(2,1)S(1)} %slice.73), channel_id=1, source_target_pairs={{0,2},{1,3},{2,0},{3,1},{4,6},{5,7},{6,4},{7,5},{8,10},{9,11},{10,... | collective-permute-start | bytes 1105928 | tf_op jit(solution)/shard_map/ppermute | solution.py:100
  76.3 14.4 %collective-permute-start.20 = (bf16[4,24,1920]{2,1,0:T(8,128)(2,1)S(1)}, bf16[4,24,1920]{2,1,0:T(8,128)(2,1)}, u32[]{:S(2)}, u32[]{:S(2)}) collective-permute-start(bf16[4,24,1920]{2,1,0:T(8,128)(2,1)S(1)} %slice.72), channel_id=1, source_target_pairs={{0,4},{1,5},{2,6},{3,7},{4,0},{5,1},{6,2},{7,3},{8,12},{9,13},{10,... | collective-permute-start | bytes 1105928 | tf_op jit(solution)/shard_map/ppermute | solution.py:100
  91.4 42.3 %collective-permute-start.31 = (bf16[4,24,6144]{2,1,0:T(8,128)(2,1)S(1)}, bf16[4,24,6144]{2,1,0:T(8,128)(2,1)}, u32[]{:S(2)}, u32[]{:S(2)}) collective-permute-start(bf16[4,24,6144]{2,1,0:T(8,128)(2,1)S(1)} %pad_maximum_fusion.refs_0_), channel_id=1, source_target_pairs={{0,1},{1,0},{2,3},{3,2},{4,5},{5,4},{6,7},{7,6},{8,9},{9,8},{10,11... | collective-permute-start | bytes 3538952 | tf_op jit(solution)/shard_map/ppermute | solution.py:100
  91.5 28.3 %collective-permute-start.28 = (bf16[4,24,6144]{2,1,0:T(8,128)(2,1)S(1)}, bf16[4,24,6144]{2,1,0:T(8,128)(2,1)S(1)}, u32[]{:S(2)}, u32[]{:S(2)}) collective-permute-start(bf16[4,24,6144]{2,1,0:T(8,128)(2,1)S(1)} %pad_maximum_fusion.refs_0_), channel_id=1, source_target_pairs={{0,4},{1,5},{2,6},{3,7},{4,0},{5,1},{6,2},{7,3},{8,12},{9,13},{10,... | collective-permute-start | bytes 3538952 | tf_op jit(solution)/shard_map/ppermute | solution.py:100
  92.0 28.1 %collective-permute-start.27 = (bf16[4,24,6144]{2,1,0:T(8,128)(2,1)S(1)}, bf16[4,24,6144]{2,1,0:T(8,128)(2,1)}, u32[]{:S(2)}, u32[]{:S(2)}) collective-permute-start(bf16[4,24,6144]{2,1,0:T(8,128)(2,1)S(1)} %pad_maximum_fusion.refs_0_), channel_id=1, source_target_pairs={{0,2},{1,3},{2,0},{3,1},{4,6},{5,7},{6,4},{7,5},{8,10},{9,11},{10,... | collective-permute-start | bytes 3538952 | tf_op jit(solution)/shard_map/ppermute | solution.py:100
  120.1 19.0 %collective-permute-start.32 = (bf16[4,24,6144]{2,1,0:T(8,128)(2,1)}, bf16[4,24,6144]{2,1,0:T(8,128)(2,1)}, u32[]{:S(2)}, u32[]{:S(2)}) collective-permute-start(bf16[4,24,6144]{2,1,0:T(8,128)(2,1)} %collective-permute-done.27.refs_1_), channel_id=1, source_target_pairs={{0,1},{1,0},{2,3},{3,2},{4,5},{5,4},{6,7},{7,6},{8,9},{9,8},{10,11... | collective-permute-start | bytes 3538952 | tf_op jit(solution)/shard_map/ppermute | solution.py:100
  120.1 19.0 %collective-permute-start.33 = (bf16[4,24,6144]{2,1,0:T(8,128)(2,1)S(1)}, bf16[4,24,6144]{2,1,0:T(8,128)(2,1)}, u32[]{:S(2)}, u32[]{:S(2)}) collective-permute-start(bf16[4,24,6144]{2,1,0:T(8,128)(2,1)S(1)} %collective-permute-done.28.refs_2_), channel_id=1, source_target_pairs={{0,1},{1,0},{2,3},{3,2},{4,5},{5,4},{6,7},{7,6},{8,9},{9,8},{10,11... | collective-permute-start | bytes 3538952 | tf_op jit(solution)/shard_map/ppermute | solution.py:100
  122.5 15.4 %collective-permute-start.30 = (bf16[4,24,3072]{2,1,0:T(8,128)(2,1)S(1)}, bf16[4,24,3072]{2,1,0:T(8,128)(2,1)}, u32[]{:S(2)}, u32[]{:S(2)}) collective-permute-start(bf16[4,24,3072]{2,1,0:T(8,128)(2,1)S(1)} %slice.75), channel_id=1, source_target_pairs={{0,2},{1,3},{2,0},{3,1},{4,6},{5,7},{6,4},{7,5},{8,10},{9,11},{10,... | collective-permute-start | bytes 1769480 | tf_op jit(solution)/shard_map/ppermute | solution.py:100
  124.0 15.1 %collective-permute-start.29 = (bf16[4,24,3072]{2,1,0:T(8,128)(2,1)S(1)}, bf16[4,24,3072]{2,1,0:T(8,128)(2,1)}, u32[]{:S(2)}, u32[]{:S(2)}) collective-permute-start(bf16[4,24,3072]{2,1,0:T(8,128)(2,1)S(1)} %slice.74), channel_id=1, source_target_pairs={{0,4},{1,5},{2,6},{3,7},{4,0},{5,1},{6,2},{7,3},{8,12},{9,13},{10,... | collective-permute-start | bytes 1769480 | tf_op jit(solution)/shard_map/ppermute | solution.py:100
  210.4 20.4 %collective-permute-start.36 = (bf16[4,2,2,24,6144]{4,3,2,1,0:T(8,128)(2,1)}, bf16[4,2,2,24,6144]{4,3,2,1,0:T(8,128)(2,1)}, u32[]{:S(2)}, u32[]{:S(2)}) collective-permute-start(bf16[4,2,2,24,6144]{4,3,2,1,0:T(8,128)(2,1)} %get-tuple-element.192), channel_id=1, source_target_pairs={{0,1},{1,0},{2,3},{3,2},{4,5},{5,4},{6,7},{7,6},{8,9},{9,8},{10,11... | collective-permute-start | bytes 14155784 | tf_op jit(solution)/shard_map/ppermute | solution.py:100
  237.8 28.6 %collective-permute-start.37 = (bf16[4,2,24,3072]{3,2,1,0:T(8,128)(2,1)}, bf16[4,2,24,3072]{3,2,1,0:T(8,128)(2,1)}, u32[]{:S(2)}, u32[]{:S(2)}) collective-permute-start(bf16[4,2,24,3072]{3,2,1,0:T(8,128)(2,1)} %get-tuple-element.198), channel_id=1, source_target_pairs={{0,4},{1,5},{2,6},{3,7},{4,0},{5,1},{6,2},{7,3},{8,12},{9,13},{10,... | collective-permute-start | bytes 3538952 | tf_op jit(solution)/shard_map/ppermute | solution.py:100
  239.4 28.3 %collective-permute-start.38 = (bf16[4,2,24,3072]{3,2,1,0:T(8,128)(2,1)}, bf16[4,2,24,3072]{3,2,1,0:T(8,128)(2,1)}, u32[]{:S(2)}, u32[]{:S(2)}) collective-permute-start(bf16[4,2,24,3072]{3,2,1,0:T(8,128)(2,1)} %get-tuple-element.200), channel_id=1, source_target_pairs={{0,2},{1,3},{2,0},{3,1},{4,6},{5,7},{6,4},{7,5},{8,10},{9,11},{10,... | collective-permute-start | bytes 3538952 | tf_op jit(solution)/shard_map/ppermute | solution.py:100
  261.8 33.3 %collective-permute-start.41 = (bf16[4,2,2,24,3840]{4,3,2,1,0:T(8,128)(2,1)}, bf16[4,2,2,24,3840]{4,3,2,1,0:T(8,128)(2,1)S(1)}, u32[]{:S(2)}, u32[]{:S(2)}) collective-permute-start(bf16[4,2,2,24,3840]{4,3,2,1,0:T(8,128)(2,1)} %get-tuple-element.209), channel_id=1, source_target_pairs={{0,1},{1,0},{2,3},{3,2},{4,5},{5,4},{6,7},{7,6},{8,9},{9,8},{10,11... | collective-permute-start | bytes 8847368 | tf_op jit(solution)/shard_map/ppermute | solution.py:100
  271.9 16.6 %collective-permute-start.39 = (bf16[4,24,3072]{2,1,0:T(8,128)(2,1)}, bf16[4,24,3072]{2,1,0:T(8,128)(2,1)}, u32[]{:S(2)}, u32[]{:S(2)}) collective-permute-start(bf16[4,24,3072]{2,1,0:T(8,128)(2,1)} %get-tuple-element.215), channel_id=1, source_target_pairs={{0,2},{1,3},{2,0},{3,1},{4,6},{5,7},{6,4},{7,5},{8,10},{9,11},{10,... | collective-permute-start | bytes 1769480 | tf_op jit(solution)/shard_map/ppermute | solution.py:100
  272.5 16.0 %collective-permute-start.40 = (bf16[4,24,3072]{2,1,0:T(8,128)(2,1)}, bf16[4,24,3072]{2,1,0:T(8,128)(2,1)}, u32[]{:S(2)}, u32[]{:S(2)}) collective-permute-start(bf16[4,24,3072]{2,1,0:T(8,128)(2,1)} %get-tuple-element.217), channel_id=1, source_target_pairs={{0,4},{1,5},{2,6},{3,7},{4,0},{5,1},{6,2},{7,3},{8,12},{9,13},{10,... | collective-permute-start | bytes 1769480 | tf_op jit(solution)/shard_map/ppermute | solution.py:100
  291.2 44.8 %collective-permute-start.46 = (bf16[24,6144]{1,0:T(8,128)(2,1)}, bf16[24,6144]{1,0:T(8,128)(2,1)S(1)}, u32[]{:S(2)}, u32[]{:S(2)}) collective-permute-start(bf16[24,6144]{1,0:T(8,128)(2,1)} %get-tuple-element.225), channel_id=1, source_target_pairs={{0,8},{1,9},{2,10},{3,11},{4,12},{5,13},{6,14},{7,15},{8,16},{9,17... | collective-permute-start | bytes 884744 | tf_op jit(solution)/shard_map/ppermute | solution.py:100
  291.2 44.9 %collective-permute-start.47 = (bf16[24,6144]{1,0:T(8,128)(2,1)}, bf16[24,6144]{1,0:T(8,128)(2,1)}, u32[]{:S(2)}, u32[]{:S(2)}) collective-permute-start(bf16[24,6144]{1,0:T(8,128)(2,1)} %get-tuple-element.226), channel_id=1, source_target_pairs={{0,16},{1,17},{2,18},{3,19},{4,20},{5,21},{6,22},{7,23},{8,24},{9,... | collective-permute-start | bytes 884744 | tf_op jit(solution)/shard_map/ppermute | solution.py:100
  291.9 44.3 %collective-permute-start.48 = (bf16[24,6144]{1,0:T(8,128)(2,1)}, bf16[24,6144]{1,0:T(8,128)(2,1)}, u32[]{:S(2)}, u32[]{:S(2)}) collective-permute-start(bf16[24,6144]{1,0:T(8,128)(2,1)} %get-tuple-element.227), channel_id=1, source_target_pairs={{0,24},{1,25},{2,26},{3,27},{4,28},{5,29},{6,30},{7,31},{8,0},{9,1... | collective-permute-start | bytes 884744 | tf_op jit(solution)/shard_map/ppermute | solution.py:100
  302.2 18.4 %collective-permute-start.42 = (bf16[4,2,24,1920]{3,2,1,0:T(8,128)(2,1)}, bf16[4,2,24,1920]{3,2,1,0:T(8,128)(2,1)S(1)}, u32[]{:S(2)}, u32[]{:S(2)}) collective-permute-start(bf16[4,2,24,1920]{3,2,1,0:T(8,128)(2,1)} %get-tuple-element.231), channel_id=1, source_target_pairs={{0,4},{1,5},{2,6},{3,7},{4,0},{5,1},{6,2},{7,3},{8,12},{9,13},{10,... | collective-permute-start | bytes 2211848 | tf_op jit(solution)/shard_map/ppermute | solution.py:100
  303.7 16.8 %collective-permute-start.43 = (bf16[4,2,24,1920]{3,2,1,0:T(8,128)(2,1)}, bf16[4,2,24,1920]{3,2,1,0:T(8,128)(2,1)S(1)}, u32[]{:S(2)}, u32[]{:S(2)}) collective-permute-start(bf16[4,2,24,1920]{3,2,1,0:T(8,128)(2,1)} %get-tuple-element.233), channel_id=1, source_target_pairs={{0,2},{1,3},{2,0},{3,1},{4,6},{5,7},{6,4},{7,5},{8,10},{9,11},{10,... | collective-permute-start | bytes 2211848 | tf_op jit(solution)/shard_map/ppermute | solution.py:100
  326.2 12.7 %collective-permute-start.44 = (bf16[4,24,1920]{2,1,0:T(8,128)(2,1)}, bf16[4,24,1920]{2,1,0:T(8,128)(2,1)S(1)}, u32[]{:S(2)}, u32[]{:S(2)}) collective-permute-start(bf16[4,24,1920]{2,1,0:T(8,128)(2,1)} %get-tuple-element.241), channel_id=1, source_target_pairs={{0,2},{1,3},{2,0},{3,1},{4,6},{5,7},{6,4},{7,5},{8,10},{9,11},{10,... | collective-permute-start | bytes 1105928 | tf_op jit(solution)/shard_map/ppermute | solution.py:100
  326.8 12.1 %collective-permute-start.45 = (bf16[4,24,1920]{2,1,0:T(8,128)(2,1)}, bf16[4,24,1920]{2,1,0:T(8,128)(2,1)S(1)}, u32[]{:S(2)}, u32[]{:S(2)}) collective-permute-start(bf16[4,24,1920]{2,1,0:T(8,128)(2,1)} %get-tuple-element.243), channel_id=1, source_target_pairs={{0,4},{1,5},{2,6},{3,7},{4,0},{5,1},{6,2},{7,3},{8,12},{9,13},{10,... | collective-permute-start | bytes 1105928 | tf_op jit(solution)/shard_map/ppermute | solution.py:100
  336.1 24.5 %collective-permute-start.49 = (bf16[4,2,2,24,2304]{4,3,2,1,0:T(8,128)(2,1)}, bf16[4,2,2,24,2304]{4,3,2,1,0:T(8,128)(2,1)S(1)}, u32[]{:S(2)}, u32[]{:S(2)}) collective-permute-start(bf16[4,2,2,24,2304]{4,3,2,1,0:T(8,128)(2,1)} %get-tuple-element.245), channel_id=1, source_target_pairs={{0,1},{1,0},{2,3},{3,2},{4,5},{5,4},{6,7},{7,6},{8,9},{9,8},{10,11... | collective-permute-start | bytes 5308424 | tf_op jit(solution)/shard_map/ppermute | solution.py:100
  354.0 33.1 %collective-permute-start.55 = (bf16[24,3840]{1,0:T(8,128)(2,1)S(1)}, bf16[24,3840]{1,0:T(8,128)(2,1)S(1)}, u32[]{:S(2)}, u32[]{:S(2)}) collective-permute-start(bf16[24,3840]{1,0:T(8,128)(2,1)S(1)} %copy-done.44), channel_id=1, source_target_pairs={{0,8},{1,9},{2,10},{3,11},{4,12},{5,13},{6,14},{7,15},{8,16},{9,17... | collective-permute-start | bytes 552968 | tf_op jit(solution)/shard_map/ppermute | solution.py:100
  354.6 32.5 %collective-permute-start.56 = (bf16[24,3840]{1,0:T(8,128)(2,1)S(1)}, bf16[24,3840]{1,0:T(8,128)(2,1)S(1)}, u32[]{:S(2)}, u32[]{:S(2)}) collective-permute-start(bf16[24,3840]{1,0:T(8,128)(2,1)S(1)} %copy-done.43), channel_id=1, source_target_pairs={{0,16},{1,17},{2,18},{3,19},{4,20},{5,21},{6,22},{7,23},{8,24},{9,... | collective-permute-start | bytes 552968 | tf_op jit(solution)/shard_map/ppermute | solution.py:100
  355.9 31.2 %collective-permute-start.57 = (bf16[24,3840]{1,0:T(8,128)(2,1)S(1)}, bf16[24,3840]{1,0:T(8,128)(2,1)}, u32[]{:S(2)}, u32[]{:S(2)}) collective-permute-start(bf16[24,3840]{1,0:T(8,128)(2,1)S(1)} %copy-done.42), channel_id=1, source_target_pairs={{0,24},{1,25},{2,26},{3,27},{4,28},{5,29},{6,30},{7,31},{8,0},{9,1... | collective-permute-start | bytes 552968 | tf_op jit(solution)/shard_map/ppermute | solution.py:100
  366.5 11.9 %collective-permute-start.51 = (bf16[4,2,24,1152]{3,2,1,0:T(8,128)(2,1)}, bf16[4,2,24,1152]{3,2,1,0:T(8,128)(2,1)S(1)}, u32[]{:S(2)}, u32[]{:S(2)}) collective-permute-start(bf16[4,2,24,1152]{3,2,1,0:T(8,128)(2,1)} %get-tuple-element.271), channel_id=1, source_target_pairs={{0,4},{1,5},{2,6},{3,7},{4,0},{5,1},{6,2},{7,3},{8,12},{9,13},{10,... | collective-permute-start | bytes 1327112 | tf_op jit(solution)/shard_map/ppermute | solution.py:100
  368.1 12.7 %collective-permute-start.52 = (bf16[4,2,24,1280]{3,2,1,0:T(8,128)(2,1)}, bf16[4,2,24,1280]{3,2,1,0:T(8,128)(2,1)S(1)}, u32[]{:S(2)}, u32[]{:S(2)}) collective-permute-start(bf16[4,2,24,1280]{3,2,1,0:T(8,128)(2,1)} %get-tuple-element.273), channel_id=1, source_target_pairs={{0,2},{1,3},{2,0},{3,1},{4,6},{5,7},{6,4},{7,5},{8,10},{9,11},{10,... | collective-permute-start | bytes 1474568 | tf_op jit(solution)/shard_map/ppermute | solution.py:100
  394.6 9.7 %collective-permute-start.59 = (bf16[24,2432]{1,0:T(8,128)(2,1)}, bf16[24,2432]{1,0:T(8,128)(2,1)S(1)}, u32[]{:S(2)}, u32[]{:S(2)}) collective-permute-start(bf16[24,2432]{1,0:T(8,128)(2,1)} %get-tuple-element.294), channel_id=1, source_target_pairs={{0,16},{1,17},{2,18},{3,19},{4,20},{5,21},{6,22},{7,23},{8,24},{9,... | collective-permute-start | bytes 350216 | tf_op jit(solution)/shard_map/ppermute | solution.py:100
  395.8 8.5 %collective-permute-start.60 = (bf16[24,2432]{1,0:T(8,128)(2,1)}, bf16[24,2432]{1,0:T(8,128)(2,1)S(1)}, u32[]{:S(2)}, u32[]{:S(2)}) collective-permute-start(bf16[24,2432]{1,0:T(8,128)(2,1)} %get-tuple-element.295), channel_id=1, source_target_pairs={{0,24},{1,25},{2,26},{3,27},{4,28},{5,29},{6,30},{7,31},{8,0},{9,1... | collective-permute-start | bytes 350216 | tf_op jit(solution)/shard_map/ppermute | solution.py:100
  (63 other events, 589.0 us)
